TPU v7x, 32 devices: a whole 2x2x4 slice. The times are simulated.
32 devices in a mesh: row: 4 (over y, x), col: 8 (over z, core).
Axes of the slice: x: 2, y: 2, z: 4, core: 2. Of those that a mesh axis runs over, the one named last changes fastest.
Arguments:
- tokens: bfloat16 [9216, 2048], P(('row', 'col')), may hold values from -6 to 6
- cotangent: bfloat16 [9216, 2048], P(('row', 'col')), may hold values from -6 to 6
- segment_numbers: int32 [9216], P('row'), may hold values from 0 to 8, as said below
- positions: int32 [9216], P('row'), may hold values from 0 to 2095, as said below
- attention_norm_gain: float32 [2048], P(('row', 'col')), may hold values from 0.1 to 1.9
- query_matrix: float32 [2048, 2048], P(('row', 'col')), may hold values from -0.1875 to 0.1875
- key_value_matrix: float32 [2048, 512], P(('row', 'col')), may hold values from -0.125 to 0.125
- output_matrix: float32 [2048, 2048], P(('row', 'col')), may hold values from -1 to 1
- output_adapter_first: float32 [2048, 256], P(('row', 'col')), may hold values from -1 to 1
- output_adapter_second: float32 [256, 2048], P(('row', 'col')), may hold values from -0.375 to 0.375
- feedforward_norm_gain: float32 [2048], P(('row', 'col')), may hold values from 0.1 to 1.9
- gate_matrix: float32 [2048, 16384], P('row', 'col'), may hold values from -0.125 to 0.125
- up_matrix: float32 [2048, 16384], P('row', 'col'), may hold values from -0.125 to 0.125
- down_matrix: float32 [2048, 16384], P('row', 'col'), may hold values from -0.046875 to 0.046875
- down_adapter_first: float32 [256, 16384], P('row', 'col'), may hold values from -0.046875 to 0.046875
- down_adapter_second: float32 [256, 2048], P(('row', 'col')), may hold values from -0.375 to 0.375
Outputs:
- layer_out: bfloat16 [9216, 2048], P(('row', 'col'))
- input_grad: bfloat16 [9216, 2048], P(('row', 'col'))
- grad_norm_attn: float32 [2048], P(('row', 'col'))
- grad_w_query: float32 [2048, 2048], P(('row', 'col'))
- grad_w_keyval: float32 [2048, 512], P(('row', 'col'))
- grad_w_out: float32 [2048, 2048], P(('row', 'col'))
- grad_lora_out_a: float32 [2048, 256], P(('row', 'col'))
- grad_lora_out_b: float32 [256, 2048], P(('row', 'col'))
- grad_norm_mlp: float32 [2048], P(('row', 'col'))
- grad_w_gate: float32 [2048, 16384], P('row', 'col')
- grad_w_up: float32 [2048, 16384], P('row', 'col')
- grad_w_down: float32 [2048, 16384], P('row', 'col')
- grad_lora_down_a: float32 [256, 16384], P('row', 'col')
- grad_lora_down_b: float32 [256, 2048], P(('row', 'col'))
Inputs may be any that keep to these rules, and one draw needn't show every extreme that they name: `segment_numbers`: in each block of 2304 tokens the first 2048 have id 0, the rest form 8 contiguous continuations with ids 1 to 8 in order, each of 16 to 48 tokens, one of exactly 48. `positions`: A prompt token's position is its index in the prompt; a continuation token's is 2048 plus its index in its continuation.
All inputs are finite; a program needn't handle non-finite values.
Results may differ from a plain program's by a relative error of at most 0.02.
The roundings to bfloat16 on the way count: a program that leaves them out, or rounds other values in their place, can miss the bound.
Values may be sent and summed in bfloat16 or wider, within the bound.
No kernel may reach another device: no remote copies, remote signals or barrier semaphores. Data moves between devices by JAX's collectives and lax.ppermute only.
A program may use at most 384 MiB of HBM per device.

v0:
```python
from functools import partial

import jax
import jax.numpy as jnp
from jax import lax
from jax.sharding import PartitionSpec as P

MODEL_WIDTH = 2048
NH = 8
HD = 256


masked_score = -1e30
epsilon = 1e-06
contract_last = (((1,), (1,)), ((), ()))
contract_first = (((0,), (0,)), ((), ()))


def convert_half(values):
    return values.astype(jnp.bfloat16)


def product(left_side, right_side, dims):
    return lax.dot_general(left_side, right_side, dims, preferred_element_type=jnp.float32)


def matrix_product(left_side, right_side):
    return jnp.dot(left_side, right_side, preferred_element_type=jnp.float32)


def rms_scale(values, gain):
    return values * lax.rsqrt(jnp.mean(values * values, axis=-1, keepdims=True) + epsilon) * gain


def rope_tables(positions):
    half_width = HD // 2
    inverse = 10000.0 ** (-jnp.arange(half_width, dtype=jnp.float32) * 2.0 / HD)
    angles = positions.astype(jnp.float32)[:, None] * inverse[None, :]
    return (jnp.cos(angles), jnp.sin(angles))


def rotate(tensor, cosine, sine_part):
    half_width = tensor.shape[-1] // 2
    leading = tensor[..., :half_width]
    trailing = tensor[..., half_width:]
    return jnp.concatenate(
        [leading * cosine - trailing * sine_part, trailing * cosine + leading * sine_part], axis=-1
    )


def unrotate(tensor, cosine, sine_part):
    half_width = tensor.shape[-1] // 2
    leading = tensor[..., :half_width]
    trailing = tensor[..., half_width:]
    return jnp.concatenate(
        [leading * cosine + trailing * sine_part, trailing * cosine - leading * sine_part], axis=-1
    )


def per_device(
    tokens,
    cotangent,
    segment_numbers,
    positions,
    attention_norm_gain,
    query_matrix,
    key_value_matrix,
    output_matrix,
    output_adapter_first,
    output_adapter_second,
    feedforward_norm_gain,
    gate_matrix,
    up_matrix,
    down_matrix,
    down_adapter_first,
    down_adapter_second,
):
    tok_dev = tokens.shape[0]
    group_len = segment_numbers.shape[0]
    row_total = tok_dev * NH
    start_row = lax.axis_index("col") * tok_dev
    scale = HD ** (-0.5)
    (
        gain_attn,
        query_weight,
        keyval_weight,
        out_weight,
        out_down,
        out_upper,
        gain_mlp,
        down_upper,
    ) = (
        lax.all_gather(convert_half(attention_norm_gain), ("row", "col"), axis=0, tiled=True),
        lax.all_gather(convert_half(query_matrix), ("row", "col"), axis=0, tiled=True),
        lax.all_gather(convert_half(key_value_matrix), ("row", "col"), axis=0, tiled=True),
        lax.all_gather(convert_half(output_matrix), ("row", "col"), axis=0, tiled=True),
        lax.all_gather(convert_half(output_adapter_first), ("row", "col"), axis=0, tiled=True),
        lax.all_gather(convert_half(output_adapter_second), ("row", "col"), axis=0, tiled=True),
        lax.all_gather(convert_half(feedforward_norm_gain), ("row", "col"), axis=0, tiled=True),
        lax.all_gather(convert_half(down_adapter_second), ("row", "col"), axis=0, tiled=True),
    )
    gain_attn = gain_attn.astype(jnp.float32)
    gain_mlp = gain_mlp.astype(jnp.float32)
    inputs = tokens.astype(jnp.float32)
    normed = convert_half(rms_scale(inputs, gain_attn))
    own_seg = lax.dynamic_slice_in_dim(segment_numbers, start_row, tok_dev)
    own_pos = lax.dynamic_slice_in_dim(positions, start_row, tok_dev)
    cosine, sine_part = rope_tables(own_pos)
    query_pre = matrix_product(normed, query_weight)
    query_rows = convert_half(
        rotate(query_pre.reshape(tok_dev, NH, HD), cosine[:, None, :], sine_part[:, None, :])
        * scale
    ).reshape(row_total, HD)
    keyval_pre = matrix_product(normed, keyval_weight)
    key_own = convert_half(rotate(keyval_pre[:, :HD], cosine, sine_part))
    value_own = convert_half(keyval_pre[:, HD:])
    key_rows, value_rows = (
        lax.all_gather(key_own, "col", axis=0, tiled=True),
        lax.all_gather(value_own, "col", axis=0, tiled=True),
    )
    row_index = start_row + jnp.arange(row_total, dtype=jnp.int32) // NH
    row_seg = jnp.repeat(own_seg, NH)
    block_count = group_len // group_len

    def block_scores(counter):
        offset = counter * group_len
        key_index = offset + jnp.arange(group_len, dtype=jnp.int32)
        allowed = (key_index[None, :] <= row_index[:, None]) & (
            (segment_numbers[None, :] == 0) | (segment_numbers[None, :] == row_seg[:, None])
        )
        scores = jnp.where(allowed, product(query_rows, key_rows, contract_last), masked_score)
        return (scores, key_rows, value_rows)

    def stats_pass(counter, carry_in):
        top_prev, total_prev = carry_in
        scores = block_scores(counter)[0]
        top_next = jnp.maximum(top_prev, jnp.max(scores, axis=1))
        total_next = total_prev * jnp.exp(top_prev - top_next) + jnp.sum(
            jnp.exp(scores - top_next[:, None]), axis=1
        )
        return (top_next, total_next)

    top_value, total_value = lax.fori_loop(
        0,
        block_count,
        stats_pass,
        (jnp.full((row_total,), masked_score, jnp.float32), jnp.zeros((row_total,), jnp.float32)),
    )
    log_norm = top_value + jnp.log(total_value)

    def mix_pass(counter, accum):
        scores, key_block, value_block = block_scores(counter)
        weights = convert_half(jnp.exp(scores - log_norm[:, None]))
        return accum + matrix_product(weights, value_block)

    mixed_rows = lax.fori_loop(0, block_count, mix_pass, jnp.zeros((row_total, HD), jnp.float32))
    head_context = convert_half(mixed_rows.reshape(tok_dev, NH * HD))
    output_rank_rows = convert_half(matrix_product(head_context, out_down))
    attention_result = matrix_product(head_context, out_weight) + matrix_product(
        output_rank_rows, out_upper
    )
    layer_state = inputs + attention_result
    normed_mlp = convert_half(rms_scale(layer_state, gain_mlp))
    gate_weight, up_weight, down_weight, rank_weight = (
        lax.all_gather(convert_half(gate_matrix), "row", axis=0, tiled=True),
        lax.all_gather(convert_half(up_matrix), "row", axis=0, tiled=True),
        lax.all_gather(convert_half(down_matrix), "row", axis=0, tiled=True),
        lax.all_gather(convert_half(down_adapter_first), "row", axis=0, tiled=True),
    )
    ffn_in = lax.all_gather(normed_mlp, "col", axis=0, tiled=True)
    gate_values = matrix_product(ffn_in, gate_weight)
    up_values = matrix_product(ffn_in, up_weight)
    hidden_activated = convert_half(jax.nn.gelu(gate_values, approximate=True) * up_values)
    summed = lax.psum_scatter(
        jnp.concatenate(
            [
                product(hidden_activated, down_weight, contract_last),
                product(hidden_activated, rank_weight, contract_last),
            ],
            axis=1,
        ).astype(jnp.bfloat16),
        "col",
        scatter_dimension=0,
        tiled=True,
    ).astype(jnp.float32)
    down_rank_rows = convert_half(summed[:, MODEL_WIDTH:])
    layer_out = convert_half(
        layer_state + summed[:, :MODEL_WIDTH] + matrix_product(down_rank_rows, down_upper)
    )
    cot_grad = cotangent.astype(jnp.float32)
    rank_grad = convert_half(product(cotangent, down_upper, contract_last))
    cot_rows, rank_rows = (
        lax.all_gather(cotangent, "col", axis=0, tiled=True),
        lax.all_gather(rank_grad, "col", axis=0, tiled=True),
    )
    hidden_grad = matrix_product(cot_rows, down_weight) + matrix_product(rank_rows, rank_weight)
    grad_down = product(cot_rows, hidden_activated, contract_first)
    grad_rank = product(rank_rows, hidden_activated, contract_first)
    gelu_out, gelu_pull = jax.vjp(partial(jax.nn.gelu, approximate=True), gate_values)
    gate_grad = convert_half(gelu_pull(hidden_grad * up_values)[0])
    up_grad = convert_half(hidden_grad * gelu_out)
    grad_gate = product(ffn_in, gate_grad, contract_first)
    grad_up = product(ffn_in, up_grad, contract_first)
    up_rows = lax.slice_in_dim(up_grad, 0, tok_dev * lax.axis_size("col"), axis=0)
    normed_grad = lax.psum_scatter(
        product(gate_grad, gate_weight, contract_last) + product(up_rows, up_weight, contract_last),
        "col",
        scatter_dimension=0,
        tiled=True,
    )
    gate_sum, up_sum, down_sum, rank_sum = (
        lax.psum_scatter(
            grad_gate.astype(jnp.bfloat16), "row", scatter_dimension=0, tiled=True
        ).astype(jnp.float32),
        lax.psum_scatter(
            grad_up.astype(jnp.bfloat16), "row", scatter_dimension=0, tiled=True
        ).astype(jnp.float32),
        lax.psum_scatter(
            grad_down.astype(jnp.bfloat16), "row", scatter_dimension=0, tiled=True
        ).astype(jnp.float32),
        lax.psum_scatter(
            grad_rank.astype(jnp.bfloat16), "row", scatter_dimension=0, tiled=True
        ).astype(jnp.float32),
    )
    state_out, norm_pull = jax.vjp(rms_scale, layer_state, gain_mlp)
    state_part, grad_gain_mlp = norm_pull(normed_grad)
    state_grad = cot_grad + state_part
    attn_grad = convert_half(state_grad)
    rank_out_grad = convert_half(product(attn_grad, out_upper, contract_last))
    context_grad = convert_half(
        product(attn_grad, out_weight, contract_last)
        + product(rank_out_grad, out_down, contract_last)
    )
    grad_rows = context_grad.reshape(row_total, HD)

    def delta_pass(counter, accum):
        scores, key_block, value_block = block_scores(counter)
        weights = jnp.exp(scores - log_norm[:, None])
        weight_grad = product(grad_rows, value_block, contract_last)
        return accum + jnp.sum(weights * weight_grad, axis=1)

    delta = lax.fori_loop(0, block_count, delta_pass, jnp.zeros((row_total,), jnp.float32))

    def grad_pass(counter, carry_in):
        query_acc, key_acc, value_acc = carry_in
        scores, key_block, value_block = block_scores(counter)
        weights = jnp.exp(scores - log_norm[:, None])
        weight_grad = product(grad_rows, value_block, contract_last)
        score_grad = convert_half(weights * (weight_grad - delta[:, None]))
        query_acc = query_acc + matrix_product(score_grad, key_block)
        key_acc = product(score_grad, query_rows, contract_first)
        value_acc = product(convert_half(weights), grad_rows, contract_first)
        return (query_acc, key_acc, value_acc)

    query_acc, key_acc, value_acc = lax.fori_loop(
        0,
        block_count,
        grad_pass,
        (
            jnp.zeros((row_total, HD), jnp.float32),
            jnp.zeros((group_len, HD), jnp.float32),
            jnp.zeros((group_len, HD), jnp.float32),
        ),
    )
    key_grad, value_grad = (
        lax.psum_scatter(
            key_acc.astype(jnp.bfloat16), "col", scatter_dimension=0, tiled=True
        ).astype(jnp.float32),
        lax.psum_scatter(
            value_acc.astype(jnp.bfloat16), "col", scatter_dimension=0, tiled=True
        ).astype(jnp.float32),
    )
    keyval_grad = convert_half(
        jnp.concatenate([unrotate(key_grad, cosine, sine_part), value_grad], axis=1)
    )
    query_grad = convert_half(
        unrotate(
            query_acc.reshape(tok_dev, NH, HD) * scale, cosine[:, None, :], sine_part[:, None, :]
        ).reshape(tok_dev, NH * HD)
    )
    normed_back = product(query_grad, query_weight, contract_last) + product(
        keyval_grad, keyval_weight, contract_last
    )
    normed_out, first_pull = jax.vjp(rms_scale, inputs, gain_attn)
    input_part, grad_gain_attn = first_pull(normed_back)
    input_grad = convert_half(state_grad + input_part)
    grad_query = product(normed, query_grad, contract_first)
    grad_keyval = product(normed, keyval_grad, contract_first)
    grad_out = product(head_context, attn_grad, contract_first)
    grad_out_upper = product(output_rank_rows, attn_grad, contract_first)
    grad_out_down = product(head_context, rank_out_grad, contract_first)
    grad_down_upper = product(down_rank_rows, cotangent, contract_first)
    sums = (
        lax.psum_scatter(grad_gain_attn, ("row", "col"), scatter_dimension=0, tiled=True),
        lax.psum_scatter(grad_query, ("row", "col"), scatter_dimension=0, tiled=True),
        lax.psum_scatter(grad_keyval, ("row", "col"), scatter_dimension=0, tiled=True),
        lax.psum_scatter(grad_out, ("row", "col"), scatter_dimension=0, tiled=True),
        lax.psum_scatter(grad_out_down, ("row", "col"), scatter_dimension=0, tiled=True),
        lax.psum_scatter(grad_out_upper, ("row", "col"), scatter_dimension=0, tiled=True),
        lax.psum_scatter(grad_gain_mlp, ("row", "col"), scatter_dimension=0, tiled=True),
        lax.psum_scatter(grad_down_upper, ("row", "col"), scatter_dimension=0, tiled=True),
    )
    results = (sums[0], sums[1], sums[2], sums[3], sums[4], sums[5], sums[6], sums[7])
    return (
        layer_out,
        input_grad,
        results[0],
        results[1],
        results[2],
        results[3],
        results[4],
        results[5],
        results[6],
        gate_sum,
        up_sum,
        down_sum,
        rank_sum,
        results[7],
    )


def solution(mesh):
    return jax.shard_map(
        per_device,
        mesh=mesh,
        in_specs=(
            P(("row", "col"), None),
            P(("row", "col"), None),
            P("row"),
            P("row"),
            P(("row", "col")),
            P(("row", "col"), None),
            P(("row", "col"), None),
            P(("row", "col"), None),
            P(("row", "col"), None),
            P(("row", "col"), None),
            P(("row", "col")),
            P("row", "col"),
            P("row", "col"),
            P("row", "col"),
            P("row", "col"),
            P(("row", "col"), None),
        ),
        out_specs=(
            P(("row", "col"), None),
            P(("row", "col"), None),
            P(("row", "col")),
            P(("row", "col"), None),
            P(("row", "col"), None),
            P(("row", "col"), None),
            P(("row", "col"), None),
            P(("row", "col"), None),
            P(("row", "col")),
            P("row", "col"),
            P("row", "col"),
            P("row", "col"),
            P("row", "col"),
            P(("row", "col"), None),
        ),
        check_vma=False,
    )
```

profile of v0, /device:TPU:0, one launch (start us, length us, event | category | flops | bytes accessed | tf_op | source)
XLA Modules:
  0.0 2645.9 jit_solution(12094815841941052341)
XLA Ops:
  12.5 42.2 %all-reduce.5 = (bf16[2048]{0:T(1024)(128)(2,1)S(1)}, bf16[2048]{0:T(1024)(128)(2,1)S(1)}) all-reduce(bf16[2048]{0:T(1024)(128)(2,1)S(1)} %dynamic-update-slice, bf16[2048]{0:T(1024)(128)(2,1)S(1)} %dynamic-update-slice.1), channel_id=1, replica_groups=mesh['row'=4,'col'=8] {'row','col'}, use_global_device_ids=true, to_apply=%add | all-reduce | flops 4096 | bytes 16384
  87.4 62.8 %all-gather.16.cloned.1.call-done = bf16[2048,2048]{1,0:T(8,128)(2,1)} async-done(((bf16[64,2048]{1,0:T(8,128)(2,1)}), bf16[2048,2048]{1,0:T(8,128)(2,1)}) %all-gather.16.cloned.1.call-update) | async-done | bytes 8388624 | tf_op jit(solution)/shard_map/all_gather | solution.py:94
  209.8 45.6 %all-gather.26.cloned.1.call-done = bf16[2048,256]{1,0:T(8,128)(2,1)} async-done(((bf16[64,256]{1,0:T(8,128)(2,1)}), bf16[2048,256]{1,0:T(8,128)(2,1)}) %all-gather.26.cloned.1.call-update) | async-done | bytes 1048592 | tf_op jit(solution)/shard_map/all_gather | solution.py:97
  257.1 77.8 %all-gather.24.cloned.1.call-done = bf16[2048,2048]{1,0:T(8,128)(2,1)} async-done(((bf16[64,2048]{1,0:T(8,128)(2,1)}), bf16[2048,2048]{1,0:T(8,128)(2,1)}) %all-gather.24.cloned.1.call-update) | async-done | bytes 8388624 | tf_op jit(solution)/shard_map/all_gather | solution.py:96
  342.3 48.7 %all-gather.28.cloned.1.call-done = bf16[256,2048]{1,0:T(8,128)(2,1)} async-done(((bf16[8,2048]{1,0:T(8,128)(2,1)}), bf16[256,2048]{1,0:T(8,128)(2,1)}) %all-gather.28.cloned.1.call-update) | async-done | bytes 1048592 | tf_op jit(solution)/shard_map/all_gather | solution.py:98
  402.1 45.3 %all-gather.40.cloned.1.call-done = bf16[256,2048]{1,0:T(8,128)(2,1)} async-done(((bf16[8,2048]{1,0:T(8,128)(2,1)}), bf16[256,2048]{1,0:T(8,128)(2,1)}) %all-gather.40.cloned.1.call-update) | async-done | bytes 1048592 | tf_op jit(solution)/shard_map/all_gather | solution.py:100
  449.8 86.5 %all-gather.36.cloned.1.call-done = bf16[2048,2048]{1,0:T(8,128)(2,1)} async-done(((bf16[512,2048]{1,0:T(8,128)(2,1)}), bf16[2048,2048]{1,0:T(8,128)(2,1)}) %all-gather.36.cloned.1.call-update) | async-done | bytes 8388624 | tf_op jit(solution)/shard_map/all_gather | solution.py:167
  536.3 92.2 %all-gather.42.cloned.1.call-done = bf16[2304,2048]{1,0:T(8,128)(2,1)} async-done(((bf16[288,2048]{1,0:T(8,128)(2,1)}), bf16[2304,2048]{1,0:T(8,128)(2,1)}) %all-gather.42.cloned.1.call-update) | async-done | bytes 9437200 | tf_op jit(solution)/shard_map/all_gather | solution.py:193
  628.5 26.8 %fusion.71 = f32[2304,2048]{1,0:T(8,128)} fusion(bf16[2304,2048]{1,0:T(8,128)(2,1)} %all-gather.42.cloned.1.call-done, bf16[2048,2048]{1,0:T(8,128)(2,1)} %all-gather.36.cloned.1.call-done), kind=kOutput, calls=%fused_computation.128 | convolution fusion | flops 19327352832 | bytes 36700160 | tf_op jit(solution)/shard_map/dot_general | solution.py:28
  655.3 61.5 %all-gather.32.cloned.1.call-done = bf16[2048,2048]{1,0:T(8,128)(2,1)} async-done(((bf16[512,2048]{1,0:T(8,128)(2,1)}), bf16[2048,2048]{1,0:T(8,128)(2,1)}) %all-gather.32.cloned.1.call-update) | async-done | bytes 8388624 | tf_op jit(solution)/shard_map/all_gather | solution.py:165
  716.8 92.8 %all-gather.30.cloned.1.call-done = bf16[2304,2048]{1,0:T(8,128)(2,1)} async-done(((bf16[288,2048]{1,0:T(8,128)(2,1)}), bf16[2304,2048]{1,0:T(8,128)(2,1)}) %all-gather.30.cloned.1.call-update) | async-done | bytes 9437200 | tf_op jit(solution)/shard_map/all_gather | solution.py:170
  809.6 26.4 fusion.69
  836.0 62.0 %all-gather.34.cloned.1.call-done = bf16[2048,2048]{1,0:T(8,128)(2,1)} async-done(((bf16[512,2048]{1,0:T(8,128)(2,1)}), bf16[2048,2048]{1,0:T(8,128)(2,1)}) %all-gather.34.cloned.1.call-update) | async-done | bytes 8388624 | tf_op jit(solution)/shard_map/all_gather | solution.py:166
  898.0 26.4 fusion.70
  926.8 24.9 all-gather.44.cloned.1.call-done
  951.7 33.0 %multiply_convert_fusion.1 = (bf16[2304,2048]{1,0:T(8,128)(2,1)}, bf16[2304,2048]{1,0:T(8,128)(2,1)}, bf16[2304,2048]{1,0:T(8,128)(2,1)}) fusion(f32[2304,2048]{1,0:T(8,128)} %fusion.69, f32[2304,2048]{1,0:T(8,128)} %fusion.70, f32[2304,2048]{1,0:T(8,128)} %fusion.71, bf16[2304,256]{1,0:T(8,128)(2,1)} %all-gather.44.cloned.1.call-done, ...), kind=kOutput, calls=%fused_computation.16 | convolution fusion | flops 2543321088 | bytes 87162880 | tf_op jit(solution)/shard_map/dot_general | solution.py:28
  984.7 26.5 %fusion.72 = f32[2304,2048]{1,0:T(8,128)} fusion(bf16[2304,2048]{1,0:T(8,128)(2,1)} %get-tuple-element.195, bf16[2048,2048]{1,0:T(8,128)(2,1)} %all-gather.32.cloned.1.call-done), kind=kOutput, calls=%fused_computation.129 | convolution fusion | flops 19327352832 | bytes 36700160 | tf_op jit(solution)/shard_map/dot_general | solution.py:24
  1011.2 29.0 %convolution_add_fusion.1 = f32[2304,2048]{1,0:T(8,128)} fusion(f32[2304,2048]{1,0:T(8,128)} %fusion.72, bf16[2304,2048]{1,0:T(8,128)(2,1)} %get-tuple-element.194, bf16[2048,2048]{1,0:T(8,128)(2,1)} %all-gather.34.cloned.1.call-done), kind=kOutput, calls=%fused_computation.21 | convolution fusion | flops 19332071424 | bytes 55574528 | tf_op jit(solution)/shard_map/dot_general | solution.py:24
  1077.2 150.8 %reduce-scatter.17.cloned.1.call-done = f32[288,2048]{1,0:T(8,128)} async-done(((f32[2304,2048]{1,0:T(8,128)}), f32[288,2048]{1,0:T(8,128)}) %reduce-scatter.17.cloned.1.call-update) | async-done | bytes 2359312 | tf_op jit(solution)/shard_map/reduce_scatter | solution.py:205
  1298.3 26.4 convolution_convert_fusion.2
  1324.8 26.4 convolution_convert_fusion.1
  1351.5 26.4 convert_bitcast_fusion
  1438.7 87.5 %reduce-scatter.33.cloned.1.call-done = bf16[512,2048]{1,0:T(8,128)(2,1)} async-done(((bf16[2048,2048]{1,0:T(8,128)(2,1)}), bf16[512,2048]{1,0:T(8,128)(2,1)}) %reduce-scatter.33.cloned.1.call-update) | async-done | bytes 2097168 | tf_op jit(solution)/shard_map/reduce_scatter | solution.py:212
  1530.3 85.3 %reduce-scatter.35.cloned.1.call-done = bf16[512,2048]{1,0:T(8,128)(2,1)} async-done(((bf16[2048,2048]{1,0:T(8,128)(2,1)}), bf16[512,2048]{1,0:T(8,128)(2,1)}) %reduce-scatter.35.cloned.1.call-update) | async-done | bytes 2097168 | tf_op jit(solution)/shard_map/reduce_scatter | solution.py:215
  1619.8 85.3 %reduce-scatter.37.cloned.1.call-done = bf16[512,2048]{0,1:T(8,128)(2,1)} async-done(((bf16[2048,2048]{0,1:T(8,128)(2,1)}), bf16[512,2048]{0,1:T(8,128)(2,1)}) %reduce-scatter.37.cloned.1.call-update) | async-done | bytes 2097168 | tf_op jit(solution)/shard_map/reduce_scatter | solution.py:218
  1720.7 39.7 %all-reduce.4 = (f32[2048]{0:T(1024)}, f32[2048]{0:T(1024)}) all-reduce(f32[2048]{0:T(1024)} %get-tuple-element.188, f32[2048]{0:T(1024)} %get-tuple-element.186), channel_id=6, replica_groups=mesh['row'=4,'col'=8] {'row','col'}, use_global_device_ids=true, to_apply=%region_12.13.clone | all-reduce | flops 4096 | bytes 32768
  1768.7 77.8 %reduce-scatter.41.cloned.1.call-done = f32[8,2048]{1,0:T(8,128)} async-done(((f32[256,2048]{1,0:T(8,128)}), f32[8,2048]{1,0:T(8,128)}) %reduce-scatter.41.cloned.1.call-update) | async-done | bytes 65552 | tf_op jit(solution)/shard_map/reduce_scatter | solution.py:301
  1846.4 137.5 %reduce-scatter.29.cloned.1.call-done = f32[64,256]{1,0:T(8,128)} async-done(((f32[2048,256]{1,0:T(8,128)}), f32[64,256]{1,0:T(8,128)}) %reduce-scatter.29.cloned.1.call-update) | async-done | bytes 65552 | tf_op jit(solution)/shard_map/reduce_scatter | solution.py:298
  1984.0 137.8 %reduce-scatter.31.cloned.1.call-done = f32[8,2048]{1,0:T(8,128)} async-done(((f32[256,2048]{1,0:T(8,128)}), f32[8,2048]{1,0:T(8,128)}) %reduce-scatter.31.cloned.1.call-update) | async-done | bytes 65552 | tf_op jit(solution)/shard_map/reduce_scatter | solution.py:299
  2121.8 143.3 %reduce-scatter.25.cloned.1.call-done = f32[64,512]{1,0:T(8,128)} async-done(((f32[2048,512]{1,0:T(8,128)}), f32[64,512]{1,0:T(8,128)}) %reduce-scatter.25.cloned.1.call-update) | async-done | bytes 131088 | tf_op jit(solution)/shard_map/reduce_scatter | solution.py:296
  2265.1 186.6 %reduce-scatter.23.cloned.1.call-done = f32[64,2048]{1,0:T(8,128)} async-done(((f32[2048,2048]{1,0:T(8,128)}), f32[64,2048]{1,0:T(8,128)}) %reduce-scatter.23.cloned.1.call-update) | async-done | bytes 524304 | tf_op jit(solution)/shard_map/reduce_scatter | solution.py:295
  2451.7 187.2 %reduce-scatter.27.cloned.1.call-done = f32[64,2048]{1,0:T(8,128)} async-done(((f32[2048,2048]{1,0:T(8,128)}), f32[64,2048]{1,0:T(8,128)}) %reduce-scatter.27.cloned.1.call-update) | async-done | bytes 524304 | tf_op jit(solution)/shard_map/reduce_scatter | solution.py:297
  (268 shorter events, 322.1 us)
Async XLA Ops:
  7.2 63.5 %all-gather.18.cloned.1.call-start = ((), (), s32[]{:S(2)}) async-start(), calls=%async_computation.15 | async-start | bytes 2162688 | tf_op jit(solution)/shard_map/all_gather | solution.py:95
  8.9 141.3 %all-gather.16.cloned.1.call-start = ((), (), s32[]{:S(2)}) async-start(), calls=%async_computation.14 | async-start | bytes 8650752 | tf_op jit(solution)/shard_map/all_gather | solution.py:94
  10.7 163.2 %all-gather.20.cloned.1.call-start = ((), (), s32[]{:S(2)}) async-start(), calls=%async_computation.16 | async-start | bytes 1327104 | tf_op jit(solution)/shard_map/all_gather | solution.py:118
  74.6 123.8 %all-gather.22.cloned.1.call-start = ((), (), s32[]{:S(2)}) async-start(), calls=%async_computation.17 | async-start | bytes 1327104 | tf_op jit(solution)/shard_map/all_gather | solution.py:119
  75.4 180.0 %all-gather.26.cloned.1.call-start = ((), (), s32[]{:S(2)}) async-start(), calls=%async_computation.19 | async-start | bytes 1081344 | tf_op jit(solution)/shard_map/all_gather | solution.py:97
  76.1 258.8 %all-gather.24.cloned.1.call-start = ((), (), s32[]{:S(2)}) async-start(), calls=%async_computation.18 | async-start | bytes 8650752 | tf_op jit(solution)/shard_map/all_gather | solution.py:96
  76.9 314.0 %all-gather.28.cloned.1.call-start = ((), (), s32[]{:S(2)}) async-start(), calls=%async_computation.20 | async-start | bytes 1081344 | tf_op jit(solution)/shard_map/all_gather | solution.py:98
  77.6 369.7 %all-gather.40.cloned.1.call-start = ((), (), s32[]{:S(2)}) async-start(), calls=%async_computation.27 | async-start | bytes 1081344 | tf_op jit(solution)/shard_map/all_gather | solution.py:100
  78.4 457.9 %all-gather.36.cloned.1.call-start = ((), (), s32[]{:S(2)}) async-start(), calls=%async_computation.24 | async-start | bytes 10485760 | tf_op jit(solution)/shard_map/all_gather | solution.py:167
  82.3 546.2 %all-gather.42.cloned.1.call-start = ((), (), s32[]{:S(2)}) async-start(), calls=%async_computation.28 | async-start | bytes 10616832 | tf_op jit(solution)/shard_map/all_gather | solution.py:193
  82.9 633.9 %all-gather.32.cloned.1.call-start = ((), (), s32[]{:S(2)}) async-start(), calls=%async_computation.22 | async-start | bytes 10485760 | tf_op jit(solution)/shard_map/all_gather | solution.py:165
  86.8 722.8 %all-gather.30.cloned.1.call-start = ((), (), s32[]{:S(2)}) async-start(), calls=%async_computation.21 | async-start | bytes 10616832 | tf_op jit(solution)/shard_map/all_gather | solution.py:170
  87.4 306.3 %copy-start.37 = (f32[2048]{0:T(1024)}, f32[2048]{0:T(1024)S(1)}, u32[]{:S(2)}) copy-start(f32[2048]{0:T(1024)S(1)} %convert_element_type.170) | copy-start | bytes 24580
  396.3 501.6 %all-gather.34.cloned.1.call-start = ((), (), s32[]{:S(2)}) async-start(), calls=%async_computation.23 | async-start | bytes 10485760 | tf_op jit(solution)/shard_map/all_gather | solution.py:166
  400.3 526.5 %all-gather.38.cloned.1.call-start = ((), (), s32[]{:S(2)}) async-start(), calls=%async_computation.25 | async-start | bytes 1310720 | tf_op jit(solution)/shard_map/all_gather | solution.py:168
  402.0 549.6 %all-gather.44.cloned.1.call-start = ((), (), s32[]{:S(2)}) async-start(), calls=%async_computation.29 | async-start | bytes 1327104 | tf_op jit(solution)/shard_map/all_gather | solution.py:194
  449.8 778.2 %reduce-scatter.17.cloned.1.call-start = ((), (), s32[]{:S(2)}) async-start(), calls=%async_computation.30 | async-start | bytes 21233664 | tf_op jit(solution)/shard_map/reduce_scatter | solution.py:205
  1040.2 337.8 %reduce-scatter.15.cloned.1.call-start = ((), (), s32[]{:S(2)}) async-start(), calls=%async_computation.26 | async-start | bytes 11943936 | tf_op jit(solution)/shard_map/reduce_scatter | solution.py:174
  1077.1 153.8 %copy-start.55 = (f32[288]{0:T(512)S(1)}, f32[288]{0:T(512)}, u32[]{:S(2)}) copy-start(f32[288]{0:T(512)} %copy-done.54) | copy-start | bytes 3460
  1077.1 153.8 %copy-start.8 = (bf16[288,2048]{1,0:T(8,128)(2,1)S(1)}, bf16[288,2048]{1,0:T(8,128)(2,1)}, u32[]{:S(2)}) copy-start(bf16[288,2048]{1,0:T(8,128)(2,1)} %param.17) | copy-start | bytes 3538948
  1077.1 309.4 %reduce-scatter.19.cloned.1.call-start = ((), (), s32[]{:S(2)}) async-start(), calls=%async_computation.31 | async-start | bytes 1327104 | tf_op jit(solution)/shard_map/reduce_scatter | solution.py:266
  1278.0 129.3 %reduce-scatter.21.cloned.1.call-start = ((), (), s32[]{:S(2)}) async-start(), calls=%async_computation.32 | async-start | bytes 1327104 | tf_op jit(solution)/shard_map/reduce_scatter | solution.py:269
  1289.6 147.3 %reduce-scatter.39.cloned.1.call-start = ((), (), s32[]{:S(2)}) async-start(), calls=%async_computation.41 | async-start | bytes 1310720 | tf_op jit(solution)/shard_map/reduce_scatter | solution.py:221
  1298.2 228.0 %reduce-scatter.33.cloned.1.call-start = ((), (), s32[]{:S(2)}) async-start(), calls=%async_computation.38 | async-start | bytes 10485760 | tf_op jit(solution)/shard_map/reduce_scatter | solution.py:212
  1324.7 290.9 %reduce-scatter.35.cloned.1.call-start = ((), (), s32[]{:S(2)}) async-start(), calls=%async_computation.39 | async-start | bytes 10485760 | tf_op jit(solution)/shard_map/reduce_scatter | solution.py:215
  1351.2 353.8 %reduce-scatter.37.cloned.1.call-start = ((), (), s32[]{:S(2)}) async-start(), calls=%async_computation.40 | async-start | bytes 10485760 | tf_op jit(solution)/shard_map/reduce_scatter | solution.py:218
  1377.9 468.5 %reduce-scatter.41.cloned.1.call-start = ((), (), s32[]{:S(2)}) async-start(), calls=%async_computation.42 | async-start | bytes 2162688 | tf_op jit(solution)/shard_map/reduce_scatter | solution.py:301
  1381.1 602.9 %reduce-scatter.29.cloned.1.call-start = ((), (), s32[]{:S(2)}) async-start(), calls=%async_computation.36 | async-start | bytes 2162688 | tf_op jit(solution)/shard_map/reduce_scatter | solution.py:298
  1383.3 738.5 %reduce-scatter.31.cloned.1.call-start = ((), (), s32[]{:S(2)}) async-start(), calls=%async_computation.37 | async-start | bytes 2162688 | tf_op jit(solution)/shard_map/reduce_scatter | solution.py:299
  1386.5 878.7 %reduce-scatter.25.cloned.1.call-start = ((), (), s32[]{:S(2)}) async-start(), calls=%async_computation.34 | async-start | bytes 4325376 | tf_op jit(solution)/shard_map/reduce_scatter | solution.py:296
  1411.8 1039.9 %reduce-scatter.23.cloned.1.call-start = ((), (), s32[]{:S(2)}) async-start(), calls=%async_computation.33 | async-start | bytes 17301504 | tf_op jit(solution)/shard_map/reduce_scatter | solution.py:295
  1428.6 1210.3 %reduce-scatter.27.cloned.1.call-start = ((), (), s32[]{:S(2)}) async-start(), calls=%async_computation.35 | async-start | bytes 17301504 | tf_op jit(solution)/shard_map/reduce_scatter | solution.py:297
  (56 other events, 1649.8 us)
Sparse Core Ops, SparseCore 0:
  11.6 59.1 all-gather.17
  74.3 75.9 all-gather.15
  152.5 21.4 all-gather.19
  176.0 22.4 all-gather.21
  201.9 53.4 all-gather.25
  258.8 76.0 all-gather.23
  338.4 52.4 all-gather.27
  394.5 52.7 all-gather.39
  449.8 86.4 all-gather.35
  537.7 90.6 all-gather.41
  630.9 85.8 all-gather.31
  718.9 90.6 all-gather.29
  812.1 85.8 all-gather.33
  900.3 26.4 all-gather.37
  928.8 22.7 all-gather.43
  1040.4 187.5 reduce-scatter.16
  1230.1 109.0 reduce-scatter.14
  1341.9 31.4 reduce-scatter.18
  1376.2 31.1 reduce-scatter.20
  1410.7 26.0 reduce-scatter.38
  1439.9 86.3 reduce-scatter.32
  1529.3 86.3 reduce-scatter.34
  1618.7 86.3 reduce-scatter.36
  1707.7 138.6 reduce-scatter.40
  1849.3 134.6 reduce-scatter.28
  1986.7 135.1 reduce-scatter.30
  2124.5 140.5 reduce-scatter.24
  2268.0 183.6 reduce-scatter.22
  2454.6 184.2 reduce-scatter.26
where the time goes:
time: 2650 us
  waiting for transfers between devices  2040 us (77%)
  matrix products  411 us (16%)
  blocking collectives  81.8 us (3%)
  other arithmetic  71.8 us (3%)
    dot_general x24, matrix products, product(): lax.dot_general(left_side, right_side, dims, preferred_element_type=jnp.f...  259 us
    reduce_scatter x1, waiting for transfers between devices, per_device(): lax.psum_scatter(grad_out, ('row', 'col'), scatter_dimension=0, tiled=True)  187 us
    reduce_scatter x1, waiting for transfers between devices, per_device(): lax.psum_scatter(grad_query, ('row', 'col'), scatter_dimension=0, tiled=T...  187 us
    dot_general x12, matrix products, matrix_product(): return jnp.dot(left_side, right_side, preferred_element_type=jnp.float32)  152 us
    reduce_scatter x1, waiting for transfers between devices, per_device(): lax.psum_scatter(product(gate_grad, gate_weight, contract_last) + product...  151 us
    reduce_scatter x1, waiting for transfers between devices, per_device(): lax.psum_scatter(grad_keyval, ('row', 'col'), scatter_dimension=0, tiled=...  143 us
    reduce_scatter x1, waiting for transfers between devices, per_device(): lax.psum_scatter(grad_out_upper, ('row', 'col'), scatter_dimension=0, til...  138 us
    reduce_scatter x1, waiting for transfers between devices, per_device(): lax.psum_scatter(grad_out_down, ('row', 'col'), scatter_dimension=0, tile...  138 us
  transfers between devices with their start and end apart: 29, of which 26 were waited for; matrix products, arithmetic and copies ran while one was open for 15% of the time, Pallas kernels for 0%

commit v1 on v0

v1 whole, which is shorter than its diff:
```python
from functools import partial

import jax
import jax.numpy as jnp
from jax import lax
from jax.sharding import PartitionSpec as P

MODEL_WIDTH = 2048
NH = 8
HD = 256


masked_score = -1e30
epsilon = 1e-06
contract_last = (((1,), (1,)), ((), ()))
contract_first = (((0,), (0,)), ((), ()))


def convert_half(values):
    return values.astype(jnp.bfloat16)


def product(left_side, right_side, dims):
    return lax.dot_general(left_side, right_side, dims, preferred_element_type=jnp.float32)


def matrix_product(left_side, right_side):
    return jnp.dot(left_side, right_side, preferred_element_type=jnp.float32)


def rms_scale(values, gain):
    return values * lax.rsqrt(jnp.mean(values * values, axis=-1, keepdims=True) + epsilon) * gain


def rope_tables(positions):
    half_width = HD // 2
    inverse = 10000.0 ** (-jnp.arange(half_width, dtype=jnp.float32) * 2.0 / HD)
    angles = positions.astype(jnp.float32)[:, None] * inverse[None, :]
    return (jnp.cos(angles), jnp.sin(angles))


def rotate(tensor, cosine, sine_part):
    half_width = tensor.shape[-1] // 2
    leading = tensor[..., :half_width]
    trailing = tensor[..., half_width:]
    return jnp.concatenate(
        [leading * cosine - trailing * sine_part, trailing * cosine + leading * sine_part], axis=-1
    )


def unrotate(tensor, cosine, sine_part):
    half_width = tensor.shape[-1] // 2
    leading = tensor[..., :half_width]
    trailing = tensor[..., half_width:]
    return jnp.concatenate(
        [leading * cosine + trailing * sine_part, trailing * cosine - leading * sine_part], axis=-1
    )


def is_power(count):
    return count & (count - 1) == 0


def swap(values, axis, size, bit):
    return lax.ppermute(values, axis, [(i, i ^ bit) for i in range(size)])


def partner(own, step, size):
    return own ^ step if is_power(size) else (own + step) % size


def source_step(own, block, size):
    return own ^ block if is_power(size) else (block - own) % size


def to_partner(values, axis, step, size):
    return lax.ppermute(values, axis, [(i, partner(i, step, size)) for i in range(size)])


def from_partner(values, axis, step, size):
    return lax.ppermute(values, axis, [(partner(i, step, size), i) for i in range(size)])


def reorder(values, order):
    width = values.shape[-1] // len(order)
    return jnp.concatenate(
        [lax.dynamic_slice_in_dim(values, place * width, width, axis=-1) for place in order], axis=-1
    )


def gather_rows(shard, size):
    if size != 4:
        return [shard] + [from_partner(shard, "row", step, size) for step in range(1, size)]
    half = shard.shape[0] // 2
    upper, lower = shard[:half], shard[half:]
    first_upper_y = swap(upper, "row", size, 2)
    first_lower_x = swap(lower, "row", size, 1)
    upper_x = swap(upper, "row", size, 1)
    lower_y = swap(lower, "row", size, 2)
    far_upper = swap(first_upper_y, "row", size, 1)
    far_lower = swap(first_lower_x, "row", size, 2)
    return [shard, upper_x, first_lower_x, first_upper_y, lower_y, far_upper, far_lower]


def scatter_rows(blocks, size):
    if size != 4:
        total = blocks[0].astype(jnp.float32)
        for step in range(1, size):
            total = total + to_partner(blocks[step], "row", step, size).astype(jnp.float32)
        return total
    own, near_x, near_y, far = blocks
    half = own.shape[0] // 2
    far_upper = swap(far[:half], "row", size, 1)
    far_lower = swap(far[half:], "row", size, 2)
    upper_x = swap(near_x[:half], "row", size, 1)
    lower_y = swap(near_y[half:], "row", size, 2)
    upper_y = swap(add_half(near_y[:half], far_upper), "row", size, 2)
    lower_x = swap(add_half(near_x[half:], far_lower), "row", size, 1)
    return jnp.concatenate(
        [
            add_full(own[:half], upper_x, upper_y),
            add_full(own[half:], lower_x, lower_y),
        ],
        axis=0,
    )


def add_half(first, second):
    return convert_half(first.astype(jnp.float32) + second.astype(jnp.float32))


def add_full(first, second, third):
    return first.astype(jnp.float32) + second.astype(jnp.float32) + third.astype(jnp.float32)


def halve(values, stages, bits, sizes):
    for place, (axis, bit) in enumerate(stages):
        dim = bits.index((axis, bit))
        own = (lax.axis_index(axis) // bit) % 2
        kept = lax.dynamic_slice_in_dim(values, own, 1, axis=dim)
        sent = lax.dynamic_slice_in_dim(values, 1 - own, 1, axis=dim)
        got = swap(sent, axis, sizes[axis], bit)
        values = kept.astype(jnp.float32) + got.astype(jnp.float32)
        if place < len(stages) - 1:
            values = convert_half(values)
    return values.reshape(values.shape[-2:])


def scatter_all(values, row_size, col_size):
    devices, rows, width = values.shape
    if not (is_power(row_size) and is_power(col_size)):
        return lax.psum_scatter(
            values.astype(jnp.float32), ("row", "col"), scatter_dimension=0, tiled=True
        ).reshape(rows, width)
    sizes = {"row": row_size, "col": col_size}
    row_bits = [("row", 1 << k) for k in reversed(range(row_size.bit_length() - 1))]
    col_bits = [("col", 1 << k) for k in reversed(range(col_size.bit_length() - 1))]
    bits = row_bits + col_bits
    shaped = convert_half(values).reshape((2,) * len(bits) + (rows, width))
    half = width // 2
    pieces = []
    for row_order, piece in (
        (row_bits, shaped[..., :half]),
        (row_bits[::-1], shaped[..., half:]),
    ):
        pieces.append(halve(piece, col_bits[-1:] + row_order + col_bits[:-1], bits, sizes))
    return jnp.concatenate(pieces, axis=-1)


def per_device(
    tokens,
    cotangent,
    segment_numbers,
    positions,
    attention_norm_gain,
    query_matrix,
    key_value_matrix,
    output_matrix,
    output_adapter_first,
    output_adapter_second,
    feedforward_norm_gain,
    gate_matrix,
    up_matrix,
    down_matrix,
    down_adapter_first,
    down_adapter_second,
):
    row_size = lax.axis_size("row")
    col_size = lax.axis_size("col")
    devices = row_size * col_size
    row_at = lax.axis_index("row")
    tok_dev, width = tokens.shape
    group_len = segment_numbers.shape[0]
    row_total = tok_dev * NH
    query_width = query_matrix.shape[1]
    adapter_rows = output_adapter_second.shape[0]
    gain_len = attention_norm_gain.shape[0]
    start_row = lax.axis_index("col") * tok_dev
    scale = HD ** (-0.5)
    order = [partner(row_at, step, row_size) for step in range(row_size)]
    back_order = [source_step(row_at, block, row_size) for block in range(row_size)]

    small_rows = 2 * adapter_rows + 1
    small_pad = -small_rows % 8
    small = jnp.concatenate(
        [
            convert_half(output_adapter_second),
            convert_half(down_adapter_second),
            jnp.concatenate(
                [
                    convert_half(attention_norm_gain),
                    convert_half(feedforward_norm_gain),
                    jnp.zeros((width - 2 * gain_len,), jnp.bfloat16),
                ]
            )[None],
            jnp.zeros((small_pad, width), jnp.bfloat16),
        ],
        axis=0,
    )[None]
    small = lax.all_gather(small, ("row", "col"), axis=0, tiled=True)
    out_upper = small[:, :adapter_rows].reshape(-1, width)
    down_upper = small[:, adapter_rows : 2 * adapter_rows].reshape(-1, width)
    gain_attn = small[:, 2 * adapter_rows, :gain_len].reshape(width).astype(jnp.float32)
    gain_mlp = (
        small[:, 2 * adapter_rows, gain_len : 2 * gain_len].reshape(width).astype(jnp.float32)
    )
    in_weight = lax.all_gather(
        jnp.concatenate([convert_half(query_matrix), convert_half(key_value_matrix)], axis=1),
        ("row", "col"),
        axis=0,
        tiled=True,
    )
    out_weight = lax.all_gather(
        jnp.concatenate([convert_half(output_matrix), convert_half(output_adapter_first)], axis=1),
        ("row", "col"),
        axis=0,
        tiled=True,
    )
    gate_weight = jnp.concatenate(gather_rows(convert_half(gate_matrix), row_size), axis=0)
    up_weight = jnp.concatenate(gather_rows(convert_half(up_matrix), row_size), axis=0)
    down_weight = jnp.concatenate(
        gather_rows(convert_half(down_matrix), row_size)
        + gather_rows(convert_half(down_adapter_first), row_size),
        axis=0,
    )

    cot_grad = cotangent.astype(jnp.float32)
    rank_grad = convert_half(product(cotangent, down_upper, contract_last))
    cot_rows = lax.all_gather(
        jnp.concatenate([reorder(cotangent, order), reorder(rank_grad, order)], axis=1),
        "col",
        axis=0,
        tiled=True,
    )

    inputs = tokens.astype(jnp.float32)
    normed = convert_half(rms_scale(inputs, gain_attn))
    own_seg = lax.dynamic_slice_in_dim(segment_numbers, start_row, tok_dev)
    own_pos = lax.dynamic_slice_in_dim(positions, start_row, tok_dev)
    cosine, sine_part = rope_tables(own_pos)
    in_pre = matrix_product(normed, in_weight)
    query_pre = in_pre[:, :query_width]
    keyval_pre = in_pre[:, query_width:]
    query_rows = convert_half(
        rotate(query_pre.reshape(tok_dev, NH, HD), cosine[:, None, :], sine_part[:, None, :])
        * scale
    ).reshape(row_total, HD)
    keyval_rows = lax.all_gather(
        jnp.concatenate(
            [
                convert_half(rotate(keyval_pre[:, :HD], cosine, sine_part)),
                convert_half(keyval_pre[:, HD:]),
            ],
            axis=1,
        ),
        "col",
        axis=0,
        tiled=True,
    )
    key_rows = keyval_rows[:, :HD]
    value_rows = keyval_rows[:, HD:]
    row_index = start_row + jnp.arange(row_total, dtype=jnp.int32) // NH
    row_seg = jnp.repeat(own_seg, NH)
    key_index = jnp.arange(group_len, dtype=jnp.int32)
    allowed = (key_index[None, :] <= row_index[:, None]) & (
        (segment_numbers[None, :] == 0) | (segment_numbers[None, :] == row_seg[:, None])
    )
    scores = jnp.where(allowed, product(query_rows, key_rows, contract_last), masked_score)
    top_value = jnp.max(scores, axis=1)
    total_value = jnp.sum(jnp.exp(scores - top_value[:, None]), axis=1)
    log_norm = top_value + jnp.log(total_value)
    probs = convert_half(jnp.exp(scores - log_norm[:, None]))
    mixed_rows = matrix_product(probs, value_rows)
    head_context = convert_half(mixed_rows.reshape(tok_dev, NH * HD))
    out_pre = matrix_product(head_context, out_weight)
    output_rank_rows = convert_half(out_pre[:, width:])
    layer_state = inputs + out_pre[:, :width] + matrix_product(output_rank_rows, out_upper)
    normed_mlp = convert_half(rms_scale(layer_state, gain_mlp))

    ffn_in = lax.all_gather(reorder(normed_mlp, order), "col", axis=0, tiled=True)
    gate_values = matrix_product(ffn_in, gate_weight)
    up_values = matrix_product(ffn_in, up_weight)
    hidden_activated = convert_half(jax.nn.gelu(gate_values, approximate=True) * up_values)
    summed = lax.psum_scatter(
        convert_half(product(hidden_activated, down_weight, contract_last)),
        "col",
        scatter_dimension=0,
        tiled=True,
    )
    down_rank_rows = reorder(summed[:, width:], back_order)
    layer_out = convert_half(
        layer_state
        + reorder(summed[:, :width], back_order).astype(jnp.float32)
        + matrix_product(down_rank_rows, down_upper)
    )

    grad_down = convert_half(product(cot_rows, hidden_activated, contract_first))
    hidden_grad = matrix_product(cot_rows, down_weight)
    gelu_out, gelu_pull = jax.vjp(partial(jax.nn.gelu, approximate=True), gate_values)
    gate_grad = convert_half(gelu_pull(hidden_grad * up_values)[0])
    up_grad = convert_half(hidden_grad * gelu_out)
    normed_grad = lax.psum_scatter(
        convert_half(
            product(gate_grad, gate_weight, contract_last)
            + product(up_grad, up_weight, contract_last)
        ),
        "col",
        scatter_dimension=0,
        tiled=True,
    )
    grad_gate = convert_half(product(ffn_in, gate_grad, contract_first))
    grad_up = convert_half(product(ffn_in, up_grad, contract_first))

    def blocks_of(values):
        size = values.shape[0] // row_size
        return [values[size * step : size * (step + 1)] for step in range(row_size)]

    down_sum = scatter_rows(blocks_of(grad_down[:width]), row_size)
    rank_sum = scatter_rows(blocks_of(grad_down[width:]), row_size)
    gate_sum = scatter_rows(blocks_of(grad_gate), row_size)
    up_sum = scatter_rows(blocks_of(grad_up), row_size)

    normed_grad = reorder(normed_grad, back_order).astype(jnp.float32)
    state_out, norm_pull = jax.vjp(rms_scale, layer_state, gain_mlp)
    state_part, grad_gain_mlp = norm_pull(normed_grad)
    state_grad = cot_grad + state_part
    attn_grad = convert_half(state_grad)
    rank_out_grad = convert_half(product(attn_grad, out_upper, contract_last))
    out_grad = jnp.concatenate([attn_grad, rank_out_grad], axis=1)
    context_grad = product(out_grad, out_weight, contract_last)
    grad_rows = convert_half(context_grad).reshape(row_total, HD)
    delta = jnp.sum(grad_rows.astype(jnp.float32) * mixed_rows, axis=1)
    weight_grad = product(grad_rows, value_rows, contract_last)
    score_grad = convert_half(probs.astype(jnp.float32) * (weight_grad - delta[:, None]))
    query_acc = matrix_product(score_grad, key_rows)
    key_acc = product(score_grad, query_rows, contract_first)
    value_acc = product(probs, grad_rows, contract_first)
    keyval_sum = lax.psum_scatter(
        jnp.concatenate([convert_half(key_acc), convert_half(value_acc)], axis=1),
        "col",
        scatter_dimension=0,
        tiled=True,
    ).astype(jnp.float32)
    query_grad = convert_half(
        unrotate(
            query_acc.reshape(tok_dev, NH, HD) * scale, cosine[:, None, :], sine_part[:, None, :]
        ).reshape(tok_dev, NH * HD)
    )
    in_grad = jnp.concatenate(
        [
            query_grad,
            convert_half(unrotate(keyval_sum[:, :HD], cosine, sine_part)),
            convert_half(keyval_sum[:, HD:]),
        ],
        axis=1,
    )
    normed_back = product(in_grad, in_weight, contract_last)
    normed_out, first_pull = jax.vjp(rms_scale, inputs, gain_attn)
    input_part, grad_gain_attn = first_pull(normed_back)
    input_grad = convert_half(state_grad + input_part)

    grad_out = product(head_context, out_grad, contract_first)
    grad_in = product(normed, in_grad, contract_first)
    grad_out_upper = product(output_rank_rows, attn_grad, contract_first)
    grad_down_upper = product(down_rank_rows, cotangent, contract_first)
    out_sum = scatter_all(grad_out.reshape(devices, -1, grad_out.shape[1]), row_size, col_size)
    upper_sum = scatter_all(
        jnp.concatenate(
            [
                grad_out_upper.reshape(devices, adapter_rows, width),
                grad_down_upper.reshape(devices, adapter_rows, width),
            ],
            axis=1,
        ),
        row_size,
        col_size,
    )
    in_sum = scatter_all(grad_in.reshape(devices, -1, grad_in.shape[1]), row_size, col_size)
    gain_sum = scatter_all(
        jnp.pad(
            jnp.stack(
                [
                    grad_gain_attn.reshape(devices, gain_len),
                    grad_gain_mlp.reshape(devices, gain_len),
                ],
                axis=1,
            ),
            ((0, 0), (0, 6), (0, 256 - gain_len)),
        ),
        row_size,
        col_size,
    )
    return (
        layer_out,
        input_grad,
        gain_sum[0, :gain_len],
        in_sum[:, :query_width],
        in_sum[:, query_width:],
        out_sum[:, :width],
        out_sum[:, width:],
        upper_sum[:adapter_rows],
        gain_sum[1, :gain_len],
        gate_sum,
        up_sum,
        down_sum,
        rank_sum,
        upper_sum[adapter_rows:],
    )


def solution(mesh):
    return jax.shard_map(
        per_device,
        mesh=mesh,
        in_specs=(
            P(("row", "col"), None),
            P(("row", "col"), None),
            P("row"),
            P("row"),
            P(("row", "col")),
            P(("row", "col"), None),
            P(("row", "col"), None),
            P(("row", "col"), None),
            P(("row", "col"), None),
            P(("row", "col"), None),
            P(("row", "col")),
            P("row", "col"),
            P("row", "col"),
            P("row", "col"),
            P("row", "col"),
            P(("row", "col"), None),
        ),
        out_specs=(
            P(("row", "col"), None),
            P(("row", "col"), None),
            P(("row", "col")),
            P(("row", "col"), None),
            P(("row", "col"), None),
            P(("row", "col"), None),
            P(("row", "col"), None),
            P(("row", "col"), None),
            P(("row", "col")),
            P("row", "col"),
            P("row", "col"),
            P("row", "col"),
            P("row", "col"),
            P(("row", "col"), None),
        ),
        check_vma=False,
    )
```

time: 2650 us -> 1360 us (0.51)
  waiting for transfers between devices: 2040 us -> 712 us
  starting transfers between devices: 2.06 us -> 87.2 us
  blocking collectives: 81.8 us -> 0 us
  local copies, waits for them, and re-layouts: 25.3 us -> 88.9 us
  matrix products: 411 us -> 372 us
    reduce_scatter x14 -> x3, waiting for transfers between devices: 1300 us -> 0.02 us  [the longest x1 0.02 us: per_device(): lax.psum_scatter(convert_half(product(gate_grad, gate_weight, contract_la...]
    all_gather x15 -> x6, waiting for transfers between devices: 740 us -> 220 us  [the longest x1 86.6 us: per_device(): lax.all_gather(jnp.concatenate([convert_half(query_matrix), convert_half(...]
    ppermute x0 -> x83, waiting for transfers between devices: none -> 491 us  [swap(): return lax.ppermute(values, axis, [(i, i ^ bit) for i in range(size)])]
    ppermute x0 -> x83, starting transfers between devices: none -> 86.3 us  [swap(): return lax.ppermute(values, axis, [(i, i ^ bit) for i in range(size)])]
    unnamed x2 -> x0, blocking collectives: 81.8 us -> none
    slice x1 -> x21, local copies, waits for them, and re-layouts: 0.68 us -> 28.3 us  [the longest x3 16.7 us: scatter_all(): shaped[..., :half]]
    dot_general x24 -> x18, matrix products: 259 us -> 238 us  [product(): lax.dot_general(left_side, right_side, dims, preferred_element_type=jnp.f...]
    dot_general x12 -> x9, matrix products: 152 us -> 135 us  [matrix_product(): return jnp.dot(left_side, right_side, preferred_element_type=jnp.float32)]
  transfers between devices with their start and end apart: 29 -> 92, of which waited for: 26 -> 51; matrix products, arithmetic and copies ran while one was open for 15% -> 28% of each run, Pallas kernels for 0% -> 0%
where the time goes in v1:
time: 1360 us
  waiting for transfers between devices  712 us (52%)
  matrix products  372 us (27%)
  local copies, waits for them, and re-layouts  88.9 us (7%)
  starting transfers between devices  87.2 us (6%)
  other arithmetic  83.6 us (6%)
  between operations  16.3 us (1%)
    ppermute x83, waiting for transfers between devices, swap(): return lax.ppermute(values, axis, [(i, i ^ bit) for i in range(size)])  491 us
    dot_general x18, matrix products, product(): lax.dot_general(left_side, right_side, dims, preferred_element_type=jnp.f...  238 us
    dot_general x9, matrix products, matrix_product(): return jnp.dot(left_side, right_side, preferred_element_type=jnp.float32)  135 us
    all_gather x1, waiting for transfers between devices, per_device(): lax.all_gather(jnp.concatenate([convert_half(query_matrix), convert_half(...  86.6 us
    ppermute x83, starting transfers between devices, swap(): return lax.ppermute(values, axis, [(i, i ^ bit) for i in range(size)])  86.3 us
    all_gather x1, waiting for transfers between devices, per_device(): small = lax.all_gather(small, ('row', 'col'), axis=0, tiled=True)  58.3 us
    all_gather x1, waiting for transfers between devices, per_device(): lax.all_gather(jnp.concatenate([convert_half(output_matrix), convert_half...  56.4 us
    convert_element_type x44, other arithmetic, convert_half(): return values.astype(jnp.bfloat16)  29.6 us
  transfers between devices with their start and end apart: 92, of which 51 were waited for; matrix products, arithmetic and copies ran while one was open for 28% of the time, Pallas kernels for 0%

profile of v1, /device:TPU:0, one launch (start us, length us, event | category | flops | bytes accessed | tf_op | source)
XLA Modules:
  0.0 1359.8 jit_solution(16223250133146245494)
XLA Ops:
  15.3 58.3 %all-gather.18.cloned.1.call-done = bf16[768,2048]{1,0:T(8,128)(2,1)} async-done(((bf16[24,2048]{1,0:T(8,128)(2,1)}), bf16[768,2048]{1,0:T(8,128)(2,1)}) %all-gather.18.cloned.1.call-update) | async-done | bytes 3145744 | tf_op jit(solution)/shard_map/all_gather | solution.py:220
  75.3 86.6 %all-gather.8.cloned.1.call-done = bf16[2048,2560]{1,0:T(8,128)(2,1)} async-done(((bf16[64,2560]{1,0:T(8,128)(2,1)}), bf16[2048,2560]{1,0:T(8,128)(2,1)}) %all-gather.8.cloned.1.call-update) | async-done | bytes 10485776 | tf_op jit(solution)/shard_map/all_gather | solution.py:227
  182.4 18.8 %all-gather.10.cloned.1.call-done = bf16[2304,512]{1,0:T(8,128)(2,1)} async-done(((bf16[288,512]{1,0:T(8,128)(2,1)}), bf16[2304,512]{1,0:T(8,128)(2,1)}) %all-gather.10.cloned.1.call-update) | async-done | bytes 2359312 | tf_op jit(solution)/shard_map/all_gather | solution.py:268
  229.1 56.4 %all-gather.12.cloned.1.call-done = bf16[2048,2304]{1,0:T(8,128)(2,1)} async-done(((bf16[64,2304]{1,0:T(8,128)(2,1)}), bf16[2048,2304]{1,0:T(8,128)(2,1)}) %all-gather.12.cloned.1.call-update) | async-done | bytes 9437200 | tf_op jit(solution)/shard_map/all_gather | solution.py:233
  309.1 17.2 %collective-permute-done.6 = bf16[256,2048]{1,0:T(8,128)(2,1)S(1)} collective-permute-done((bf16[256,2048]{1,0:T(8,128)(2,1)S(1)}, bf16[256,2048]{1,0:T(8,128)(2,1)S(1)}, u32[]{:S(2)}, u32[]{:S(2)}) %collective-permute-start.6) | collective-permute-done | bytes 1048608 | tf_op jit(solution)/shard_map/ppermute | solution.py:65
  327.9 20.9 %collective-permute-done.7 = bf16[256,2048]{1,0:T(8,128)(2,1)S(1)} collective-permute-done((bf16[256,2048]{1,0:T(8,128)(2,1)S(1)}, bf16[256,2048]{1,0:T(8,128)(2,1)S(1)}, u32[]{:S(2)}, u32[]{:S(2)}) %collective-permute-start.7) | collective-permute-done | bytes 1048608 | tf_op jit(solution)/shard_map/ppermute | solution.py:65
  352.7 18.5 %collective-permute-done.12 = bf16[256,2048]{1,0:T(8,128)(2,1)S(1)} collective-permute-done((bf16[256,2048]{1,0:T(8,128)(2,1)S(1)}, bf16[256,2048]{1,0:T(8,128)(2,1)S(1)}, u32[]{:S(2)}, u32[]{:S(2)}) %collective-permute-start.12) | collective-permute-done | bytes 1048608 | tf_op jit(solution)/shard_map/ppermute | solution.py:65
  373.8 19.9 %collective-permute-done.13 = bf16[256,2048]{1,0:T(8,128)(2,1)S(1)} collective-permute-done((bf16[256,2048]{1,0:T(8,128)(2,1)S(1)}, bf16[256,2048]{1,0:T(8,128)(2,1)S(1)}, u32[]{:S(2)}, u32[]{:S(2)}) %collective-permute-start.13) | collective-permute-done | bytes 1048608 | tf_op jit(solution)/shard_map/ppermute | solution.py:65
  400.4 15.8 %collective-permute-done = bf16[256,2048]{1,0:T(8,128)(2,1)S(1)} collective-permute-done((bf16[256,2048]{1,0:T(8,128)(2,1)S(1)}, bf16[256,2048]{1,0:T(8,128)(2,1)S(1)}, u32[]{:S(2)}, u32[]{:S(2)}) %collective-permute-start) | collective-permute-done | bytes 1048608 | tf_op jit(solution)/shard_map/ppermute | solution.py:65
  417.8 20.9 %collective-permute-done.1 = bf16[256,2048]{1,0:T(8,128)(2,1)S(1)} collective-permute-done((bf16[256,2048]{1,0:T(8,128)(2,1)S(1)}, bf16[256,2048]{1,0:T(8,128)(2,1)S(1)}, u32[]{:S(2)}, u32[]{:S(2)}) %collective-permute-start.1) | collective-permute-done | bytes 1048608 | tf_op jit(solution)/shard_map/ppermute | solution.py:65
  443.8 17.3 %collective-permute-done.16 = bf16[256,2048]{1,0:T(8,128)(2,1)S(1)} collective-permute-done((bf16[256,2048]{1,0:T(8,128)(2,1)S(1)}, bf16[256,2048]{1,0:T(8,128)(2,1)S(1)}, u32[]{:S(2)}, u32[]{:S(2)}) %collective-permute-start.16) | collective-permute-done | bytes 1048608 | tf_op jit(solution)/shard_map/ppermute | solution.py:65
  488.7 17.3 %collective-permute-done.4 = bf16[256,2048]{1,0:T(8,128)(2,1)S(1)} collective-permute-done((bf16[256,2048]{1,0:T(8,128)(2,1)S(1)}, bf16[256,2048]{1,0:T(8,128)(2,1)S(1)}, u32[]{:S(2)}, u32[]{:S(2)}) %collective-permute-start.4) | collective-permute-done | bytes 1048608 | tf_op jit(solution)/shard_map/ppermute | solution.py:65
  520.0 29.3 %fusion.88 = f32[2304,2048]{1,0:T(8,128)} fusion(bf16[2304,2304]{1,0:T(8,128)(2,1)} %all-gather.16.cloned.1.call-done, bf16[2304,2048]{1,0:T(8,128)(2,1)} %constant_dynamic-update-slice_fusion.14), kind=kOutput, calls=%fused_computation.317 | convolution fusion | flops 21743271936 | bytes 38928384 | tf_op jit(solution)/shard_map/dot_general | solution.py:28
  549.3 26.4 %fusion.87 = f32[2304,2048]{1,0:T(8,128)} fusion(bf16[2304,2048]{1,0:T(8,128)(2,1)} %all-gather.14.cloned.1.call-done, bf16[2048,2048]{1,0:T(8,128)(2,1)} %copy-done.55), kind=kOutput, calls=%fused_computation.316 | convolution fusion | flops 19327352832 | bytes 36700160 | tf_op jit(solution)/shard_map/dot_general | solution.py:28
  575.7 46.6 %fusion.8 = (bf16[2304,2048]{1,0:T(8,128)(2,1)}, bf16[2304,2048]{1,0:T(8,128)(2,1)}, bf16[2304,2048]{1,0:T(8,128)(2,1)}) fusion(f32[2304,2048]{1,0:T(8,128)} %fusion.88, f32[2304,2048]{1,0:T(8,128)} %fusion.87, bf16[2304,2048]{1,0:T(8,128)(2,1)} %all-gather.14.cloned.1.call-done, bf16[2048,2048]{1,0:T(8,128)(2,1)} %copy-done.54), kind=kOutput, calls=%fused_computation.14 | convolution fusion | flops 19450036224 | bytes 83886080 | tf_op jit(solution)/shard_map/dot_general | solution.py:28
  622.3 28.6 %convolution_convert_fusion = bf16[2304,2304]{1,0:T(8,128)(2,1)} fusion(bf16[2304,2048]{1,0:T(8,128)(2,1)} %get-tuple-element.30, bf16[2304,2048]{1,0:T(8,128)(2,1)} %constant_dynamic-update-slice_fusion.14), kind=kOutput, calls=%fused_computation.19 | convolution fusion | flops 21748580352 | bytes 29491200 | tf_op jit(solution)/shard_map/dot_general | solution.py:24
  654.2 27.6 %fusion.89 = f32[2304,2048]{1,0:T(8,128)} fusion(bf16[2304,2048]{1,0:T(8,128)(2,1)} %get-tuple-element.29, bf16[2048,2048]{1,0:T(8,128)(2,1)} %copy-done.55), kind=kOutput, calls=%fused_computation.318 | convolution fusion | flops 19327352832 | bytes 36700160 | tf_op jit(solution)/shard_map/dot_general | solution.py:24
  681.8 28.1 %add_convert_fusion = bf16[2304,2048]{1,0:T(8,128)(2,1)} fusion(f32[2304,2048]{1,0:T(8,128)} %fusion.89, bf16[2304,2048]{1,0:T(8,128)(2,1)} %get-tuple-element.28, bf16[2048,2048]{1,0:T(8,128)(2,1)} %copy-done.54), kind=kOutput, calls=%fused_computation.15 | convolution fusion | flops 19336790016 | bytes 46137344 | tf_op jit(solution)/shard_map/dot_general | solution.py:24
  709.9 28.0 %convolution_convert_fusion.1 = bf16[2304,2048]{1,0:T(8,128)(2,1)S(1)} fusion(bf16[2304,2304]{1,0:T(8,128)(2,1)} %all-gather.16.cloned.1.call-done, bf16[2304,2048]{1,0:T(8,128)(2,1)} %get-tuple-element.30), kind=kOutput, calls=%fused_computation.20 | convolution fusion | flops 21747990528 | bytes 29491200 | tf_op jit(solution)/shard_map/dot_general | solution.py:24
  745.0 24.9 %convolution_convert_fusion.4 = bf16[2048,2048]{1,0:T(8,128)(2,1)S(1)} fusion(bf16[2304,2048]{1,0:T(8,128)(2,1)} %all-gather.14.cloned.1.call-done, bf16[2304,2048]{1,0:T(8,128)(2,1)} %get-tuple-element.29), kind=kOutput, calls=%fused_computation.23 | convolution fusion | flops 19331547136 | bytes 27262976 | tf_op jit(solution)/shard_map/dot_general | solution.py:24
  769.9 25.3 %convolution_convert_fusion.5 = bf16[2048,2048]{1,0:T(8,128)(2,1)S(1)} fusion(bf16[2304,2048]{1,0:T(8,128)(2,1)} %all-gather.14.cloned.1.call-done, bf16[2304,2048]{1,0:T(8,128)(2,1)} %get-tuple-element.28), kind=kOutput, calls=%fused_computation.24 | convolution fusion | flops 19331547136 | bytes 27262976 | tf_op jit(solution)/shard_map/dot_general | solution.py:24
  805.7 21.4 %collective-permute-done.81 = bf16[32,2048]{1,0:T(8,128)(2,1)S(1)} collective-permute-done((bf16[32,2048]{1,0:T(8,128)(2,1)S(1)}, bf16[32,2048]{1,0:T(8,128)(2,1)S(1)}, u32[]{:S(2)}, u32[]{:S(2)}) %collective-permute-start.81) | collective-permute-done | bytes 131104 | tf_op jit(solution)/shard_map/ppermute | solution.py:65
  831.3 18.3 %collective-permute-done.66 = bf16[256,2048]{1,0:T(8,128)(2,1)S(1)} collective-permute-done((bf16[256,2048]{1,0:T(8,128)(2,1)S(1)}, bf16[256,2048]{1,0:T(8,128)(2,1)S(1)}, u32[]{:S(2)}, u32[]{:S(2)}) %collective-permute-start.66) | collective-permute-done | bytes 1048608 | tf_op jit(solution)/shard_map/ppermute | solution.py:65
  852.1 38.4 %collective-permute-done.60 = bf16[256,2048]{1,0:T(8,128)(2,1)S(1)} collective-permute-done((bf16[256,2048]{1,0:T(8,128)(2,1)}, bf16[256,2048]{1,0:T(8,128)(2,1)S(1)}, u32[]{:S(2)}, u32[]{:S(2)}) %collective-permute-start.60) | collective-permute-done | bytes 1048608 | tf_op jit(solution)/shard_map/ppermute | solution.py:65
  922.5 16.6 %collective-permute-done.62 = bf16[256,2048]{1,0:T(8,128)(2,1)} collective-permute-done((bf16[256,2048]{1,0:T(8,128)(2,1)S(1)}, bf16[256,2048]{1,0:T(8,128)(2,1)}, u32[]{:S(2)}, u32[]{:S(2)}) %collective-permute-start.62) | collective-permute-done | bytes 1048608 | tf_op jit(solution)/shard_map/ppermute | solution.py:65
  940.0 21.6 %collective-permute-done.61 = bf16[256,2048]{1,0:T(8,128)(2,1)} collective-permute-done((bf16[256,2048]{1,0:T(8,128)(2,1)S(1)}, bf16[256,2048]{1,0:T(8,128)(2,1)}, u32[]{:S(2)}, u32[]{:S(2)}) %collective-permute-start.61) | collective-permute-done | bytes 1048608 | tf_op jit(solution)/shard_map/ppermute | solution.py:65
  966.0 18.0 %collective-permute-done.76 = bf16[256,2048]{1,0:T(8,128)(2,1)S(1)} collective-permute-done((bf16[256,2048]{1,0:T(8,128)(2,1)}, bf16[256,2048]{1,0:T(8,128)(2,1)S(1)}, u32[]{:S(2)}, u32[]{:S(2)}) %collective-permute-start.76) | collective-permute-done | bytes 1048608 | tf_op jit(solution)/shard_map/ppermute | solution.py:65
  988.0 17.1 %collective-permute-done.70 = bf16[256,2048]{1,0:T(8,128)(2,1)} collective-permute-done((bf16[256,2048]{1,0:T(8,128)(2,1)}, bf16[256,2048]{1,0:T(8,128)(2,1)}, u32[]{:S(2)}, u32[]{:S(2)}) %collective-permute-start.70) | collective-permute-done | bytes 1048608 | tf_op jit(solution)/shard_map/ppermute | solution.py:65
  1150.0 19.8 %collective-permute-done.40 = bf16[1,2,2,2,1,64,1152]{6,5,4,3,2,1,0:T(8,128)(2,1)S(1)} collective-permute-done((bf16[1,2,2,2,1,64,1152]{6,5,4,3,2,1,0:T(8,128)(2,1)S(1)}, bf16[1,2,2,2,1,64,1152]{6,5,4,3,2,1,0:T(8,128)(2,1)S(1)}, u32[]{:S(2)}, u32[]{:S(2)}) %collective-permute-start.40) | collective-permute-done | bytes 1179680 | tf_op jit(solution)/shard_map/ppermute | solution.py:65
  1189.9 16.8 %collective-permute-done.42 = bf16[1,1,1,2,1,64,1152]{6,5,4,3,2,1,0:T(8,128)(2,1)S(1)} collective-permute-done((bf16[1,1,1,2,1,64,1152]{6,5,4,3,2,1,0:T(8,128)(2,1)S(1)}, bf16[1,1,1,2,1,64,1152]{6,5,4,3,2,1,0:T(8,128)(2,1)S(1)}, u32[]{:S(2)}, u32[]{:S(2)}) %collective-permute-start.42) | collective-permute-done | bytes 294944 | tf_op jit(solution)/shard_map/ppermute | solution.py:65
  1279.0 21.1 %collective-permute-done.35 = bf16[2,1,2,2,1,64,1280]{6,5,4,3,2,1,0:T(8,128)(2,1)S(1)} collective-permute-done((bf16[2,1,2,2,1,64,1280]{6,5,4,3,2,1,0:T(8,128)(2,1)S(1)}, bf16[2,1,2,2,1,64,1280]{6,5,4,3,2,1,0:T(8,128)(2,1)S(1)}, u32[]{:S(2)}, u32[]{:S(2)}) %collective-permute-start.35) | collective-permute-done | bytes 1310752 | tf_op jit(solution)/shard_map/ppermute | solution.py:65
  1319.2 19.9 %collective-permute-done.37 = bf16[1,1,1,2,1,64,1280]{6,5,4,3,2,1,0:T(8,128)(2,1)S(1)} collective-permute-done((bf16[1,1,1,2,1,64,1280]{6,5,4,3,2,1,0:T(8,128)(2,1)S(1)}, bf16[1,1,1,2,1,64,1280]{6,5,4,3,2,1,0:T(8,128)(2,1)S(1)}, u32[]{:S(2)}, u32[]{:S(2)}) %collective-permute-start.37) | collective-permute-done | bytes 327712 | tf_op jit(solution)/shard_map/ppermute | solution.py:65
  (606 shorter events, 482.1 us)
Async XLA Ops:
  7.2 66.4 %all-gather.18.cloned.1.call-start = ((), (), s32[]{:S(2)}) async-start(), calls=%async_computation.11 | async-start | bytes 3244032 | tf_op jit(solution)/shard_map/all_gather | solution.py:220
  11.3 150.7 %all-gather.8.cloned.1.call-start = ((), (), s32[]{:S(2)}) async-start(), calls=%async_computation.3 | async-start | bytes 10813440 | tf_op jit(solution)/shard_map/all_gather | solution.py:227
  14.1 187.1 %all-gather.10.cloned.1.call-start = ((), (), s32[]{:S(2)}) async-start(), calls=%async_computation.4 | async-start | bytes 2654208 | tf_op jit(solution)/shard_map/all_gather | solution.py:268
  171.0 114.4 %all-gather.12.cloned.1.call-start = ((), (), s32[]{:S(2)}) async-start(), calls=%async_computation.5 | async-start | bytes 9732096 | tf_op jit(solution)/shard_map/all_gather | solution.py:233
  171.9 348.1 %all-gather.16.cloned.1.call-start = ((), (), s32[]{:S(2)}) async-start(), calls=%async_computation.8 | async-start | bytes 11943936 | tf_op jit(solution)/shard_map/all_gather | solution.py:249
  177.6 371.7 %all-gather.14.cloned.1.call-start = ((), (), s32[]{:S(2)}) async-start(), calls=%async_computation.6 | async-start | bytes 10616832 | tf_op jit(solution)/shard_map/all_gather | solution.py:300
  296.9 723.9 %reduce-scatter.4.cloned.1.call-start = ((), (), s32[]{:S(2)}) async-start(), calls=%async_computation.7 | async-start | bytes 11943936 | tf_op jit(solution)/shard_map/reduce_scatter | solution.py:304
  306.3 65.0 %collective-permute-start.12 = (bf16[256,2048]{1,0:T(8,128)(2,1)S(1)}, bf16[256,2048]{1,0:T(8,128)(2,1)S(1)}, u32[]{:S(2)}, u32[]{:S(2)}) collective-permute-start(bf16[256,2048]{1,0:T(8,128)(2,1)S(1)} %get-tuple-element.66), channel_id=1, source_target_pairs={{0,8},{8,0},{16,24},{24,16},{1,9},{9,1},{17,25},{25,17},{2,10},{10... | collective-permute-start | bytes 3145736 | tf_op jit(solution)/shard_map/ppermute | solution.py:65
  326.3 67.4 %collective-permute-start.13 = (bf16[256,2048]{1,0:T(8,128)(2,1)S(1)}, bf16[256,2048]{1,0:T(8,128)(2,1)S(1)}, u32[]{:S(2)}, u32[]{:S(2)}) collective-permute-start(bf16[256,2048]{1,0:T(8,128)(2,1)S(1)} %get-tuple-element.65), channel_id=1, source_target_pairs={{0,8},{8,0},{16,24},{24,16},{1,9},{9,1},{17,25},{25,17},{2,10},{10... | collective-permute-start | bytes 3145736 | tf_op jit(solution)/shard_map/ppermute | solution.py:65
  351.1 65.1 %collective-permute-start = (bf16[256,2048]{1,0:T(8,128)(2,1)S(1)}, bf16[256,2048]{1,0:T(8,128)(2,1)S(1)}, u32[]{:S(2)}, u32[]{:S(2)}) collective-permute-start(bf16[256,2048]{1,0:T(8,128)(2,1)S(1)} %get-tuple-element.68), channel_id=1, source_target_pairs={{0,8},{8,0},{16,24},{24,16},{1,9},{9,1},{17,25},{25,17},{2,10},{10... | collective-permute-start | bytes 3145736 | tf_op jit(solution)/shard_map/ppermute | solution.py:65
  371.2 67.4 %collective-permute-start.1 = (bf16[256,2048]{1,0:T(8,128)(2,1)S(1)}, bf16[256,2048]{1,0:T(8,128)(2,1)S(1)}, u32[]{:S(2)}, u32[]{:S(2)}) collective-permute-start(bf16[256,2048]{1,0:T(8,128)(2,1)S(1)} %get-tuple-element.67), channel_id=1, source_target_pairs={{0,8},{8,0},{16,24},{24,16},{1,9},{9,1},{17,25},{25,17},{2,10},{10... | collective-permute-start | bytes 3145736 | tf_op jit(solution)/shard_map/ppermute | solution.py:65
  397.9 63.2 %collective-permute-start.16 = (bf16[256,2048]{1,0:T(8,128)(2,1)S(1)}, bf16[256,2048]{1,0:T(8,128)(2,1)S(1)}, u32[]{:S(2)}, u32[]{:S(2)}) collective-permute-start(bf16[256,2048]{1,0:T(8,128)(2,1)S(1)} %collective-permute-done.14), channel_id=1, source_target_pairs={{0,8},{8,0},{16,24},{24,16},{1,9},{9,1},{17,25},{25,17},{2,10},{10... | collective-permute-start | bytes 3145736 | tf_op jit(solution)/shard_map/ppermute | solution.py:65
  442.2 63.9 %collective-permute-start.4 = (bf16[256,2048]{1,0:T(8,128)(2,1)S(1)}, bf16[256,2048]{1,0:T(8,128)(2,1)S(1)}, u32[]{:S(2)}, u32[]{:S(2)}) collective-permute-start(bf16[256,2048]{1,0:T(8,128)(2,1)S(1)} %collective-permute-done.2), channel_id=1, source_target_pairs={{0,8},{8,0},{16,24},{24,16},{1,9},{9,1},{17,25},{25,17},{2,10},{10... | collective-permute-start | bytes 3145736 | tf_op jit(solution)/shard_map/ppermute | solution.py:65
  651.0 369.9 %reduce-scatter.6.cloned.1.call-start = ((), (), s32[]{:S(2)}) async-start(), calls=%async_computation.9 | async-start | bytes 10616832 | tf_op jit(solution)/shard_map/reduce_scatter | solution.py:322
  709.9 506.4 %reduce-scatter.8.cloned.1.call-start = ((), (), s32[]{:S(2)}) async-start(), calls=%async_computation.10 | async-start | bytes 2654208 | tf_op jit(solution)/shard_map/reduce_scatter | solution.py:358
  738.7 56.6 %collective-permute-start.78 = (bf16[32,2048]{1,0:T(8,128)(2,1)S(1)}, bf16[32,2048]{1,0:T(8,128)(2,1)S(1)}, u32[]{:S(2)}, u32[]{:S(2)}) collective-permute-start(bf16[32,2048]{1,0:T(8,128)(2,1)S(1)} %get-tuple-element.38), channel_id=1, source_target_pairs={{0,8},{8,0},{16,24},{24,16},{1,9},{9,1},{17,25},{25,17},{2,10},{10... | collective-permute-start | bytes 393224 | tf_op jit(solution)/shard_map/ppermute | solution.py:65
  739.1 59.0 %collective-permute-start.77 = (bf16[32,2048]{1,0:T(8,128)(2,1)S(1)}, bf16[32,2048]{1,0:T(8,128)(2,1)S(1)}, u32[]{:S(2)}, u32[]{:S(2)}) collective-permute-start(bf16[32,2048]{1,0:T(8,128)(2,1)S(1)} %get-tuple-element.35), channel_id=1, source_target_pairs={{0,8},{8,0},{16,24},{24,16},{1,9},{9,1},{17,25},{25,17},{2,10},{10... | collective-permute-start | bytes 393224 | tf_op jit(solution)/shard_map/ppermute | solution.py:65
  740.7 58.3 %collective-permute-start.80 = (bf16[32,2048]{1,0:T(8,128)(2,1)S(1)}, bf16[32,2048]{1,0:T(8,128)(2,1)S(1)}, u32[]{:S(2)}, u32[]{:S(2)}) collective-permute-start(bf16[32,2048]{1,0:T(8,128)(2,1)S(1)} %get-tuple-element.37), channel_id=1, source_target_pairs={{0,16},{8,24},{16,0},{24,8},{1,17},{9,25},{17,1},{25,9},{2,18},{10... | collective-permute-start | bytes 393224 | tf_op jit(solution)/shard_map/ppermute | solution.py:65
  741.4 64.0 %collective-permute-start.82 = (bf16[32,2048]{1,0:T(8,128)(2,1)}, bf16[32,2048]{1,0:T(8,128)(2,1)}, u32[]{:S(2)}, u32[]{:S(2)}) collective-permute-start(bf16[32,2048]{1,0:T(8,128)(2,1)} %get-tuple-element.36), channel_id=1, source_target_pairs={{0,16},{8,24},{16,0},{24,8},{1,17},{9,25},{17,1},{25,9},{2,18},{10... | collective-permute-start | bytes 393224 | tf_op jit(solution)/shard_map/ppermute | solution.py:65
  744.5 85.3 %collective-permute-start.72 = (bf16[256,2048]{1,0:T(8,128)(2,1)}, bf16[256,2048]{1,0:T(8,128)(2,1)S(1)}, u32[]{:S(2)}, u32[]{:S(2)}) collective-permute-start(bf16[256,2048]{1,0:T(8,128)(2,1)} %get-tuple-element.44), channel_id=1, source_target_pairs={{0,8},{8,0},{16,24},{24,16},{1,9},{9,1},{17,25},{25,17},{2,10},{10... | collective-permute-start | bytes 3145736 | tf_op jit(solution)/shard_map/ppermute | solution.py:65
  799.0 92.8 %collective-permute-start.74 = (bf16[256,2048]{1,0:T(8,128)(2,1)S(1)}, bf16[256,2048]{1,0:T(8,128)(2,1)S(1)}, u32[]{:S(2)}, u32[]{:S(2)}) collective-permute-start(bf16[256,2048]{1,0:T(8,128)(2,1)S(1)} %get-tuple-element.43), channel_id=1, source_target_pairs={{0,16},{8,24},{16,0},{24,8},{1,17},{9,25},{17,1},{25,9},{2,18},{10... | collective-permute-start | bytes 3145736 | tf_op jit(solution)/shard_map/ppermute | solution.py:65
  827.1 66.3 %collective-permute-start.65 = (bf16[256,2048]{1,0:T(8,128)(2,1)S(1)}, bf16[256,2048]{1,0:T(8,128)(2,1)S(1)}, u32[]{:S(2)}, u32[]{:S(2)}) collective-permute-start(bf16[256,2048]{1,0:T(8,128)(2,1)S(1)} %get-tuple-element.49), channel_id=1, source_target_pairs={{0,8},{8,0},{16,24},{24,16},{1,9},{9,1},{17,25},{25,17},{2,10},{10... | collective-permute-start | bytes 3145736 | tf_op jit(solution)/shard_map/ppermute | solution.py:65
  829.8 60.7 %collective-permute-start.60 = (bf16[256,2048]{1,0:T(8,128)(2,1)}, bf16[256,2048]{1,0:T(8,128)(2,1)S(1)}, u32[]{:S(2)}, u32[]{:S(2)}) collective-permute-start(bf16[256,2048]{1,0:T(8,128)(2,1)} %get-tuple-element.58), channel_id=1, source_target_pairs={{0,8},{8,0},{16,24},{24,16},{1,9},{9,1},{17,25},{25,17},{2,10},{10... | collective-permute-start | bytes 3145736 | tf_op jit(solution)/shard_map/ppermute | solution.py:65
  895.3 66.2 %collective-permute-start.61 = (bf16[256,2048]{1,0:T(8,128)(2,1)S(1)}, bf16[256,2048]{1,0:T(8,128)(2,1)}, u32[]{:S(2)}, u32[]{:S(2)}) collective-permute-start(bf16[256,2048]{1,0:T(8,128)(2,1)S(1)} %add_convert_fusion.14), channel_id=1, source_target_pairs={{0,16},{8,24},{16,0},{24,8},{1,17},{9,25},{17,1},{25,9},{2,18},{10... | collective-permute-start | bytes 3145736 | tf_op jit(solution)/shard_map/ppermute | solution.py:65
  900.2 83.7 %collective-permute-start.76 = (bf16[256,2048]{1,0:T(8,128)(2,1)}, bf16[256,2048]{1,0:T(8,128)(2,1)S(1)}, u32[]{:S(2)}, u32[]{:S(2)}) collective-permute-start(bf16[256,2048]{1,0:T(8,128)(2,1)} %get-tuple-element.42), channel_id=1, source_target_pairs={{0,16},{8,24},{16,0},{24,8},{1,17},{9,25},{17,1},{25,9},{2,18},{10... | collective-permute-start | bytes 3145736 | tf_op jit(solution)/shard_map/ppermute | solution.py:65
  916.6 68.3 %collective-permute-start.75 = (bf16[256,2048]{1,0:T(8,128)(2,1)}, bf16[256,2048]{1,0:T(8,128)(2,1)S(1)}, u32[]{:S(2)}, u32[]{:S(2)}) collective-permute-start(bf16[256,2048]{1,0:T(8,128)(2,1)} %get-tuple-element.40), channel_id=1, source_target_pairs={{0,8},{8,0},{16,24},{24,16},{1,9},{9,1},{17,25},{25,17},{2,10},{10... | collective-permute-start | bytes 3145736 | tf_op jit(solution)/shard_map/ppermute | solution.py:65
  921.1 84.0 %collective-permute-start.70 = (bf16[256,2048]{1,0:T(8,128)(2,1)}, bf16[256,2048]{1,0:T(8,128)(2,1)}, u32[]{:S(2)}, u32[]{:S(2)}) collective-permute-start(bf16[256,2048]{1,0:T(8,128)(2,1)} %get-tuple-element.50), channel_id=1, source_target_pairs={{0,16},{8,24},{16,0},{24,8},{1,17},{9,25},{17,1},{25,9},{2,18},{10... | collective-permute-start | bytes 3145736 | tf_op jit(solution)/shard_map/ppermute | solution.py:65
  939.1 77.2 %collective-permute-start.64 = (bf16[256,2048]{1,0:T(8,128)(2,1)}, bf16[256,2048]{1,0:T(8,128)(2,1)}, u32[]{:S(2)}, u32[]{:S(2)}) collective-permute-start(bf16[256,2048]{1,0:T(8,128)(2,1)} %get-tuple-element.56), channel_id=1, source_target_pairs={{0,16},{8,24},{16,0},{24,8},{1,17},{9,25},{17,1},{25,9},{2,18},{10... | collective-permute-start | bytes 3145736 | tf_op jit(solution)/shard_map/ppermute | solution.py:65
  1057.1 53.8 %collective-permute-start.49 = (bf16[2,2,2,2,1,16,1024]{6,5,4,3,2,1,0:T(8,128)(2,1)}, bf16[2,2,2,2,1,16,1024]{6,5,4,3,2,1,0:T(8,128)(2,1)}, u32[]{:S(2)}, u32[]{:S(2)}) collective-permute-start(bf16[2,2,2,2,1,16,1024]{6,5,4,3,2,1,0:T(8,128)(2,1)} %constant_dynamic-slice_fusion.8), channel_id=1, source_target_pairs={{0,1},{1,0},{2,3},{3,2},{4,5},{5,4},{6,7},{7,6},{8,9},{9,8},{10,11... | collective-permute-start | bytes 1572872 | tf_op jit(solution)/shard_map/ppermute | solution.py:65
  1057.1 56.5 %collective-permute-start.54 = (bf16[2,2,2,2,1,16,1024]{6,5,4,3,2,1,0:T(8,128)(2,1)}, bf16[2,2,2,2,1,16,1024]{6,5,4,3,2,1,0:T(8,128)(2,1)}, u32[]{:S(2)}, u32[]{:S(2)}) collective-permute-start(bf16[2,2,2,2,1,16,1024]{6,5,4,3,2,1,0:T(8,128)(2,1)} %fusion.32), channel_id=1, source_target_pairs={{0,1},{1,0},{2,3},{3,2},{4,5},{5,4},{6,7},{7,6},{8,9},{9,8},{10,11... | collective-permute-start | bytes 1572872 | tf_op jit(solution)/shard_map/ppermute | solution.py:65
  1077.8 62.7 %collective-permute-start.39 = (bf16[2,2,2,2,1,64,1152]{6,5,4,3,2,1,0:T(8,128)(2,1)}, bf16[2,2,2,2,1,64,1152]{6,5,4,3,2,1,0:T(8,128)(2,1)}, u32[]{:S(2)}, u32[]{:S(2)}) collective-permute-start(bf16[2,2,2,2,1,64,1152]{6,5,4,3,2,1,0:T(8,128)(2,1)} %constant_dynamic-slice_fusion.18), channel_id=1, source_target_pairs={{0,1},{1,0},{2,3},{3,2},{4,5},{5,4},{6,7},{7,6},{8,9},{9,8},{10,11... | collective-permute-start | bytes 7077896 | tf_op jit(solution)/shard_map/ppermute | solution.py:65
  1079.4 66.1 %collective-permute-start.44 = (bf16[2,2,2,2,1,64,1152]{6,5,4,3,2,1,0:T(8,128)(2,1)}, bf16[2,2,2,2,1,64,1152]{6,5,4,3,2,1,0:T(8,128)(2,1)}, u32[]{:S(2)}, u32[]{:S(2)}) collective-permute-start(bf16[2,2,2,2,1,64,1152]{6,5,4,3,2,1,0:T(8,128)(2,1)} %constant_dynamic-slice_fusion.13), channel_id=1, source_target_pairs={{0,1},{1,0},{2,3},{3,2},{4,5},{5,4},{6,7},{7,6},{8,9},{9,8},{10,11... | collective-permute-start | bytes 7077896 | tf_op jit(solution)/shard_map/ppermute | solution.py:65
  (168 other events, 3003.7 us)
Sparse Core Ops, SparseCore 0:
  11.6 61.9 all-gather.17
  77.0 84.8 all-gather.7
  171.1 30.0 all-gather.9
  204.6 80.7 all-gather.11
  287.5 98.9 all-gather.15
  388.6 89.0 all-gather.13
  651.1 109.7 reduce-scatter.3
  763.2 97.8 reduce-scatter.5
  1098.8 37.2 reduce-scatter.7

commit v2 on v1

v2 whole, which is shorter than its diff:
```python
from functools import partial

import jax
import jax.numpy as jnp
from jax import lax
from jax.sharding import PartitionSpec as P

MODEL_WIDTH = 2048
NH = 8
HD = 256


masked_score = -1e30
epsilon = 1e-06
contract_last = (((1,), (1,)), ((), ()))
contract_first = (((0,), (0,)), ((), ()))


def convert_half(values):
    return values.astype(jnp.bfloat16)


def product(left_side, right_side, dims):
    return lax.dot_general(left_side, right_side, dims, preferred_element_type=jnp.float32)


def matrix_product(left_side, right_side):
    return jnp.dot(left_side, right_side, preferred_element_type=jnp.float32)


def rms_scale(values, gain):
    return values * lax.rsqrt(jnp.mean(values * values, axis=-1, keepdims=True) + epsilon) * gain


def rope_tables(positions):
    half_width = HD // 2
    inverse = 10000.0 ** (-jnp.arange(half_width, dtype=jnp.float32) * 2.0 / HD)
    angles = positions.astype(jnp.float32)[:, None] * inverse[None, :]
    return (jnp.cos(angles), jnp.sin(angles))


def rotate(tensor, cosine, sine_part):
    half_width = tensor.shape[-1] // 2
    leading = tensor[..., :half_width]
    trailing = tensor[..., half_width:]
    return jnp.concatenate(
        [leading * cosine - trailing * sine_part, trailing * cosine + leading * sine_part], axis=-1
    )


def unrotate(tensor, cosine, sine_part):
    half_width = tensor.shape[-1] // 2
    leading = tensor[..., :half_width]
    trailing = tensor[..., half_width:]
    return jnp.concatenate(
        [leading * cosine + trailing * sine_part, trailing * cosine - leading * sine_part], axis=-1
    )


def is_power(count):
    return count & (count - 1) == 0


def swap(values, axis, size, bit):
    return lax.ppermute(values, axis, [(i, i ^ bit) for i in range(size)])


def partner(own, step, size):
    return own ^ step if is_power(size) else (own + step) % size


def source_step(own, block, size):
    return own ^ block if is_power(size) else (block - own) % size


def to_partner(values, axis, step, size):
    return lax.ppermute(values, axis, [(i, partner(i, step, size)) for i in range(size)])


def from_partner(values, axis, step, size):
    return lax.ppermute(values, axis, [(partner(i, step, size), i) for i in range(size)])


def reorder(values, order):
    width = values.shape[-1] // len(order)
    return jnp.concatenate(
        [lax.dynamic_slice_in_dim(values, place * width, width, axis=-1) for place in order], axis=-1
    )


def tie(*values):
    return lax.optimization_barrier(values)


def place_blocks(blocks, places, count):
    rows = blocks[0].shape[0]
    whole = jnp.zeros((rows * count, blocks[0].shape[1]), blocks[0].dtype)
    for block, place in zip(blocks, places):
        whole = lax.dynamic_update_slice_in_dim(whole, block, place * rows, axis=0)
    return whole


def rows_of(pieces, start, stop):
    found = []
    for parts in pieces:
        offset = 0
        for part in parts:
            first, last = max(start - offset, 0), min(stop - offset, part.shape[0])
            if first < last:
                found.append(part[first:last])
            offset += part.shape[0]
    return jnp.concatenate(found, axis=0)


def far_round(blocks, size):
    if size != 4:
        return blocks
    far = blocks[3]
    half = far.shape[0] // 2
    return [
        blocks[0],
        blocks[1],
        blocks[2],
        swap(far[:half], "row", size, 1),
        swap(far[half:], "row", size, 2),
    ]


def near_sums(state, size):
    if size != 4:
        return state
    own, near_x, near_y, far_upper, far_lower = state
    half = own.shape[0] // 2
    near_x = jnp.concatenate([near_x[:half], add_half(near_x[half:], far_lower)], axis=0)
    near_y = jnp.concatenate([add_half(near_y[:half], far_upper), near_y[half:]], axis=0)
    return [own, near_x, near_y]


def near_round(state, size):
    if size != 4:
        return [state[0]] + [
            to_partner(state[step], "row", step, size) for step in range(1, size)
        ]
    own, near_x, near_y = state
    return [own, swap(near_x, "row", size, 1), swap(near_y, "row", size, 2)]


def add_all(state):
    total = state[0].astype(jnp.float32)
    for part in state[1:]:
        total = total + part.astype(jnp.float32)
    return total


def add_half(first, second):
    return convert_half(first.astype(jnp.float32) + second.astype(jnp.float32))


def halve(values, stages, bits, sizes):
    for place, (axis, bit) in enumerate(stages):
        dim = bits.index((axis, bit))
        own = (lax.axis_index(axis) // bit) % 2
        kept = lax.dynamic_slice_in_dim(values, own, 1, axis=dim)
        sent = lax.dynamic_slice_in_dim(values, 1 - own, 1, axis=dim)
        got = swap(sent, axis, sizes[axis], bit)
        values = kept.astype(jnp.float32) + got.astype(jnp.float32)
        if place < len(stages) - 1:
            values = convert_half(values)
    return values.reshape(values.shape[-2:])


def scatter_all(values, row_size, col_size, pieces=2):
    devices, rows, width = values.shape
    if not (is_power(row_size) and is_power(col_size)):
        return lax.psum_scatter(
            values.astype(jnp.float32), ("row", "col"), scatter_dimension=0, tiled=True
        ).reshape(rows, width)
    sizes = {"row": row_size, "col": col_size}
    row_bits = [("row", 1 << k) for k in reversed(range(row_size.bit_length() - 1))]
    col_bits = [("col", 1 << k) for k in reversed(range(col_size.bit_length() - 1))]
    bits = row_bits + col_bits
    shaped = convert_half(values).reshape((2,) * len(bits) + (rows, width))
    part = width // pieces
    sums = []
    for place in range(pieces):
        order = row_bits if place % 2 == 0 else row_bits[::-1]
        piece = shaped[..., part * place : part * (place + 1)]
        sums.append(halve(piece, col_bits[-1:] + order + col_bits[:-1], bits, sizes))
    return jnp.concatenate(sums, axis=-1)


def per_device(
    tokens,
    cotangent,
    segment_numbers,
    positions,
    attention_norm_gain,
    query_matrix,
    key_value_matrix,
    output_matrix,
    output_adapter_first,
    output_adapter_second,
    feedforward_norm_gain,
    gate_matrix,
    up_matrix,
    down_matrix,
    down_adapter_first,
    down_adapter_second,
):
    row_size = lax.axis_size("row")
    col_size = lax.axis_size("col")
    devices = row_size * col_size
    row_at = lax.axis_index("row")
    tok_dev, width = tokens.shape
    group_len = segment_numbers.shape[0]
    row_total = tok_dev * NH
    query_width = query_matrix.shape[1]
    adapter_rows = output_adapter_second.shape[0]
    gain_len = attention_norm_gain.shape[0]
    start_row = lax.axis_index("col") * tok_dev
    scale = HD ** (-0.5)
    order = [partner(row_at, step, row_size) for step in range(row_size)]
    back_order = [source_step(row_at, block, row_size) for block in range(row_size)]

    in_gathered = lax.all_gather(
        jnp.concatenate(
            [
                convert_half(query_matrix),
                convert_half(key_value_matrix),
                convert_half(
                    jnp.pad(
                        jnp.stack([attention_norm_gain, feedforward_norm_gain], axis=1),
                        ((0, 0), (0, 126)),
                    )
                ),
            ],
            axis=1,
        ),
        ("row", "col"),
        axis=0,
        tiled=True,
    )
    shard = jnp.concatenate(
        [
            convert_half(gate_matrix),
            convert_half(up_matrix),
            convert_half(down_matrix),
            convert_half(down_adapter_first),
        ],
        axis=0,
    )
    model_rows = gate_matrix.shape[0]
    by_pairs = row_size == 4 and col_size == 8
    cot_grad = cotangent.astype(jnp.float32)
    cot_mixed = reorder(cotangent, order)
    if by_pairs:
        half = shard.shape[0] // 2
        upper, lower = shard[:half], shard[half:]
        upper_y = swap(upper, "row", 4, 2)
        lower_x = swap(lower, "row", 4, 1)
        cot_two = swap(cot_mixed, "col", 8, 2)
        cot_four = swap(cot_mixed, "col", 8, 4)
        in_gathered, upper_y, lower_x, cot_two, cot_four, upper, lower, cot_last = tie(
            in_gathered, upper_y, lower_x, cot_two, cot_four, upper, lower, cot_mixed
        )
        upper_x = swap(upper, "row", 4, 1)
        lower_y = swap(lower, "row", 4, 2)
        cot_six = swap(cot_last, "col", 8, 6)
    in_width = in_gathered.shape[1] - 128
    in_weight = in_gathered[:, :in_width]
    gains = in_gathered[:, in_width:].astype(jnp.float32)
    gain_attn = gains[:, 0]
    gain_mlp = gains[:, 1]
    own_seg = lax.dynamic_slice_in_dim(segment_numbers, start_row, tok_dev)
    own_pos = lax.dynamic_slice_in_dim(positions, start_row, tok_dev)
    cosine, sine_part = rope_tables(own_pos)
    inputs = tokens.astype(jnp.float32)
    normed = convert_half(rms_scale(inputs, gain_attn))
    in_pre = matrix_product(normed, in_weight)
    query_pre = in_pre[:, :query_width]
    keyval_pre = in_pre[:, query_width:]
    query_rows = convert_half(
        rotate(query_pre.reshape(tok_dev, NH, HD), cosine[:, None, :], sine_part[:, None, :])
        * scale
    ).reshape(row_total, HD)
    keyval_rows = lax.all_gather(
        jnp.concatenate(
            [
                convert_half(rotate(keyval_pre[:, :HD], cosine, sine_part)),
                convert_half(keyval_pre[:, HD:]),
            ],
            axis=1,
        ),
        "col",
        axis=0,
        tiled=True,
    )
    out_packed = jnp.concatenate(
        [
            convert_half(output_matrix),
            convert_half(output_adapter_first),
            convert_half(output_adapter_second).reshape(gain_len, -1),
            convert_half(down_adapter_second).reshape(gain_len, -1),
        ],
        axis=1,
    )
    if by_pairs:
        (
            keyval_rows,
            out_packed,
            upper_x,
            lower_y,
            cot_six,
            upper_y,
            lower_x,
            cot_mixed,
            cot_two,
            cot_four,
        ) = tie(
            keyval_rows,
            out_packed,
            upper_x,
            lower_y,
            cot_six,
            upper_y,
            lower_x,
            cot_mixed,
            cot_two,
            cot_four,
        )
        far_upper = swap(upper_y, "row", 4, 1)
        far_lower = swap(lower_x, "row", 4, 2)
        cot_mine = jnp.concatenate([cot_mixed, cot_two, cot_four, cot_six], axis=0)
        cot_other = swap(cot_mine, "col", 8, 1)
    else:
        keyval_rows, out_packed = tie(keyval_rows, out_packed)
    out_gathered = lax.all_gather(out_packed, ("row", "col"), axis=0, tiled=True)
    key_rows = keyval_rows[:, :HD]
    value_rows = keyval_rows[:, HD:]
    row_index = start_row + jnp.arange(row_total, dtype=jnp.int32) // NH
    row_seg = jnp.repeat(own_seg, NH)
    key_index = jnp.arange(group_len, dtype=jnp.int32)
    allowed = (key_index[None, :] <= row_index[:, None]) & (
        (segment_numbers[None, :] == 0) | (segment_numbers[None, :] == row_seg[:, None])
    )
    scores = jnp.where(allowed, product(query_rows, key_rows, contract_last), masked_score)
    top_value = jnp.max(scores, axis=1)
    total_value = jnp.sum(jnp.exp(scores - top_value[:, None]), axis=1)
    log_norm = top_value + jnp.log(total_value)
    probs = convert_half(jnp.exp(scores - log_norm[:, None]))
    mixed_rows = matrix_product(probs, value_rows)
    head_context = convert_half(mixed_rows.reshape(tok_dev, NH * HD))
    if by_pairs:
        out_gathered, far_upper, far_lower, cot_other, head_context = tie(
            out_gathered, far_upper, far_lower, cot_other, head_context
        )
        pieces = [[shard], [upper_x, lower_x], [upper_y, lower_y], [far_upper, far_lower]]
        places = [lax.axis_index("col") ^ (2 * step) for step in range(4)]
        cot_rows = place_blocks(
            [cot_mine[tok_dev * step : tok_dev * (step + 1)] for step in range(4)]
            + [cot_other[tok_dev * step : tok_dev * (step + 1)] for step in range(4)],
            places + [place ^ 1 for place in places],
            8,
        )
    else:
        pieces = [[shard]] + [
            [from_partner(shard, "row", step, row_size)] for step in range(1, row_size)
        ]
        cot_rows = lax.all_gather(cot_mixed, "col", axis=0, tiled=True)
    gate_weight = rows_of(pieces, 0, model_rows)
    up_weight = rows_of(pieces, model_rows, 2 * model_rows)
    down_weight = jnp.concatenate(
        [
            rows_of(pieces, 2 * model_rows, 3 * model_rows),
            rows_of(pieces, 3 * model_rows, 3 * model_rows + down_adapter_first.shape[0]),
        ],
        axis=0,
    )
    rank_width = output_adapter_first.shape[1]
    out_width = width + rank_width
    upper_width = adapter_rows * width // gain_len
    out_weight = out_gathered[:, :out_width]
    out_upper = out_gathered[:, out_width : out_width + upper_width].reshape(-1, width)
    down_upper = out_gathered[:, out_width + upper_width :].reshape(-1, width)
    out_pre = matrix_product(head_context, out_weight)
    output_rank_rows = convert_half(out_pre[:, width:])
    layer_state = inputs + out_pre[:, :width] + matrix_product(output_rank_rows, out_upper)
    normed_mlp = convert_half(rms_scale(layer_state, gain_mlp))

    ffn_in = lax.all_gather(reorder(normed_mlp, order), "col", axis=0, tiled=True)
    rank_part = rank_width // row_size
    upper_mixed = jnp.concatenate(
        [
            lax.dynamic_slice_in_dim(reorder(down_upper, order), place * rank_part, rank_part)
            for place in order
        ],
        axis=0,
    )
    rank_rows = convert_half(product(cot_rows, upper_mixed, contract_last))
    cot_rows = jnp.concatenate([cot_rows, rank_rows], axis=1)
    hidden_grad = matrix_product(cot_rows, down_weight)
    ffn_in, hidden_grad, gate_weight, up_weight = tie(
        ffn_in, hidden_grad, gate_weight, up_weight
    )
    gate_values = matrix_product(ffn_in, gate_weight)
    up_values = matrix_product(ffn_in, up_weight)
    hidden_activated = convert_half(jax.nn.gelu(gate_values, approximate=True) * up_values)
    gelu_out, gelu_pull = jax.vjp(partial(jax.nn.gelu, approximate=True), gate_values)
    gate_grad = convert_half(gelu_pull(hidden_grad * up_values)[0])
    up_grad = convert_half(hidden_grad * gelu_out)

    def blocks_of(values):
        size = values.shape[0] // row_size
        return [values[size * step : size * (step + 1)] for step in range(row_size)]

    grad_down = convert_half(product(cot_rows, hidden_activated, contract_first))
    grad_down, gate_grad, up_grad = tie(grad_down, gate_grad, up_grad)
    down_state = far_round(
        [
            jnp.concatenate([one, two], axis=0)
            for one, two in zip(blocks_of(grad_down[:width]), blocks_of(grad_down[width:]))
        ],
        row_size,
    )
    normed_sum = convert_half(
        product(gate_grad, gate_weight, contract_last)
        + product(up_grad, up_weight, contract_last)
    )
    *down_state, normed_sum, gate_grad, up_grad = tie(
        *near_sums(down_state, row_size), normed_sum, gate_grad, up_grad
    )
    down_state = near_round(down_state, row_size)
    normed_grad = lax.psum_scatter(normed_sum, "col", scatter_dimension=0, tiled=True)
    grad_gate = convert_half(product(ffn_in, gate_grad, contract_first))
    grad_gate, up_grad = tie(grad_gate, up_grad)
    gate_state = far_round(blocks_of(grad_gate), row_size)
    grad_up = convert_half(product(ffn_in, up_grad, contract_first))
    gate_state = near_sums(gate_state, row_size)
    count = len(down_state)
    *states, grad_up, hidden_activated = tie(*down_state, *gate_state, grad_up, hidden_activated)
    down_total = add_all(states[:count])
    gate_state = near_round(states[count:], row_size)
    up_state = far_round(blocks_of(grad_up), row_size)
    down_partial = convert_half(product(hidden_activated, down_weight, contract_last))
    down_partial, normed_grad = tie(down_partial, normed_grad)

    normed_grad = reorder(normed_grad, back_order).astype(jnp.float32)
    state_out, norm_pull = jax.vjp(rms_scale, layer_state, gain_mlp)
    state_part, grad_gain_mlp = norm_pull(normed_grad)
    state_grad = cot_grad + state_part
    attn_grad = convert_half(state_grad)
    rank_out_grad = convert_half(product(attn_grad, out_upper, contract_last))
    out_grad = jnp.concatenate([attn_grad, rank_out_grad], axis=1)
    context_grad = product(out_grad, out_weight, contract_last)
    grad_rows = convert_half(context_grad).reshape(row_total, HD)
    up_state = near_sums(up_state, row_size)
    count = len(gate_state)
    *states, grad_rows = tie(*gate_state, *up_state, grad_rows)
    gate_sum = add_all(states[:count])
    up_state = near_round(states[count:], row_size)
    delta = jnp.sum(grad_rows.astype(jnp.float32) * mixed_rows, axis=1)
    weight_grad = product(grad_rows, value_rows, contract_last)
    score_grad = convert_half(probs.astype(jnp.float32) * (weight_grad - delta[:, None]))
    query_acc = matrix_product(score_grad, key_rows)
    key_acc = product(score_grad, query_rows, contract_first)
    value_acc = product(probs, grad_rows, contract_first)
    keyval_sum = lax.psum_scatter(
        jnp.concatenate([convert_half(key_acc), convert_half(value_acc)], axis=1),
        "col",
        scatter_dimension=0,
        tiled=True,
    )
    query_grad = convert_half(
        unrotate(
            query_acc.reshape(tok_dev, NH, HD) * scale, cosine[:, None, :], sine_part[:, None, :]
        ).reshape(tok_dev, NH * HD)
    )
    grad_query = convert_half(product(normed, query_grad, contract_first))
    *up_state, keyval_sum, down_partial, grad_query = tie(
        *up_state, keyval_sum, down_partial, grad_query
    )
    up_sum = add_all(up_state)
    keyval_sum = keyval_sum.astype(jnp.float32)
    down_sum, rank_sum = down_total[:model_rows], down_total[model_rows:]
    summed = lax.psum_scatter(down_partial, "col", scatter_dimension=0, tiled=True)
    down_rank_rows = reorder(summed[:, width:], back_order)
    layer_out = convert_half(
        layer_state
        + reorder(summed[:, :width], back_order).astype(jnp.float32)
        + matrix_product(down_rank_rows, down_upper)
    )
    keyval_grad = jnp.concatenate(
        [convert_half(unrotate(keyval_sum[:, :HD], cosine, sine_part)), convert_half(keyval_sum[:, HD:])],
        axis=1,
    )
    in_grad = jnp.concatenate([query_grad, keyval_grad], axis=1)
    normed_back = product(in_grad, in_weight, contract_last)
    normed_out, first_pull = jax.vjp(rms_scale, inputs, gain_attn)
    input_part, grad_gain_attn = first_pull(normed_back)
    input_grad = convert_half(state_grad + input_part)

    grad_out = product(head_context, out_grad, contract_first)
    grad_keyval = product(normed, keyval_grad, contract_first)
    grad_out_upper = product(output_rank_rows, attn_grad, contract_first)
    grad_down_upper = product(down_rank_rows, cotangent, contract_first)

    def shared(values):
        return convert_half(values).reshape(devices, gain_len, -1)

    out_sum = scatter_all(
        jnp.concatenate([shared(grad_out), shared(grad_out_upper)], axis=2),
        row_size,
        col_size,
    )
    query_sum = scatter_all(shared(grad_query), row_size, col_size)
    keyval_total = scatter_all(
        jnp.concatenate(
            [
                shared(grad_keyval),
                shared(grad_down_upper),
                jnp.pad(
                    jnp.stack([shared(grad_gain_attn)[..., 0], shared(grad_gain_mlp)[..., 0]], axis=2),
                    ((0, 0), (0, 0), (0, 126)),
                ),
            ],
            axis=2,
        ),
        row_size,
        col_size,
        pieces=1,
    )
    keyval_width = grad_keyval.shape[1]
    gain_at = keyval_width + upper_width
    return (
        layer_out,
        input_grad,
        keyval_total[:, gain_at],
        query_sum,
        keyval_total[:, :keyval_width],
        out_sum[:, :width],
        out_sum[:, width:out_width],
        out_sum[:, out_width:].reshape(adapter_rows, width),
        keyval_total[:, gain_at + 1],
        gate_sum,
        up_sum,
        down_sum,
        rank_sum,
        keyval_total[:, keyval_width:gain_at].reshape(adapter_rows, width),
    )


def solution(mesh):
    return jax.shard_map(
        per_device,
        mesh=mesh,
        in_specs=(
            P(("row", "col"), None),
            P(("row", "col"), None),
            P("row"),
            P("row"),
            P(("row", "col")),
            P(("row", "col"), None),
            P(("row", "col"), None),
            P(("row", "col"), None),
            P(("row", "col"), None),
            P(("row", "col"), None),
            P(("row", "col")),
            P("row", "col"),
            P("row", "col"),
            P("row", "col"),
            P("row", "col"),
            P(("row", "col"), None),
        ),
        out_specs=(
            P(("row", "col"), None),
            P(("row", "col"), None),
            P(("row", "col")),
            P(("row", "col"), None),
            P(("row", "col"), None),
            P(("row", "col"), None),
            P(("row", "col"), None),
            P(("row", "col"), None),
            P(("row", "col")),
            P("row", "col"),
            P("row", "col"),
            P("row", "col"),
            P("row", "col"),
            P(("row", "col"), None),
        ),
        check_vma=False,
    )
```

time: 1360 us -> 1160 us (0.85)
  waiting for transfers between devices: 712 us -> 445 us
  local copies, waits for them, and re-layouts: 88.9 us -> 144 us
  other arithmetic: 83.6 us -> 124 us
  starting transfers between devices: 87.2 us -> 49.6 us
    all_gather x3 -> x1, waiting for transfers between devices: 115 us -> 8.1 us  [per_device(): lax.all_gather(out_packed, ('row', 'col'), axis=0, tiled=True)]
    ppermute x83 -> x47, waiting for transfers between devices: 491 us -> 403 us  [swap(): return lax.ppermute(values, axis, [(i, i ^ bit) for i in range(size)])]
    all_gather x1, waiting for transfers between devices: 86.6 us -> 33.1 us  [per_device(): lax.all_gather(jnp.concatenate([convert_half(query_matrix), convert_half(...]
    ppermute x83 -> x47, starting transfers between devices: 86.3 us -> 49.1 us  [swap(): return lax.ppermute(values, axis, [(i, i ^ bit) for i in range(size)])]
    unnamed x234 -> x229, local copies, waits for them, and re-layouts: 26.4 us -> 49.4 us
    concatenate x10 -> x15, other arithmetic: 12.3 us -> 34.4 us  [the longest x3 5.24 us: near_sums(): jnp.concatenate([add_half(near_y[:half], far_upper), near_y[half:]], axis=0)]
    all_gather x1, waiting for transfers between devices: 18.8 us -> 0.01 us  [per_device(): lax.all_gather(jnp.concatenate([convert_half(rotate(keyval_pre[:, :HD], c...]
    convert_element_type x44 -> x36, other arithmetic: 29.6 us -> 48.2 us  [convert_half(): return values.astype(jnp.bfloat16)]
  transfers between devices with their start and end apart: 92 -> 54, of which waited for: 51 -> 30; matrix products, arithmetic and copies ran while one was open for 28% -> 36% of each run, Pallas kernels for 0% -> 0%
where the time goes in v2:
time: 1160 us; the launch traced here: 1150 us
  waiting for transfers between devices  445 us (38%)
  matrix products  375 us (32%)
  local copies, waits for them, and re-layouts  144 us (12%)
  other arithmetic  124 us (11%)
  starting transfers between devices  49.6 us (4%)
  between operations  16.6 us (1%)
    ppermute x47, waiting for transfers between devices, swap(): return lax.ppermute(values, axis, [(i, i ^ bit) for i in range(size)])  403 us
    dot_general x19, matrix products, product(): lax.dot_general(left_side, right_side, dims, preferred_element_type=jnp.f...  241 us
    dot_general x9, matrix products, matrix_product(): return jnp.dot(left_side, right_side, preferred_element_type=jnp.float32)  134 us
    unnamed x229, local copies, waits for them, and re-layouts  49.4 us
    ppermute x47, starting transfers between devices, swap(): return lax.ppermute(values, axis, [(i, i ^ bit) for i in range(size)])  49.1 us
    convert_element_type x36, other arithmetic, convert_half(): return values.astype(jnp.bfloat16)  48.2 us
    all_gather x1, waiting for transfers between devices, per_device(): lax.all_gather(jnp.concatenate([convert_half(query_matrix), convert_half(...  33.1 us
  transfers between devices with their start and end apart: 54, of which 30 were waited for; matrix products, arithmetic and copies ran while one was open for 36% of the time, Pallas kernels for 0%

profile of v2, /device:TPU:0, one launch (start us, length us, event | category | flops | bytes accessed | tf_op | source)
XLA Modules:
  0.0 1153.8 jit_solution(1929028762150045949)
XLA Ops:
  33.9 62.8 %collective-permute-done.2 = bf16[288,2048]{1,0:T(8,128)(2,1)} collective-permute-done((bf16[288,2048]{1,0:T(8,128)(2,1)S(1)}, bf16[288,2048]{1,0:T(8,128)(2,1)}, u32[]{:S(2)}, u32[]{:S(2)}) %collective-permute-start.2) | collective-permute-done | bytes 1179680 | tf_op jit(solution)/shard_map/ppermute | solution.py:65
  110.1 33.1 %all-gather.5.cloned.1.call-done = bf16[2048,2688]{1,0:T(8,128)(2,1)} async-done(((bf16[64,2688]{1,0:T(8,128)(2,1)}), bf16[2048,2688]{1,0:T(8,128)(2,1)}) %all-gather.5.cloned.1.call-update) | async-done | bytes 11010064 | tf_op jit(solution)/shard_map/all_gather | solution.py:225
  165.3 31.9 %collective-permute-done.6 = bf16[288,2048]{1,0:T(8,128)(2,1)} collective-permute-done((bf16[288,2048]{1,0:T(8,128)(2,1)S(1)}, bf16[288,2048]{1,0:T(8,128)(2,1)}, u32[]{:S(2)}, u32[]{:S(2)}) %collective-permute-start.6) | collective-permute-done | bytes 1179680 | tf_op jit(solution)/shard_map/ppermute | solution.py:65
  197.2 31.5 %collective-permute-done.4 = bf16[800,2048]{1,0:T(8,128)(2,1)} collective-permute-done((bf16[800,2048]{1,0:T(8,128)(2,1)}, bf16[800,2048]{1,0:T(8,128)(2,1)}, u32[]{:S(2)}, u32[]{:S(2)}) %collective-permute-start.4) | collective-permute-done | bytes 3276832 | tf_op jit(solution)/shard_map/ppermute | solution.py:65
  241.9 8.6 fusion.118
  259.6 8.8 fusion.119
  273.8 70.5 %collective-permute-done.7 = bf16[800,2048]{1,0:T(8,128)(2,1)} collective-permute-done((bf16[800,2048]{1,0:T(8,128)(2,1)}, bf16[800,2048]{1,0:T(8,128)(2,1)}, u32[]{:S(2)}, u32[]{:S(2)}) %collective-permute-start.7) | collective-permute-done | bytes 3276832 | tf_op jit(solution)/shard_map/ppermute | solution.py:65
  344.3 8.1 all-gather.9.cloned.1.call-done
  355.5 8.1 fusion.15
  414.4 7.4 convolution_convert_fusion.8
  444.5 27.1 %fusion.17 = f32[2304,2048]{1,0:T(8,128)} fusion(bf16[2304,2048]{1,0:T(8,128)(2,1)} %slice_dynamic-update-slice_fusion.13, bf16[2304,256]{1,0:T(8,128)(2,1)S(1)} %copy.37, bf16[2304,2048]{1,0:T(8,128)(2,1)S(1)} %bitcast.65), kind=kOutput, calls=%fused_computation.35 | convolution fusion | flops 21764505600 | bytes 38928384 | tf_op jit(solution)/shard_map/dot_general | solution.py:28
  471.6 26.6 %fusion.120 = f32[2304,2048]{1,0:T(8,128)} fusion(bf16[2304,2048]{1,0:T(8,128)(2,1)} %all-gather.11.cloned.1.call-done, bf16[2048,2048]{1,0:T(8,128)(2,1)} %slice_dynamic-update-slice_fusion.10), kind=kOutput, calls=%fused_computation.321 | convolution fusion | flops 19327352832 | bytes 36700160 | tf_op jit(solution)/shard_map/dot_general | solution.py:28
  498.2 46.4 %multiply_convert_fusion.1 = (bf16[2304,2048]{1,0:T(8,128)(2,1)}, bf16[2304,2048]{1,0:T(8,128)(2,1)}, bf16[2304,2048]{1,0:T(8,128)(2,1)}) fusion(f32[2304,2048]{1,0:T(8,128)} %fusion.17, f32[2304,2048]{1,0:T(8,128)} %fusion.120, bf16[2304,2048]{1,0:T(8,128)(2,1)} %all-gather.11.cloned.1.call-done, bf16[2048,2048]{1,0:T(8,128)(2,1)} %pad_maximum_fusion.1), kind=kOutput, calls=%fused_computation.16 | convolution fusion | flops 19450036224 | bytes 83886080 | tf_op jit(solution)/shard_map/dot_general | solution.py:28
  544.6 27.8 %convolution_convert_fusion.1 = bf16[2304,2048]{1,0:T(8,128)(2,1)S(1)} fusion(bf16[2304,2048]{1,0:T(8,128)(2,1)} %get-tuple-element.116, bf16[2304,256]{1,0:T(8,128)(2,1)S(1)} %copy.37, bf16[2304,2048]{1,0:T(8,128)(2,1)} %slice_dynamic-update-slice_fusion.6), kind=kOutput, calls=%fused_computation.20 | convolution fusion | flops 21769224192 | bytes 29491200 | tf_op jit(solution)/shard_map/dot_general | solution.py:24
  579.1 26.7 %fusion.121 = f32[2304,2048]{1,0:T(8,128)} fusion(bf16[2304,2048]{1,0:T(8,128)(2,1)} %get-tuple-element.108, bf16[2048,2048]{1,0:T(8,128)(2,1)} %pad_maximum_fusion.1), kind=kOutput, calls=%fused_computation.322 | convolution fusion | flops 19327352832 | bytes 36700160 | tf_op jit(solution)/shard_map/dot_general | solution.py:24
  608.6 28.0 %add_convert_fusion = bf16[2304,2048]{1,0:T(8,128)(2,1)} fusion(f32[2304,2048]{1,0:T(8,128)} %fusion.121, bf16[2304,2048]{1,0:T(8,128)(2,1)} %get-tuple-element.111, bf16[2048,2048]{1,0:T(8,128)(2,1)} %slice_dynamic-update-slice_fusion.10), kind=kOutput, calls=%fused_computation.15 | convolution fusion | flops 19336790016 | bytes 46137344 | tf_op jit(solution)/shard_map/dot_general | solution.py:24
  647.2 25.1 %convolution_convert_fusion.5 = bf16[2048,2048]{1,0:T(8,128)(2,1)S(1)} fusion(bf16[2304,2048]{1,0:T(8,128)(2,1)} %all-gather.11.cloned.1.call-done, bf16[2304,2048]{1,0:T(8,128)(2,1)} %get-tuple-element.108), kind=kOutput, calls=%fused_computation.34 | convolution fusion | flops 19331547136 | bytes 27262976 | tf_op jit(solution)/shard_map/dot_general | solution.py:24
  679.7 25.0 %convolution_convert_fusion.4 = bf16[2048,2048]{1,0:T(8,128)(2,1)S(1)} fusion(bf16[2304,2048]{1,0:T(8,128)(2,1)} %all-gather.11.cloned.1.call-done, bf16[2304,2048]{1,0:T(8,128)(2,1)} %get-tuple-element.111), kind=kOutput, calls=%fused_computation.33 | convolution fusion | flops 19331547136 | bytes 27262976 | tf_op jit(solution)/shard_map/dot_general | solution.py:24
  709.4 41.4 %collective-permute-done.12 = bf16[576,2048]{1,0:T(8,128)(2,1)S(1)} collective-permute-done((bf16[576,2048]{1,0:T(8,128)(2,1)S(1)}, bf16[576,2048]{1,0:T(8,128)(2,1)S(1)}, u32[]{:S(2)}, u32[]{:S(2)}) %collective-permute-start.12) | collective-permute-done | bytes 2359328 | tf_op jit(solution)/shard_map/ppermute | solution.py:65
  755.7 29.0 %convolution_convert_fusion = bf16[2304,2304]{1,0:T(8,128)(2,1)} fusion(bf16[2304,2048]{1,0:T(8,128)(2,1)} %get-tuple-element.116, bf16[2304,2048]{1,0:T(8,128)(2,1)} %slice_dynamic-update-slice_fusion.13), kind=kOutput, calls=%fused_computation.19 | convolution fusion | flops 21748580352 | bytes 29491200 | tf_op jit(solution)/shard_map/dot_general | solution.py:24
  798.3 7.6 fusion.23
  809.0 21.3 %collective-permute-done.16 = bf16[512,2048]{1,0:T(8,128)(2,1)} collective-permute-done((bf16[512,2048]{1,0:T(8,128)(2,1)}, bf16[512,2048]{1,0:T(8,128)(2,1)}, u32[]{:S(2)}, u32[]{:S(2)}) %collective-permute-start.16) | collective-permute-done | bytes 2097184 | tf_op jit(solution)/shard_map/ppermute | solution.py:65
  833.9 7.4 convolution_convert_fusion.6
  842.5 9.0 multiply_convert_fusion
  869.8 7.0 convolution_convert_fusion.3
  876.9 28.2 %collective-permute-done.20 = bf16[512,2048]{1,0:T(8,128)(2,1)} collective-permute-done((bf16[512,2048]{1,0:T(8,128)(2,1)}, bf16[512,2048]{1,0:T(8,128)(2,1)}, u32[]{:S(2)}, u32[]{:S(2)}) %collective-permute-start.20) | collective-permute-done | bytes 2097184 | tf_op jit(solution)/shard_map/ppermute | solution.py:65
  951.7 19.3 %collective-permute-done.38 = bf16[1,2,2,2,1,64,1280]{6,5,4,3,2,1,0:T(8,128)(2,1)S(1)} collective-permute-done((bf16[1,2,2,2,1,64,1280]{6,5,4,3,2,1,0:T(8,128)(2,1)S(1)}, bf16[1,2,2,2,1,64,1280]{6,5,4,3,2,1,0:T(8,128)(2,1)S(1)}, u32[]{:S(2)}, u32[]{:S(2)}) %collective-permute-start.38) | collective-permute-done | bytes 1310752 | tf_op jit(solution)/shard_map/ppermute | solution.py:65
  977.9 11.6 %collective-permute-done.39 = bf16[1,1,2,2,1,64,1280]{6,5,4,3,2,1,0:T(8,128)(2,1)S(1)} collective-permute-done((bf16[1,1,2,2,1,64,1280]{6,5,4,3,2,1,0:T(8,128)(2,1)S(1)}, bf16[1,1,2,2,1,64,1280]{6,5,4,3,2,1,0:T(8,128)(2,1)S(1)}, u32[]{:S(2)}, u32[]{:S(2)}) %collective-permute-start.39) | collective-permute-done | bytes 655392 | tf_op jit(solution)/shard_map/ppermute | solution.py:65
  1001.3 9.4 fusion.30
  1031.5 7.6 collective-permute-done.45
  1100.8 10.9 collective-permute-done.30
  1131.9 7.6 collective-permute-done.25
  (523 shorter events, 416.3 us)
Async XLA Ops:
  7.2 136.1 %all-gather.5.cloned.1.call-start = ((), (), s32[]{:S(2)}) async-start(), calls=%async_computation.3 | async-start | bytes 11354112 | tf_op jit(solution)/shard_map/all_gather | solution.py:225
  10.8 219.1 %all-gather.7.cloned.1.call-start = ((), (), s32[]{:S(2)}) async-start(), calls=%async_computation.4 | async-start | bytes 2654208 | tf_op jit(solution)/shard_map/all_gather | solution.py:286
  22.5 80.9 %collective-permute-start = (bf16[800,2048]{1,0:T(8,128)(2,1)}, bf16[800,2048]{1,0:T(8,128)(2,1)}, u32[]{:S(2)}, u32[]{:S(2)}) collective-permute-start(bf16[800,2048]{1,0:T(8,128)(2,1)} %get-tuple-element.76), channel_id=1, source_target_pairs={{0,16},{8,24},{16,0},{24,8},{1,17},{9,25},{17,1},{25,9},{2,18},{10... | collective-permute-start | bytes 9830408 | tf_op jit(solution)/shard_map/ppermute | solution.py:65
  25.5 84.6 %collective-permute-start.1 = (bf16[800,2048]{1,0:T(8,128)(2,1)}, bf16[800,2048]{1,0:T(8,128)(2,1)}, u32[]{:S(2)}, u32[]{:S(2)}) collective-permute-start(bf16[800,2048]{1,0:T(8,128)(2,1)} %get-tuple-element.77), channel_id=1, source_target_pairs={{0,8},{8,0},{16,24},{24,16},{1,9},{9,1},{17,25},{25,17},{2,10},{10... | collective-permute-start | bytes 9830408 | tf_op jit(solution)/shard_map/ppermute | solution.py:65
  27.3 69.4 %collective-permute-start.2 = (bf16[288,2048]{1,0:T(8,128)(2,1)S(1)}, bf16[288,2048]{1,0:T(8,128)(2,1)}, u32[]{:S(2)}, u32[]{:S(2)}) collective-permute-start(bf16[288,2048]{1,0:T(8,128)(2,1)S(1)} %pad_maximum_fusion.19), channel_id=1, source_target_pairs={{0,2},{1,3},{2,0},{3,1},{4,6},{5,7},{6,4},{7,5},{8,10},{9,11},{10,... | collective-permute-start | bytes 3538952 | tf_op jit(solution)/shard_map/ppermute | solution.py:65
  28.9 67.8 %collective-permute-start.3 = (bf16[288,2048]{1,0:T(8,128)(2,1)S(1)}, bf16[288,2048]{1,0:T(8,128)(2,1)}, u32[]{:S(2)}, u32[]{:S(2)}) collective-permute-start(bf16[288,2048]{1,0:T(8,128)(2,1)S(1)} %pad_maximum_fusion.19), channel_id=1, source_target_pairs={{0,4},{1,5},{2,6},{3,7},{4,0},{5,1},{6,2},{7,3},{8,12},{9,13},{10,... | collective-permute-start | bytes 3538952 | tf_op jit(solution)/shard_map/ppermute | solution.py:65
  155.2 197.2 %all-gather.9.cloned.1.call-start = ((), (), s32[]{:S(2)}) async-start(), calls=%async_computation.5 | async-start | bytes 11894784 | tf_op jit(solution)/shard_map/all_gather | solution.py:337
  155.2 73.4 %collective-permute-start.4 = (bf16[800,2048]{1,0:T(8,128)(2,1)}, bf16[800,2048]{1,0:T(8,128)(2,1)}, u32[]{:S(2)}, u32[]{:S(2)}) collective-permute-start(bf16[800,2048]{1,0:T(8,128)(2,1)} %get-tuple-element.76), channel_id=1, source_target_pairs={{0,8},{8,0},{16,24},{24,16},{1,9},{9,1},{17,25},{25,17},{2,10},{10... | collective-permute-start | bytes 9830408 | tf_op jit(solution)/shard_map/ppermute | solution.py:65
  156.8 73.1 %collective-permute-start.5 = (bf16[800,2048]{1,0:T(8,128)(2,1)}, bf16[800,2048]{1,0:T(8,128)(2,1)}, u32[]{:S(2)}, u32[]{:S(2)}) collective-permute-start(bf16[800,2048]{1,0:T(8,128)(2,1)} %get-tuple-element.77), channel_id=1, source_target_pairs={{0,16},{8,24},{16,0},{24,8},{1,17},{9,25},{17,1},{25,9},{2,18},{10... | collective-permute-start | bytes 9830408 | tf_op jit(solution)/shard_map/ppermute | solution.py:65
  157.3 39.9 %collective-permute-start.6 = (bf16[288,2048]{1,0:T(8,128)(2,1)S(1)}, bf16[288,2048]{1,0:T(8,128)(2,1)}, u32[]{:S(2)}, u32[]{:S(2)}) collective-permute-start(bf16[288,2048]{1,0:T(8,128)(2,1)S(1)} %pad_maximum_fusion.19), channel_id=1, source_target_pairs={{0,6},{1,7},{2,4},{3,5},{4,2},{5,3},{6,0},{7,1},{8,14},{9,15},{10,... | collective-permute-start | bytes 3538952 | tf_op jit(solution)/shard_map/ppermute | solution.py:65
  229.9 241.7 %all-gather.11.cloned.1.call-start = ((), (), s32[]{:S(2)}) async-start(), calls=%async_computation.6 | async-start | bytes 10616832 | tf_op jit(solution)/shard_map/all_gather | solution.py:390
  239.8 104.5 %collective-permute-start.9 = (bf16[1152,2048]{1,0:T(8,128)(2,1)}, bf16[1152,2048]{1,0:T(8,128)(2,1)}, u32[]{:S(2)}, u32[]{:S(2)}) collective-permute-start(bf16[1152,2048]{1,0:T(8,128)(2,1)} %pad_maximum_fusion.4), channel_id=1, source_target_pairs={{0,1},{1,0},{2,3},{3,2},{4,5},{5,4},{6,7},{7,6},{8,9},{9,8},{10,11... | collective-permute-start | bytes 14155784 | tf_op jit(solution)/shard_map/ppermute | solution.py:65
  239.8 104.4 %collective-permute-start.7 = (bf16[800,2048]{1,0:T(8,128)(2,1)}, bf16[800,2048]{1,0:T(8,128)(2,1)}, u32[]{:S(2)}, u32[]{:S(2)}) collective-permute-start(bf16[800,2048]{1,0:T(8,128)(2,1)} %collective-permute-done), channel_id=1, source_target_pairs={{0,8},{8,0},{16,24},{24,16},{1,9},{9,1},{17,25},{25,17},{2,10},{10... | collective-permute-start | bytes 9830408 | tf_op jit(solution)/shard_map/ppermute | solution.py:65
  240.3 104.0 %collective-permute-start.8 = (bf16[800,2048]{1,0:T(8,128)(2,1)}, bf16[800,2048]{1,0:T(8,128)(2,1)}, u32[]{:S(2)}, u32[]{:S(2)}) collective-permute-start(bf16[800,2048]{1,0:T(8,128)(2,1)} %collective-permute-done.1), channel_id=1, source_target_pairs={{0,16},{8,24},{16,0},{24,8},{1,17},{9,25},{17,1},{25,9},{2,18},{10... | collective-permute-start | bytes 9830408 | tf_op jit(solution)/shard_map/ppermute | solution.py:65
  371.7 420.6 %reduce-scatter.4.cloned.1.call-start = ((), (), s32[]{:S(2)}) async-start(), calls=%async_computation.7 | async-start | bytes 10616832 | tf_op jit(solution)/shard_map/reduce_scatter | solution.py:433
  605.7 37.7 %collective-permute-start.11 = (bf16[288,2048]{1,0:T(8,128)(2,1)}, bf16[288,2048]{1,0:T(8,128)(2,1)}, u32[]{:S(2)}, u32[]{:S(2)}) collective-permute-start(bf16[288,2048]{1,0:T(8,128)(2,1)} %get-tuple-element.153), channel_id=1, source_target_pairs={{0,8},{8,0},{16,24},{24,16},{1,9},{9,1},{17,25},{25,17},{2,10},{10... | collective-permute-start | bytes 3538952 | tf_op jit(solution)/shard_map/ppermute | solution.py:65
  608.0 32.0 %collective-permute-start.10 = (bf16[288,2048]{1,0:T(8,128)(2,1)}, bf16[288,2048]{1,0:T(8,128)(2,1)}, u32[]{:S(2)}, u32[]{:S(2)}) collective-permute-start(bf16[288,2048]{1,0:T(8,128)(2,1)} %pad_maximum_fusion.17), channel_id=1, source_target_pairs={{0,16},{8,24},{16,0},{24,8},{1,17},{9,25},{17,1},{25,9},{2,18},{10... | collective-permute-start | bytes 3538952 | tf_op jit(solution)/shard_map/ppermute | solution.py:65
  647.2 258.4 %reduce-scatter.6.cloned.1.call-start = ((), (), s32[]{:S(2)}) async-start(), calls=%async_computation.8 | async-start | bytes 2654208 | tf_op jit(solution)/shard_map/reduce_scatter | solution.py:467
  676.6 74.3 %collective-permute-start.12 = (bf16[576,2048]{1,0:T(8,128)(2,1)S(1)}, bf16[576,2048]{1,0:T(8,128)(2,1)S(1)}, u32[]{:S(2)}, u32[]{:S(2)}) collective-permute-start(bf16[576,2048]{1,0:T(8,128)(2,1)S(1)} %copy-done.43), channel_id=1, source_target_pairs={{0,8},{8,0},{16,24},{24,16},{1,9},{9,1},{17,25},{25,17},{2,10},{10... | collective-permute-start | bytes 7077896 | tf_op jit(solution)/shard_map/ppermute | solution.py:65
  678.3 72.6 %collective-permute-start.13 = (bf16[576,2048]{1,0:T(8,128)(2,1)S(1)}, bf16[576,2048]{1,0:T(8,128)(2,1)S(1)}, u32[]{:S(2)}, u32[]{:S(2)}) collective-permute-start(bf16[576,2048]{1,0:T(8,128)(2,1)S(1)} %copy-done.46), channel_id=1, source_target_pairs={{0,16},{8,24},{16,0},{24,8},{1,17},{9,25},{17,1},{25,9},{2,18},{10... | collective-permute-start | bytes 7077896 | tf_op jit(solution)/shard_map/ppermute | solution.py:65
  753.6 33.0 %collective-permute-start.18 = (bf16[256,2048]{1,0:T(8,128)(2,1)}, bf16[256,2048]{1,0:T(8,128)(2,1)S(1)}, u32[]{:S(2)}, u32[]{:S(2)}) collective-permute-start(bf16[256,2048]{1,0:T(8,128)(2,1)} %get-tuple-element.169), channel_id=1, source_target_pairs={{0,16},{8,24},{16,0},{24,8},{1,17},{9,25},{17,1},{25,9},{2,18},{10... | collective-permute-start | bytes 3145736 | tf_op jit(solution)/shard_map/ppermute | solution.py:65
  754.4 32.2 %collective-permute-start.19 = (bf16[256,2048]{1,0:T(8,128)(2,1)}, bf16[256,2048]{1,0:T(8,128)(2,1)}, u32[]{:S(2)}, u32[]{:S(2)}) collective-permute-start(bf16[256,2048]{1,0:T(8,128)(2,1)} %get-tuple-element.167), channel_id=1, source_target_pairs={{0,8},{8,0},{16,24},{24,16},{1,9},{9,1},{17,25},{25,17},{2,10},{10... | collective-permute-start | bytes 3145736 | tf_op jit(solution)/shard_map/ppermute | solution.py:65
  784.7 45.7 %collective-permute-start.16 = (bf16[512,2048]{1,0:T(8,128)(2,1)}, bf16[512,2048]{1,0:T(8,128)(2,1)}, u32[]{:S(2)}, u32[]{:S(2)}) collective-permute-start(bf16[512,2048]{1,0:T(8,128)(2,1)} %pad_maximum_fusion.12), channel_id=1, source_target_pairs={{0,8},{8,0},{16,24},{24,16},{1,9},{9,1},{17,25},{25,17},{2,10},{10... | collective-permute-start | bytes 6291464 | tf_op jit(solution)/shard_map/ppermute | solution.py:65
  785.4 45.7 %collective-permute-start.17 = (bf16[512,2048]{1,0:T(8,128)(2,1)}, bf16[512,2048]{1,0:T(8,128)(2,1)}, u32[]{:S(2)}, u32[]{:S(2)}) collective-permute-start(bf16[512,2048]{1,0:T(8,128)(2,1)} %pad_maximum_fusion.13), channel_id=1, source_target_pairs={{0,16},{8,24},{16,0},{24,8},{1,17},{9,25},{17,1},{25,9},{2,18},{10... | collective-permute-start | bytes 6291464 | tf_op jit(solution)/shard_map/ppermute | solution.py:65
  860.2 202.1 %reduce-scatter.8.cloned.1.call-start = ((), (), s32[]{:S(2)}) async-start(), calls=%async_computation.9 | async-start | bytes 11943936 | tf_op jit(solution)/shard_map/reduce_scatter | solution.py:485
  860.2 44.9 %collective-permute-start.20 = (bf16[512,2048]{1,0:T(8,128)(2,1)}, bf16[512,2048]{1,0:T(8,128)(2,1)}, u32[]{:S(2)}, u32[]{:S(2)}) collective-permute-start(bf16[512,2048]{1,0:T(8,128)(2,1)} %pad_maximum_fusion.14), channel_id=1, source_target_pairs={{0,8},{8,0},{16,24},{24,16},{1,9},{9,1},{17,25},{25,17},{2,10},{10... | collective-permute-start | bytes 6291464 | tf_op jit(solution)/shard_map/ppermute | solution.py:65
  861.3 44.3 %collective-permute-start.21 = (bf16[512,2048]{1,0:T(8,128)(2,1)}, bf16[512,2048]{1,0:T(8,128)(2,1)}, u32[]{:S(2)}, u32[]{:S(2)}) collective-permute-start(bf16[512,2048]{1,0:T(8,128)(2,1)} %pad_maximum_fusion.15), channel_id=1, source_target_pairs={{0,16},{8,24},{16,0},{24,8},{1,17},{9,25},{17,1},{25,9},{2,18},{10... | collective-permute-start | bytes 6291464 | tf_op jit(solution)/shard_map/ppermute | solution.py:65
  944.8 31.7 %collective-permute-start.43 = (bf16[2,1,2,2,1,64,1280]{6,5,4,3,2,1,0:T(8,128)(2,1)S(1)}, bf16[2,1,2,2,1,64,1280]{6,5,4,3,2,1,0:T(8,128)(2,1)S(1)}, u32[]{:S(2)}, u32[]{:S(2)}) collective-permute-start(bf16[2,1,2,2,1,64,1280]{6,5,4,3,2,1,0:T(8,128)(2,1)S(1)} %constant_dynamic-slice_fusion.3), channel_id=1, source_target_pairs={{0,8},{8,0},{16,24},{24,16},{1,9},{9,1},{17,25},{25,17},{2,10},{10... | collective-permute-start | bytes 3932168 | tf_op jit(solution)/shard_map/ppermute | solution.py:65
  990.6 49.7 %collective-permute-start.40 = (bf16[1,1,1,2,1,64,1280]{6,5,4,3,2,1,0:T(8,128)(2,1)}, bf16[1,1,1,2,1,64,1280]{6,5,4,3,2,1,0:T(8,128)(2,1)}, u32[]{:S(2)}, u32[]{:S(2)}) collective-permute-start(bf16[1,1,1,2,1,64,1280]{6,5,4,3,2,1,0:T(8,128)(2,1)} %constant_dynamic-slice_fusion.5), channel_id=1, source_target_pairs={{0,4},{1,5},{2,6},{3,7},{4,0},{5,1},{6,2},{7,3},{8,12},{9,13},{10,... | collective-permute-start | bytes 983048 | tf_op jit(solution)/shard_map/ppermute | solution.py:65
  993.3 45.8 %collective-permute-start.45 = (bf16[1,1,1,2,1,64,1280]{6,5,4,3,2,1,0:T(8,128)(2,1)}, bf16[1,1,1,2,1,64,1280]{6,5,4,3,2,1,0:T(8,128)(2,1)}, u32[]{:S(2)}, u32[]{:S(2)}) collective-permute-start(bf16[1,1,1,2,1,64,1280]{6,5,4,3,2,1,0:T(8,128)(2,1)} %constant_dynamic-slice_fusion.1), channel_id=1, source_target_pairs={{0,4},{1,5},{2,6},{3,7},{4,0},{5,1},{6,2},{7,3},{8,12},{9,13},{10,... | collective-permute-start | bytes 983048 | tf_op jit(solution)/shard_map/ppermute | solution.py:65
  997.4 52.7 %collective-permute-start.27 = (bf16[2,2,2,2,1,64,1024]{6,5,4,3,2,1,0:T(8,128)(2,1)}, bf16[2,2,2,2,1,64,1024]{6,5,4,3,2,1,0:T(8,128)(2,1)}, u32[]{:S(2)}, u32[]{:S(2)}) collective-permute-start(bf16[2,2,2,2,1,64,1024]{6,5,4,3,2,1,0:T(8,128)(2,1)} %constant_dynamic-slice_fusion.18), channel_id=1, source_target_pairs={{0,1},{1,0},{2,3},{3,2},{4,5},{5,4},{6,7},{7,6},{8,9},{9,8},{10,11... | collective-permute-start | bytes 6291464 | tf_op jit(solution)/shard_map/ppermute | solution.py:65
  1000.5 55.1 %collective-permute-start.32 = (bf16[2,2,2,2,1,64,1024]{6,5,4,3,2,1,0:T(8,128)(2,1)}, bf16[2,2,2,2,1,64,1024]{6,5,4,3,2,1,0:T(8,128)(2,1)}, u32[]{:S(2)}, u32[]{:S(2)}) collective-permute-start(bf16[2,2,2,2,1,64,1024]{6,5,4,3,2,1,0:T(8,128)(2,1)} %constant_dynamic-slice_fusion.13), channel_id=1, source_target_pairs={{0,1},{1,0},{2,3},{3,2},{4,5},{5,4},{6,7},{7,6},{8,9},{9,8},{10,11... | collective-permute-start | bytes 6291464 | tf_op jit(solution)/shard_map/ppermute | solution.py:65
  (134 other events, 1864.9 us)
Sparse Core Ops, SparseCore 0:
  11.6 131.6 all-gather.4
  155.3 61.4 all-gather.6
  230.0 122.3 all-gather.8
  371.8 89.1 all-gather.10
  647.3 98.2 reduce-scatter.3
  860.3 35.3 reduce-scatter.5
  905.7 123.3 reduce-scatter.7

commit v3 on v2

--- a/solution.py
+++ b/solution.py
@@ -57,28 +57,16 @@
     )
 
 
-def is_power(count):
-    return count & (count - 1) == 0
-
-
 def swap(values, axis, size, bit):
     return lax.ppermute(values, axis, [(i, i ^ bit) for i in range(size)])
 
 
-def partner(own, step, size):
-    return own ^ step if is_power(size) else (own + step) % size
-
-
-def source_step(own, block, size):
-    return own ^ block if is_power(size) else (block - own) % size
+def partner(own, step):
+    return own ^ step
 
 
 def to_partner(values, axis, step, size):
-    return lax.ppermute(values, axis, [(i, partner(i, step, size)) for i in range(size)])
-
-
-def from_partner(values, axis, step, size):
-    return lax.ppermute(values, axis, [(partner(i, step, size), i) for i in range(size)])
+    return lax.ppermute(values, axis, [(i, partner(i, step)) for i in range(size)])
 
 
 def reorder(values, order):
@@ -112,81 +100,98 @@
     return jnp.concatenate(found, axis=0)
 
 
-def far_round(blocks, size):
-    if size != 4:
-        return blocks
-    far = blocks[3]
-    half = far.shape[0] // 2
-    return [
-        blocks[0],
-        blocks[1],
-        blocks[2],
-        swap(far[:half], "row", size, 1),
-        swap(far[half:], "row", size, 2),
-    ]
-
-
-def near_sums(state, size):
-    if size != 4:
-        return state
-    own, near_x, near_y, far_upper, far_lower = state
+def split_blocks(blocks):
+    own, near_x, near_y, far = blocks
     half = own.shape[0] // 2
-    near_x = jnp.concatenate([near_x[:half], add_half(near_x[half:], far_lower)], axis=0)
-    near_y = jnp.concatenate([add_half(near_y[:half], far_upper), near_y[half:]], axis=0)
-    return [own, near_x, near_y]
-
-
-def near_round(state, size):
-    if size != 4:
-        return [state[0]] + [
-            to_partner(state[step], "row", step, size) for step in range(1, size)
-        ]
-    own, near_x, near_y = state
-    return [own, swap(near_x, "row", size, 1), swap(near_y, "row", size, 2)]
-
-
-def add_all(state):
-    total = state[0].astype(jnp.float32)
-    for part in state[1:]:
-        total = total + part.astype(jnp.float32)
+    return (
+        own,
+        (far[:half], far[half:]),
+        (near_x[:half], near_y[half:]),
+        (near_x[half:], near_y[:half]),
+    )
+
+
+def send_pair(pair):
+    return swap(pair[0], "row", 4, 1), swap(pair[1], "row", 4, 2)
+
+
+def add_pair(pair, got):
+    return add_half(pair[0], got[1]), add_half(pair[1], got[0])
+
+
+def finish_sum(own, free, last):
+    half = own.shape[0] // 2
+    upper = add_full(own[:half], free[0], last[1])
+    lower = add_full(own[half:], last[0], free[1])
+    return jnp.concatenate([upper, lower], axis=0)
+
+
+def row_sum(blocks, size):
+    total = blocks[0].astype(jnp.float32)
+    for step in range(1, size):
+        total = total + to_partner(blocks[step], "row", step, size).astype(jnp.float32)
     return total
+
+
+def add_full(first, second, third):
+    return first.astype(jnp.float32) + second.astype(jnp.float32) + third.astype(jnp.float32)
 
 
 def add_half(first, second):
     return convert_half(first.astype(jnp.float32) + second.astype(jnp.float32))
 
 
-def halve(values, stages, bits, sizes):
-    for place, (axis, bit) in enumerate(stages):
-        dim = bits.index((axis, bit))
-        own = (lax.axis_index(axis) // bit) % 2
-        kept = lax.dynamic_slice_in_dim(values, own, 1, axis=dim)
-        sent = lax.dynamic_slice_in_dim(values, 1 - own, 1, axis=dim)
-        got = swap(sent, axis, sizes[axis], bit)
-        values = kept.astype(jnp.float32) + got.astype(jnp.float32)
-        if place < len(stages) - 1:
-            values = convert_half(values)
-    return values.reshape(values.shape[-2:])
-
-
-def scatter_all(values, row_size, col_size, pieces=2):
-    devices, rows, width = values.shape
-    if not (is_power(row_size) and is_power(col_size)):
-        return lax.psum_scatter(
-            values.astype(jnp.float32), ("row", "col"), scatter_dimension=0, tiled=True
-        ).reshape(rows, width)
-    sizes = {"row": row_size, "col": col_size}
-    row_bits = [("row", 1 << k) for k in reversed(range(row_size.bit_length() - 1))]
-    col_bits = [("col", 1 << k) for k in reversed(range(col_size.bit_length() - 1))]
-    bits = row_bits + col_bits
-    shaped = convert_half(values).reshape((2,) * len(bits) + (rows, width))
-    part = width // pieces
-    sums = []
-    for place in range(pieces):
-        order = row_bits if place % 2 == 0 else row_bits[::-1]
+def halve(values, dim, axis, size, bit):
+    own = (lax.axis_index(axis) // bit) % 2
+    kept = lax.dynamic_slice_in_dim(values, own, 1, axis=dim)
+    sent = lax.dynamic_slice_in_dim(values, 1 - own, 1, axis=dim)
+    return add_half(kept, swap(sent, axis, size, bit))
+
+
+def scatter_chips(values, row_size, col_size, parts=2):
+    chips, rows, width = values.shape
+    line = col_size // 2
+    bits = [1 << k for k in reversed(range(row_size.bit_length() - 1))]
+    shaped = values.reshape((2,) * len(bits) + (line, rows, width))
+    part = width // parts
+    pieces = []
+    for place in range(parts):
         piece = shaped[..., part * place : part * (place + 1)]
-        sums.append(halve(piece, col_bits[-1:] + order + col_bits[:-1], bits, sizes))
-    return jnp.concatenate(sums, axis=-1)
+        for bit in bits if place % 2 == 0 else bits[::-1]:
+            piece = halve(piece, bits.index(bit), "row", row_size, bit)
+        pieces.append(piece.reshape(line, rows, part))
+    whole = jnp.concatenate(pieces, axis=-1)
+    at = lax.axis_index("col") // 2
+    total = lax.dynamic_index_in_dim(whole, at, 0, keepdims=False).astype(jnp.float32)
+    for step in range(1, line):
+        block = lax.dynamic_index_in_dim(whole, at ^ step, 0, keepdims=False)
+        total = total + swap(block, "col", col_size, 2 * step).astype(jnp.float32)
+    return total
+
+
+def share_cores(values, col_size):
+    core = lax.axis_index("col") % 2
+    rows = values.shape[0] // 2
+    kept = lax.dynamic_slice_in_dim(values, core * rows, rows)
+    got = swap(lax.dynamic_slice_in_dim(values, (1 - core) * rows, rows), "col", col_size, 1)
+    first = core == 0
+    return jnp.where(first, kept, got), jnp.where(first, got, kept)
+
+
+def core_half(values, core):
+    half = values.shape[-1] // 2
+    return lax.dynamic_slice_in_dim(values, core * half, half, axis=-1)
+
+
+def with_partner(values, col_size):
+    got = swap(values, "col", col_size, 1)
+    return jnp.concatenate([values, got], axis=0)
+
+
+def halves_with_partner(values, col_size):
+    core = lax.axis_index("col") % 2
+    got = swap(core_half(values, 1 - core), "col", col_size, 1)
+    return jnp.concatenate([core_half(values, core), got], axis=0)
 
 
 def per_device(
@@ -219,8 +224,7 @@
     gain_len = attention_norm_gain.shape[0]
     start_row = lax.axis_index("col") * tok_dev
     scale = HD ** (-0.5)
-    order = [partner(row_at, step, row_size) for step in range(row_size)]
-    back_order = [source_step(row_at, block, row_size) for block in range(row_size)]
+    order = [partner(row_at, step) for step in range(row_size)]
 
     in_gathered = lax.all_gather(
         jnp.concatenate(
@@ -255,17 +259,13 @@
     cot_mixed = reorder(cotangent, order)
     if by_pairs:
         half = shard.shape[0] // 2
-        upper, lower = shard[:half], shard[half:]
+        in_gathered, upper, lower, cot_mixed = tie(
+            in_gathered, shard[:half], shard[half:], cot_mixed
+        )
         upper_y = swap(upper, "row", 4, 2)
         lower_x = swap(lower, "row", 4, 1)
         cot_two = swap(cot_mixed, "col", 8, 2)
         cot_four = swap(cot_mixed, "col", 8, 4)
-        in_gathered, upper_y, lower_x, cot_two, cot_four, upper, lower, cot_last = tie(
-            in_gathered, upper_y, lower_x, cot_two, cot_four, upper, lower, cot_mixed
-        )
-        upper_x = swap(upper, "row", 4, 1)
-        lower_y = swap(lower, "row", 4, 2)
-        cot_six = swap(cot_last, "col", 8, 6)
     in_width = in_gathered.shape[1] - 128
     in_weight = in_gathered[:, :in_width]
     gains = in_gathered[:, in_width:].astype(jnp.float32)
@@ -304,36 +304,24 @@
         ],
         axis=1,
     )
+    keyval_rows, out_packed = tie(keyval_rows, out_packed)
     if by_pairs:
-        (
-            keyval_rows,
-            out_packed,
-            upper_x,
-            lower_y,
-            cot_six,
-            upper_y,
-            lower_x,
-            cot_mixed,
-            cot_two,
-            cot_four,
-        ) = tie(
-            keyval_rows,
-            out_packed,
-            upper_x,
-            lower_y,
-            cot_six,
-            upper_y,
-            lower_x,
-            cot_mixed,
-            cot_two,
-            cot_four,
-        )
-        far_upper = swap(upper_y, "row", 4, 1)
-        far_lower = swap(lower_x, "row", 4, 2)
-        cot_mine = jnp.concatenate([cot_mixed, cot_two, cot_four, cot_six], axis=0)
-        cot_other = swap(cot_mine, "col", 8, 1)
-    else:
-        keyval_rows, out_packed = tie(keyval_rows, out_packed)
+        (keyval_rows, out_packed, upper_y, lower_x, cot_two, cot_four, upper, lower, cot_mixed) = (
+            tie(
+                keyval_rows,
+                out_packed,
+                upper_y,
+                lower_x,
+                cot_two,
+                cot_four,
+                upper,
+                lower,
+                cot_mixed,
+            )
+        )
+        upper_x = swap(upper, "row", 4, 1)
+        lower_y = swap(lower, "row", 4, 2)
+        cot_six = swap(cot_mixed, "col", 8, 6)
     out_gathered = lax.all_gather(out_packed, ("row", "col"), axis=0, tiled=True)
     key_rows = keyval_rows[:, :HD]
     value_rows = keyval_rows[:, HD:]
@@ -351,9 +339,13 @@
     mixed_rows = matrix_product(probs, value_rows)
     head_context = convert_half(mixed_rows.reshape(tok_dev, NH * HD))
     if by_pairs:
-        out_gathered, far_upper, far_lower, cot_other, head_context = tie(
-            out_gathered, far_upper, far_lower, cot_other, head_context
-        )
+        out_gathered, upper_x, lower_y, cot_six, head_context, upper_y, lower_x = tie(
+            out_gathered, upper_x, lower_y, cot_six, head_context, upper_y, lower_x
+        )
+        far_upper = swap(upper_y, "row", 4, 1)
+        far_lower = swap(lower_x, "row", 4, 2)
+        cot_mine = jnp.concatenate([cot_mixed, cot_two, cot_four, cot_six], axis=0)
+        cot_other = swap(cot_mine, "col", 8, 1)
         pieces = [[shard], [upper_x, lower_x], [upper_y, lower_y], [far_upper, far_lower]]
         places = [lax.axis_index("col") ^ (2 * step) for step in range(4)]
         cot_rows = place_blocks(
@@ -364,7 +356,7 @@
         )
     else:
         pieces = [[shard]] + [
-            [from_partner(shard, "row", step, row_size)] for step in range(1, row_size)
+            [to_partner(shard, "row", step, row_size)] for step in range(1, row_size)
         ]
         cot_rows = lax.all_gather(cot_mixed, "col", axis=0, tiled=True)
     gate_weight = rows_of(pieces, 0, model_rows)
@@ -386,6 +378,10 @@
     output_rank_rows = convert_half(out_pre[:, width:])
     layer_state = inputs + out_pre[:, :width] + matrix_product(output_rank_rows, out_upper)
     normed_mlp = convert_half(rms_scale(layer_state, gain_mlp))
+    normed_both = with_partner(normed, col_size)
+    context_both = with_partner(head_context, col_size)
+    rank_both = with_partner(output_rank_rows, col_size)
+    cot_both = halves_with_partner(cotangent, col_size)
 
     ffn_in = lax.all_gather(reorder(normed_mlp, order), "col", axis=0, tiled=True)
     rank_part = rank_width // row_size
@@ -415,36 +411,59 @@
 
     grad_down = convert_half(product(cot_rows, hidden_activated, contract_first))
     grad_down, gate_grad, up_grad = tie(grad_down, gate_grad, up_grad)
-    down_state = far_round(
-        [
-            jnp.concatenate([one, two], axis=0)
-            for one, two in zip(blocks_of(grad_down[:width]), blocks_of(grad_down[width:]))
-        ],
-        row_size,
-    )
-    normed_sum = convert_half(
-        product(gate_grad, gate_weight, contract_last)
-        + product(up_grad, up_weight, contract_last)
-    )
-    *down_state, normed_sum, gate_grad, up_grad = tie(
-        *near_sums(down_state, row_size), normed_sum, gate_grad, up_grad
-    )
-    down_state = near_round(down_state, row_size)
-    normed_grad = lax.psum_scatter(normed_sum, "col", scatter_dimension=0, tiled=True)
-    grad_gate = convert_half(product(ffn_in, gate_grad, contract_first))
-    grad_gate, up_grad = tie(grad_gate, up_grad)
-    gate_state = far_round(blocks_of(grad_gate), row_size)
-    grad_up = convert_half(product(ffn_in, up_grad, contract_first))
-    gate_state = near_sums(gate_state, row_size)
-    count = len(down_state)
-    *states, grad_up, hidden_activated = tie(*down_state, *gate_state, grad_up, hidden_activated)
-    down_total = add_all(states[:count])
-    gate_state = near_round(states[count:], row_size)
-    up_state = far_round(blocks_of(grad_up), row_size)
-    down_partial = convert_half(product(hidden_activated, down_weight, contract_last))
-    down_partial, normed_grad = tie(down_partial, normed_grad)
-
-    normed_grad = reorder(normed_grad, back_order).astype(jnp.float32)
+    down_blocks = [
+        jnp.concatenate([one, two], axis=0)
+        for one, two in zip(blocks_of(grad_down[:width]), blocks_of(grad_down[width:]))
+    ]
+    if row_size == 4:
+        own_down, far, free, last = split_blocks(down_blocks)
+        far = send_pair(far)
+        partial_sum = product(gate_grad, gate_weight, contract_last)
+        *far, partial_sum, up_grad, free_x, free_y = tie(*far, partial_sum, up_grad, *free)
+        last = add_pair(last, far)
+        free = send_pair((free_x, free_y))
+        normed_sum = convert_half(partial_sum + product(up_grad, up_weight, contract_last))
+        *free, normed_sum, gate_grad, up_grad, last_x, last_y = tie(
+            *free, normed_sum, gate_grad, up_grad, *last
+        )
+        normed_grad = lax.psum_scatter(normed_sum, "col", scatter_dimension=0, tiled=True)
+        last = send_pair((last_x, last_y))
+        grad_gate = convert_half(product(ffn_in, gate_grad, contract_first))
+        *down_parts, grad_gate, up_grad = tie(own_down, *free, *last, grad_gate, up_grad)
+        down_total = finish_sum(down_parts[0], down_parts[1:3], down_parts[3:])
+        own_gate, far, free, last = split_blocks(blocks_of(grad_gate))
+        far = send_pair(far)
+        grad_up = convert_half(product(ffn_in, up_grad, contract_first))
+        *far, grad_up, hidden_activated, free_x, free_y = tie(
+            *far, grad_up, hidden_activated, *free
+        )
+        gate_last = add_pair(last, far)
+        gate_free = send_pair((free_x, free_y))
+        own_up, far, up_free, up_last = split_blocks(blocks_of(grad_up))
+        far = send_pair(far)
+        down_partial = convert_half(product(hidden_activated, down_weight, contract_last))
+        *gate_free, far_x, far_y, normed_grad, down_partial = tie(
+            *gate_free, *far, normed_grad, down_partial
+        )
+        up_last = add_pair(up_last, (far_x, far_y))
+        gate_last = send_pair(gate_last)
+        up_free = send_pair(up_free)
+    else:
+        normed_sum = convert_half(
+            product(gate_grad, gate_weight, contract_last)
+            + product(up_grad, up_weight, contract_last)
+        )
+        normed_grad = lax.psum_scatter(normed_sum, "col", scatter_dimension=0, tiled=True)
+        grad_gate = convert_half(product(ffn_in, gate_grad, contract_first))
+        grad_up = convert_half(product(ffn_in, up_grad, contract_first))
+        down_partial = convert_half(product(hidden_activated, down_weight, contract_last))
+        down_total = row_sum(down_blocks, row_size)
+        gate_sum = row_sum(blocks_of(grad_gate), row_size)
+        up_sum = row_sum(blocks_of(grad_up), row_size)
+    down_sum, rank_sum = down_total[:model_rows], down_total[model_rows:]
+    summed = lax.psum_scatter(down_partial, "col", scatter_dimension=0, tiled=True)
+
+    normed_grad = reorder(normed_grad, order).astype(jnp.float32)
     state_out, norm_pull = jax.vjp(rms_scale, layer_state, gain_mlp)
     state_part, grad_gain_mlp = norm_pull(normed_grad)
     state_grad = cot_grad + state_part
@@ -453,40 +472,38 @@
     out_grad = jnp.concatenate([attn_grad, rank_out_grad], axis=1)
     context_grad = product(out_grad, out_weight, contract_last)
     grad_rows = convert_half(context_grad).reshape(row_total, HD)
-    up_state = near_sums(up_state, row_size)
-    count = len(gate_state)
-    *states, grad_rows = tie(*gate_state, *up_state, grad_rows)
-    gate_sum = add_all(states[:count])
-    up_state = near_round(states[count:], row_size)
     delta = jnp.sum(grad_rows.astype(jnp.float32) * mixed_rows, axis=1)
     weight_grad = product(grad_rows, value_rows, contract_last)
     score_grad = convert_half(probs.astype(jnp.float32) * (weight_grad - delta[:, None]))
+    if row_size == 4:
+        *gate_last, up_free_x, up_free_y, score_grad, up_last_x, up_last_y = tie(
+            *gate_last, *up_free, score_grad, *up_last
+        )
+        gate_sum = finish_sum(own_gate, gate_free, gate_last)
+        up_last = send_pair((up_last_x, up_last_y))
     query_acc = matrix_product(score_grad, key_rows)
+    if row_size == 4:
+        *up_last, query_acc = tie(*up_last, query_acc)
+        up_sum = finish_sum(own_up, (up_free_x, up_free_y), up_last)
     key_acc = product(score_grad, query_rows, contract_first)
     value_acc = product(probs, grad_rows, contract_first)
-    keyval_sum = lax.psum_scatter(
-        jnp.concatenate([convert_half(key_acc), convert_half(value_acc)], axis=1),
-        "col",
-        scatter_dimension=0,
-        tiled=True,
-    )
+    keyval_part = jnp.concatenate([convert_half(key_acc), convert_half(value_acc)], axis=1)
+    keyval_part, summed = tie(keyval_part, summed)
+    keyval_sum = lax.psum_scatter(keyval_part, "col", scatter_dimension=0, tiled=True)
     query_grad = convert_half(
         unrotate(
             query_acc.reshape(tok_dev, NH, HD) * scale, cosine[:, None, :], sine_part[:, None, :]
         ).reshape(tok_dev, NH * HD)
     )
-    grad_query = convert_half(product(normed, query_grad, contract_first))
-    *up_state, keyval_sum, down_partial, grad_query = tie(
-        *up_state, keyval_sum, down_partial, grad_query
-    )
-    up_sum = add_all(up_state)
+    core = lax.axis_index("col") % 2
+    query_right = halves_with_partner(query_grad, col_size)
+    grad_query = convert_half(product(normed_both, query_right, contract_first))
+    keyval_sum, grad_query = tie(keyval_sum, grad_query)
     keyval_sum = keyval_sum.astype(jnp.float32)
-    down_sum, rank_sum = down_total[:model_rows], down_total[model_rows:]
-    summed = lax.psum_scatter(down_partial, "col", scatter_dimension=0, tiled=True)
-    down_rank_rows = reorder(summed[:, width:], back_order)
+    down_rank_rows = reorder(summed[:, width:], order)
     layer_out = convert_half(
         layer_state
-        + reorder(summed[:, :width], back_order).astype(jnp.float32)
+        + reorder(summed[:, :width], order).astype(jnp.float32)
         + matrix_product(down_rank_rows, down_upper)
     )
     keyval_grad = jnp.concatenate(
@@ -499,53 +516,84 @@
     input_part, grad_gain_attn = first_pull(normed_back)
     input_grad = convert_half(state_grad + input_part)
 
-    grad_out = product(head_context, out_grad, contract_first)
-    grad_keyval = product(normed, keyval_grad, contract_first)
-    grad_out_upper = product(output_rank_rows, attn_grad, contract_first)
-    grad_down_upper = product(down_rank_rows, cotangent, contract_first)
+    chips = devices // 2
 
     def shared(values):
-        return convert_half(values).reshape(devices, gain_len, -1)
-
-    out_sum = scatter_all(
-        jnp.concatenate([shared(grad_out), shared(grad_out_upper)], axis=2),
-        row_size,
+        return convert_half(values).reshape(chips, 2 * gain_len, -1)
+
+    out_right = halves_with_partner(out_grad[:, :width], col_size)
+    rank_right = halves_with_partner(out_grad[:, width:], col_size)
+    grad_out = product(
+        context_both, jnp.concatenate([out_right, rank_right], axis=1), contract_first
+    )
+    grad_out_upper = product(rank_both, out_right, contract_first)
+    grad_keyval = product(
+        normed_both, halves_with_partner(keyval_grad, col_size), contract_first
+    )
+    grad_down_upper = product(
+        with_partner(down_rank_rows, col_size), cot_both, contract_first
+    )
+    gains = jnp.stack([grad_gain_attn, grad_gain_mlp])
+    gain = lax.dynamic_index_in_dim(gains, core, 0, keepdims=False) + swap(
+        lax.dynamic_index_in_dim(gains, 1 - core, 0, keepdims=False), "col", col_size, 1
+    )
+    out_first, out_second = share_cores(
+        scatter_chips(
+            jnp.concatenate([shared(grad_out), shared(grad_out_upper)], axis=2), row_size, col_size
+        ),
         col_size,
     )
-    query_sum = scatter_all(shared(grad_query), row_size, col_size)
-    keyval_total = scatter_all(
-        jnp.concatenate(
+    query_first, query_second = share_cores(
+        scatter_chips(shared(grad_query), row_size, col_size), col_size
+    )
+    keyval_first, keyval_second = share_cores(
+        scatter_chips(
+            jnp.concatenate(
+                [
+                    shared(grad_keyval),
+                    shared(grad_down_upper),
+                    jnp.pad(shared(gain), ((0, 0), (0, 0), (0, 127))),
+                ],
+                axis=2,
+            ),
+            row_size,
+            col_size,
+            parts=1,
+        ),
+        col_size,
+    )
+
+    def joined(first, second, start, size):
+        return jnp.concatenate([first[:, start : start + size], second[:, start : start + size]], axis=1)
+
+    def joined_rows(first, second, start, size):
+        return jnp.concatenate(
             [
-                shared(grad_keyval),
-                shared(grad_down_upper),
-                jnp.pad(
-                    jnp.stack([shared(grad_gain_attn)[..., 0], shared(grad_gain_mlp)[..., 0]], axis=2),
-                    ((0, 0), (0, 0), (0, 126)),
-                ),
+                half[:, start : start + size].reshape(adapter_rows, -1)
+                for half in (first, second)
             ],
-            axis=2,
-        ),
-        row_size,
-        col_size,
-        pieces=1,
-    )
-    keyval_width = grad_keyval.shape[1]
-    gain_at = keyval_width + upper_width
+            axis=1,
+        )
+
+    half_width = width // 2
+    half_rank = rank_width // 2
+    half_keyval = key_value_matrix.shape[1] // 2
+    half_upper = upper_width // 2
     return (
         layer_out,
         input_grad,
-        keyval_total[:, gain_at],
-        query_sum,
-        keyval_total[:, :keyval_width],
-        out_sum[:, :width],
-        out_sum[:, width:out_width],
-        out_sum[:, out_width:].reshape(adapter_rows, width),
-        keyval_total[:, gain_at + 1],
+        keyval_first[:, half_keyval + half_upper],
+        joined(query_first, query_second, 0, query_width // 2),
+        joined(keyval_first, keyval_second, 0, half_keyval),
+        joined(out_first, out_second, 0, half_width),
+        joined(out_first, out_second, half_width, half_rank),
+        joined_rows(out_first, out_second, half_width + half_rank, half_upper),
+        keyval_second[:, half_keyval + half_upper],
         gate_sum,
         up_sum,
         down_sum,
         rank_sum,
-        keyval_total[:, keyval_width:gain_at].reshape(adapter_rows, width),
+        joined_rows(keyval_first, keyval_second, half_keyval, half_upper),
     )
 
 

time: 1160 us -> 1160 us (level)
  other arithmetic: 124 us -> 165 us
  matrix products: 375 us -> 344 us
  waiting for transfers between devices: 445 us -> 427 us
    ppermute x47 -> x60, waiting for transfers between devices: 403 us -> 273 us  [swap(): return lax.ppermute(values, axis, [(i, i ^ bit) for i in range(size)])]
    all_gather x1, waiting for transfers between devices: 0.01 us -> 51.3 us  [per_device(): lax.all_gather(jnp.concatenate([convert_half(rotate(keyval_pre[:, :HD], c...]
    all_gather x1, waiting for transfers between devices: 33.1 us -> 77.1 us  [per_device(): lax.all_gather(jnp.concatenate([convert_half(query_matrix), convert_half(...]
    convert_element_type x36 -> x25, other arithmetic: 48.2 us -> 83.7 us  [convert_half(): return values.astype(jnp.bfloat16)]
    dot_general x9, matrix products: 134 us -> 114 us  [matrix_product(): return jnp.dot(left_side, right_side, preferred_element_type=jnp.float32)]
    all_gather x1, waiting for transfers between devices: 8.1 us -> 25.6 us  [per_device(): lax.all_gather(out_packed, ('row', 'col'), axis=0, tiled=True)]
    unnamed x229 -> x249, local copies, waits for them, and re-layouts: 49.4 us -> 37.8 us
    ppermute x47 -> x60, starting transfers between devices: 49.1 us -> 60.2 us  [swap(): return lax.ppermute(values, axis, [(i, i ^ bit) for i in range(size)])]
  transfers between devices with their start and end apart: 54 -> 67, of which waited for: 30 -> 33; matrix products, arithmetic and copies ran while one was open for 36% -> 38% of each run, Pallas kernels for 0% -> 0%
where the time goes in v3:
time: 1160 us; the launch traced here: 1150 us
  waiting for transfers between devices  427 us (37%)
  matrix products  344 us (30%)
  other arithmetic  165 us (14%)
  local copies, waits for them, and re-layouts  138 us (12%)
  starting transfers between devices  61.1 us (5%)
  between operations  16.3 us (1%)
    ppermute x60, waiting for transfers between devices, swap(): return lax.ppermute(values, axis, [(i, i ^ bit) for i in range(size)])  273 us
    dot_general x19, matrix products, product(): lax.dot_general(left_side, right_side, dims, preferred_element_type=jnp.f...  230 us
    dot_general x9, matrix products, matrix_product(): return jnp.dot(left_side, right_side, preferred_element_type=jnp.float32)  114 us
    convert_element_type x25, other arithmetic, convert_half(): return values.astype(jnp.bfloat16)  83.7 us
    all_gather x1, waiting for transfers between devices, per_device(): lax.all_gather(jnp.concatenate([convert_half(query_matrix), convert_half(...  77.1 us
    ppermute x60, starting transfers between devices, swap(): return lax.ppermute(values, axis, [(i, i ^ bit) for i in range(size)])  60.2 us
    all_gather x1, waiting for transfers between devices, per_device(): lax.all_gather(jnp.concatenate([convert_half(rotate(keyval_pre[:, :HD], c...  51.3 us
    unnamed x249, local copies, waits for them, and re-layouts  37.8 us
  transfers between devices with their start and end apart: 67, of which 33 were waited for; matrix products, arithmetic and copies ran while one was open for 38% of the time, Pallas kernels for 0%

profile of v3, /device:TPU:0, one launch (start us, length us, event | category | flops | bytes accessed | tf_op | source)
XLA Modules:
  0.0 1150.0 jit_solution(3446211372971699518)
XLA Ops:
  25.6 77.1 %all-gather.5.cloned.1.call-done = bf16[2048,2688]{1,0:T(8,128)(2,1)} async-done(((bf16[64,2688]{1,0:T(8,128)(2,1)}), bf16[2048,2688]{1,0:T(8,128)(2,1)}) %all-gather.5.cloned.1.call-update) | async-done | bytes 11010064 | tf_op jit(solution)/shard_map/all_gather | solution.py:229
  126.8 51.3 %all-gather.7.cloned.1.call-done = bf16[2304,512]{1,0:T(8,128)(2,1)} async-done(((bf16[288,512]{1,0:T(8,128)(2,1)}), bf16[2304,512]{1,0:T(8,128)(2,1)}) %all-gather.7.cloned.1.call-update) | async-done | bytes 2359312 | tf_op jit(solution)/shard_map/all_gather | solution.py:286
  178.1 11.6 %collective-permute-done.2 = bf16[288,2048]{1,0:T(8,128)(2,1)} collective-permute-done((bf16[288,2048]{1,0:T(8,128)(2,1)}, bf16[288,2048]{1,0:T(8,128)(2,1)}, u32[]{:S(2)}, u32[]{:S(2)}) %collective-permute-start.2) | collective-permute-done | bytes 1179680 | tf_op jit(solution)/shard_map/ppermute | solution.py:61
  200.0 8.6 fusion.174
  219.5 9.1 fusion.175
  243.9 8.9 collective-permute-done.6
  252.8 39.4 %collective-permute-done.4 = bf16[800,2048]{1,0:T(8,128)(2,1)} collective-permute-done((bf16[800,2048]{1,0:T(8,128)(2,1)}, bf16[800,2048]{1,0:T(8,128)(2,1)}, u32[]{:S(2)}, u32[]{:S(2)}) %collective-permute-start.4) | collective-permute-done | bytes 3276832 | tf_op jit(solution)/shard_map/ppermute | solution.py:61
  292.2 25.6 %all-gather.9.cloned.1.call-done = bf16[2048,2816]{1,0:T(8,128)(2,1)} async-done(((bf16[64,2816]{1,0:T(8,128)(2,1)}), bf16[2048,2816]{1,0:T(8,128)(2,1)}) %all-gather.9.cloned.1.call-update) | async-done | bytes 11534352 | tf_op jit(solution)/shard_map/all_gather | solution.py:325
  320.8 8.5 fusion.15
  369.4 43.4 %collective-permute-done.9 = bf16[800,2048]{1,0:T(8,128)(2,1)} collective-permute-done((bf16[800,2048]{1,0:T(8,128)(2,1)}, bf16[800,2048]{1,0:T(8,128)(2,1)}, u32[]{:S(2)}, u32[]{:S(2)}) %collective-permute-start.9) | collective-permute-done | bytes 3276832 | tf_op jit(solution)/shard_map/ppermute | solution.py:61
  443.9 29.9 %fusion.17 = f32[2304,2048]{1,0:T(8,128)} fusion(bf16[2304,2048]{1,0:T(8,128)(2,1)} %slice_dynamic-update-slice_fusion.13, bf16[2304,256]{1,0:T(8,128)(2,1)S(1)} %copy.37, bf16[2304,2048]{1,0:T(8,128)(2,1)} %slice_dynamic-update-slice_fusion.4), kind=kOutput, calls=%fused_computation.34 | convolution fusion | flops 21764505600 | bytes 38928384 | tf_op jit(solution)/shard_map/dot_general | solution.py:28
  473.9 27.1 %fusion.178 = f32[2304,2048]{1,0:T(8,128)} fusion(bf16[2304,2048]{1,0:T(8,128)(2,1)} %all-gather.11.cloned.1.call-done, bf16[2048,2048]{1,0:T(8,128)(2,1)} %slice_dynamic-update-slice_fusion.10), kind=kOutput, calls=%fused_computation.403 | convolution fusion | flops 19327352832 | bytes 36700160 | tf_op jit(solution)/shard_map/dot_general | solution.py:28
  501.0 24.4 %fusion.177 = f32[2304,2048]{1,0:T(8,128)} fusion(bf16[2304,2048]{1,0:T(8,128)(2,1)S(1)} %copy-done.91, bf16[2048,2048]{1,0:T(8,128)(2,1)} %pad_maximum_fusion.1), kind=kOutput, calls=%fused_computation.402 | convolution fusion | flops 19327352832 | bytes 36700160 | tf_op jit(solution)/shard_map/dot_general | solution.py:28
  525.4 29.9 %multiply_convert_fusion.1 = (bf16[2304,2048]{1,0:T(8,128)(2,1)}, bf16[2304,2048]{1,0:T(8,128)(2,1)}, bf16[2304,2048]{1,0:T(8,128)(2,1)}) fusion(f32[2304,2048]{1,0:T(8,128)S(1)} %bitcast.97, f32[2304,2048]{1,0:T(8,128)} %fusion.177, f32[2304,2048]{1,0:T(8,128)} %fusion.178), kind=kLoop, calls=%fused_computation.16 | loop fusion | flops 122683392 | bytes 84934656 | tf_op jit(solution)/shard_map/convert_element_type | solution.py:20
  555.3 28.8 %convolution_convert_fusion.1 = bf16[2304,2048]{1,0:T(8,128)(2,1)S(1)} fusion(bf16[2304,2048]{1,0:T(8,128)(2,1)} %get-tuple-element.138, bf16[2304,256]{1,0:T(8,128)(2,1)} %copy-done.55, bf16[2304,2048]{1,0:T(8,128)(2,1)} %slice_dynamic-update-slice_fusion.4), kind=kOutput, calls=%fused_computation.20 | convolution fusion | flops 21769224192 | bytes 29491200 | tf_op jit(solution)/shard_map/dot_general | solution.py:24
  593.3 26.9 %fusion.179 = f32[2304,2048]{1,0:T(8,128)} fusion(bf16[2304,2048]{1,0:T(8,128)(2,1)} %get-tuple-element.128, bf16[2048,2048]{1,0:T(8,128)(2,1)} %pad_maximum_fusion.1), kind=kOutput, calls=%fused_computation.404 | convolution fusion | flops 19327352832 | bytes 36700160 | tf_op jit(solution)/shard_map/dot_general | solution.py:24
  621.4 25.6 %fusion.180 = f32[2304,2048]{1,0:T(8,128)} fusion(bf16[2304,2048]{1,0:T(8,128)(2,1)S(1)} %bitcast.105, bf16[2048,2048]{1,0:T(8,128)(2,1)} %slice_dynamic-update-slice_fusion.10), kind=kOutput, calls=%fused_computation.405 | convolution fusion | flops 19327352832 | bytes 36700160 | tf_op jit(solution)/shard_map/dot_general | solution.py:24
  649.0 16.5 %add_convert_fusion = bf16[2304,2048]{1,0:T(8,128)(2,1)} fusion(f32[2304,2048]{1,0:T(8,128)} %fusion.179, f32[2304,2048]{1,0:T(8,128)} %fusion.180), kind=kLoop, calls=%fused_computation.15 | loop fusion | flops 9437184 | bytes 47185920 | tf_op jit(solution)/shard_map/convert_element_type | solution.py:20
  679.2 26.8 %convolution_convert_fusion.4 = bf16[2048,2048]{1,0:T(8,128)(2,1)} fusion(bf16[2304,2048]{1,0:T(8,128)(2,1)} %all-gather.11.cloned.1.call-done, bf16[2304,2048]{1,0:T(8,128)(2,1)} %get-tuple-element.128), kind=kOutput, calls=%fused_computation.33 | convolution fusion | flops 19331547136 | bytes 27262976 | tf_op jit(solution)/shard_map/dot_general | solution.py:24
  713.6 24.8 %convolution_convert_fusion.3 = bf16[2048,2048]{1,0:T(8,128)(2,1)} fusion(bf16[2304,2048]{1,0:T(8,128)(2,1)} %all-gather.11.cloned.1.call-done, bf16[2304,2048]{1,0:T(8,128)(2,1)S(1)} %bitcast.107), kind=kOutput, calls=%fused_computation.32 | convolution fusion | flops 19331547136 | bytes 27262976 | tf_op jit(solution)/shard_map/dot_general | solution.py:24
  747.7 27.2 %convolution_convert_fusion = bf16[2304,2304]{1,0:T(8,128)(2,1)} fusion(bf16[2304,2048]{1,0:T(8,128)(2,1)S(1)} %bitcast.103, bf16[2304,2048]{1,0:T(8,128)(2,1)} %slice_dynamic-update-slice_fusion.13), kind=kOutput, calls=%fused_computation.19 | convolution fusion | flops 21748580352 | bytes 29491200 | tf_op jit(solution)/shard_map/dot_general | solution.py:24
  774.8 12.7 %collective-permute-done.22 = bf16[256,2048]{1,0:T(8,128)(2,1)} collective-permute-done((bf16[256,2048]{1,0:T(8,128)(2,1)}, bf16[256,2048]{1,0:T(8,128)(2,1)}, u32[]{:S(2)}, u32[]{:S(2)}) %collective-permute-start.22) | collective-permute-done | bytes 1048608 | tf_op jit(solution)/shard_map/ppermute | solution.py:61
  825.5 8.5 multiply_convert_fusion
  839.1 12.9 %collective-permute-done.20 = bf16[256,2048]{1,0:T(8,128)(2,1)} collective-permute-done((bf16[256,2048]{1,0:T(8,128)(2,1)}, bf16[256,2048]{1,0:T(8,128)(2,1)}, u32[]{:S(2)}, u32[]{:S(2)}) %collective-permute-start.20) | collective-permute-done | bytes 1048608 | tf_op jit(solution)/shard_map/ppermute | solution.py:61
  898.2 7.3 collective-permute-done.26
  918.6 13.9 %collective-permute-done.54 = bf16[2,1,4,128,640]{4,3,2,1,0:T(8,128)(2,1)S(1)} collective-permute-done((bf16[2,1,4,128,640]{4,3,2,1,0:T(8,128)(2,1)S(1)}, bf16[2,1,4,128,640]{4,3,2,1,0:T(8,128)(2,1)S(1)}, u32[]{:S(2)}, u32[]{:S(2)}) %collective-permute-start.54) | collective-permute-done | bytes 1310752 | tf_op jit(solution)/shard_map/ppermute | solution.py:61
  945.9 7.4 collective-permute-done.55
  966.4 18.4 %collective-permute-done.56 = bf16[128,1280]{1,0:T(8,128)(2,1)S(1)} collective-permute-done((bf16[128,1280]{1,0:T(8,128)(2,1)S(1)}, bf16[128,1280]{1,0:T(8,128)(2,1)S(1)}, u32[]{:S(2)}, u32[]{:S(2)}) %collective-permute-start.56) | collective-permute-done | bytes 327712 | tf_op jit(solution)/shard_map/ppermute | solution.py:61
  1025.4 10.1 fusion.27
  1051.9 12.3 %collective-permute-done.42 = bf16[2,1,4,128,512]{4,3,2,1,0:T(8,128)(2,1)} collective-permute-done((bf16[2,1,4,128,512]{4,3,2,1,0:T(8,128)(2,1)}, bf16[2,1,4,128,512]{4,3,2,1,0:T(8,128)(2,1)}, u32[]{:S(2)}, u32[]{:S(2)}) %collective-permute-start.42) | collective-permute-done | bytes 1048608 | tf_op jit(solution)/shard_map/ppermute | solution.py:61
  1070.5 19.4 %collective-permute-done.34 = bf16[1,2,4,128,512]{4,3,2,1,0:T(8,128)(2,1)S(1)} collective-permute-done((bf16[1,2,4,128,512]{4,3,2,1,0:T(8,128)(2,1)S(1)}, bf16[1,2,4,128,512]{4,3,2,1,0:T(8,128)(2,1)S(1)}, u32[]{:S(2)}, u32[]{:S(2)}) %collective-permute-start.34) | collective-permute-done | bytes 1048608 | tf_op jit(solution)/shard_map/ppermute | solution.py:61
  1124.6 14.6 %collective-permute-done.45 = bf16[128,1024]{1,0:T(8,128)(2,1)S(1)} collective-permute-done((bf16[128,1024]{1,0:T(8,128)(2,1)S(1)}, bf16[128,1024]{1,0:T(8,128)(2,1)S(1)}, u32[]{:S(2)}, u32[]{:S(2)}) %collective-permute-start.45) | collective-permute-done | bytes 262176 | tf_op jit(solution)/shard_map/ppermute | solution.py:61
  (573 shorter events, 424.9 us)
Async XLA Ops:
  7.2 95.5 %all-gather.5.cloned.1.call-start = ((), (), s32[]{:S(2)}) async-start(), calls=%async_computation.3 | async-start | bytes 11354112 | tf_op jit(solution)/shard_map/all_gather | solution.py:229
  10.8 167.3 %all-gather.7.cloned.1.call-start = ((), (), s32[]{:S(2)}) async-start(), calls=%async_computation.4 | async-start | bytes 2654208 | tf_op jit(solution)/shard_map/all_gather | solution.py:286
  116.1 201.7 %all-gather.9.cloned.1.call-start = ((), (), s32[]{:S(2)}) async-start(), calls=%async_computation.5 | async-start | bytes 11894784 | tf_op jit(solution)/shard_map/all_gather | solution.py:325
  116.1 76.2 %collective-permute-start = (bf16[800,2048]{1,0:T(8,128)(2,1)}, bf16[800,2048]{1,0:T(8,128)(2,1)}, u32[]{:S(2)}, u32[]{:S(2)}) collective-permute-start(bf16[800,2048]{1,0:T(8,128)(2,1)} %get-tuple-element.96), channel_id=1, source_target_pairs={{0,16},{8,24},{16,0},{24,8},{1,17},{9,25},{17,1},{25,9},{2,18},{10... | collective-permute-start | bytes 9830408 | tf_op jit(solution)/shard_map/ppermute | solution.py:61
  117.6 74.7 %collective-permute-start.1 = (bf16[800,2048]{1,0:T(8,128)(2,1)}, bf16[800,2048]{1,0:T(8,128)(2,1)}, u32[]{:S(2)}, u32[]{:S(2)}) collective-permute-start(bf16[800,2048]{1,0:T(8,128)(2,1)} %get-tuple-element.97), channel_id=1, source_target_pairs={{0,8},{8,0},{16,24},{24,16},{1,9},{9,1},{17,25},{25,17},{2,10},{10... | collective-permute-start | bytes 9830408 | tf_op jit(solution)/shard_map/ppermute | solution.py:61
  118.2 71.5 %collective-permute-start.2 = (bf16[288,2048]{1,0:T(8,128)(2,1)}, bf16[288,2048]{1,0:T(8,128)(2,1)}, u32[]{:S(2)}, u32[]{:S(2)}) collective-permute-start(bf16[288,2048]{1,0:T(8,128)(2,1)} %pad_maximum_fusion.20), channel_id=1, source_target_pairs={{0,2},{1,3},{2,0},{3,1},{4,6},{5,7},{6,4},{7,5},{8,10},{9,11},{10,... | collective-permute-start | bytes 3538952 | tf_op jit(solution)/shard_map/ppermute | solution.py:61
  119.5 72.8 %collective-permute-start.3 = (bf16[288,2048]{1,0:T(8,128)(2,1)}, bf16[288,2048]{1,0:T(8,128)(2,1)}, u32[]{:S(2)}, u32[]{:S(2)}) collective-permute-start(bf16[288,2048]{1,0:T(8,128)(2,1)} %pad_maximum_fusion.20), channel_id=1, source_target_pairs={{0,4},{1,5},{2,6},{3,7},{4,0},{5,1},{6,2},{7,3},{8,12},{9,13},{10,... | collective-permute-start | bytes 3538952 | tf_op jit(solution)/shard_map/ppermute | solution.py:61
  192.4 281.5 %all-gather.11.cloned.1.call-start = ((), (), s32[]{:S(2)}) async-start(), calls=%async_computation.6 | async-start | bytes 10616832 | tf_op jit(solution)/shard_map/all_gather | solution.py:386
  197.9 94.3 %collective-permute-start.4 = (bf16[800,2048]{1,0:T(8,128)(2,1)}, bf16[800,2048]{1,0:T(8,128)(2,1)}, u32[]{:S(2)}, u32[]{:S(2)}) collective-permute-start(bf16[800,2048]{1,0:T(8,128)(2,1)} %get-tuple-element.96), channel_id=1, source_target_pairs={{0,8},{8,0},{16,24},{24,16},{1,9},{9,1},{17,25},{25,17},{2,10},{10... | collective-permute-start | bytes 9830408 | tf_op jit(solution)/shard_map/ppermute | solution.py:61
  199.4 92.8 %collective-permute-start.5 = (bf16[800,2048]{1,0:T(8,128)(2,1)}, bf16[800,2048]{1,0:T(8,128)(2,1)}, u32[]{:S(2)}, u32[]{:S(2)}) collective-permute-start(bf16[800,2048]{1,0:T(8,128)(2,1)} %get-tuple-element.97), channel_id=1, source_target_pairs={{0,16},{8,24},{16,0},{24,8},{1,17},{9,25},{17,1},{25,9},{2,18},{10... | collective-permute-start | bytes 9830408 | tf_op jit(solution)/shard_map/ppermute | solution.py:61
  217.5 35.3 %collective-permute-start.6 = (bf16[288,2048]{1,0:T(8,128)(2,1)}, bf16[288,2048]{1,0:T(8,128)(2,1)}, u32[]{:S(2)}, u32[]{:S(2)}) collective-permute-start(bf16[288,2048]{1,0:T(8,128)(2,1)} %pad_maximum_fusion.20), channel_id=1, source_target_pairs={{0,6},{1,7},{2,4},{3,5},{4,2},{5,3},{6,0},{7,1},{8,14},{9,15},{10,... | collective-permute-start | bytes 3538952 | tf_op jit(solution)/shard_map/ppermute | solution.py:61
  337.0 451.0 %reduce-scatter.4.cloned.1.call-start = ((), (), s32[]{:S(2)}) async-start(), calls=%async_computation.7 | async-start | bytes 10616832 | tf_op jit(solution)/shard_map/reduce_scatter | solution.py:429
  339.5 73.4 %collective-permute-start.9 = (bf16[800,2048]{1,0:T(8,128)(2,1)}, bf16[800,2048]{1,0:T(8,128)(2,1)}, u32[]{:S(2)}, u32[]{:S(2)}) collective-permute-start(bf16[800,2048]{1,0:T(8,128)(2,1)} %collective-permute-done), channel_id=1, source_target_pairs={{0,8},{8,0},{16,24},{24,16},{1,9},{9,1},{17,25},{25,17},{2,10},{10... | collective-permute-start | bytes 9830408 | tf_op jit(solution)/shard_map/ppermute | solution.py:61
  340.6 74.2 %collective-permute-start.8 = (bf16[800,2048]{1,0:T(8,128)(2,1)}, bf16[800,2048]{1,0:T(8,128)(2,1)}, u32[]{:S(2)}, u32[]{:S(2)}) collective-permute-start(bf16[800,2048]{1,0:T(8,128)(2,1)} %collective-permute-done.1), channel_id=1, source_target_pairs={{0,16},{8,24},{16,0},{24,8},{1,17},{9,25},{17,1},{25,9},{2,18},{10... | collective-permute-start | bytes 9830408 | tf_op jit(solution)/shard_map/ppermute | solution.py:61
  347.1 85.3 %collective-permute-start.7 = (bf16[1152,2048]{1,0:T(8,128)(2,1)S(1)}, bf16[1152,2048]{1,0:T(8,128)(2,1)S(1)}, u32[]{:S(2)}, u32[]{:S(2)}) collective-permute-start(bf16[1152,2048]{1,0:T(8,128)(2,1)S(1)} %pad_maximum_fusion.4), channel_id=1, source_target_pairs={{0,1},{1,0},{2,3},{3,2},{4,5},{5,4},{6,7},{7,6},{8,9},{9,8},{10,11... | collective-permute-start | bytes 14155784 | tf_op jit(solution)/shard_map/ppermute | solution.py:61
  675.0 268.2 %reduce-scatter.6.cloned.1.call-start = ((), (), s32[]{:S(2)}) async-start(), calls=%async_computation.8 | async-start | bytes 11943936 | tf_op jit(solution)/shard_map/reduce_scatter | solution.py:464
  743.5 31.3 %collective-permute-start.24 = (bf16[256,2048]{1,0:T(8,128)(2,1)}, bf16[256,2048]{1,0:T(8,128)(2,1)}, u32[]{:S(2)}, u32[]{:S(2)}) collective-permute-start(bf16[256,2048]{1,0:T(8,128)(2,1)} %get-tuple-element.197), channel_id=1, source_target_pairs={{0,8},{8,0},{16,24},{24,16},{1,9},{9,1},{17,25},{25,17},{2,10},{10... | collective-permute-start | bytes 3145736 | tf_op jit(solution)/shard_map/ppermute | solution.py:61
  745.1 42.5 %collective-permute-start.22 = (bf16[256,2048]{1,0:T(8,128)(2,1)}, bf16[256,2048]{1,0:T(8,128)(2,1)}, u32[]{:S(2)}, u32[]{:S(2)}) collective-permute-start(bf16[256,2048]{1,0:T(8,128)(2,1)} %get-tuple-element.135), channel_id=1, source_target_pairs={{0,8},{8,0},{16,24},{24,16},{1,9},{9,1},{17,25},{25,17},{2,10},{10... | collective-permute-start | bytes 3145736 | tf_op jit(solution)/shard_map/ppermute | solution.py:61
  746.5 41.5 %collective-permute-start.23 = (bf16[256,2048]{1,0:T(8,128)(2,1)}, bf16[256,2048]{1,0:T(8,128)(2,1)}, u32[]{:S(2)}, u32[]{:S(2)}) collective-permute-start(bf16[256,2048]{1,0:T(8,128)(2,1)} %get-tuple-element.136), channel_id=1, source_target_pairs={{0,16},{8,24},{16,0},{24,8},{1,17},{9,25},{17,1},{25,9},{2,18},{10... | collective-permute-start | bytes 3145736 | tf_op jit(solution)/shard_map/ppermute | solution.py:61
  788.0 234.0 %reduce-scatter.8.cloned.1.call-start = ((), (), s32[]{:S(2)}) async-start(), calls=%async_computation.9 | async-start | bytes 2654208 | tf_op jit(solution)/shard_map/reduce_scatter | solution.py:492
  789.4 227.7 %collective-permute-start.32 = (bf16[288,1024]{1,0:T(8,128)(2,1)}, bf16[288,1024]{1,0:T(8,128)(2,1)}, u32[]{:S(2)}, u32[]{:S(2)}) collective-permute-start(bf16[288,1024]{1,0:T(8,128)(2,1)} %get-tuple-element.223), channel_id=1, source_target_pairs={{0,1},{1,0},{2,3},{3,2},{4,5},{5,4},{6,7},{7,6},{8,9},{9,8},{10,11... | collective-permute-start | bytes 1769480 | tf_op jit(solution)/shard_map/ppermute | solution.py:61
  803.7 34.8 %collective-permute-start.18 = (bf16[256,2048]{1,0:T(8,128)(2,1)}, bf16[256,2048]{1,0:T(8,128)(2,1)}, u32[]{:S(2)}, u32[]{:S(2)}) collective-permute-start(bf16[256,2048]{1,0:T(8,128)(2,1)} %get-tuple-element.200), channel_id=1, source_target_pairs={{0,8},{8,0},{16,24},{24,16},{1,9},{9,1},{17,25},{25,17},{2,10},{10... | collective-permute-start | bytes 3145736 | tf_op jit(solution)/shard_map/ppermute | solution.py:61
  804.6 33.9 %collective-permute-start.19 = (bf16[256,2048]{1,0:T(8,128)(2,1)}, bf16[256,2048]{1,0:T(8,128)(2,1)}, u32[]{:S(2)}, u32[]{:S(2)}) collective-permute-start(bf16[256,2048]{1,0:T(8,128)(2,1)} %get-tuple-element.199), channel_id=1, source_target_pairs={{0,16},{8,24},{16,0},{24,8},{1,17},{9,25},{17,1},{25,9},{2,18},{10... | collective-permute-start | bytes 3145736 | tf_op jit(solution)/shard_map/ppermute | solution.py:61
  805.5 46.5 %collective-permute-start.20 = (bf16[256,2048]{1,0:T(8,128)(2,1)}, bf16[256,2048]{1,0:T(8,128)(2,1)}, u32[]{:S(2)}, u32[]{:S(2)}) collective-permute-start(bf16[256,2048]{1,0:T(8,128)(2,1)} %get-tuple-element.198), channel_id=1, source_target_pairs={{0,8},{8,0},{16,24},{24,16},{1,9},{9,1},{17,25},{25,17},{2,10},{10... | collective-permute-start | bytes 3145736 | tf_op jit(solution)/shard_map/ppermute | solution.py:61
  807.5 45.5 %collective-permute-start.21 = (bf16[256,2048]{1,0:T(8,128)(2,1)}, bf16[256,2048]{1,0:T(8,128)(2,1)}, u32[]{:S(2)}, u32[]{:S(2)}) collective-permute-start(bf16[256,2048]{1,0:T(8,128)(2,1)} %get-tuple-element.195), channel_id=1, source_target_pairs={{0,16},{8,24},{16,0},{24,8},{1,17},{9,25},{17,1},{25,9},{2,18},{10... | collective-permute-start | bytes 3145736 | tf_op jit(solution)/shard_map/ppermute | solution.py:61
  838.5 156.8 %collective-permute-start.28 = (bf16[288,2048]{1,0:T(8,128)(2,1)}, bf16[288,2048]{1,0:T(8,128)(2,1)}, u32[]{:S(2)}, u32[]{:S(2)}) collective-permute-start(bf16[288,2048]{1,0:T(8,128)(2,1)} %fusion.26), channel_id=1, source_target_pairs={{0,1},{1,0},{2,3},{3,2},{4,5},{5,4},{6,7},{7,6},{8,9},{9,8},{10,11... | collective-permute-start | bytes 3538952 | tf_op jit(solution)/shard_map/ppermute | solution.py:61
  838.6 46.7 %collective-permute-start.48 = (bf16[288,2048]{1,0:T(8,128)(2,1)}, bf16[288,2048]{1,0:T(8,128)(2,1)}, u32[]{:S(2)}, u32[]{:S(2)}) collective-permute-start(bf16[288,2048]{1,0:T(8,128)(2,1)} %convert_element_type.419), channel_id=1, source_target_pairs={{0,1},{1,0},{2,3},{3,2},{4,5},{5,4},{6,7},{7,6},{8,9},{9,8},{10,11... | collective-permute-start | bytes 3538952 | tf_op jit(solution)/shard_map/ppermute | solution.py:61
  893.4 39.1 %collective-permute-start.54 = (bf16[2,1,4,128,640]{4,3,2,1,0:T(8,128)(2,1)S(1)}, bf16[2,1,4,128,640]{4,3,2,1,0:T(8,128)(2,1)S(1)}, u32[]{:S(2)}, u32[]{:S(2)}) collective-permute-start(bf16[2,1,4,128,640]{4,3,2,1,0:T(8,128)(2,1)S(1)} %fusion.56), channel_id=1, source_target_pairs={{0,8},{8,0},{16,24},{24,16},{1,9},{9,1},{17,25},{25,17},{2,10},{10... | collective-permute-start | bytes 3932168 | tf_op jit(solution)/shard_map/ppermute | solution.py:61
  905.5 34.1 %collective-permute-start.51 = (bf16[1,2,4,128,640]{4,3,2,1,0:T(8,128)(2,1)S(1)}, bf16[1,2,4,128,640]{4,3,2,1,0:T(8,128)(2,1)S(1)}, u32[]{:S(2)}, u32[]{:S(2)}) collective-permute-start(bf16[1,2,4,128,640]{4,3,2,1,0:T(8,128)(2,1)S(1)} %constant_dynamic-slice_fusion.5), channel_id=1, source_target_pairs={{0,16},{8,24},{16,0},{24,8},{1,17},{9,25},{17,1},{25,9},{2,18},{10... | collective-permute-start | bytes 3932168 | tf_op jit(solution)/shard_map/ppermute | solution.py:61
  961.1 33.9 %collective-permute-start.58 = (bf16[128,1280]{1,0:T(8,128)(2,1)S(1)}, bf16[128,1280]{1,0:T(8,128)(2,1)S(1)}, u32[]{:S(2)}, u32[]{:S(2)}) collective-permute-start(bf16[128,1280]{1,0:T(8,128)(2,1)S(1)} %get-tuple-element.219), channel_id=1, source_target_pairs={{0,6},{1,7},{2,4},{3,5},{4,2},{5,3},{6,0},{7,1},{8,14},{9,15},{10,... | collective-permute-start | bytes 983048 | tf_op jit(solution)/shard_map/ppermute | solution.py:61
  1049.1 40.9 %collective-permute-start.34 = (bf16[1,2,4,128,512]{4,3,2,1,0:T(8,128)(2,1)S(1)}, bf16[1,2,4,128,512]{4,3,2,1,0:T(8,128)(2,1)S(1)}, u32[]{:S(2)}, u32[]{:S(2)}) collective-permute-start(bf16[1,2,4,128,512]{4,3,2,1,0:T(8,128)(2,1)S(1)} %constant_dynamic-slice_fusion.17), channel_id=1, source_target_pairs={{0,16},{8,24},{16,0},{24,8},{1,17},{9,25},{17,1},{25,9},{2,18},{10... | collective-permute-start | bytes 3145736 | tf_op jit(solution)/shard_map/ppermute | solution.py:61
  1065.8 34.3 %collective-permute-start.43 = (bf16[1,1,4,128,512]{4,3,2,1,0:T(8,128)(2,1)S(1)}, bf16[1,1,4,128,512]{4,3,2,1,0:T(8,128)(2,1)S(1)}, u32[]{:S(2)}, u32[]{:S(2)}) collective-permute-start(bf16[1,1,4,128,512]{4,3,2,1,0:T(8,128)(2,1)S(1)} %constant_dynamic-slice_fusion.11), channel_id=1, source_target_pairs={{0,16},{8,24},{16,0},{24,8},{1,17},{9,25},{17,1},{25,9},{2,18},{10... | collective-permute-start | bytes 1572872 | tf_op jit(solution)/shard_map/ppermute | solution.py:61
  (155 other events, 2654.6 us)
Sparse Core Ops, SparseCore 0:
  11.6 91.0 all-gather.4
  116.2 61.8 all-gather.6
  192.5 125.2 all-gather.8
  337.1 89.1 all-gather.10
  675.2 97.6 reduce-scatter.3
  788.2 108.7 reduce-scatter.5
  943.4 43.5 reduce-scatter.7

commit v4 on v3

--- a/solution.py
+++ b/solution.py
@@ -253,6 +253,10 @@
         ],
         axis=0,
     )
+    own_seg = lax.dynamic_slice_in_dim(segment_numbers, start_row, tok_dev)
+    own_pos = lax.dynamic_slice_in_dim(positions, start_row, tok_dev)
+    cosine, sine_part = rope_tables(own_pos)
+    in_gathered, cosine, sine_part = tie(in_gathered, cosine, sine_part)
     model_rows = gate_matrix.shape[0]
     by_pairs = row_size == 4 and col_size == 8
     cot_grad = cotangent.astype(jnp.float32)
@@ -271,9 +275,6 @@
     gains = in_gathered[:, in_width:].astype(jnp.float32)
     gain_attn = gains[:, 0]
     gain_mlp = gains[:, 1]
-    own_seg = lax.dynamic_slice_in_dim(segment_numbers, start_row, tok_dev)
-    own_pos = lax.dynamic_slice_in_dim(positions, start_row, tok_dev)
-    cosine, sine_part = rope_tables(own_pos)
     inputs = tokens.astype(jnp.float32)
     normed = convert_half(rms_scale(inputs, gain_attn))
     in_pre = matrix_product(normed, in_weight)
@@ -339,14 +340,32 @@
     mixed_rows = matrix_product(probs, value_rows)
     head_context = convert_half(mixed_rows.reshape(tok_dev, NH * HD))
     if by_pairs:
-        out_gathered, upper_x, lower_y, cot_six, head_context, upper_y, lower_x = tie(
-            out_gathered, upper_x, lower_y, cot_six, head_context, upper_y, lower_x
-        )
-        far_upper = swap(upper_y, "row", 4, 1)
-        far_lower = swap(lower_x, "row", 4, 2)
+        head_context, upper_x, lower_y, cot_six, upper_y, lower_x = tie(
+            head_context, upper_x, lower_y, cot_six, upper_y, lower_x
+        )
+        quarter = upper_y.shape[0] // 2
         cot_mine = jnp.concatenate([cot_mixed, cot_two, cot_four, cot_six], axis=0)
         cot_other = swap(cot_mine, "col", 8, 1)
-        pieces = [[shard], [upper_x, lower_x], [upper_y, lower_y], [far_upper, far_lower]]
+        far_upper = [swap(upper_y[:quarter], "row", 4, 1)]
+        far_lower = [swap(lower_x[:quarter], "row", 4, 2)]
+    rank_width = output_adapter_first.shape[1]
+    out_width = width + rank_width
+    upper_width = adapter_rows * width // gain_len
+    out_weight = out_gathered[:, :out_width]
+    out_upper = out_gathered[:, out_width : out_width + upper_width].reshape(-1, width)
+    down_upper = out_gathered[:, out_width + upper_width :].reshape(-1, width)
+    out_pre = matrix_product(head_context, out_weight)
+    output_rank_rows = convert_half(out_pre[:, width:])
+    layer_state = inputs + out_pre[:, :width] + matrix_product(output_rank_rows, out_upper)
+    normed_mlp = convert_half(rms_scale(layer_state, gain_mlp))
+    normed_mlp = reorder(normed_mlp, order)
+    if by_pairs:
+        normed_mlp, far_upper[0], far_lower[0], cot_other, upper_y, lower_x = tie(
+            normed_mlp, far_upper[0], far_lower[0], cot_other, upper_y, lower_x
+        )
+        far_upper.append(swap(upper_y[quarter:], "row", 4, 1))
+        far_lower.append(swap(lower_x[quarter:], "row", 4, 2))
+        pieces = [[shard], [upper_x, lower_x], [upper_y, lower_y], [*far_upper, *far_lower]]
         places = [lax.axis_index("col") ^ (2 * step) for step in range(4)]
         cot_rows = place_blocks(
             [cot_mine[tok_dev * step : tok_dev * (step + 1)] for step in range(4)]
@@ -368,22 +387,11 @@
         ],
         axis=0,
     )
-    rank_width = output_adapter_first.shape[1]
-    out_width = width + rank_width
-    upper_width = adapter_rows * width // gain_len
-    out_weight = out_gathered[:, :out_width]
-    out_upper = out_gathered[:, out_width : out_width + upper_width].reshape(-1, width)
-    down_upper = out_gathered[:, out_width + upper_width :].reshape(-1, width)
-    out_pre = matrix_product(head_context, out_weight)
-    output_rank_rows = convert_half(out_pre[:, width:])
-    layer_state = inputs + out_pre[:, :width] + matrix_product(output_rank_rows, out_upper)
-    normed_mlp = convert_half(rms_scale(layer_state, gain_mlp))
+    ffn_in = lax.all_gather(normed_mlp, "col", axis=0, tiled=True)
     normed_both = with_partner(normed, col_size)
     context_both = with_partner(head_context, col_size)
     rank_both = with_partner(output_rank_rows, col_size)
     cot_both = halves_with_partner(cotangent, col_size)
-
-    ffn_in = lax.all_gather(reorder(normed_mlp, order), "col", axis=0, tiled=True)
     rank_part = rank_width // row_size
     upper_mixed = jnp.concatenate(
         [
@@ -395,8 +403,17 @@
     rank_rows = convert_half(product(cot_rows, upper_mixed, contract_last))
     cot_rows = jnp.concatenate([cot_rows, rank_rows], axis=1)
     hidden_grad = matrix_product(cot_rows, down_weight)
-    ffn_in, hidden_grad, gate_weight, up_weight = tie(
-        ffn_in, hidden_grad, gate_weight, up_weight
+    ffn_in, hidden_grad, gate_weight, up_weight, normed_both, context_both, rank_both, cot_both = (
+        tie(
+            ffn_in,
+            hidden_grad,
+            gate_weight,
+            up_weight,
+            normed_both,
+            context_both,
+            rank_both,
+            cot_both,
+        )
     )
     gate_values = matrix_product(ffn_in, gate_weight)
     up_values = matrix_product(ffn_in, up_weight)
@@ -415,18 +432,38 @@
         jnp.concatenate([one, two], axis=0)
         for one, two in zip(blocks_of(grad_down[:width]), blocks_of(grad_down[width:]))
     ]
+    half_width = width // 2
+    down_split = half_width + rank_width
+
+    def normed_part(start, left_gate, left_up):
+        stop = start + half_width
+        return convert_half(
+            product(left_gate, gate_weight[start:stop], contract_last)
+            + product(left_up, up_weight[start:stop], contract_last)
+        )
+
+    def col_sum(values):
+        return lax.psum_scatter(values, "col", scatter_dimension=0, tiled=True)
+
+    def down_product():
+        weight = jnp.concatenate([down_weight[half_width:], down_weight[:half_width]], axis=0)
+        return convert_half(product(hidden_activated, weight, contract_last))
+
     if row_size == 4:
         own_down, far, free, last = split_blocks(down_blocks)
         far = send_pair(far)
-        partial_sum = product(gate_grad, gate_weight, contract_last)
-        *far, partial_sum, up_grad, free_x, free_y = tie(*far, partial_sum, up_grad, *free)
+        first_part = normed_part(0, gate_grad, up_grad)
+        *far, first_part, gate_grad, up_grad, free_x, free_y = tie(
+            *far, first_part, gate_grad, up_grad, *free
+        )
+        first_sum = col_sum(first_part)
         last = add_pair(last, far)
         free = send_pair((free_x, free_y))
-        normed_sum = convert_half(partial_sum + product(up_grad, up_weight, contract_last))
-        *free, normed_sum, gate_grad, up_grad, last_x, last_y = tie(
-            *free, normed_sum, gate_grad, up_grad, *last
-        )
-        normed_grad = lax.psum_scatter(normed_sum, "col", scatter_dimension=0, tiled=True)
+        second_part = normed_part(half_width, gate_grad, up_grad)
+        *free, second_part, gate_grad, up_grad, last_x, last_y = tie(
+            *free, second_part, gate_grad, up_grad, *last
+        )
+        second_sum = col_sum(second_part)
         last = send_pair((last_x, last_y))
         grad_gate = convert_half(product(ffn_in, gate_grad, contract_first))
         *down_parts, grad_gate, up_grad = tie(own_down, *free, *last, grad_gate, up_grad)
@@ -439,29 +476,26 @@
         )
         gate_last = add_pair(last, far)
         gate_free = send_pair((free_x, free_y))
+        down_partial = down_product()
+        *gate_free, last_x, last_y, down_partial, grad_up = tie(
+            *gate_free, *gate_last, down_partial, grad_up
+        )
         own_up, far, up_free, up_last = split_blocks(blocks_of(grad_up))
-        far = send_pair(far)
-        down_partial = convert_half(product(hidden_activated, down_weight, contract_last))
-        *gate_free, far_x, far_y, normed_grad, down_partial = tie(
-            *gate_free, *far, normed_grad, down_partial
-        )
-        up_last = add_pair(up_last, (far_x, far_y))
-        gate_last = send_pair(gate_last)
-        up_free = send_pair(up_free)
+        gate_last = send_pair((last_x, last_y))
+        up_far = send_pair(far)
     else:
-        normed_sum = convert_half(
-            product(gate_grad, gate_weight, contract_last)
-            + product(up_grad, up_weight, contract_last)
-        )
-        normed_grad = lax.psum_scatter(normed_sum, "col", scatter_dimension=0, tiled=True)
+        first_sum = col_sum(normed_part(0, gate_grad, up_grad))
+        second_sum = col_sum(normed_part(half_width, gate_grad, up_grad))
         grad_gate = convert_half(product(ffn_in, gate_grad, contract_first))
         grad_up = convert_half(product(ffn_in, up_grad, contract_first))
-        down_partial = convert_half(product(hidden_activated, down_weight, contract_last))
+        down_partial = down_product()
         down_total = row_sum(down_blocks, row_size)
         gate_sum = row_sum(blocks_of(grad_gate), row_size)
         up_sum = row_sum(blocks_of(grad_up), row_size)
     down_sum, rank_sum = down_total[:model_rows], down_total[model_rows:]
-    summed = lax.psum_scatter(down_partial, "col", scatter_dimension=0, tiled=True)
+    summed = col_sum(down_partial[:, :down_split])
+    down_rest = down_partial[:, down_split:]
+    normed_grad = jnp.concatenate([first_sum, second_sum], axis=1)
 
     normed_grad = reorder(normed_grad, order).astype(jnp.float32)
     state_out, norm_pull = jax.vjp(rms_scale, layer_state, gain_mlp)
@@ -476,36 +510,58 @@
     weight_grad = product(grad_rows, value_rows, contract_last)
     score_grad = convert_half(probs.astype(jnp.float32) * (weight_grad - delta[:, None]))
     if row_size == 4:
-        *gate_last, up_free_x, up_free_y, score_grad, up_last_x, up_last_y = tie(
-            *gate_last, *up_free, score_grad, *up_last
+        *gate_last, far_x, far_y, score_grad, free_x, free_y = tie(
+            *gate_last, *up_far, score_grad, *up_free
         )
         gate_sum = finish_sum(own_gate, gate_free, gate_last)
-        up_last = send_pair((up_last_x, up_last_y))
+        up_last = add_pair(up_last, (far_x, far_y))
+        up_free = send_pair((free_x, free_y))
     query_acc = matrix_product(score_grad, key_rows)
-    if row_size == 4:
-        *up_last, query_acc = tie(*up_last, query_acc)
-        up_sum = finish_sum(own_up, (up_free_x, up_free_y), up_last)
-    key_acc = product(score_grad, query_rows, contract_first)
-    value_acc = product(probs, grad_rows, contract_first)
-    keyval_part = jnp.concatenate([convert_half(key_acc), convert_half(value_acc)], axis=1)
-    keyval_part, summed = tie(keyval_part, summed)
-    keyval_sum = lax.psum_scatter(keyval_part, "col", scatter_dimension=0, tiled=True)
     query_grad = convert_half(
         unrotate(
             query_acc.reshape(tok_dev, NH, HD) * scale, cosine[:, None, :], sine_part[:, None, :]
         ).reshape(tok_dev, NH * HD)
     )
+    query_grad, score_grad = tie(query_grad, score_grad)
+    key_acc = product(score_grad, query_rows, contract_first)
+    value_acc = product(probs, grad_rows, contract_first)
+    keyval_part = jnp.concatenate([convert_half(key_acc), convert_half(value_acc)], axis=1)
+    if row_size == 4:
+        *up_free, keyval_part, query_grad, last_x, last_y = tie(
+            *up_free, keyval_part, query_grad, *up_last
+        )
+        up_last = send_pair((last_x, last_y))
+    keyval_part, summed = tie(keyval_part, summed)
+    keyval_sum = col_sum(keyval_part)
     core = lax.axis_index("col") % 2
     query_right = halves_with_partner(query_grad, col_size)
     grad_query = convert_half(product(normed_both, query_right, contract_first))
-    keyval_sum, grad_query = tie(keyval_sum, grad_query)
-    keyval_sum = keyval_sum.astype(jnp.float32)
-    down_rank_rows = reorder(summed[:, width:], order)
+    chips = devices // 2
+
+    def shared(values):
+        return convert_half(values).reshape(chips, 2 * gain_len, -1)
+
+    out_right = halves_with_partner(out_grad[:, :width], col_size)
+    rank_right = halves_with_partner(out_grad[:, width:], col_size)
+    grad_out = product(
+        context_both, jnp.concatenate([out_right, rank_right], axis=1), contract_first
+    )
+    grad_out_upper = product(rank_both, out_right, contract_first)
+    out_group = jnp.concatenate([shared(grad_out), shared(grad_out_upper)], axis=2)
+    query_group = shared(grad_query)
+    if row_size == 4:
+        *up_last, out_group, query_group = tie(*up_last, out_group, query_group)
+        up_sum = finish_sum(own_up, up_free, up_last)
+    down_rank_rows = reorder(summed[:, half_width:], order)
+    keyval_sum, down_rest = tie(keyval_sum, down_rest)
+    down_rest = col_sum(down_rest)
+    down_all = jnp.concatenate([down_rest, summed[:, :half_width]], axis=1)
     layer_out = convert_half(
         layer_state
-        + reorder(summed[:, :width], order).astype(jnp.float32)
+        + reorder(down_all, order).astype(jnp.float32)
         + matrix_product(down_rank_rows, down_upper)
     )
+    keyval_sum = keyval_sum.astype(jnp.float32)
     keyval_grad = jnp.concatenate(
         [convert_half(unrotate(keyval_sum[:, :HD], cosine, sine_part)), convert_half(keyval_sum[:, HD:])],
         axis=1,
@@ -516,17 +572,6 @@
     input_part, grad_gain_attn = first_pull(normed_back)
     input_grad = convert_half(state_grad + input_part)
 
-    chips = devices // 2
-
-    def shared(values):
-        return convert_half(values).reshape(chips, 2 * gain_len, -1)
-
-    out_right = halves_with_partner(out_grad[:, :width], col_size)
-    rank_right = halves_with_partner(out_grad[:, width:], col_size)
-    grad_out = product(
-        context_both, jnp.concatenate([out_right, rank_right], axis=1), contract_first
-    )
-    grad_out_upper = product(rank_both, out_right, contract_first)
     grad_keyval = product(
         normed_both, halves_with_partner(keyval_grad, col_size), contract_first
     )
@@ -538,13 +583,10 @@
         lax.dynamic_index_in_dim(gains, 1 - core, 0, keepdims=False), "col", col_size, 1
     )
     out_first, out_second = share_cores(
-        scatter_chips(
-            jnp.concatenate([shared(grad_out), shared(grad_out_upper)], axis=2), row_size, col_size
-        ),
-        col_size,
+        scatter_chips(out_group, row_size, col_size), col_size
     )
     query_first, query_second = share_cores(
-        scatter_chips(shared(grad_query), row_size, col_size), col_size
+        scatter_chips(query_group, row_size, col_size), col_size
     )
     keyval_first, keyval_second = share_cores(
         scatter_chips(
@@ -575,7 +617,6 @@
             axis=1,
         )
 
-    half_width = width // 2
     half_rank = rank_width // 2
     half_keyval = key_value_matrix.shape[1] // 2
     half_upper = upper_width // 2

time: 1160 us -> 1170 us (level)
  waiting for transfers between devices: 427 us -> 372 us
  local copies, waits for them, and re-layouts: 138 us -> 190 us
    all_gather x1, waiting for transfers between devices: 25.6 us -> 0.01 us  [per_device(): lax.all_gather(out_packed, ('row', 'col'), axis=0, tiled=True)]
    unnamed x249 -> x268, local copies, waits for them, and re-layouts: 37.8 us -> 62.8 us
    ppermute x60 -> x62, waiting for transfers between devices: 273 us -> 249 us  [swap(): return lax.ppermute(values, axis, [(i, i ^ bit) for i in range(size)])]
    slice x6 -> x9, local copies, waits for them, and re-layouts: 6.5 us -> 19.5 us  [the longest x1 5.01 us: per_device(): down_rest = down_partial[:, down_split:]]
    convert_element_type x25 -> x23, other arithmetic: 83.7 us -> 73.9 us  [convert_half(): return values.astype(jnp.bfloat16)]
    ppermute x60 -> x62, starting transfers between devices: 60.2 us -> 68.3 us  [swap(): return lax.ppermute(values, axis, [(i, i ^ bit) for i in range(size)])]
    dot_general x19 -> x21, matrix products: 230 us -> 237 us  [product(): lax.dot_general(left_side, right_side, dims, preferred_element_type=jnp.f...]
  transfers between devices with their start and end apart: 67 -> 71, of which waited for: 33 -> 27; matrix products, arithmetic and copies ran while one was open for 38% -> 46% of each run, Pallas kernels for 0% -> 0%
where the time goes in v4:
time: 1170 us; the launch traced here: 1160 us
  waiting for transfers between devices  372 us (32%)
  matrix products  351 us (30%)
  local copies, waits for them, and re-layouts  190 us (16%)
  other arithmetic  165 us (14%)
  starting transfers between devices  69.3 us (6%)
  between operations  15.9 us (1%)
    ppermute x62, waiting for transfers between devices, swap(): return lax.ppermute(values, axis, [(i, i ^ bit) for i in range(size)])  249 us
    dot_general x21, matrix products, product(): lax.dot_general(left_side, right_side, dims, preferred_element_type=jnp.f...  237 us
    dot_general x9, matrix products, matrix_product(): return jnp.dot(left_side, right_side, preferred_element_type=jnp.float32)  114 us
    all_gather x1, waiting for transfers between devices, per_device(): lax.all_gather(jnp.concatenate([convert_half(query_matrix), convert_half(...  75.4 us
    convert_element_type x23, other arithmetic, convert_half(): return values.astype(jnp.bfloat16)  73.9 us
    ppermute x62, starting transfers between devices, swap(): return lax.ppermute(values, axis, [(i, i ^ bit) for i in range(size)])  68.3 us
    unnamed x268, local copies, waits for them, and re-layouts  62.8 us
    all_gather x1, waiting for transfers between devices, per_device(): lax.all_gather(jnp.concatenate([convert_half(rotate(keyval_pre[:, :HD], c...  47 us
  transfers between devices with their start and end apart: 71, of which 27 were waited for; matrix products, arithmetic and copies ran while one was open for 46% of the time, Pallas kernels for 0%

profile of v4, /device:TPU:0, one launch (start us, length us, event | category | flops | bytes accessed | tf_op | source)
XLA Modules:
  0.0 1162.4 jit_solution(6789167277984493248)
XLA Ops:
  27.3 75.4 %all-gather.5.cloned.1.call-done = bf16[2048,2688]{1,0:T(8,128)(2,1)} async-done(((bf16[64,2688]{1,0:T(8,128)(2,1)}), bf16[2048,2688]{1,0:T(8,128)(2,1)}) %all-gather.5.cloned.1.call-update) | async-done | bytes 11010064 | tf_op jit(solution)/shard_map/all_gather | solution.py:229
  130.1 47.0 %all-gather.7.cloned.1.call-done = bf16[2304,512]{1,0:T(8,128)(2,1)} async-done(((bf16[288,512]{1,0:T(8,128)(2,1)}), bf16[2304,512]{1,0:T(8,128)(2,1)}) %all-gather.7.cloned.1.call-update) | async-done | bytes 2359312 | tf_op jit(solution)/shard_map/all_gather | solution.py:287
  177.2 11.6 %collective-permute-done.2 = bf16[288,2048]{1,0:T(8,128)(2,1)} collective-permute-done((bf16[288,2048]{1,0:T(8,128)(2,1)S(1)}, bf16[288,2048]{1,0:T(8,128)(2,1)}, u32[]{:S(2)}, u32[]{:S(2)}) %collective-permute-start.2) | collective-permute-done | bytes 1179680 | tf_op jit(solution)/shard_map/ppermute | solution.py:61
  206.6 8.6 fusion.158
  226.3 8.8 fusion.159
  251.2 11.3 collective-permute-done.6
  262.6 41.1 %collective-permute-done.4 = bf16[800,2048]{1,0:T(8,128)(2,1)} collective-permute-done((bf16[800,2048]{1,0:T(8,128)(2,1)}, bf16[800,2048]{1,0:T(8,128)(2,1)}, u32[]{:S(2)}, u32[]{:S(2)}) %collective-permute-start.4) | collective-permute-done | bytes 3276832 | tf_op jit(solution)/shard_map/ppermute | solution.py:61
  327.3 8.1 fusion.15
  393.4 21.2 %collective-permute-done.10 = bf16[400,2048]{1,0:T(8,128)(2,1)S(1)} collective-permute-done((bf16[400,2048]{1,0:T(8,128)(2,1)S(1)}, bf16[400,2048]{1,0:T(8,128)(2,1)S(1)}, u32[]{:S(2)}, u32[]{:S(2)}) %collective-permute-start.10) | collective-permute-done | bytes 1638432 | tf_op jit(solution)/shard_map/ppermute | solution.py:61
  443.9 29.4 %fusion.17 = f32[2304,2048]{1,0:T(8,128)} fusion(bf16[2304,2048]{1,0:T(8,128)(2,1)} %slice_dynamic-update-slice_fusion.22, bf16[2304,256]{1,0:T(8,128)(2,1)S(1)} %copy.37, bf16[2304,2048]{1,0:T(8,128)(2,1)} %slice_dynamic-update-slice_fusion.11), kind=kOutput, calls=%fused_computation.34 | convolution fusion | flops 21764505600 | bytes 38928384 | tf_op jit(solution)/shard_map/dot_general | solution.py:28
  473.4 26.5 %fusion.162 = f32[2304,2048]{1,0:T(8,128)} fusion(bf16[2304,2048]{1,0:T(8,128)(2,1)} %all-gather.11.cloned.1.call-done, bf16[2048,2048]{1,0:T(8,128)(2,1)} %slice_dynamic-update-slice_fusion.15), kind=kOutput, calls=%fused_computation.415 | convolution fusion | flops 19327352832 | bytes 36700160 | tf_op jit(solution)/shard_map/dot_general | solution.py:28
  499.9 24.6 %fusion.161 = f32[2304,2048]{1,0:T(8,128)} fusion(bf16[2304,2048]{1,0:T(8,128)(2,1)S(1)} %copy-done.107, bf16[2048,2048]{1,0:T(8,128)(2,1)} %slice_dynamic-update-slice_fusion.20), kind=kOutput, calls=%fused_computation.414 | convolution fusion | flops 19327352832 | bytes 36700160 | tf_op jit(solution)/shard_map/dot_general | solution.py:28
  524.5 29.9 %multiply_convert_fusion.1 = (bf16[2304,2048]{1,0:T(8,128)(2,1)}, bf16[2304,2048]{1,0:T(8,128)(2,1)}, bf16[2304,2048]{1,0:T(8,128)(2,1)}) fusion(f32[2304,2048]{1,0:T(8,128)S(1)} %bitcast.102, f32[2304,2048]{1,0:T(8,128)} %fusion.161, f32[2304,2048]{1,0:T(8,128)} %fusion.162), kind=kLoop, calls=%fused_computation.15 | loop fusion | flops 122683392 | bytes 84934656 | tf_op jit(solution)/shard_map/convert_element_type | solution.py:20
  554.4 28.6 %convolution_convert_fusion.1 = bf16[2304,2048]{1,0:T(8,128)(2,1)S(1)} fusion(bf16[2304,2048]{1,0:T(8,128)(2,1)} %get-tuple-element.166, bf16[2304,256]{1,0:T(8,128)(2,1)} %copy-done.67, bf16[2304,2048]{1,0:T(8,128)(2,1)} %slice_dynamic-update-slice_fusion.11), kind=kOutput, calls=%fused_computation.19 | convolution fusion | flops 21769224192 | bytes 29491200 | tf_op jit(solution)/shard_map/dot_general | solution.py:24
  592.7 15.0 %fusion.22 = f32[2304,1024]{1,0:T(8,128)} fusion(bf16[2304,2048]{1,0:T(8,128)(2,1)S(1)} %copy-done.14, bf16[2048,2048]{1,0:T(8,128)(2,1)} %slice_dynamic-update-slice_fusion.20), kind=kOutput, calls=%fused_computation.49 | convolution fusion | flops 9663676416 | bytes 23068672 | tf_op jit(solution)/shard_map/dot_general | solution.py:24
  612.1 14.7 %add_convert_fusion.1 = bf16[2304,1024]{1,0:T(8,128)(2,1)} fusion(f32[2304,1024]{1,0:T(8,128)} %fusion.22, bf16[2304,2048]{1,0:T(8,128)(2,1)S(1)} %bitcast.108, bf16[2048,2048]{1,0:T(8,128)(2,1)} %slice_dynamic-update-slice_fusion.15), kind=kOutput, calls=%fused_computation.22 | convolution fusion | flops 9668395008 | bytes 27787264 | tf_op jit(solution)/shard_map/dot_general | solution.py:24
  640.8 14.3 %fusion.18 = f32[2304,1024]{1,0:T(8,128)S(1)} fusion(bf16[2304,2048]{1,0:T(8,128)(2,1)} %get-tuple-element.161, bf16[2048,2048]{1,0:T(8,128)(2,1)} %slice_dynamic-update-slice_fusion.15), kind=kOutput, calls=%fused_computation.45 | convolution fusion | flops 9663676416 | bytes 23068672 | tf_op jit(solution)/shard_map/dot_general | solution.py:24
  655.2 15.8 %add_convert_fusion = bf16[2304,1024]{1,0:T(8,128)(2,1)} fusion(f32[2304,1024]{1,0:T(8,128)S(1)} %fusion.18, bf16[2304,2048]{1,0:T(8,128)(2,1)} %get-tuple-element.158, bf16[2048,2048]{1,0:T(8,128)(2,1)} %slice_dynamic-update-slice_fusion.20), kind=kOutput, calls=%fused_computation.21 | convolution fusion | flops 9668395008 | bytes 27787264 | tf_op jit(solution)/shard_map/dot_general | solution.py:24
  678.8 26.4 %convolution_convert_fusion.4 = bf16[2048,2048]{1,0:T(8,128)(2,1)} fusion(bf16[2304,2048]{1,0:T(8,128)(2,1)} %all-gather.11.cloned.1.call-done, bf16[2304,2048]{1,0:T(8,128)(2,1)} %get-tuple-element.158), kind=kOutput, calls=%fused_computation.33 | convolution fusion | flops 19331547136 | bytes 27262976 | tf_op jit(solution)/shard_map/dot_general | solution.py:24
  711.5 26.6 %convolution_convert_fusion.3 = bf16[2048,2048]{1,0:T(8,128)(2,1)} fusion(bf16[2304,2048]{1,0:T(8,128)(2,1)} %all-gather.11.cloned.1.call-done, bf16[2304,2048]{1,0:T(8,128)(2,1)} %get-tuple-element.161), kind=kOutput, calls=%fused_computation.32 | convolution fusion | flops 19331547136 | bytes 27262976 | tf_op jit(solution)/shard_map/dot_general | solution.py:24
  746.5 27.5 %convolution_convert_fusion = bf16[2304,2304]{1,0:T(8,128)(2,1)S(1)} fusion(bf16[2304,2048]{1,0:T(8,128)(2,1)} %get-tuple-element.166, bf16[2304,2048]{1,0:T(8,128)(2,1)} %get-tuple-element.255), kind=kOutput, calls=%fused_computation.18 | convolution fusion | flops 21748580352 | bytes 29491200 | tf_op jit(solution)/shard_map/dot_general | solution.py:24
  822.0 8.2 multiply_convert_fusion
  864.4 8.6 convolution_convert_fusion.2
  889.4 10.6 collective-permute-done.41
  917.7 38.7 %collective-permute-done.48 = bf16[2,1,4,128,512]{4,3,2,1,0:T(8,128)(2,1)} collective-permute-done((bf16[2,1,4,128,512]{4,3,2,1,0:T(8,128)(2,1)}, bf16[2,1,4,128,512]{4,3,2,1,0:T(8,128)(2,1)}, u32[]{:S(2)}, u32[]{:S(2)}) %collective-permute-start.48) | collective-permute-done | bytes 1048608 | tf_op jit(solution)/shard_map/ppermute | solution.py:61
  986.6 8.0 collective-permute-done.51
  1011.3 12.9 %collective-permute-done.58 = bf16[128,1280]{1,0:T(8,128)(2,1)S(1)} collective-permute-done((bf16[128,1280]{1,0:T(8,128)(2,1)S(1)}, bf16[128,1280]{1,0:T(8,128)(2,1)S(1)}, u32[]{:S(2)}, u32[]{:S(2)}) %collective-permute-start.58) | collective-permute-done | bytes 327712 | tf_op jit(solution)/shard_map/ppermute | solution.py:61
  1030.1 15.7 %collective-permute-done.60 = bf16[128,1280]{1,0:T(8,128)(2,1)S(1)} collective-permute-done((bf16[128,1280]{1,0:T(8,128)(2,1)S(1)}, bf16[128,1280]{1,0:T(8,128)(2,1)S(1)}, u32[]{:S(2)}, u32[]{:S(2)}) %collective-permute-start.60) | collective-permute-done | bytes 327712 | tf_op jit(solution)/shard_map/ppermute | solution.py:61
  1054.4 10.1 fusion.33
  1083.6 15.5 %collective-permute-done.35 = bf16[1,2,4,128,512]{4,3,2,1,0:T(8,128)(2,1)} collective-permute-done((bf16[1,2,4,128,512]{4,3,2,1,0:T(8,128)(2,1)}, bf16[1,2,4,128,512]{4,3,2,1,0:T(8,128)(2,1)}, u32[]{:S(2)}, u32[]{:S(2)}) %collective-permute-start.35) | collective-permute-done | bytes 1048608 | tf_op jit(solution)/shard_map/ppermute | solution.py:61
  1104.7 9.5 collective-permute-done.36
  1114.4 13.2 %collective-permute-start.37 = (bf16[128,512]{1,0:T(8,128)(2,1)S(1)}, bf16[128,512]{1,0:T(8,128)(2,1)S(1)}, u32[]{:S(2)}, u32[]{:S(2)}) collective-permute-start(bf16[128,512]{1,0:T(8,128)(2,1)S(1)} %get-tuple-element.309), channel_id=1, source_target_pairs={{0,2},{1,3},{2,0},{3,1},{4,6},{5,7},{6,4},{7,5},{8,10},{9,11},{10,... | collective-permute-start | bytes 393224 | tf_op jit(solution)/shard_map/ppermute | solution.py:61
  (610 shorter events, 482.8 us)
Async XLA Ops:
  7.2 95.5 %all-gather.5.cloned.1.call-start = ((), (), s32[]{:S(2)}) async-start(), calls=%async_computation.5 | async-start | bytes 11354112 | tf_op jit(solution)/shard_map/all_gather | solution.py:229
  11.1 166.1 %all-gather.7.cloned.1.call-start = ((), (), s32[]{:S(2)}) async-start(), calls=%async_computation.6 | async-start | bytes 2654208 | tf_op jit(solution)/shard_map/all_gather | solution.py:287
  115.4 211.9 %all-gather.9.cloned.1.call-start = ((), (), s32[]{:S(2)}) async-start(), calls=%async_computation.7 | async-start | bytes 11894784 | tf_op jit(solution)/shard_map/all_gather | solution.py:326
  115.4 76.0 %collective-permute-start = (bf16[800,2048]{1,0:T(8,128)(2,1)}, bf16[800,2048]{1,0:T(8,128)(2,1)}, u32[]{:S(2)}, u32[]{:S(2)}) collective-permute-start(bf16[800,2048]{1,0:T(8,128)(2,1)} %get-tuple-element.121), channel_id=1, source_target_pairs={{0,16},{8,24},{16,0},{24,8},{1,17},{9,25},{17,1},{25,9},{2,18},{10... | collective-permute-start | bytes 9830408 | tf_op jit(solution)/shard_map/ppermute | solution.py:61
  117.0 74.5 %collective-permute-start.1 = (bf16[800,2048]{1,0:T(8,128)(2,1)}, bf16[800,2048]{1,0:T(8,128)(2,1)}, u32[]{:S(2)}, u32[]{:S(2)}) collective-permute-start(bf16[800,2048]{1,0:T(8,128)(2,1)} %get-tuple-element.122), channel_id=1, source_target_pairs={{0,8},{8,0},{16,24},{24,16},{1,9},{9,1},{17,25},{25,17},{2,10},{10... | collective-permute-start | bytes 9830408 | tf_op jit(solution)/shard_map/ppermute | solution.py:61
  117.5 71.3 %collective-permute-start.2 = (bf16[288,2048]{1,0:T(8,128)(2,1)S(1)}, bf16[288,2048]{1,0:T(8,128)(2,1)}, u32[]{:S(2)}, u32[]{:S(2)}) collective-permute-start(bf16[288,2048]{1,0:T(8,128)(2,1)S(1)} %pad_maximum_fusion.19), channel_id=1, source_target_pairs={{0,2},{1,3},{2,0},{3,1},{4,6},{5,7},{6,4},{7,5},{8,10},{9,11},{10,... | collective-permute-start | bytes 3538952 | tf_op jit(solution)/shard_map/ppermute | solution.py:61
  118.9 72.6 %collective-permute-start.3 = (bf16[288,2048]{1,0:T(8,128)(2,1)S(1)}, bf16[288,2048]{1,0:T(8,128)(2,1)}, u32[]{:S(2)}, u32[]{:S(2)}) collective-permute-start(bf16[288,2048]{1,0:T(8,128)(2,1)S(1)} %pad_maximum_fusion.19), channel_id=1, source_target_pairs={{0,4},{1,5},{2,6},{3,7},{4,0},{5,1},{6,2},{7,3},{8,12},{9,13},{10,... | collective-permute-start | bytes 3538952 | tf_op jit(solution)/shard_map/ppermute | solution.py:61
  191.5 281.9 %all-gather.11.cloned.1.call-start = ((), (), s32[]{:S(2)}) async-start(), calls=%async_computation.8 | async-start | bytes 10616832 | tf_op jit(solution)/shard_map/all_gather | solution.py:390
  204.7 99.0 %collective-permute-start.4 = (bf16[800,2048]{1,0:T(8,128)(2,1)}, bf16[800,2048]{1,0:T(8,128)(2,1)}, u32[]{:S(2)}, u32[]{:S(2)}) collective-permute-start(bf16[800,2048]{1,0:T(8,128)(2,1)} %get-tuple-element.121), channel_id=1, source_target_pairs={{0,8},{8,0},{16,24},{24,16},{1,9},{9,1},{17,25},{25,17},{2,10},{10... | collective-permute-start | bytes 9830408 | tf_op jit(solution)/shard_map/ppermute | solution.py:61
  206.2 97.5 %collective-permute-start.5 = (bf16[800,2048]{1,0:T(8,128)(2,1)}, bf16[800,2048]{1,0:T(8,128)(2,1)}, u32[]{:S(2)}, u32[]{:S(2)}) collective-permute-start(bf16[800,2048]{1,0:T(8,128)(2,1)} %get-tuple-element.122), channel_id=1, source_target_pairs={{0,16},{8,24},{16,0},{24,8},{1,17},{9,25},{17,1},{25,9},{2,18},{10... | collective-permute-start | bytes 9830408 | tf_op jit(solution)/shard_map/ppermute | solution.py:61
  224.3 38.3 %collective-permute-start.6 = (bf16[288,2048]{1,0:T(8,128)(2,1)S(1)}, bf16[288,2048]{1,0:T(8,128)(2,1)S(1)}, u32[]{:S(2)}, u32[]{:S(2)}) collective-permute-start(bf16[288,2048]{1,0:T(8,128)(2,1)S(1)} %pad_maximum_fusion.19), channel_id=1, source_target_pairs={{0,6},{1,7},{2,4},{3,5},{4,2},{5,3},{6,0},{7,1},{8,14},{9,15},{10,... | collective-permute-start | bytes 3538952 | tf_op jit(solution)/shard_map/ppermute | solution.py:61
  307.4 46.5 %collective-permute-start.9 = (bf16[1152,2048]{1,0:T(8,128)(2,1)}, bf16[1152,2048]{1,0:T(8,128)(2,1)}, u32[]{:S(2)}, u32[]{:S(2)}) collective-permute-start(bf16[1152,2048]{1,0:T(8,128)(2,1)} %pad_maximum_fusion.4), channel_id=1, source_target_pairs={{0,1},{1,0},{2,3},{3,2},{4,5},{5,4},{6,7},{7,6},{8,9},{9,8},{10,11... | collective-permute-start | bytes 14155784 | tf_op jit(solution)/shard_map/ppermute | solution.py:61
  310.2 39.4 %collective-permute-start.7 = (bf16[400,2048]{1,0:T(8,128)(2,1)}, bf16[400,2048]{1,0:T(8,128)(2,1)}, u32[]{:S(2)}, u32[]{:S(2)}) collective-permute-start(bf16[400,2048]{1,0:T(8,128)(2,1)} %slice.391), channel_id=1, source_target_pairs={{0,8},{8,0},{16,24},{24,16},{1,9},{9,1},{17,25},{25,17},{2,10},{10... | collective-permute-start | bytes 4915208 | tf_op jit(solution)/shard_map/ppermute | solution.py:61
  315.5 38.4 %collective-permute-start.8 = (bf16[400,2048]{1,0:T(8,128)(2,1)}, bf16[400,2048]{1,0:T(8,128)(2,1)}, u32[]{:S(2)}, u32[]{:S(2)}) collective-permute-start(bf16[400,2048]{1,0:T(8,128)(2,1)} %slice.392), channel_id=1, source_target_pairs={{0,16},{8,24},{16,0},{24,8},{1,17},{9,25},{17,1},{25,9},{2,18},{10... | collective-permute-start | bytes 4915208 | tf_op jit(solution)/shard_map/ppermute | solution.py:61
  356.6 80.7 %collective-permute-start.11 = (bf16[400,2048]{1,0:T(8,128)(2,1)}, bf16[400,2048]{1,0:T(8,128)(2,1)}, u32[]{:S(2)}, u32[]{:S(2)}) collective-permute-start(bf16[400,2048]{1,0:T(8,128)(2,1)} %slice.408), channel_id=1, source_target_pairs={{0,8},{8,0},{16,24},{24,16},{1,9},{9,1},{17,25},{25,17},{2,10},{10... | collective-permute-start | bytes 4915208 | tf_op jit(solution)/shard_map/ppermute | solution.py:61
  357.7 440.7 %reduce-scatter.6.cloned.1.call-start = ((), (), s32[]{:S(2)}) async-start(), calls=%async_computation.9 | async-start | bytes 5308416 | tf_op jit(solution)/shard_map/reduce_scatter | solution.py:446
  377.4 37.3 %collective-permute-start.10 = (bf16[400,2048]{1,0:T(8,128)(2,1)S(1)}, bf16[400,2048]{1,0:T(8,128)(2,1)S(1)}, u32[]{:S(2)}, u32[]{:S(2)}) collective-permute-start(bf16[400,2048]{1,0:T(8,128)(2,1)S(1)} %slice.401), channel_id=1, source_target_pairs={{0,16},{8,24},{16,0},{24,8},{1,17},{9,25},{17,1},{25,9},{2,18},{10... | collective-permute-start | bytes 4915208 | tf_op jit(solution)/shard_map/ppermute | solution.py:61
  638.5 38.5 %collective-permute-start.18 = (bf16[288,2048]{1,0:T(8,128)(2,1)}, bf16[288,2048]{1,0:T(8,128)(2,1)S(1)}, u32[]{:S(2)}, u32[]{:S(2)}) collective-permute-start(bf16[288,2048]{1,0:T(8,128)(2,1)} %get-tuple-element.148), channel_id=1, source_target_pairs={{0,8},{8,0},{16,24},{24,16},{1,9},{9,1},{17,25},{25,17},{2,10},{10... | collective-permute-start | bytes 3538952 | tf_op jit(solution)/shard_map/ppermute | solution.py:61
  639.8 37.2 %collective-permute-start.19 = (bf16[288,2048]{1,0:T(8,128)(2,1)}, bf16[288,2048]{1,0:T(8,128)(2,1)}, u32[]{:S(2)}, u32[]{:S(2)}) collective-permute-start(bf16[288,2048]{1,0:T(8,128)(2,1)} %pad_maximum_fusion.17), channel_id=1, source_target_pairs={{0,16},{8,24},{16,0},{24,8},{1,17},{9,25},{17,1},{25,9},{2,18},{10... | collective-permute-start | bytes 3538952 | tf_op jit(solution)/shard_map/ppermute | solution.py:61
  640.8 158.9 %reduce-scatter.8.cloned.1.call-start = ((), (), s32[]{:S(2)}) async-start(), calls=%async_computation.10 | async-start | bytes 5308416 | tf_op jit(solution)/shard_map/reduce_scatter | solution.py:446
  705.3 204.7 %reduce-scatter.10.cloned.1.call-start = ((), (), s32[]{:S(2)}) async-start(), calls=%async_computation.11 | async-start | bytes 6635520 | tf_op jit(solution)/shard_map/reduce_scatter | solution.py:446
  744.5 37.0 %collective-permute-start.24 = (bf16[256,2048]{1,0:T(8,128)(2,1)}, bf16[256,2048]{1,0:T(8,128)(2,1)S(1)}, u32[]{:S(2)}, u32[]{:S(2)}) collective-permute-start(bf16[256,2048]{1,0:T(8,128)(2,1)} %get-tuple-element.162), channel_id=1, source_target_pairs={{0,8},{8,0},{16,24},{24,16},{1,9},{9,1},{17,25},{25,17},{2,10},{10... | collective-permute-start | bytes 3145736 | tf_op jit(solution)/shard_map/ppermute | solution.py:61
  745.5 36.1 %collective-permute-start.25 = (bf16[256,2048]{1,0:T(8,128)(2,1)}, bf16[256,2048]{1,0:T(8,128)(2,1)S(1)}, u32[]{:S(2)}, u32[]{:S(2)}) collective-permute-start(bf16[256,2048]{1,0:T(8,128)(2,1)} %get-tuple-element.163), channel_id=1, source_target_pairs={{0,16},{8,24},{16,0},{24,8},{1,17},{9,25},{17,1},{25,9},{2,18},{10... | collective-permute-start | bytes 3145736 | tf_op jit(solution)/shard_map/ppermute | solution.py:61
  796.4 41.6 %collective-permute-start.26 = (bf16[256,2048]{1,0:T(8,128)(2,1)}, bf16[256,2048]{1,0:T(8,128)(2,1)}, u32[]{:S(2)}, u32[]{:S(2)}) collective-permute-start(bf16[256,2048]{1,0:T(8,128)(2,1)} %get-tuple-element.168), channel_id=1, source_target_pairs={{0,8},{8,0},{16,24},{24,16},{1,9},{9,1},{17,25},{25,17},{2,10},{10... | collective-permute-start | bytes 3145736 | tf_op jit(solution)/shard_map/ppermute | solution.py:61
  797.3 41.8 %collective-permute-start.27 = (bf16[256,2048]{1,0:T(8,128)(2,1)}, bf16[256,2048]{1,0:T(8,128)(2,1)}, u32[]{:S(2)}, u32[]{:S(2)}) collective-permute-start(bf16[256,2048]{1,0:T(8,128)(2,1)} %get-tuple-element.169), channel_id=1, source_target_pairs={{0,16},{8,24},{16,0},{24,8},{1,17},{9,25},{17,1},{25,9},{2,18},{10... | collective-permute-start | bytes 3145736 | tf_op jit(solution)/shard_map/ppermute | solution.py:61
  798.3 199.2 %reduce-scatter.12.cloned.1.call-start = ((), (), s32[]{:S(2)}) async-start(), calls=%async_computation.12 | async-start | bytes 2654208 | tf_op jit(solution)/shard_map/reduce_scatter | solution.py:446
  904.0 57.8 %collective-permute-start.56 = (bf16[2,1,4,128,640]{4,3,2,1,0:T(8,128)(2,1)}, bf16[2,1,4,128,640]{4,3,2,1,0:T(8,128)(2,1)}, u32[]{:S(2)}, u32[]{:S(2)}) collective-permute-start(bf16[2,1,4,128,640]{4,3,2,1,0:T(8,128)(2,1)} %constant_dynamic-slice_fusion.2), channel_id=1, source_target_pairs={{0,8},{8,0},{16,24},{24,16},{1,9},{9,1},{17,25},{25,17},{2,10},{10... | collective-permute-start | bytes 3932168 | tf_op jit(solution)/shard_map/ppermute | solution.py:61
  906.7 49.7 %collective-permute-start.48 = (bf16[2,1,4,128,512]{4,3,2,1,0:T(8,128)(2,1)}, bf16[2,1,4,128,512]{4,3,2,1,0:T(8,128)(2,1)}, u32[]{:S(2)}, u32[]{:S(2)}) collective-permute-start(bf16[2,1,4,128,512]{4,3,2,1,0:T(8,128)(2,1)} %constant_dynamic-slice_fusion.9), channel_id=1, source_target_pairs={{0,8},{8,0},{16,24},{24,16},{1,9},{9,1},{17,25},{25,17},{2,10},{10... | collective-permute-start | bytes 3145736 | tf_op jit(solution)/shard_map/ppermute | solution.py:61
  908.7 50.7 %collective-permute-start.46 = (bf16[1,2,4,128,512]{4,3,2,1,0:T(8,128)(2,1)}, bf16[1,2,4,128,512]{4,3,2,1,0:T(8,128)(2,1)}, u32[]{:S(2)}, u32[]{:S(2)}) collective-permute-start(bf16[1,2,4,128,512]{4,3,2,1,0:T(8,128)(2,1)} %constant_dynamic-slice_fusion.11), channel_id=1, source_target_pairs={{0,16},{8,24},{16,0},{24,8},{1,17},{9,25},{17,1},{25,9},{2,18},{10... | collective-permute-start | bytes 3145736 | tf_op jit(solution)/shard_map/ppermute | solution.py:61
  910.0 242.4 %reduce-scatter.14.cloned.1.call-start = ((), (), s32[]{:S(2)}) async-start(), calls=%async_computation.13 | async-start | bytes 5308416 | tf_op jit(solution)/shard_map/reduce_scatter | solution.py:446
  914.4 50.3 %collective-permute-start.54 = (bf16[1,2,4,128,640]{4,3,2,1,0:T(8,128)(2,1)S(1)}, bf16[1,2,4,128,640]{4,3,2,1,0:T(8,128)(2,1)S(1)}, u32[]{:S(2)}, u32[]{:S(2)}) collective-permute-start(bf16[1,2,4,128,640]{4,3,2,1,0:T(8,128)(2,1)S(1)} %constant_dynamic-slice_fusion.4), channel_id=1, source_target_pairs={{0,16},{8,24},{16,0},{24,8},{1,17},{9,25},{17,1},{25,9},{2,18},{10... | collective-permute-start | bytes 3932168 | tf_op jit(solution)/shard_map/ppermute | solution.py:61
  1003.7 42.1 %collective-permute-start.60 = (bf16[128,1280]{1,0:T(8,128)(2,1)S(1)}, bf16[128,1280]{1,0:T(8,128)(2,1)S(1)}, u32[]{:S(2)}, u32[]{:S(2)}) collective-permute-start(bf16[128,1280]{1,0:T(8,128)(2,1)S(1)} %get-tuple-element.269), channel_id=1, source_target_pairs={{0,6},{1,7},{2,4},{3,5},{4,2},{5,3},{6,0},{7,1},{8,14},{9,15},{10,... | collective-permute-start | bytes 983048 | tf_op jit(solution)/shard_map/ppermute | solution.py:61
  (163 other events, 2555.5 us)
Sparse Core Ops, SparseCore 0:
  11.6 91.0 all-gather.4
  115.5 61.6 all-gather.6
  191.6 130.8 all-gather.8
  357.8 89.6 all-gather.10
  640.9 53.4 reduce-scatter.5
  705.4 53.6 reduce-scatter.7
  798.4 64.8 reduce-scatter.9
  910.1 35.4 reduce-scatter.11
  997.7 77.6 reduce-scatter.13

commit v5 on v4

--- a/solution.py
+++ b/solution.py
@@ -148,7 +148,7 @@
     return add_half(kept, swap(sent, axis, size, bit))
 
 
-def scatter_chips(values, row_size, col_size, parts=2):
+def row_stages(values, row_size, col_size, parts=2):
     chips, rows, width = values.shape
     line = col_size // 2
     bits = [1 << k for k in reversed(range(row_size.bit_length() - 1))]
@@ -160,7 +160,11 @@
         for bit in bits if place % 2 == 0 else bits[::-1]:
             piece = halve(piece, bits.index(bit), "row", row_size, bit)
         pieces.append(piece.reshape(line, rows, part))
-    whole = jnp.concatenate(pieces, axis=-1)
+    return jnp.concatenate(pieces, axis=-1)
+
+
+def line_stage(whole, col_size):
+    line = col_size // 2
     at = lax.axis_index("col") // 2
     total = lax.dynamic_index_in_dim(whole, at, 0, keepdims=False).astype(jnp.float32)
     for step in range(1, line):
@@ -256,7 +260,17 @@
     own_seg = lax.dynamic_slice_in_dim(segment_numbers, start_row, tok_dev)
     own_pos = lax.dynamic_slice_in_dim(positions, start_row, tok_dev)
     cosine, sine_part = rope_tables(own_pos)
-    in_gathered, cosine, sine_part = tie(in_gathered, cosine, sine_part)
+    out_packed = jnp.concatenate(
+        [
+            convert_half(output_matrix),
+            convert_half(output_adapter_first),
+            convert_half(output_adapter_second).reshape(gain_len, -1),
+            convert_half(down_adapter_second).reshape(gain_len, -1),
+        ],
+        axis=1,
+    )
+    in_gathered, cosine, sine_part, out_packed = tie(in_gathered, cosine, sine_part, out_packed)
+    out_gathered = lax.all_gather(out_packed, ("row", "col"), axis=0, tiled=True)
     model_rows = gate_matrix.shape[0]
     by_pairs = row_size == 4 and col_size == 8
     cot_grad = cotangent.astype(jnp.float32)
@@ -269,7 +283,6 @@
         upper_y = swap(upper, "row", 4, 2)
         lower_x = swap(lower, "row", 4, 1)
         cot_two = swap(cot_mixed, "col", 8, 2)
-        cot_four = swap(cot_mixed, "col", 8, 4)
     in_width = in_gathered.shape[1] - 128
     in_weight = in_gathered[:, :in_width]
     gains = in_gathered[:, in_width:].astype(jnp.float32)
@@ -284,46 +297,31 @@
         rotate(query_pre.reshape(tok_dev, NH, HD), cosine[:, None, :], sine_part[:, None, :])
         * scale
     ).reshape(row_total, HD)
-    keyval_rows = lax.all_gather(
-        jnp.concatenate(
-            [
-                convert_half(rotate(keyval_pre[:, :HD], cosine, sine_part)),
-                convert_half(keyval_pre[:, HD:]),
-            ],
-            axis=1,
-        ),
-        "col",
-        axis=0,
-        tiled=True,
-    )
-    out_packed = jnp.concatenate(
+    keyval_own = jnp.concatenate(
         [
-            convert_half(output_matrix),
-            convert_half(output_adapter_first),
-            convert_half(output_adapter_second).reshape(gain_len, -1),
-            convert_half(down_adapter_second).reshape(gain_len, -1),
+            convert_half(rotate(keyval_pre[:, :HD], cosine, sine_part)),
+            convert_half(keyval_pre[:, HD:]),
         ],
         axis=1,
     )
-    keyval_rows, out_packed = tie(keyval_rows, out_packed)
     if by_pairs:
-        (keyval_rows, out_packed, upper_y, lower_x, cot_two, cot_four, upper, lower, cot_mixed) = (
-            tie(
-                keyval_rows,
-                out_packed,
-                upper_y,
-                lower_x,
-                cot_two,
-                cot_four,
-                upper,
-                lower,
-                cot_mixed,
-            )
-        )
-        upper_x = swap(upper, "row", 4, 1)
-        lower_y = swap(lower, "row", 4, 2)
-        cot_six = swap(cot_mixed, "col", 8, 6)
-    out_gathered = lax.all_gather(out_packed, ("row", "col"), axis=0, tiled=True)
+        places = [lax.axis_index("col") ^ (2 * step) for step in range(4)]
+        places = places + [place ^ 1 for place in places]
+
+        def gathered(mine, other):
+            parts = [
+                side[tok_dev * step : tok_dev * (step + 1)]
+                for side in (mine, other)
+                for step in range(4)
+            ]
+            return place_blocks(parts, places, 8)
+
+        keyval_mine = jnp.concatenate(
+            [keyval_own] + [swap(keyval_own, "col", 8, 2 * step) for step in range(1, 4)], axis=0
+        )
+        keyval_rows = gathered(keyval_mine, swap(keyval_mine, "col", 8, 1))
+    else:
+        keyval_rows = lax.all_gather(keyval_own, "col", axis=0, tiled=True)
     key_rows = keyval_rows[:, :HD]
     value_rows = keyval_rows[:, HD:]
     row_index = start_row + jnp.arange(row_total, dtype=jnp.int32) // NH
@@ -336,18 +334,17 @@
     top_value = jnp.max(scores, axis=1)
     total_value = jnp.sum(jnp.exp(scores - top_value[:, None]), axis=1)
     log_norm = top_value + jnp.log(total_value)
+    if by_pairs:
+        log_norm, upper_y, lower_x, cot_two, upper, lower, cot_mixed = tie(
+            log_norm, upper_y, lower_x, cot_two, upper, lower, cot_mixed
+        )
+        upper_x = swap(upper, "row", 4, 1)
+        lower_y = swap(lower, "row", 4, 2)
+        cot_four = swap(cot_mixed, "col", 8, 4)
+        cot_six = swap(cot_mixed, "col", 8, 6)
     probs = convert_half(jnp.exp(scores - log_norm[:, None]))
     mixed_rows = matrix_product(probs, value_rows)
     head_context = convert_half(mixed_rows.reshape(tok_dev, NH * HD))
-    if by_pairs:
-        head_context, upper_x, lower_y, cot_six, upper_y, lower_x = tie(
-            head_context, upper_x, lower_y, cot_six, upper_y, lower_x
-        )
-        quarter = upper_y.shape[0] // 2
-        cot_mine = jnp.concatenate([cot_mixed, cot_two, cot_four, cot_six], axis=0)
-        cot_other = swap(cot_mine, "col", 8, 1)
-        far_upper = [swap(upper_y[:quarter], "row", 4, 1)]
-        far_lower = [swap(lower_x[:quarter], "row", 4, 2)]
     rank_width = output_adapter_first.shape[1]
     out_width = width + rank_width
     upper_width = adapter_rows * width // gain_len
@@ -360,19 +357,14 @@
     normed_mlp = convert_half(rms_scale(layer_state, gain_mlp))
     normed_mlp = reorder(normed_mlp, order)
     if by_pairs:
-        normed_mlp, far_upper[0], far_lower[0], cot_other, upper_y, lower_x = tie(
-            normed_mlp, far_upper[0], far_lower[0], cot_other, upper_y, lower_x
-        )
-        far_upper.append(swap(upper_y[quarter:], "row", 4, 1))
-        far_lower.append(swap(lower_x[quarter:], "row", 4, 2))
+        normed_mlp, upper_x, lower_y, cot_four, cot_six, upper_y, lower_x = tie(
+            normed_mlp, upper_x, lower_y, cot_four, cot_six, upper_y, lower_x
+        )
+        far_upper = [swap(upper_y, "row", 4, 1)]
+        far_lower = [swap(lower_x, "row", 4, 2)]
+        cot_mine = jnp.concatenate([cot_mixed, cot_two, cot_four, cot_six], axis=0)
+        cot_rows = gathered(cot_mine, swap(cot_mine, "col", 8, 1))
         pieces = [[shard], [upper_x, lower_x], [upper_y, lower_y], [*far_upper, *far_lower]]
-        places = [lax.axis_index("col") ^ (2 * step) for step in range(4)]
-        cot_rows = place_blocks(
-            [cot_mine[tok_dev * step : tok_dev * (step + 1)] for step in range(4)]
-            + [cot_other[tok_dev * step : tok_dev * (step + 1)] for step in range(4)],
-            places + [place ^ 1 for place in places],
-            8,
-        )
     else:
         pieces = [[shard]] + [
             [to_partner(shard, "row", step, row_size)] for step in range(1, row_size)
@@ -433,7 +425,6 @@
         for one, two in zip(blocks_of(grad_down[:width]), blocks_of(grad_down[width:]))
     ]
     half_width = width // 2
-    down_split = half_width + rank_width
 
     def normed_part(start, left_gate, left_up):
         stop = start + half_width
@@ -445,9 +436,8 @@
     def col_sum(values):
         return lax.psum_scatter(values, "col", scatter_dimension=0, tiled=True)
 
-    def down_product():
-        weight = jnp.concatenate([down_weight[half_width:], down_weight[:half_width]], axis=0)
-        return convert_half(product(hidden_activated, weight, contract_last))
+    def down_product(start, stop):
+        return convert_half(product(hidden_activated, down_weight[start:stop], contract_last))
 
     if row_size == 4:
         own_down, far, free, last = split_blocks(down_blocks)
@@ -462,6 +452,10 @@
         second_part = normed_part(half_width, gate_grad, up_grad)
         *free, second_part, gate_grad, up_grad, last_x, last_y = tie(
             *free, second_part, gate_grad, up_grad, *last
+        )
+        rank_partial = down_product(width, width + rank_width)
+        second_part, rank_partial, hidden_activated = tie(
+            second_part, rank_partial, hidden_activated
         )
         second_sum = col_sum(second_part)
         last = send_pair((last_x, last_y))
@@ -471,30 +465,22 @@
         own_gate, far, free, last = split_blocks(blocks_of(grad_gate))
         far = send_pair(far)
         grad_up = convert_half(product(ffn_in, up_grad, contract_first))
-        *far, grad_up, hidden_activated, free_x, free_y = tie(
-            *far, grad_up, hidden_activated, *free
-        )
+        *far, grad_up, free_x, free_y = tie(*far, grad_up, *free)
         gate_last = add_pair(last, far)
         gate_free = send_pair((free_x, free_y))
-        down_partial = down_product()
-        *gate_free, last_x, last_y, down_partial, grad_up = tie(
-            *gate_free, *gate_last, down_partial, grad_up
-        )
         own_up, far, up_free, up_last = split_blocks(blocks_of(grad_up))
-        gate_last = send_pair((last_x, last_y))
         up_far = send_pair(far)
     else:
         first_sum = col_sum(normed_part(0, gate_grad, up_grad))
         second_sum = col_sum(normed_part(half_width, gate_grad, up_grad))
+        rank_partial = down_product(width, width + rank_width)
         grad_gate = convert_half(product(ffn_in, gate_grad, contract_first))
         grad_up = convert_half(product(ffn_in, up_grad, contract_first))
-        down_partial = down_product()
         down_total = row_sum(down_blocks, row_size)
         gate_sum = row_sum(blocks_of(grad_gate), row_size)
         up_sum = row_sum(blocks_of(grad_up), row_size)
     down_sum, rank_sum = down_total[:model_rows], down_total[model_rows:]
-    summed = col_sum(down_partial[:, :down_split])
-    down_rest = down_partial[:, down_split:]
+    rank_sums = col_sum(rank_partial)
     normed_grad = jnp.concatenate([first_sum, second_sum], axis=1)
 
     normed_grad = reorder(normed_grad, order).astype(jnp.float32)
@@ -506,16 +492,16 @@
     out_grad = jnp.concatenate([attn_grad, rank_out_grad], axis=1)
     context_grad = product(out_grad, out_weight, contract_last)
     grad_rows = convert_half(context_grad).reshape(row_total, HD)
+    if row_size == 4:
+        *gate_free, far_x, far_y, grad_rows, last_x, last_y, free_x, free_y = tie(
+            *gate_free, *up_far, grad_rows, *gate_last, *up_free
+        )
+        up_last = add_pair(up_last, (far_x, far_y))
+        gate_last = send_pair((last_x, last_y))
+        up_free = (free_x, free_y)
     delta = jnp.sum(grad_rows.astype(jnp.float32) * mixed_rows, axis=1)
     weight_grad = product(grad_rows, value_rows, contract_last)
     score_grad = convert_half(probs.astype(jnp.float32) * (weight_grad - delta[:, None]))
-    if row_size == 4:
-        *gate_last, far_x, far_y, score_grad, free_x, free_y = tie(
-            *gate_last, *up_far, score_grad, *up_free
-        )
-        gate_sum = finish_sum(own_gate, gate_free, gate_last)
-        up_last = add_pair(up_last, (far_x, far_y))
-        up_free = send_pair((free_x, free_y))
     query_acc = matrix_product(score_grad, key_rows)
     query_grad = convert_half(
         unrotate(
@@ -526,12 +512,11 @@
     key_acc = product(score_grad, query_rows, contract_first)
     value_acc = product(probs, grad_rows, contract_first)
     keyval_part = jnp.concatenate([convert_half(key_acc), convert_half(value_acc)], axis=1)
+    keyval_part, rank_sums = tie(keyval_part, rank_sums)
     if row_size == 4:
-        *up_free, keyval_part, query_grad, last_x, last_y = tie(
-            *up_free, keyval_part, query_grad, *up_last
-        )
-        up_last = send_pair((last_x, last_y))
-    keyval_part, summed = tie(keyval_part, summed)
+        *gate_last, keyval_part, free_x, free_y = tie(*gate_last, keyval_part, *up_free)
+        gate_sum = finish_sum(own_gate, gate_free, gate_last)
+        up_free = send_pair((free_x, free_y))
     keyval_sum = col_sum(keyval_part)
     core = lax.axis_index("col") % 2
     query_right = halves_with_partner(query_grad, col_size)
@@ -549,16 +534,21 @@
     grad_out_upper = product(rank_both, out_right, contract_first)
     out_group = jnp.concatenate([shared(grad_out), shared(grad_out_upper)], axis=2)
     query_group = shared(grad_query)
+    down_partial = down_product(0, width)
     if row_size == 4:
-        *up_last, out_group, query_group = tie(*up_last, out_group, query_group)
-        up_sum = finish_sum(own_up, up_free, up_last)
-    down_rank_rows = reorder(summed[:, half_width:], order)
-    keyval_sum, down_rest = tie(keyval_sum, down_rest)
-    down_rest = col_sum(down_rest)
-    down_all = jnp.concatenate([down_rest, summed[:, :half_width]], axis=1)
+        *up_free, keyval_sum, down_partial, out_group, query_group, last_x, last_y = tie(
+            *up_free, keyval_sum, down_partial, out_group, query_group, *up_last
+        )
+        up_sum = finish_sum(own_up, up_free, send_pair((last_x, last_y)))
+    else:
+        keyval_sum, down_partial = tie(keyval_sum, down_partial)
+    query_lines = row_stages(query_group, row_size, col_size)
+    out_lines = row_stages(out_group, row_size, col_size)
+    down_rank_rows = reorder(rank_sums, order)
+    summed = col_sum(down_partial)
     layer_out = convert_half(
         layer_state
-        + reorder(down_all, order).astype(jnp.float32)
+        + reorder(summed, order).astype(jnp.float32)
         + matrix_product(down_rank_rows, down_upper)
     )
     keyval_sum = keyval_sum.astype(jnp.float32)
@@ -582,28 +572,23 @@
     gain = lax.dynamic_index_in_dim(gains, core, 0, keepdims=False) + swap(
         lax.dynamic_index_in_dim(gains, 1 - core, 0, keepdims=False), "col", col_size, 1
     )
-    out_first, out_second = share_cores(
-        scatter_chips(out_group, row_size, col_size), col_size
-    )
-    query_first, query_second = share_cores(
-        scatter_chips(query_group, row_size, col_size), col_size
-    )
+    keyval_group = jnp.concatenate(
+        [
+            shared(grad_keyval),
+            shared(grad_down_upper),
+            jnp.pad(shared(gain), ((0, 0), (0, 0), (0, 127))),
+        ],
+        axis=2,
+    )
+    lines = jnp.concatenate([query_lines, out_lines], axis=2)
+    lines, keyval_group = tie(lines, keyval_group)
+    first, second = share_cores(line_stage(lines, col_size), col_size)
     keyval_first, keyval_second = share_cores(
-        scatter_chips(
-            jnp.concatenate(
-                [
-                    shared(grad_keyval),
-                    shared(grad_down_upper),
-                    jnp.pad(shared(gain), ((0, 0), (0, 0), (0, 127))),
-                ],
-                axis=2,
-            ),
-            row_size,
-            col_size,
-            parts=1,
-        ),
-        col_size,
-    )
+        line_stage(row_stages(keyval_group, row_size, col_size, parts=1), col_size), col_size
+    )
+    half_query = query_width // 2
+    query_first, query_second = first[:, :half_query], second[:, :half_query]
+    out_first, out_second = first[:, half_query:], second[:, half_query:]
 
     def joined(first, second, start, size):
         return jnp.concatenate([first[:, start : start + size], second[:, start : start + size]], axis=1)

time: 1170 us -> 1240 us (1.060)
  waiting for transfers between devices: 372 us -> 477 us
  local copies, waits for them, and re-layouts: 190 us -> 157 us
    ppermute x62 -> x60, waiting for transfers between devices: 249 us -> 388 us  [swap(): return lax.ppermute(values, axis, [(i, i ^ bit) for i in range(size)])]
    all_gather x1 -> x0, waiting for transfers between devices: 47 us -> none  [per_device(): lax.all_gather(jnp.concatenate([convert_half(rotate(keyval_pre[:, :HD], c...]
    unnamed x268 -> x278, local copies, waits for them, and re-layouts: 62.8 us -> 35.5 us
    all_gather x1, waiting for transfers between devices: 75.4 us -> 88.8 us  [per_device(): lax.all_gather(jnp.concatenate([convert_half(query_matrix), convert_half(...]
    dot_general x21 -> x22, matrix products: 237 us -> 247 us  [product(): lax.dot_general(left_side, right_side, dims, preferred_element_type=jnp.f...]
    convert_element_type x23 -> x24, other arithmetic: 73.9 us -> 67.4 us  [convert_half(): return values.astype(jnp.bfloat16)]
    ppermute x62 -> x60, starting transfers between devices: 68.3 us -> 71.7 us  [swap(): return lax.ppermute(values, axis, [(i, i ^ bit) for i in range(size)])]
  transfers between devices with their start and end apart: 71 -> 68, of which waited for: 27 -> 31; matrix products, arithmetic and copies ran while one was open for 46% -> 41% of each run, Pallas kernels for 0% -> 0%
where the time goes in v5:
time: 1240 us; the launch traced here: 1230 us
  waiting for transfers between devices  477 us (38%)
  matrix products  358 us (29%)
  local copies, waits for them, and re-layouts  157 us (13%)
  other arithmetic  153 us (12%)
  starting transfers between devices  71.9 us (6%)
  between operations  16.6 us (1%)
    ppermute x60, waiting for transfers between devices, swap(): return lax.ppermute(values, axis, [(i, i ^ bit) for i in range(size)])  388 us
    dot_general x22, matrix products, product(): lax.dot_general(left_side, right_side, dims, preferred_element_type=jnp.f...  247 us
    dot_general x9, matrix products, matrix_product(): return jnp.dot(left_side, right_side, preferred_element_type=jnp.float32)  111 us
    all_gather x1, waiting for transfers between devices, per_device(): lax.all_gather(jnp.concatenate([convert_half(query_matrix), convert_half(...  88.8 us
    ppermute x60, starting transfers between devices, swap(): return lax.ppermute(values, axis, [(i, i ^ bit) for i in range(size)])  71.7 us
    convert_element_type x24, other arithmetic, convert_half(): return values.astype(jnp.bfloat16)  67.4 us
    unnamed x278, local copies, waits for them, and re-layouts  35.5 us
    slice x9, local copies, waits for them, and re-layouts, rows_of(): found.append(part[first:last])  26.5 us
  transfers between devices with their start and end apart: 68, of which 31 were waited for; matrix products, arithmetic and copies ran while one was open for 41% of the time, Pallas kernels for 0%

profile of v5, /device:TPU:0, one launch (start us, length us, event | category | flops | bytes accessed | tf_op | source)
XLA Modules:
  0.0 1232.7 jit_solution(14651517831833686135)
XLA Ops:
  14.0 88.8 %all-gather.4.cloned.1.call-done = bf16[2048,2688]{1,0:T(8,128)(2,1)} async-done(((bf16[64,2688]{1,0:T(8,128)(2,1)}), bf16[2048,2688]{1,0:T(8,128)(2,1)}) %all-gather.4.cloned.1.call-update) | async-done | bytes 11010064 | tf_op jit(solution)/shard_map/all_gather | solution.py:233
  134.0 17.9 %collective-permute-done = bf16[288,512]{1,0:T(8,128)(2,1)S(1)} collective-permute-done((bf16[288,512]{1,0:T(8,128)(2,1)S(1)}, bf16[288,512]{1,0:T(8,128)(2,1)S(1)}, u32[]{:S(2)}, u32[]{:S(2)}) %collective-permute-start) | collective-permute-done | bytes 294944 | tf_op jit(solution)/shard_map/ppermute | solution.py:61
  151.9 12.3 collective-permute-done.1
  189.3 8.9 fusion.162
  201.3 32.8 %collective-permute-done.6 = bf16[288,2048]{1,0:T(8,128)(2,1)S(1)} collective-permute-done((bf16[288,2048]{1,0:T(8,128)(2,1)S(1)}, bf16[288,2048]{1,0:T(8,128)(2,1)S(1)}, u32[]{:S(2)}, u32[]{:S(2)}) %collective-permute-start.6) | collective-permute-done | bytes 1179680 | tf_op jit(solution)/shard_map/ppermute | solution.py:61
  234.0 31.3 %collective-permute-done.4 = bf16[800,2048]{1,0:T(8,128)(2,1)} collective-permute-done((bf16[800,2048]{1,0:T(8,128)(2,1)}, bf16[800,2048]{1,0:T(8,128)(2,1)}, u32[]{:S(2)}, u32[]{:S(2)}) %collective-permute-start.4) | collective-permute-done | bytes 3276832 | tf_op jit(solution)/shard_map/ppermute | solution.py:61
  272.9 8.8 fusion.163
  326.4 72.7 %collective-permute-done.9 = bf16[288,2048]{1,0:T(8,128)(2,1)} collective-permute-done((bf16[288,2048]{1,0:T(8,128)(2,1)S(1)}, bf16[288,2048]{1,0:T(8,128)(2,1)}, u32[]{:S(2)}, u32[]{:S(2)}) %collective-permute-start.9) | collective-permute-done | bytes 1179680 | tf_op jit(solution)/shard_map/ppermute | solution.py:61
  438.6 33.6 %collective-permute-done.13 = bf16[800,2048]{1,0:T(8,128)(2,1)} collective-permute-done((bf16[800,2048]{1,0:T(8,128)(2,1)}, bf16[800,2048]{1,0:T(8,128)(2,1)}, u32[]{:S(2)}, u32[]{:S(2)}) %collective-permute-start.13) | collective-permute-done | bytes 3276832 | tf_op jit(solution)/shard_map/ppermute | solution.py:61
  512.3 29.7 %fusion.24 = f32[2304,2048]{1,0:T(8,128)} fusion(bf16[2304,2048]{1,0:T(8,128)(2,1)} %get-tuple-element.250, bf16[2304,256]{1,0:T(8,128)(2,1)S(1)} %copy.37, bf16[2304,2048]{1,0:T(8,128)(2,1)} %slice_dynamic-update-slice_fusion.1), kind=kOutput, calls=%fused_computation.42 | convolution fusion | flops 21764505600 | bytes 38928384 | tf_op jit(solution)/shard_map/dot_general | solution.py:28
  542.1 26.7 %fusion.166 = f32[2304,2048]{1,0:T(8,128)} fusion(bf16[2304,2048]{1,0:T(8,128)(2,1)} %all-gather.8.cloned.1.call-done, bf16[2048,2048]{1,0:T(8,128)(2,1)} %slice_dynamic-update-slice_fusion.7), kind=kOutput, calls=%fused_computation.395 | convolution fusion | flops 19327352832 | bytes 36700160 | tf_op jit(solution)/shard_map/dot_general | solution.py:28
  568.8 24.4 %fusion.165 = f32[2304,2048]{1,0:T(8,128)} fusion(bf16[2304,2048]{1,0:T(8,128)(2,1)S(1)} %copy-done.117, bf16[2048,2048]{1,0:T(8,128)(2,1)} %pad_maximum_fusion.1), kind=kOutput, calls=%fused_computation.394 | convolution fusion | flops 19327352832 | bytes 36700160 | tf_op jit(solution)/shard_map/dot_general | solution.py:28
  593.2 29.9 %multiply_convert_fusion.1 = (bf16[2304,2048]{1,0:T(8,128)(2,1)}, bf16[2304,2048]{1,0:T(8,128)(2,1)}, bf16[2304,2048]{1,0:T(8,128)(2,1)}) fusion(f32[2304,2048]{1,0:T(8,128)S(1)} %bitcast.91, f32[2304,2048]{1,0:T(8,128)} %fusion.165, f32[2304,2048]{1,0:T(8,128)} %fusion.166), kind=kLoop, calls=%fused_computation.15 | loop fusion | flops 122683392 | bytes 84934656 | tf_op jit(solution)/shard_map/convert_element_type | solution.py:20
  623.1 29.0 %convolution_convert_fusion.1 = bf16[2304,2048]{1,0:T(8,128)(2,1)S(1)} fusion(bf16[2304,2048]{1,0:T(8,128)(2,1)} %get-tuple-element.166, bf16[2304,256]{1,0:T(8,128)(2,1)} %copy-done.78, bf16[2304,2048]{1,0:T(8,128)(2,1)} %slice_dynamic-update-slice_fusion.1), kind=kOutput, calls=%fused_computation.19 | convolution fusion | flops 21769224192 | bytes 29491200 | tf_op jit(solution)/shard_map/dot_general | solution.py:24
  661.9 14.7 %fusion.29 = f32[2304,1024]{1,0:T(8,128)} fusion(bf16[2304,2048]{1,0:T(8,128)(2,1)S(1)} %copy-done.14, bf16[2048,2048]{1,0:T(8,128)(2,1)} %pad_maximum_fusion.1), kind=kOutput, calls=%fused_computation.58 | convolution fusion | flops 9663676416 | bytes 23068672 | tf_op jit(solution)/shard_map/dot_general | solution.py:24
  681.3 14.9 %add_convert_fusion.1 = bf16[2304,1024]{1,0:T(8,128)(2,1)} fusion(f32[2304,1024]{1,0:T(8,128)} %fusion.29, bf16[2304,2048]{1,0:T(8,128)(2,1)S(1)} %bitcast.95, bf16[2048,2048]{1,0:T(8,128)(2,1)} %slice_dynamic-update-slice_fusion.7), kind=kOutput, calls=%fused_computation.22 | convolution fusion | flops 9668395008 | bytes 27787264 | tf_op jit(solution)/shard_map/dot_general | solution.py:24
  718.4 17.1 %fusion.25 = f32[2304,1024]{1,0:T(8,128)} fusion(bf16[2304,2048]{1,0:T(8,128)(2,1)} %get-tuple-element.146, bf16[2048,2048]{1,0:T(8,128)(2,1)} %slice_dynamic-update-slice_fusion.7), kind=kOutput, calls=%fused_computation.54 | convolution fusion | flops 9663676416 | bytes 23068672 | tf_op jit(solution)/shard_map/dot_general | solution.py:24
  735.5 14.9 %add_convert_fusion = bf16[2304,1024]{1,0:T(8,128)(2,1)} fusion(f32[2304,1024]{1,0:T(8,128)} %fusion.25, bf16[2304,2048]{1,0:T(8,128)(2,1)S(1)} %bitcast.97, bf16[2048,2048]{1,0:T(8,128)(2,1)} %pad_maximum_fusion.1), kind=kOutput, calls=%fused_computation.21 | convolution fusion | flops 9668395008 | bytes 27787264 | tf_op jit(solution)/shard_map/dot_general | solution.py:24
  760.0 26.6 %convolution_convert_fusion.4 = bf16[2048,2048]{1,0:T(8,128)(2,1)} fusion(bf16[2304,2048]{1,0:T(8,128)(2,1)} %all-gather.8.cloned.1.call-done, bf16[2304,2048]{1,0:T(8,128)(2,1)} %get-tuple-element.143), kind=kOutput, calls=%fused_computation.41 | convolution fusion | flops 19331547136 | bytes 27262976 | tf_op jit(solution)/shard_map/dot_general | solution.py:24
  793.9 25.5 %convolution_convert_fusion.3 = bf16[2048,2048]{1,0:T(8,128)(2,1)S(1)} fusion(bf16[2304,2048]{1,0:T(8,128)(2,1)} %all-gather.8.cloned.1.call-done, bf16[2304,2048]{1,0:T(8,128)(2,1)} %get-tuple-element.146), kind=kOutput, calls=%fused_computation.40 | convolution fusion | flops 19331547136 | bytes 27262976 | tf_op jit(solution)/shard_map/dot_general | solution.py:24
  850.7 17.6 %collective-permute-done.26 = bf16[256,2048]{1,0:T(8,128)(2,1)} collective-permute-done((bf16[256,2048]{1,0:T(8,128)(2,1)}, bf16[256,2048]{1,0:T(8,128)(2,1)}, u32[]{:S(2)}, u32[]{:S(2)}) %collective-permute-start.26) | collective-permute-done | bytes 1048608 | tf_op jit(solution)/shard_map/ppermute | solution.py:61
  903.9 14.0 %collective-permute-done.30 = bf16[256,2048]{1,0:T(8,128)(2,1)} collective-permute-done((bf16[256,2048]{1,0:T(8,128)(2,1)}, bf16[256,2048]{1,0:T(8,128)(2,1)}, u32[]{:S(2)}, u32[]{:S(2)}) %collective-permute-start.30) | collective-permute-done | bytes 1048608 | tf_op jit(solution)/shard_map/ppermute | solution.py:61
  919.2 28.0 %convolution_convert_fusion = bf16[2304,2048]{1,0:T(8,128)(2,1)} fusion(bf16[2304,2048]{1,0:T(8,128)(2,1)} %get-tuple-element.166, bf16[512,2048]{1,0:T(8,128)(2,1)} %get-tuple-element.243, bf16[512,2048]{1,0:T(8,128)(2,1)} %get-tuple-element.241, bf16[512,2048]{1,0:T(8,128)(2,1)} %get-tuple-element.239, bf16[512,2048]{1,0:T(8,128)(2,1)} %copy-done.20), kind=kOutput, calls=%fused_computation.18 | convolution fusion | flops 19365625856 | bytes 27262976 | tf_op jit(solution)/shard_map/dot_general | solution.py:24
  1007.3 8.9 fusion.41
  1036.6 10.3 collective-permute-done.37
  1052.4 22.5 %collective-permute-done.41 = bf16[1,2,4,128,640]{4,3,2,1,0:T(8,128)(2,1)} collective-permute-done((bf16[1,2,4,128,640]{4,3,2,1,0:T(8,128)(2,1)}, bf16[1,2,4,128,640]{4,3,2,1,0:T(8,128)(2,1)}, u32[]{:S(2)}, u32[]{:S(2)}) %collective-permute-start.41) | collective-permute-done | bytes 1310752 | tf_op jit(solution)/shard_map/ppermute | solution.py:61
  1080.8 30.2 %collective-permute-done.38 = bf16[1,1,4,128,512]{4,3,2,1,0:T(8,128)(2,1)S(1)} collective-permute-done((bf16[1,1,4,128,512]{4,3,2,1,0:T(8,128)(2,1)S(1)}, bf16[1,1,4,128,512]{4,3,2,1,0:T(8,128)(2,1)S(1)}, u32[]{:S(2)}, u32[]{:S(2)}) %collective-permute-start.38) | collective-permute-done | bytes 524320 | tf_op jit(solution)/shard_map/ppermute | solution.py:61
  1111.9 12.1 collective-permute-done.42
  1134.9 15.5 %collective-permute-done.54 = bf16[128,2304]{1,0:T(8,128)(2,1)S(1)} collective-permute-done((bf16[128,2304]{1,0:T(8,128)(2,1)S(1)}, bf16[128,2304]{1,0:T(8,128)(2,1)S(1)}, u32[]{:S(2)}, u32[]{:S(2)}) %collective-permute-start.54) | collective-permute-done | bytes 589856 | tf_op jit(solution)/shard_map/ppermute | solution.py:61
  1150.4 18.2 %collective-permute-done.55 = bf16[128,2304]{1,0:T(8,128)(2,1)S(1)} collective-permute-done((bf16[128,2304]{1,0:T(8,128)(2,1)S(1)}, bf16[128,2304]{1,0:T(8,128)(2,1)S(1)}, u32[]{:S(2)}, u32[]{:S(2)}) %collective-permute-start.55) | collective-permute-done | bytes 589856 | tf_op jit(solution)/shard_map/ppermute | solution.py:61
  1178.2 9.2 collective-permute-done.49
  1188.7 9.9 collective-permute-start.50
  (617 shorter events, 459.3 us)
Async XLA Ops:
  7.2 95.5 %all-gather.4.cloned.1.call-start = ((), (), s32[]{:S(2)}) async-start(), calls=%async_computation.5 | async-start | bytes 11354112 | tf_op jit(solution)/shard_map/all_gather | solution.py:233
  10.9 299.8 %all-gather.6.cloned.1.call-start = ((), (), s32[]{:S(2)}) async-start(), calls=%async_computation.6 | async-start | bytes 11894784 | tf_op jit(solution)/shard_map/all_gather | solution.py:273
  102.7 439.3 %all-gather.8.cloned.1.call-start = ((), (), s32[]{:S(2)}) async-start(), calls=%async_computation.7 | async-start | bytes 10616832 | tf_op jit(solution)/shard_map/all_gather | solution.py:382
  133.9 153.2 %collective-permute-start.17 = (bf16[288,1024]{1,0:T(8,128)(2,1)}, bf16[288,1024]{1,0:T(8,128)(2,1)}, u32[]{:S(2)}, u32[]{:S(2)}) collective-permute-start(bf16[288,1024]{1,0:T(8,128)(2,1)} %get-tuple-element.279), channel_id=1, source_target_pairs={{0,1},{1,0},{2,3},{3,2},{4,5},{5,4},{6,7},{7,6},{8,9},{9,8},{10,11... | collective-permute-start | bytes 1769480 | tf_op jit(solution)/shard_map/ppermute | solution.py:61
  168.5 121.1 %collective-permute-start.14 = (bf16[288,2048]{1,0:T(8,128)(2,1)}, bf16[288,2048]{1,0:T(8,128)(2,1)}, u32[]{:S(2)}, u32[]{:S(2)}) collective-permute-start(bf16[288,2048]{1,0:T(8,128)(2,1)} %fusion.40), channel_id=1, source_target_pairs={{0,1},{1,0},{2,3},{3,2},{4,5},{5,4},{6,7},{7,6},{8,9},{9,8},{10,11... | collective-permute-start | bytes 3538952 | tf_op jit(solution)/shard_map/ppermute | solution.py:61
  171.1 94.2 %collective-permute-start.4 = (bf16[800,2048]{1,0:T(8,128)(2,1)}, bf16[800,2048]{1,0:T(8,128)(2,1)}, u32[]{:S(2)}, u32[]{:S(2)}) collective-permute-start(bf16[800,2048]{1,0:T(8,128)(2,1)} %get-tuple-element.115), channel_id=1, source_target_pairs={{0,16},{8,24},{16,0},{24,8},{1,17},{9,25},{17,1},{25,9},{2,18},{10... | collective-permute-start | bytes 9830408 | tf_op jit(solution)/shard_map/ppermute | solution.py:61
  172.7 93.9 %collective-permute-start.5 = (bf16[800,2048]{1,0:T(8,128)(2,1)}, bf16[800,2048]{1,0:T(8,128)(2,1)}, u32[]{:S(2)}, u32[]{:S(2)}) collective-permute-start(bf16[800,2048]{1,0:T(8,128)(2,1)} %get-tuple-element.116), channel_id=1, source_target_pairs={{0,8},{8,0},{16,24},{24,16},{1,9},{9,1},{17,25},{25,17},{2,10},{10... | collective-permute-start | bytes 9830408 | tf_op jit(solution)/shard_map/ppermute | solution.py:61
  175.8 58.2 %collective-permute-start.6 = (bf16[288,2048]{1,0:T(8,128)(2,1)S(1)}, bf16[288,2048]{1,0:T(8,128)(2,1)S(1)}, u32[]{:S(2)}, u32[]{:S(2)}) collective-permute-start(bf16[288,2048]{1,0:T(8,128)(2,1)S(1)} %copy-done.8), channel_id=1, source_target_pairs={{0,2},{1,3},{2,0},{3,1},{4,6},{5,7},{6,4},{7,5},{8,10},{9,11},{10,... | collective-permute-start | bytes 3538952 | tf_op jit(solution)/shard_map/ppermute | solution.py:61
  294.8 104.2 %collective-permute-start.9 = (bf16[288,2048]{1,0:T(8,128)(2,1)S(1)}, bf16[288,2048]{1,0:T(8,128)(2,1)}, u32[]{:S(2)}, u32[]{:S(2)}) collective-permute-start(bf16[288,2048]{1,0:T(8,128)(2,1)S(1)} %copy-done.8), channel_id=1, source_target_pairs={{0,4},{1,5},{2,6},{3,7},{4,0},{5,1},{6,2},{7,3},{8,12},{9,13},{10,... | collective-permute-start | bytes 3538952 | tf_op jit(solution)/shard_map/ppermute | solution.py:61
  298.1 100.9 %collective-permute-start.7 = (bf16[800,2048]{1,0:T(8,128)(2,1)}, bf16[800,2048]{1,0:T(8,128)(2,1)}, u32[]{:S(2)}, u32[]{:S(2)}) collective-permute-start(bf16[800,2048]{1,0:T(8,128)(2,1)} %get-tuple-element.115), channel_id=1, source_target_pairs={{0,8},{8,0},{16,24},{24,16},{1,9},{9,1},{17,25},{25,17},{2,10},{10... | collective-permute-start | bytes 9830408 | tf_op jit(solution)/shard_map/ppermute | solution.py:61
  299.6 99.5 %collective-permute-start.8 = (bf16[800,2048]{1,0:T(8,128)(2,1)}, bf16[800,2048]{1,0:T(8,128)(2,1)}, u32[]{:S(2)}, u32[]{:S(2)}) collective-permute-start(bf16[800,2048]{1,0:T(8,128)(2,1)} %get-tuple-element.116), channel_id=1, source_target_pairs={{0,16},{8,24},{16,0},{24,8},{1,17},{9,25},{17,1},{25,9},{2,18},{10... | collective-permute-start | bytes 9830408 | tf_op jit(solution)/shard_map/ppermute | solution.py:61
  399.1 73.2 %collective-permute-start.13 = (bf16[800,2048]{1,0:T(8,128)(2,1)}, bf16[800,2048]{1,0:T(8,128)(2,1)}, u32[]{:S(2)}, u32[]{:S(2)}) collective-permute-start(bf16[800,2048]{1,0:T(8,128)(2,1)} %collective-permute-done.4), channel_id=1, source_target_pairs={{0,8},{8,0},{16,24},{24,16},{1,9},{9,1},{17,25},{25,17},{2,10},{10... | collective-permute-start | bytes 9830408 | tf_op jit(solution)/shard_map/ppermute | solution.py:61
  403.6 73.0 %collective-permute-start.12 = (bf16[800,2048]{1,0:T(8,128)(2,1)}, bf16[800,2048]{1,0:T(8,128)(2,1)}, u32[]{:S(2)}, u32[]{:S(2)}) collective-permute-start(bf16[800,2048]{1,0:T(8,128)(2,1)} %collective-permute-done.5), channel_id=1, source_target_pairs={{0,16},{8,24},{16,0},{24,8},{1,17},{9,25},{17,1},{25,9},{2,18},{10... | collective-permute-start | bytes 9830408 | tf_op jit(solution)/shard_map/ppermute | solution.py:61
  405.3 426.5 %reduce-scatter.6.cloned.1.call-start = ((), (), s32[]{:S(2)}) async-start(), calls=%async_computation.8 | async-start | bytes 5308416 | tf_op jit(solution)/shard_map/reduce_scatter | solution.py:437
  412.7 83.0 %collective-permute-start.11 = (bf16[1152,2048]{1,0:T(8,128)(2,1)}, bf16[1152,2048]{1,0:T(8,128)(2,1)}, u32[]{:S(2)}, u32[]{:S(2)}) collective-permute-start(bf16[1152,2048]{1,0:T(8,128)(2,1)} %pad_maximum_fusion.5), channel_id=1, source_target_pairs={{0,1},{1,0},{2,3},{3,2},{4,5},{5,4},{6,7},{7,6},{8,9},{9,8},{10,11... | collective-permute-start | bytes 14155784 | tf_op jit(solution)/shard_map/ppermute | solution.py:61
  708.4 124.7 %reduce-scatter.8.cloned.1.call-start = ((), (), s32[]{:S(2)}) async-start(), calls=%async_computation.9 | async-start | bytes 5308416 | tf_op jit(solution)/shard_map/reduce_scatter | solution.py:437
  716.7 38.3 %collective-permute-start.20 = (bf16[288,2048]{1,0:T(8,128)(2,1)}, bf16[288,2048]{1,0:T(8,128)(2,1)}, u32[]{:S(2)}, u32[]{:S(2)}) collective-permute-start(bf16[288,2048]{1,0:T(8,128)(2,1)} %get-tuple-element.133), channel_id=1, source_target_pairs={{0,8},{8,0},{16,24},{24,16},{1,9},{9,1},{17,25},{25,17},{2,10},{10... | collective-permute-start | bytes 3538952 | tf_op jit(solution)/shard_map/ppermute | solution.py:61
  717.0 38.1 %collective-permute-start.21 = (bf16[288,2048]{1,0:T(8,128)(2,1)}, bf16[288,2048]{1,0:T(8,128)(2,1)}, u32[]{:S(2)}, u32[]{:S(2)}) collective-permute-start(bf16[288,2048]{1,0:T(8,128)(2,1)} %pad_maximum_fusion.18), channel_id=1, source_target_pairs={{0,16},{8,24},{16,0},{24,8},{1,17},{9,25},{17,1},{25,9},{2,18},{10... | collective-permute-start | bytes 3538952 | tf_op jit(solution)/shard_map/ppermute | solution.py:61
  755.1 148.9 %reduce-scatter.10.cloned.1.call-start = ((), (), s32[]{:S(2)}) async-start(), calls=%async_computation.10 | async-start | bytes 1327104 | tf_op jit(solution)/shard_map/reduce_scatter | solution.py:437
  786.6 200.6 %reduce-scatter.12.cloned.1.call-start = ((), (), s32[]{:S(2)}) async-start(), calls=%async_computation.11 | async-start | bytes 2654208 | tf_op jit(solution)/shard_map/reduce_scatter | solution.py:437
  825.9 42.5 %collective-permute-start.26 = (bf16[256,2048]{1,0:T(8,128)(2,1)}, bf16[256,2048]{1,0:T(8,128)(2,1)}, u32[]{:S(2)}, u32[]{:S(2)}) collective-permute-start(bf16[256,2048]{1,0:T(8,128)(2,1)} %get-tuple-element.147), channel_id=1, source_target_pairs={{0,8},{8,0},{16,24},{24,16},{1,9},{9,1},{17,25},{25,17},{2,10},{10... | collective-permute-start | bytes 3145736 | tf_op jit(solution)/shard_map/ppermute | solution.py:61
  826.3 42.2 %collective-permute-start.27 = (bf16[256,2048]{1,0:T(8,128)(2,1)}, bf16[256,2048]{1,0:T(8,128)(2,1)}, u32[]{:S(2)}, u32[]{:S(2)}) collective-permute-start(bf16[256,2048]{1,0:T(8,128)(2,1)} %get-tuple-element.148), channel_id=1, source_target_pairs={{0,16},{8,24},{16,0},{24,8},{1,17},{9,25},{17,1},{25,9},{2,18},{10... | collective-permute-start | bytes 3145736 | tf_op jit(solution)/shard_map/ppermute | solution.py:61
  919.1 303.7 %reduce-scatter.14.cloned.1.call-start = ((), (), s32[]{:S(2)}) async-start(), calls=%async_computation.12 | async-start | bytes 10616832 | tf_op jit(solution)/shard_map/reduce_scatter | solution.py:437
  1025.9 49.1 %collective-permute-start.41 = (bf16[1,2,4,128,640]{4,3,2,1,0:T(8,128)(2,1)}, bf16[1,2,4,128,640]{4,3,2,1,0:T(8,128)(2,1)}, u32[]{:S(2)}, u32[]{:S(2)}) collective-permute-start(bf16[1,2,4,128,640]{4,3,2,1,0:T(8,128)(2,1)} %constant_dynamic-slice_fusion.13), channel_id=1, source_target_pairs={{0,16},{8,24},{16,0},{24,8},{1,17},{9,25},{17,1},{25,9},{2,18},{10... | collective-permute-start | bytes 3932168 | tf_op jit(solution)/shard_map/ppermute | solution.py:61
  1031.1 47.0 %collective-permute-start.43 = (bf16[2,1,4,128,640]{4,3,2,1,0:T(8,128)(2,1)}, bf16[2,1,4,128,640]{4,3,2,1,0:T(8,128)(2,1)}, u32[]{:S(2)}, u32[]{:S(2)}) collective-permute-start(bf16[2,1,4,128,640]{4,3,2,1,0:T(8,128)(2,1)} %constant_dynamic-slice_fusion.11), channel_id=1, source_target_pairs={{0,8},{8,0},{16,24},{24,16},{1,9},{9,1},{17,25},{25,17},{2,10},{10... | collective-permute-start | bytes 3932168 | tf_op jit(solution)/shard_map/ppermute | solution.py:61
  1032.3 98.3 %collective-permute-start.58 = (bf16[256,2048]{1,0:T(8,128)(2,1)}, bf16[256,2048]{1,0:T(8,128)(2,1)S(1)}, u32[]{:S(2)}, u32[]{:S(2)}) collective-permute-start(bf16[256,2048]{1,0:T(8,128)(2,1)} %get-tuple-element.186), channel_id=1, source_target_pairs={{0,16},{8,24},{16,0},{24,8},{1,17},{9,25},{17,1},{25,9},{2,18},{10... | collective-permute-start | bytes 3145736 | tf_op jit(solution)/shard_map/ppermute | solution.py:61
  1046.8 83.8 %collective-permute-start.59 = (bf16[256,2048]{1,0:T(8,128)(2,1)S(1)}, bf16[256,2048]{1,0:T(8,128)(2,1)S(1)}, u32[]{:S(2)}, u32[]{:S(2)}) collective-permute-start(bf16[256,2048]{1,0:T(8,128)(2,1)S(1)} %copy-done.81), channel_id=1, source_target_pairs={{0,8},{8,0},{16,24},{24,16},{1,9},{9,1},{17,25},{25,17},{2,10},{10... | collective-permute-start | bytes 3145736 | tf_op jit(solution)/shard_map/ppermute | solution.py:61
  1049.9 61.0 %collective-permute-start.38 = (bf16[1,1,4,128,512]{4,3,2,1,0:T(8,128)(2,1)S(1)}, bf16[1,1,4,128,512]{4,3,2,1,0:T(8,128)(2,1)S(1)}, u32[]{:S(2)}, u32[]{:S(2)}) collective-permute-start(bf16[1,1,4,128,512]{4,3,2,1,0:T(8,128)(2,1)S(1)} %constant_dynamic-slice_fusion.16), channel_id=1, source_target_pairs={{0,8},{8,0},{16,24},{24,16},{1,9},{9,1},{17,25},{25,17},{2,10},{10... | collective-permute-start | bytes 1572872 | tf_op jit(solution)/shard_map/ppermute | solution.py:61
  1078.0 45.9 %collective-permute-start.42 = (bf16[1,1,4,128,640]{4,3,2,1,0:T(8,128)(2,1)S(1)}, bf16[1,1,4,128,640]{4,3,2,1,0:T(8,128)(2,1)S(1)}, u32[]{:S(2)}, u32[]{:S(2)}) collective-permute-start(bf16[1,1,4,128,640]{4,3,2,1,0:T(8,128)(2,1)S(1)} %constant_dynamic-slice_fusion.12), channel_id=1, source_target_pairs={{0,8},{8,0},{16,24},{24,16},{1,9},{9,1},{17,25},{25,17},{2,10},{10... | collective-permute-start | bytes 1966088 | tf_op jit(solution)/shard_map/ppermute | solution.py:61
  1126.2 42.4 %collective-permute-start.55 = (bf16[128,2304]{1,0:T(8,128)(2,1)S(1)}, bf16[128,2304]{1,0:T(8,128)(2,1)S(1)}, u32[]{:S(2)}, u32[]{:S(2)}) collective-permute-start(bf16[128,2304]{1,0:T(8,128)(2,1)S(1)} %get-tuple-element.261), channel_id=1, source_target_pairs={{0,4},{1,5},{2,6},{3,7},{4,0},{5,1},{6,2},{7,3},{8,12},{9,13},{10,... | collective-permute-start | bytes 1769480 | tf_op jit(solution)/shard_map/ppermute | solution.py:61
  1128.6 40.1 %collective-permute-start.56 = (bf16[128,2304]{1,0:T(8,128)(2,1)S(1)}, bf16[128,2304]{1,0:T(8,128)(2,1)S(1)}, u32[]{:S(2)}, u32[]{:S(2)}) collective-permute-start(bf16[128,2304]{1,0:T(8,128)(2,1)S(1)} %get-tuple-element.260), channel_id=1, source_target_pairs={{0,6},{1,7},{2,4},{3,5},{4,2},{5,3},{6,0},{7,1},{8,14},{9,15},{10,... | collective-permute-start | bytes 1769480 | tf_op jit(solution)/shard_map/ppermute | solution.py:61
  1134.0 37.6 %collective-permute-start.48 = (bf16[1,2,4,128,512]{4,3,2,1,0:T(8,128)(2,1)S(1)}, bf16[1,2,4,128,512]{4,3,2,1,0:T(8,128)(2,1)S(1)}, u32[]{:S(2)}, u32[]{:S(2)}) collective-permute-start(bf16[1,2,4,128,512]{4,3,2,1,0:T(8,128)(2,1)S(1)} %constant_dynamic-slice_fusion.5), channel_id=1, source_target_pairs={{0,16},{8,24},{16,0},{24,8},{1,17},{9,25},{17,1},{25,9},{2,18},{10... | collective-permute-start | bytes 3145736 | tf_op jit(solution)/shard_map/ppermute | solution.py:61
  (171 other events, 2235.1 us)
Sparse Core Ops, SparseCore 0:
  11.6 91.0 all-gather.3
  106.1 130.3 all-gather.5
  405.4 89.3 all-gather.7
  707.6 53.5 reduce-scatter.5
  763.3 53.3 reduce-scatter.7
  819.4 31.4 reduce-scatter.9
  919.3 35.6 reduce-scatter.11
  987.3 98.3 reduce-scatter.13

commit v6 on v5

--- a/solution.py
+++ b/solution.py
@@ -148,19 +148,32 @@
     return add_half(kept, swap(sent, axis, size, bit))
 
 
-def row_stages(values, row_size, col_size, parts=2):
+def row_bits(row_size, place):
+    bits = [1 << k for k in reversed(range(row_size.bit_length() - 1))]
+    return bits, bits if place % 2 == 0 else bits[::-1]
+
+
+def row_first(values, row_size, col_size, parts=2):
     chips, rows, width = values.shape
-    line = col_size // 2
-    bits = [1 << k for k in reversed(range(row_size.bit_length() - 1))]
-    shaped = values.reshape((2,) * len(bits) + (line, rows, width))
+    bits, order = row_bits(row_size, 0)
+    shaped = values.reshape((2,) * len(bits) + (col_size // 2, rows, width))
     part = width // parts
     pieces = []
     for place in range(parts):
+        bits, order = row_bits(row_size, place)
         piece = shaped[..., part * place : part * (place + 1)]
-        for bit in bits if place % 2 == 0 else bits[::-1]:
+        pieces.append(halve(piece, bits.index(order[0]), "row", row_size, order[0]))
+    return pieces
+
+
+def row_rest(pieces, row_size):
+    done = []
+    for place, piece in enumerate(pieces):
+        bits, order = row_bits(row_size, place)
+        for bit in order[1:]:
             piece = halve(piece, bits.index(bit), "row", row_size, bit)
-        pieces.append(piece.reshape(line, rows, part))
-    return jnp.concatenate(pieces, axis=-1)
+        done.append(piece.reshape(piece.shape[-3:]))
+    return jnp.concatenate(done, axis=-1)
 
 
 def line_stage(whole, col_size):
@@ -269,20 +282,23 @@
         ],
         axis=1,
     )
-    in_gathered, cosine, sine_part, out_packed = tie(in_gathered, cosine, sine_part, out_packed)
-    out_gathered = lax.all_gather(out_packed, ("row", "col"), axis=0, tiled=True)
+    in_gathered, cosine, sine_part = tie(in_gathered, cosine, sine_part)
     model_rows = gate_matrix.shape[0]
     by_pairs = row_size == 4 and col_size == 8
     cot_grad = cotangent.astype(jnp.float32)
     cot_mixed = reorder(cotangent, order)
     if by_pairs:
         half = shard.shape[0] // 2
-        in_gathered, upper, lower, cot_mixed = tie(
-            in_gathered, shard[:half], shard[half:], cot_mixed
-        )
+        upper, lower = shard[:half], shard[half:]
         upper_y = swap(upper, "row", 4, 2)
         lower_x = swap(lower, "row", 4, 1)
         cot_two = swap(cot_mixed, "col", 8, 2)
+        cot_four = swap(cot_mixed, "col", 8, 4)
+        in_gathered, upper_y, lower_x, cot_two, cot_four, upper, lower, cot_mixed = tie(
+            in_gathered, upper_y, lower_x, cot_two, cot_four, upper, lower, cot_mixed
+        )
+        upper_x = swap(upper, "row", 4, 1)
+        lower_y = swap(lower, "row", 4, 2)
     in_width = in_gathered.shape[1] - 128
     in_weight = in_gathered[:, :in_width]
     gains = in_gathered[:, in_width:].astype(jnp.float32)
@@ -316,12 +332,9 @@
             ]
             return place_blocks(parts, places, 8)
 
-        keyval_mine = jnp.concatenate(
-            [keyval_own] + [swap(keyval_own, "col", 8, 2 * step) for step in range(1, 4)], axis=0
-        )
-        keyval_rows = gathered(keyval_mine, swap(keyval_mine, "col", 8, 1))
-    else:
-        keyval_rows = lax.all_gather(keyval_own, "col", axis=0, tiled=True)
+    keyval_rows = lax.all_gather(keyval_own, "col", axis=0, tiled=True)
+    keyval_rows, out_packed = tie(keyval_rows, out_packed)
+    out_gathered = lax.all_gather(out_packed, ("row", "col"), axis=0, tiled=True)
     key_rows = keyval_rows[:, :HD]
     value_rows = keyval_rows[:, HD:]
     row_index = start_row + jnp.arange(row_total, dtype=jnp.int32) // NH
@@ -335,12 +348,11 @@
     total_value = jnp.sum(jnp.exp(scores - top_value[:, None]), axis=1)
     log_norm = top_value + jnp.log(total_value)
     if by_pairs:
-        log_norm, upper_y, lower_x, cot_two, upper, lower, cot_mixed = tie(
-            log_norm, upper_y, lower_x, cot_two, upper, lower, cot_mixed
-        )
-        upper_x = swap(upper, "row", 4, 1)
-        lower_y = swap(lower, "row", 4, 2)
-        cot_four = swap(cot_mixed, "col", 8, 4)
+        log_norm, upper_y, lower_x, upper_x, lower_y, cot_mixed = tie(
+            log_norm, upper_y, lower_x, upper_x, lower_y, cot_mixed
+        )
+        far_upper = swap(upper_y, "row", 4, 1)
+        far_lower = swap(lower_x, "row", 4, 2)
         cot_six = swap(cot_mixed, "col", 8, 6)
     probs = convert_half(jnp.exp(scores - log_norm[:, None]))
     mixed_rows = matrix_product(probs, value_rows)
@@ -357,14 +369,10 @@
     normed_mlp = convert_half(rms_scale(layer_state, gain_mlp))
     normed_mlp = reorder(normed_mlp, order)
     if by_pairs:
-        normed_mlp, upper_x, lower_y, cot_four, cot_six, upper_y, lower_x = tie(
-            normed_mlp, upper_x, lower_y, cot_four, cot_six, upper_y, lower_x
-        )
-        far_upper = [swap(upper_y, "row", 4, 1)]
-        far_lower = [swap(lower_x, "row", 4, 2)]
+        normed_mlp, far_upper, far_lower, cot_six = tie(normed_mlp, far_upper, far_lower, cot_six)
         cot_mine = jnp.concatenate([cot_mixed, cot_two, cot_four, cot_six], axis=0)
         cot_rows = gathered(cot_mine, swap(cot_mine, "col", 8, 1))
-        pieces = [[shard], [upper_x, lower_x], [upper_y, lower_y], [*far_upper, *far_lower]]
+        pieces = [[shard], [upper_x, lower_x], [upper_y, lower_y], [far_upper, far_lower]]
     else:
         pieces = [[shard]] + [
             [to_partner(shard, "row", step, row_size)] for step in range(1, row_size)
@@ -442,35 +450,43 @@
     if row_size == 4:
         own_down, far, free, last = split_blocks(down_blocks)
         far = send_pair(far)
+        grad_gate = convert_half(product(ffn_in, gate_grad, contract_first))
+        *far, grad_gate, up_grad, free_x, free_y = tie(*far, grad_gate, up_grad, *free)
+        last = add_pair(last, far)
+        down_free = send_pair((free_x, free_y))
+        own_gate, gate_far, gate_free, gate_last = split_blocks(blocks_of(grad_gate))
+        grad_up = convert_half(product(ffn_in, up_grad, contract_first))
+        *down_free, grad_up, gate_grad, last_x, last_y, far_x, far_y = tie(
+            *down_free, grad_up, gate_grad, *last, *gate_far
+        )
+        down_last = send_pair((last_x, last_y))
+        far = send_pair((far_x, far_y))
+        own_up, up_far, up_free, up_last = split_blocks(blocks_of(grad_up))
         first_part = normed_part(0, gate_grad, up_grad)
-        *far, first_part, gate_grad, up_grad, free_x, free_y = tie(
-            *far, first_part, gate_grad, up_grad, *free
+        *down_last, far_x, far_y, first_part, gate_grad, free_x, free_y, next_x, next_y = tie(
+            *down_last, *far, first_part, gate_grad, *gate_free, *up_far
         )
         first_sum = col_sum(first_part)
-        last = add_pair(last, far)
-        free = send_pair((free_x, free_y))
+        gate_last = add_pair(gate_last, (far_x, far_y))
+        gate_free = send_pair((free_x, free_y))
+        up_far = send_pair((next_x, next_y))
         second_part = normed_part(half_width, gate_grad, up_grad)
-        *free, second_part, gate_grad, up_grad, last_x, last_y = tie(
-            *free, second_part, gate_grad, up_grad, *last
-        )
+        *gate_free, far_x, far_y, second_part, last_x, last_y, free_x, free_y, hidden_activated = tie(
+            *gate_free, *up_far, second_part, *gate_last, *up_free, hidden_activated
+        )
+        second_sum = col_sum(second_part)
+        up_last = add_pair(up_last, (far_x, far_y))
+        gate_last = send_pair((last_x, last_y))
+        up_free = send_pair((free_x, free_y))
         rank_partial = down_product(width, width + rank_width)
-        second_part, rank_partial, hidden_activated = tie(
-            second_part, rank_partial, hidden_activated
-        )
-        second_sum = col_sum(second_part)
-        last = send_pair((last_x, last_y))
-        grad_gate = convert_half(product(ffn_in, gate_grad, contract_first))
-        *down_parts, grad_gate, up_grad = tie(own_down, *free, *last, grad_gate, up_grad)
-        down_total = finish_sum(down_parts[0], down_parts[1:3], down_parts[3:])
-        own_gate, far, free, last = split_blocks(blocks_of(grad_gate))
-        far = send_pair(far)
-        grad_up = convert_half(product(ffn_in, up_grad, contract_first))
-        *far, grad_up, free_x, free_y = tie(*far, grad_up, *free)
-        gate_last = add_pair(last, far)
-        gate_free = send_pair((free_x, free_y))
-        own_up, far, up_free, up_last = split_blocks(blocks_of(grad_up))
-        up_far = send_pair(far)
+        down_partial = down_product(0, width)
+        *gate_last, free_x, free_y, second_sum, down_partial, last_x, last_y = tie(
+            *gate_last, *up_free, second_sum, down_partial, *up_last
+        )
+        up_free = (free_x, free_y)
+        up_last = send_pair((last_x, last_y))
     else:
+        down_partial = down_product(0, width)
         first_sum = col_sum(normed_part(0, gate_grad, up_grad))
         second_sum = col_sum(normed_part(half_width, gate_grad, up_grad))
         rank_partial = down_product(width, width + rank_width)
@@ -479,7 +495,6 @@
         down_total = row_sum(down_blocks, row_size)
         gate_sum = row_sum(blocks_of(grad_gate), row_size)
         up_sum = row_sum(blocks_of(grad_up), row_size)
-    down_sum, rank_sum = down_total[:model_rows], down_total[model_rows:]
     rank_sums = col_sum(rank_partial)
     normed_grad = jnp.concatenate([first_sum, second_sum], axis=1)
 
@@ -493,12 +508,7 @@
     context_grad = product(out_grad, out_weight, contract_last)
     grad_rows = convert_half(context_grad).reshape(row_total, HD)
     if row_size == 4:
-        *gate_free, far_x, far_y, grad_rows, last_x, last_y, free_x, free_y = tie(
-            *gate_free, *up_far, grad_rows, *gate_last, *up_free
-        )
-        up_last = add_pair(up_last, (far_x, far_y))
-        gate_last = send_pair((last_x, last_y))
-        up_free = (free_x, free_y)
+        *up_last, grad_rows = tie(*up_last, grad_rows)
     delta = jnp.sum(grad_rows.astype(jnp.float32) * mixed_rows, axis=1)
     weight_grad = product(grad_rows, value_rows, contract_last)
     score_grad = convert_half(probs.astype(jnp.float32) * (weight_grad - delta[:, None]))
@@ -513,10 +523,6 @@
     value_acc = product(probs, grad_rows, contract_first)
     keyval_part = jnp.concatenate([convert_half(key_acc), convert_half(value_acc)], axis=1)
     keyval_part, rank_sums = tie(keyval_part, rank_sums)
-    if row_size == 4:
-        *gate_last, keyval_part, free_x, free_y = tie(*gate_last, keyval_part, *up_free)
-        gate_sum = finish_sum(own_gate, gate_free, gate_last)
-        up_free = send_pair((free_x, free_y))
     keyval_sum = col_sum(keyval_part)
     core = lax.axis_index("col") % 2
     query_right = halves_with_partner(query_grad, col_size)
@@ -534,16 +540,17 @@
     grad_out_upper = product(rank_both, out_right, contract_first)
     out_group = jnp.concatenate([shared(grad_out), shared(grad_out_upper)], axis=2)
     query_group = shared(grad_query)
-    down_partial = down_product(0, width)
+    query_parts = row_first(query_group, row_size, col_size)
+    out_parts = row_first(out_group, row_size, col_size)
+    keyval_sum, down_partial, *parts = tie(keyval_sum, down_partial, *query_parts, *out_parts)
+    query_parts, out_parts = parts[:2], parts[2:]
     if row_size == 4:
-        *up_free, keyval_sum, down_partial, out_group, query_group, last_x, last_y = tie(
-            *up_free, keyval_sum, down_partial, out_group, query_group, *up_last
-        )
-        up_sum = finish_sum(own_up, up_free, send_pair((last_x, last_y)))
-    else:
-        keyval_sum, down_partial = tie(keyval_sum, down_partial)
-    query_lines = row_stages(query_group, row_size, col_size)
-    out_lines = row_stages(out_group, row_size, col_size)
+        down_total = finish_sum(own_down, down_free, down_last)
+        gate_sum = finish_sum(own_gate, gate_free, gate_last)
+        up_sum = finish_sum(own_up, up_free, up_last)
+    down_sum, rank_sum = down_total[:model_rows], down_total[model_rows:]
+    query_lines = row_rest(query_parts, row_size)
+    out_lines = row_rest(out_parts, row_size)
     down_rank_rows = reorder(rank_sums, order)
     summed = col_sum(down_partial)
     layer_out = convert_half(
@@ -584,7 +591,7 @@
     lines, keyval_group = tie(lines, keyval_group)
     first, second = share_cores(line_stage(lines, col_size), col_size)
     keyval_first, keyval_second = share_cores(
-        line_stage(row_stages(keyval_group, row_size, col_size, parts=1), col_size), col_size
+        line_stage(row_rest(row_first(keyval_group, row_size, col_size, parts=1), row_size), col_size), col_size
     )
     half_query = query_width // 2
     query_first, query_second = first[:, :half_query], second[:, :half_query]

time: 1240 us -> 1230 us (level)
  waiting for transfers between devices: 477 us -> 464 us
    ppermute x60 -> x56, waiting for transfers between devices: 388 us -> 324 us  [swap(): return lax.ppermute(values, axis, [(i, i ^ bit) for i in range(size)])]
    all_gather x0 -> x1, waiting for transfers between devices: none -> 24.1 us  [per_device(): keyval_rows = lax.all_gather(keyval_own, 'col', axis=0, tiled=True)]
    all_gather x1, waiting for transfers between devices: 88.8 us -> 106 us  [per_device(): lax.all_gather(jnp.concatenate([convert_half(query_matrix), convert_half(...]
    unnamed x278 -> x260, local copies, waits for them, and re-layouts: 35.5 us -> 30.5 us
    ppermute x60 -> x56, starting transfers between devices: 71.7 us -> 69 us  [swap(): return lax.ppermute(values, axis, [(i, i ^ bit) for i in range(size)])]
  transfers between devices with their start and end apart: 68 -> 65, of which waited for: 31 -> 30; matrix products, arithmetic and copies ran while one was open for 41% -> 40% of each run, Pallas kernels for 0% -> 0%
where the time goes in v6:
time: 1230 us; the launch traced here: 1220 us
  waiting for transfers between devices  464 us (38%)
  matrix products  354 us (29%)
  other arithmetic  164 us (13%)
  local copies, waits for them, and re-layouts  155 us (13%)
  starting transfers between devices  70 us (6%)
  between operations  15.8 us (1%)
    ppermute x56, waiting for transfers between devices, swap(): return lax.ppermute(values, axis, [(i, i ^ bit) for i in range(size)])  324 us
    dot_general x22, matrix products, product(): lax.dot_general(left_side, right_side, dims, preferred_element_type=jnp.f...  243 us
    dot_general x9, matrix products, matrix_product(): return jnp.dot(left_side, right_side, preferred_element_type=jnp.float32)  111 us
    all_gather x1, waiting for transfers between devices, per_device(): lax.all_gather(jnp.concatenate([convert_half(query_matrix), convert_half(...  106 us
    convert_element_type x24, other arithmetic, convert_half(): return values.astype(jnp.bfloat16)  75 us
    ppermute x56, starting transfers between devices, swap(): return lax.ppermute(values, axis, [(i, i ^ bit) for i in range(size)])  69 us
    unnamed x260, local copies, waits for them, and re-layouts  30.5 us
    slice x9, local copies, waits for them, and re-layouts, rows_of(): found.append(part[first:last])  26.4 us
  transfers between devices with their start and end apart: 65, of which 30 were waited for; matrix products, arithmetic and copies ran while one was open for 40% of the time, Pallas kernels for 0%

profile of v6, /device:TPU:0, one launch (start us, length us, event | category | flops | bytes accessed | tf_op | source)
XLA Modules:
  0.0 1221.7 jit_solution(11075241653199270953)
XLA Ops:
  37.1 106.5 %all-gather.5.cloned.1.call-done = bf16[2048,2688]{1,0:T(8,128)(2,1)} async-done(((bf16[64,2688]{1,0:T(8,128)(2,1)}), bf16[2048,2688]{1,0:T(8,128)(2,1)}) %all-gather.5.cloned.1.call-update) | async-done | bytes 11010064 | tf_op jit(solution)/shard_map/all_gather | solution.py:246
  162.6 24.1 %all-gather.7.cloned.1.call-done = bf16[2304,512]{1,0:T(8,128)(2,1)} async-done(((bf16[288,512]{1,0:T(8,128)(2,1)}), bf16[2304,512]{1,0:T(8,128)(2,1)}) %all-gather.7.cloned.1.call-update) | async-done | bytes 2359312 | tf_op jit(solution)/shard_map/all_gather | solution.py:335
  203.2 8.6 fusion.163
  215.0 87.4 %collective-permute-done.4 = bf16[800,2048]{1,0:T(8,128)(2,1)} collective-permute-done((bf16[800,2048]{1,0:T(8,128)(2,1)}, bf16[800,2048]{1,0:T(8,128)(2,1)}, u32[]{:S(2)}, u32[]{:S(2)}) %collective-permute-start.4) | collective-permute-done | bytes 3276832 | tf_op jit(solution)/shard_map/ppermute | solution.py:61
  312.8 8.8 fusion.164
  358.6 16.3 %collective-permute-done.6 = bf16[800,2048]{1,0:T(8,128)(2,1)} collective-permute-done((bf16[800,2048]{1,0:T(8,128)(2,1)}, bf16[800,2048]{1,0:T(8,128)(2,1)}, u32[]{:S(2)}, u32[]{:S(2)}) %collective-permute-start.6) | collective-permute-done | bytes 3276832 | tf_op jit(solution)/shard_map/ppermute | solution.py:61
  374.9 21.8 %collective-permute-done.7 = bf16[800,2048]{1,0:T(8,128)(2,1)} collective-permute-done((bf16[800,2048]{1,0:T(8,128)(2,1)}, bf16[800,2048]{1,0:T(8,128)(2,1)}, u32[]{:S(2)}, u32[]{:S(2)}) %collective-permute-start.7) | collective-permute-done | bytes 3276832 | tf_op jit(solution)/shard_map/ppermute | solution.py:61
  467.4 29.8 %fusion.24 = f32[2304,2048]{1,0:T(8,128)} fusion(bf16[2304,2048]{1,0:T(8,128)(2,1)} %get-tuple-element.244, bf16[2304,256]{1,0:T(8,128)(2,1)S(1)} %copy.37, bf16[2304,2048]{1,0:T(8,128)(2,1)} %slice_dynamic-update-slice_fusion), kind=kOutput, calls=%fused_computation.42 | convolution fusion | flops 21764505600 | bytes 38928384 | tf_op jit(solution)/shard_map/dot_general | solution.py:28
  497.2 27.0 %fusion.167 = f32[2304,2048]{1,0:T(8,128)} fusion(bf16[2304,2048]{1,0:T(8,128)(2,1)} %all-gather.11.cloned.1.call-done, bf16[2048,2048]{1,0:T(8,128)(2,1)} %slice_dynamic-update-slice_fusion.7), kind=kOutput, calls=%fused_computation.387 | convolution fusion | flops 19327352832 | bytes 36700160 | tf_op jit(solution)/shard_map/dot_general | solution.py:28
  524.2 24.5 %fusion.166 = f32[2304,2048]{1,0:T(8,128)} fusion(bf16[2304,2048]{1,0:T(8,128)(2,1)S(1)} %copy-done.105, bf16[2048,2048]{1,0:T(8,128)(2,1)} %pad_maximum_fusion.1), kind=kOutput, calls=%fused_computation.386 | convolution fusion | flops 19327352832 | bytes 36700160 | tf_op jit(solution)/shard_map/dot_general | solution.py:28
  548.7 29.9 %multiply_convert_fusion.1 = (bf16[2304,2048]{1,0:T(8,128)(2,1)}, bf16[2304,2048]{1,0:T(8,128)(2,1)}, bf16[2304,2048]{1,0:T(8,128)(2,1)}) fusion(f32[2304,2048]{1,0:T(8,128)S(1)} %bitcast.89, f32[2304,2048]{1,0:T(8,128)} %fusion.166, f32[2304,2048]{1,0:T(8,128)} %fusion.167), kind=kLoop, calls=%fused_computation.15 | loop fusion | flops 122683392 | bytes 84934656 | tf_op jit(solution)/shard_map/convert_element_type | solution.py:20
  578.6 28.8 %convolution_convert_fusion.1 = bf16[2304,2048]{1,0:T(8,128)(2,1)S(1)} fusion(bf16[2304,2048]{1,0:T(8,128)(2,1)} %get-tuple-element.159, bf16[2304,256]{1,0:T(8,128)(2,1)} %copy-done.66, bf16[2304,2048]{1,0:T(8,128)(2,1)} %slice_dynamic-update-slice_fusion), kind=kOutput, calls=%fused_computation.19 | convolution fusion | flops 21769224192 | bytes 29491200 | tf_op jit(solution)/shard_map/dot_general | solution.py:24
  616.3 24.4 %convolution_convert_fusion.4 = bf16[2048,2048]{1,0:T(8,128)(2,1)} fusion(bf16[2304,2048]{1,0:T(8,128)(2,1)} %all-gather.11.cloned.1.call-done, bf16[2304,2048]{1,0:T(8,128)(2,1)S(1)} %bitcast.95), kind=kOutput, calls=%fused_computation.41 | convolution fusion | flops 19331547136 | bytes 27262976 | tf_op jit(solution)/shard_map/dot_general | solution.py:24
  642.9 16.4 %fusion.28 = f32[2304,1024]{1,0:T(8,128)} fusion(bf16[2304,2048]{1,0:T(8,128)(2,1)} %get-tuple-element.137, bf16[2048,2048]{1,0:T(8,128)(2,1)} %slice_dynamic-update-slice_fusion.7), kind=kOutput, calls=%fused_computation.56 | convolution fusion | flops 9663676416 | bytes 23068672 | tf_op jit(solution)/shard_map/dot_general | solution.py:24
  659.3 24.7 %convolution_convert_fusion.3 = bf16[2048,2048]{1,0:T(8,128)(2,1)} fusion(bf16[2304,2048]{1,0:T(8,128)(2,1)} %all-gather.11.cloned.1.call-done, bf16[2304,2048]{1,0:T(8,128)(2,1)S(1)} %bitcast.97), kind=kOutput, calls=%fused_computation.40 | convolution fusion | flops 19331547136 | bytes 27262976 | tf_op jit(solution)/shard_map/dot_general | solution.py:24
  695.3 17.0 %collective-permute-done.16 = bf16[288,2048]{1,0:T(8,128)(2,1)} collective-permute-done((bf16[288,2048]{1,0:T(8,128)(2,1)}, bf16[288,2048]{1,0:T(8,128)(2,1)}, u32[]{:S(2)}, u32[]{:S(2)}) %collective-permute-start.16) | collective-permute-done | bytes 1179680 | tf_op jit(solution)/shard_map/ppermute | solution.py:61
  716.7 16.8 %add_convert_fusion.1 = bf16[2304,1024]{1,0:T(8,128)(2,1)} fusion(f32[2304,1024]{1,0:T(8,128)} %fusion.28, bf16[2304,2048]{1,0:T(8,128)(2,1)} %get-tuple-element.151, bf16[2048,2048]{1,0:T(8,128)(2,1)S(1)} %bitcast.99), kind=kOutput, calls=%fused_computation.22 | convolution fusion | flops 9668395008 | bytes 27787264 | tf_op jit(solution)/shard_map/dot_general | solution.py:24
  738.0 24.2 %collective-permute-done.20 = bf16[256,2048]{1,0:T(8,128)(2,1)} collective-permute-done((bf16[256,2048]{1,0:T(8,128)(2,1)}, bf16[256,2048]{1,0:T(8,128)(2,1)}, u32[]{:S(2)}, u32[]{:S(2)}) %collective-permute-start.20) | collective-permute-done | bytes 1048608 | tf_op jit(solution)/shard_map/ppermute | solution.py:61
  763.5 13.9 %fusion.25 = f32[2304,1024]{1,0:T(8,128)S(1)} fusion(bf16[2304,2048]{1,0:T(8,128)(2,1)} %get-tuple-element.137, bf16[2048,2048]{1,0:T(8,128)(2,1)} %slice_dynamic-update-slice_fusion.7), kind=kOutput, calls=%fused_computation.53 | convolution fusion | flops 9663676416 | bytes 23068672 | tf_op jit(solution)/shard_map/dot_general | solution.py:24
  781.5 15.7 %add_convert_fusion = bf16[2304,1024]{1,0:T(8,128)(2,1)} fusion(f32[2304,1024]{1,0:T(8,128)S(1)} %fusion.25, bf16[2304,2048]{1,0:T(8,128)(2,1)} %get-tuple-element.151, bf16[2048,2048]{1,0:T(8,128)(2,1)} %pad_maximum_fusion.1), kind=kOutput, calls=%fused_computation.21 | convolution fusion | flops 9668395008 | bytes 27787264 | tf_op jit(solution)/shard_map/dot_general | solution.py:24
  804.3 18.7 %collective-permute-done.24 = bf16[256,2048]{1,0:T(8,128)(2,1)S(1)} collective-permute-done((bf16[256,2048]{1,0:T(8,128)(2,1)}, bf16[256,2048]{1,0:T(8,128)(2,1)S(1)}, u32[]{:S(2)}, u32[]{:S(2)}) %collective-permute-start.24) | collective-permute-done | bytes 1048608 | tf_op jit(solution)/shard_map/ppermute | solution.py:61
  836.0 27.6 %convolution_convert_fusion = bf16[2304,2048]{1,0:T(8,128)(2,1)} fusion(bf16[2304,2048]{1,0:T(8,128)(2,1)} %get-tuple-element.159, bf16[512,2048]{1,0:T(8,128)(2,1)} %get-tuple-element.249, bf16[512,2048]{1,0:T(8,128)(2,1)} %get-tuple-element.247, bf16[512,2048]{1,0:T(8,128)(2,1)} %get-tuple-element.245, bf16[512,2048]{1,0:T(8,128)(2,1)S(1)} %copy-done.20), kind=kOutput, calls=%fused_computation.18 | convolution fusion | flops 19365625856 | bytes 27262976 | tf_op jit(solution)/shard_map/dot_general | solution.py:24
  869.4 8.7 reduce-scatter.6.cloned.1.call-done
  896.6 9.7 collective-permute-done.30
  913.0 8.5 multiply_convert_fusion
  973.8 18.9 %collective-permute-done.38 = bf16[2,1,4,128,640]{4,3,2,1,0:T(8,128)(2,1)} collective-permute-done((bf16[2,1,4,128,640]{4,3,2,1,0:T(8,128)(2,1)}, bf16[2,1,4,128,640]{4,3,2,1,0:T(8,128)(2,1)}, u32[]{:S(2)}, u32[]{:S(2)}) %collective-permute-start.38) | collective-permute-done | bytes 1310752 | tf_op jit(solution)/shard_map/ppermute | solution.py:61
  998.8 15.9 %collective-permute-done.34 = bf16[2,1,4,128,512]{4,3,2,1,0:T(8,128)(2,1)} collective-permute-done((bf16[2,1,4,128,512]{4,3,2,1,0:T(8,128)(2,1)}, bf16[2,1,4,128,512]{4,3,2,1,0:T(8,128)(2,1)}, u32[]{:S(2)}, u32[]{:S(2)}) %collective-permute-start.34) | collective-permute-done | bytes 1048608 | tf_op jit(solution)/shard_map/ppermute | solution.py:61
  1048.7 9.8 fusion.41
  1077.5 10.8 collective-permute-done.41
  1099.8 37.1 %collective-permute-done.52 = bf16[128,2304]{1,0:T(8,128)(2,1)S(1)} collective-permute-done((bf16[128,2304]{1,0:T(8,128)(2,1)S(1)}, bf16[128,2304]{1,0:T(8,128)(2,1)S(1)}, u32[]{:S(2)}, u32[]{:S(2)}) %collective-permute-start.52) | collective-permute-done | bytes 589856 | tf_op jit(solution)/shard_map/ppermute | solution.py:61
  1139.3 16.2 %collective-permute-done.54 = bf16[128,2304]{1,0:T(8,128)(2,1)S(1)} collective-permute-done((bf16[128,2304]{1,0:T(8,128)(2,1)S(1)}, bf16[128,2304]{1,0:T(8,128)(2,1)S(1)}, u32[]{:S(2)}, u32[]{:S(2)}) %collective-permute-start.54) | collective-permute-done | bytes 589856 | tf_op jit(solution)/shard_map/ppermute | solution.py:61
  1175.5 12.8 %collective-permute-start.48 = (bf16[128,512]{1,0:T(8,128)(2,1)S(1)}, bf16[128,512]{1,0:T(8,128)(2,1)S(1)}, u32[]{:S(2)}, u32[]{:S(2)}) collective-permute-start(bf16[128,512]{1,0:T(8,128)(2,1)S(1)} %get-tuple-element.304), channel_id=1, source_target_pairs={{0,2},{1,3},{2,0},{3,1},{4,6},{5,7},{6,4},{7,5},{8,10},{9,11},{10,... | collective-permute-start | bytes 393224 | tf_op jit(solution)/shard_map/ppermute | solution.py:61
  (584 shorter events, 444.6 us)
Async XLA Ops:
  7.2 136.4 %all-gather.5.cloned.1.call-start = ((), (), s32[]{:S(2)}) async-start(), calls=%async_computation.5 | async-start | bytes 11354112 | tf_op jit(solution)/shard_map/all_gather | solution.py:246
  10.8 175.9 %all-gather.7.cloned.1.call-start = ((), (), s32[]{:S(2)}) async-start(), calls=%async_computation.6 | async-start | bytes 2654208 | tf_op jit(solution)/shard_map/all_gather | solution.py:335
  23.0 120.6 %collective-permute-start = (bf16[800,2048]{1,0:T(8,128)(2,1)}, bf16[800,2048]{1,0:T(8,128)(2,1)}, u32[]{:S(2)}, u32[]{:S(2)}) collective-permute-start(bf16[800,2048]{1,0:T(8,128)(2,1)} %get-tuple-element.112), channel_id=1, source_target_pairs={{0,16},{8,24},{16,0},{24,8},{1,17},{9,25},{17,1},{25,9},{2,18},{10... | collective-permute-start | bytes 9830408 | tf_op jit(solution)/shard_map/ppermute | solution.py:61
  26.0 117.7 %collective-permute-start.1 = (bf16[800,2048]{1,0:T(8,128)(2,1)}, bf16[800,2048]{1,0:T(8,128)(2,1)}, u32[]{:S(2)}, u32[]{:S(2)}) collective-permute-start(bf16[800,2048]{1,0:T(8,128)(2,1)} %get-tuple-element.113), channel_id=1, source_target_pairs={{0,8},{8,0},{16,24},{24,16},{1,9},{9,1},{17,25},{25,17},{2,10},{10... | collective-permute-start | bytes 9830408 | tf_op jit(solution)/shard_map/ppermute | solution.py:61
  28.8 114.8 %collective-permute-start.2 = (bf16[288,2048]{1,0:T(8,128)(2,1)}, bf16[288,2048]{1,0:T(8,128)(2,1)}, u32[]{:S(2)}, u32[]{:S(2)}) collective-permute-start(bf16[288,2048]{1,0:T(8,128)(2,1)} %pad_maximum_fusion.19), channel_id=1, source_target_pairs={{0,2},{1,3},{2,0},{3,1},{4,6},{5,7},{6,4},{7,5},{8,10},{9,11},{10,... | collective-permute-start | bytes 3538952 | tf_op jit(solution)/shard_map/ppermute | solution.py:61
  30.3 113.3 %collective-permute-start.3 = (bf16[288,2048]{1,0:T(8,128)(2,1)}, bf16[288,2048]{1,0:T(8,128)(2,1)}, u32[]{:S(2)}, u32[]{:S(2)}) collective-permute-start(bf16[288,2048]{1,0:T(8,128)(2,1)} %pad_maximum_fusion.19), channel_id=1, source_target_pairs={{0,4},{1,5},{2,6},{3,7},{4,0},{5,1},{6,2},{7,3},{8,12},{9,13},{10,... | collective-permute-start | bytes 3538952 | tf_op jit(solution)/shard_map/ppermute | solution.py:61
  156.4 186.5 %all-gather.9.cloned.1.call-start = ((), (), s32[]{:S(2)}) async-start(), calls=%async_computation.7 | async-start | bytes 11894784 | tf_op jit(solution)/shard_map/all_gather | solution.py:337
  186.7 310.5 %all-gather.11.cloned.1.call-start = ((), (), s32[]{:S(2)}) async-start(), calls=%async_computation.8 | async-start | bytes 10616832 | tf_op jit(solution)/shard_map/all_gather | solution.py:390
  195.6 106.8 %collective-permute-start.4 = (bf16[800,2048]{1,0:T(8,128)(2,1)}, bf16[800,2048]{1,0:T(8,128)(2,1)}, u32[]{:S(2)}, u32[]{:S(2)}) collective-permute-start(bf16[800,2048]{1,0:T(8,128)(2,1)} %get-tuple-element.112), channel_id=1, source_target_pairs={{0,8},{8,0},{16,24},{24,16},{1,9},{9,1},{17,25},{25,17},{2,10},{10... | collective-permute-start | bytes 9830408 | tf_op jit(solution)/shard_map/ppermute | solution.py:61
  197.1 105.3 %collective-permute-start.5 = (bf16[800,2048]{1,0:T(8,128)(2,1)}, bf16[800,2048]{1,0:T(8,128)(2,1)}, u32[]{:S(2)}, u32[]{:S(2)}) collective-permute-start(bf16[800,2048]{1,0:T(8,128)(2,1)} %get-tuple-element.113), channel_id=1, source_target_pairs={{0,16},{8,24},{16,0},{24,8},{1,17},{9,25},{17,1},{25,9},{2,18},{10... | collective-permute-start | bytes 9830408 | tf_op jit(solution)/shard_map/ppermute | solution.py:61
  302.4 72.5 %collective-permute-start.6 = (bf16[800,2048]{1,0:T(8,128)(2,1)}, bf16[800,2048]{1,0:T(8,128)(2,1)}, u32[]{:S(2)}, u32[]{:S(2)}) collective-permute-start(bf16[800,2048]{1,0:T(8,128)(2,1)} %collective-permute-done), channel_id=1, source_target_pairs={{0,8},{8,0},{16,24},{24,16},{1,9},{9,1},{17,25},{25,17},{2,10},{10... | collective-permute-start | bytes 9830408 | tf_op jit(solution)/shard_map/ppermute | solution.py:61
  324.5 72.2 %collective-permute-start.7 = (bf16[800,2048]{1,0:T(8,128)(2,1)}, bf16[800,2048]{1,0:T(8,128)(2,1)}, u32[]{:S(2)}, u32[]{:S(2)}) collective-permute-start(bf16[800,2048]{1,0:T(8,128)(2,1)} %collective-permute-done.1), channel_id=1, source_target_pairs={{0,16},{8,24},{16,0},{24,8},{1,17},{9,25},{17,1},{25,9},{2,18},{10... | collective-permute-start | bytes 9830408 | tf_op jit(solution)/shard_map/ppermute | solution.py:61
  330.8 84.0 %collective-permute-start.11 = (bf16[288,2048]{1,0:T(8,128)(2,1)}, bf16[288,2048]{1,0:T(8,128)(2,1)}, u32[]{:S(2)}, u32[]{:S(2)}) collective-permute-start(bf16[288,2048]{1,0:T(8,128)(2,1)} %convert_element_type.410), channel_id=1, source_target_pairs={{0,1},{1,0},{2,3},{3,2},{4,5},{5,4},{6,7},{7,6},{8,9},{9,8},{10,11... | collective-permute-start | bytes 3538952 | tf_op jit(solution)/shard_map/ppermute | solution.py:61
  396.8 470.9 %reduce-scatter.8.cloned.1.call-start = ((), (), s32[]{:S(2)}) async-start(), calls=%async_computation.10 | async-start | bytes 5308416 | tf_op jit(solution)/shard_map/reduce_scatter | solution.py:445
  712.7 50.7 %collective-permute-start.18 = (bf16[288,2048]{1,0:T(8,128)(2,1)}, bf16[288,2048]{1,0:T(8,128)(2,1)}, u32[]{:S(2)}, u32[]{:S(2)}) collective-permute-start(bf16[288,2048]{1,0:T(8,128)(2,1)} %add_convert_fusion.5), channel_id=1, source_target_pairs={{0,8},{8,0},{16,24},{24,16},{1,9},{9,1},{17,25},{25,17},{2,10},{10... | collective-permute-start | bytes 3538952 | tf_op jit(solution)/shard_map/ppermute | solution.py:61
  714.1 49.3 %collective-permute-start.19 = (bf16[288,2048]{1,0:T(8,128)(2,1)}, bf16[288,2048]{1,0:T(8,128)(2,1)}, u32[]{:S(2)}, u32[]{:S(2)}) collective-permute-start(bf16[288,2048]{1,0:T(8,128)(2,1)} %add_convert_fusion.4), channel_id=1, source_target_pairs={{0,16},{8,24},{16,0},{24,8},{1,17},{9,25},{17,1},{25,9},{2,18},{10... | collective-permute-start | bytes 3538952 | tf_op jit(solution)/shard_map/ppermute | solution.py:61
  715.7 46.5 %collective-permute-start.20 = (bf16[256,2048]{1,0:T(8,128)(2,1)}, bf16[256,2048]{1,0:T(8,128)(2,1)}, u32[]{:S(2)}, u32[]{:S(2)}) collective-permute-start(bf16[256,2048]{1,0:T(8,128)(2,1)} %get-tuple-element.143), channel_id=1, source_target_pairs={{0,8},{8,0},{16,24},{24,16},{1,9},{9,1},{17,25},{25,17},{2,10},{10... | collective-permute-start | bytes 3145736 | tf_op jit(solution)/shard_map/ppermute | solution.py:61
  716.2 47.2 %collective-permute-start.21 = (bf16[256,2048]{1,0:T(8,128)(2,1)}, bf16[256,2048]{1,0:T(8,128)(2,1)}, u32[]{:S(2)}, u32[]{:S(2)}) collective-permute-start(bf16[256,2048]{1,0:T(8,128)(2,1)} %get-tuple-element.144), channel_id=1, source_target_pairs={{0,16},{8,24},{16,0},{24,8},{1,17},{9,25},{17,1},{25,9},{2,18},{10... | collective-permute-start | bytes 3145736 | tf_op jit(solution)/shard_map/ppermute | solution.py:61
  763.4 114.7 %reduce-scatter.6.cloned.1.call-start = ((), (), s32[]{:S(2)}) async-start(), calls=%async_computation.9 | async-start | bytes 5308416 | tf_op jit(solution)/shard_map/reduce_scatter | solution.py:445
  779.7 43.3 %collective-permute-start.24 = (bf16[256,2048]{1,0:T(8,128)(2,1)}, bf16[256,2048]{1,0:T(8,128)(2,1)S(1)}, u32[]{:S(2)}, u32[]{:S(2)}) collective-permute-start(bf16[256,2048]{1,0:T(8,128)(2,1)} %get-tuple-element.149), channel_id=1, source_target_pairs={{0,8},{8,0},{16,24},{24,16},{1,9},{9,1},{17,25},{25,17},{2,10},{10... | collective-permute-start | bytes 3145736 | tf_op jit(solution)/shard_map/ppermute | solution.py:61
  781.2 42.3 %collective-permute-start.25 = (bf16[256,2048]{1,0:T(8,128)(2,1)}, bf16[256,2048]{1,0:T(8,128)(2,1)}, u32[]{:S(2)}, u32[]{:S(2)}) collective-permute-start(bf16[256,2048]{1,0:T(8,128)(2,1)} %get-tuple-element.150), channel_id=1, source_target_pairs={{0,16},{8,24},{16,0},{24,8},{1,17},{9,25},{17,1},{25,9},{2,18},{10... | collective-permute-start | bytes 3145736 | tf_op jit(solution)/shard_map/ppermute | solution.py:61
  823.5 114.6 %reduce-scatter.10.cloned.1.call-start = ((), (), s32[]{:S(2)}) async-start(), calls=%async_computation.11 | async-start | bytes 1327104 | tf_op jit(solution)/shard_map/reduce_scatter | solution.py:445
  823.7 45.3 %collective-permute-start.26 = (bf16[256,2048]{1,0:T(8,128)(2,1)}, bf16[256,2048]{1,0:T(8,128)(2,1)}, u32[]{:S(2)}, u32[]{:S(2)}) collective-permute-start(bf16[256,2048]{1,0:T(8,128)(2,1)} %get-tuple-element.154), channel_id=1, source_target_pairs={{0,8},{8,0},{16,24},{24,16},{1,9},{9,1},{17,25},{25,17},{2,10},{10... | collective-permute-start | bytes 3145736 | tf_op jit(solution)/shard_map/ppermute | solution.py:61
  825.2 43.8 %collective-permute-start.27 = (bf16[256,2048]{1,0:T(8,128)(2,1)}, bf16[256,2048]{1,0:T(8,128)(2,1)}, u32[]{:S(2)}, u32[]{:S(2)}) collective-permute-start(bf16[256,2048]{1,0:T(8,128)(2,1)} %get-tuple-element.155), channel_id=1, source_target_pairs={{0,16},{8,24},{16,0},{24,8},{1,17},{9,25},{17,1},{25,9},{2,18},{10... | collective-permute-start | bytes 3145736 | tf_op jit(solution)/shard_map/ppermute | solution.py:61
  835.9 183.8 %reduce-scatter.12.cloned.1.call-start = ((), (), s32[]{:S(2)}) async-start(), calls=%async_computation.12 | async-start | bytes 2654208 | tf_op jit(solution)/shard_map/reduce_scatter | solution.py:445
  938.1 274.0 %reduce-scatter.14.cloned.1.call-start = ((), (), s32[]{:S(2)}) async-start(), calls=%async_computation.13 | async-start | bytes 10616832 | tf_op jit(solution)/shard_map/reduce_scatter | solution.py:445
  970.9 43.8 %collective-permute-start.34 = (bf16[2,1,4,128,512]{4,3,2,1,0:T(8,128)(2,1)}, bf16[2,1,4,128,512]{4,3,2,1,0:T(8,128)(2,1)}, u32[]{:S(2)}, u32[]{:S(2)}) collective-permute-start(bf16[2,1,4,128,512]{4,3,2,1,0:T(8,128)(2,1)} %constant_dynamic-slice_fusion.27), channel_id=1, source_target_pairs={{0,8},{8,0},{16,24},{24,16},{1,9},{9,1},{17,25},{25,17},{2,10},{10... | collective-permute-start | bytes 3145736 | tf_op jit(solution)/shard_map/ppermute | solution.py:61
  973.3 43.9 %collective-permute-start.33 = (bf16[1,2,4,128,512]{4,3,2,1,0:T(8,128)(2,1)}, bf16[1,2,4,128,512]{4,3,2,1,0:T(8,128)(2,1)}, u32[]{:S(2)}, u32[]{:S(2)}) collective-permute-start(bf16[1,2,4,128,512]{4,3,2,1,0:T(8,128)(2,1)} %constant_dynamic-slice_fusion.28), channel_id=1, source_target_pairs={{0,16},{8,24},{16,0},{24,8},{1,17},{9,25},{17,1},{25,9},{2,18},{10... | collective-permute-start | bytes 3145736 | tf_op jit(solution)/shard_map/ppermute | solution.py:61
  1091.1 45.8 %collective-permute-start.52 = (bf16[128,2304]{1,0:T(8,128)(2,1)S(1)}, bf16[128,2304]{1,0:T(8,128)(2,1)S(1)}, u32[]{:S(2)}, u32[]{:S(2)}) collective-permute-start(bf16[128,2304]{1,0:T(8,128)(2,1)S(1)} %get-tuple-element.257), channel_id=1, source_target_pairs={{0,2},{1,3},{2,0},{3,1},{4,6},{5,7},{6,4},{7,5},{8,10},{9,11},{10,... | collective-permute-start | bytes 1769480 | tf_op jit(solution)/shard_map/ppermute | solution.py:61
  1092.9 46.4 %collective-permute-start.53 = (bf16[128,2304]{1,0:T(8,128)(2,1)S(1)}, bf16[128,2304]{1,0:T(8,128)(2,1)S(1)}, u32[]{:S(2)}, u32[]{:S(2)}) collective-permute-start(bf16[128,2304]{1,0:T(8,128)(2,1)S(1)} %get-tuple-element.259), channel_id=1, source_target_pairs={{0,4},{1,5},{2,6},{3,7},{4,0},{5,1},{6,2},{7,3},{8,12},{9,13},{10,... | collective-permute-start | bytes 1769480 | tf_op jit(solution)/shard_map/ppermute | solution.py:61
  1094.4 61.1 %collective-permute-start.54 = (bf16[128,2304]{1,0:T(8,128)(2,1)S(1)}, bf16[128,2304]{1,0:T(8,128)(2,1)S(1)}, u32[]{:S(2)}, u32[]{:S(2)}) collective-permute-start(bf16[128,2304]{1,0:T(8,128)(2,1)S(1)} %get-tuple-element.258), channel_id=1, source_target_pairs={{0,6},{1,7},{2,4},{3,5},{4,2},{5,3},{6,0},{7,1},{8,14},{9,15},{10,... | collective-permute-start | bytes 1769480 | tf_op jit(solution)/shard_map/ppermute | solution.py:61
  1098.3 60.2 %collective-permute-start.46 = (bf16[1,2,4,128,512]{4,3,2,1,0:T(8,128)(2,1)S(1)}, bf16[1,2,4,128,512]{4,3,2,1,0:T(8,128)(2,1)S(1)}, u32[]{:S(2)}, u32[]{:S(2)}) collective-permute-start(bf16[1,2,4,128,512]{4,3,2,1,0:T(8,128)(2,1)S(1)} %constant_dynamic-slice_fusion.5), channel_id=1, source_target_pairs={{0,16},{8,24},{16,0},{24,8},{1,17},{9,25},{17,1},{25,9},{2,18},{10... | collective-permute-start | bytes 3145736 | tf_op jit(solution)/shard_map/ppermute | solution.py:61
  (159 other events, 2792.2 us)
Sparse Core Ops, SparseCore 0:
  11.6 131.9 all-gather.4
  156.6 30.0 all-gather.6
  190.1 123.3 all-gather.8
  396.9 89.1 all-gather.10
  763.5 53.7 reduce-scatter.7
  823.6 54.5 reduce-scatter.5
  881.0 31.4 reduce-scatter.9
  938.2 36.4 reduce-scatter.11
  1019.9 119.8 reduce-scatter.13

commit v7 on v6

--- a/solution.py
+++ b/solution.py
@@ -124,6 +124,14 @@
     upper = add_full(own[:half], free[0], last[1])
     lower = add_full(own[half:], last[0], free[1])
     return jnp.concatenate([upper, lower], axis=0)
+
+
+def row_scatter(values, order):
+    size = values.shape[0] // len(order)
+    natural = jnp.concatenate(
+        [lax.dynamic_slice_in_dim(values, place * size, size) for place in order], axis=0
+    )
+    return lax.psum_scatter(natural, "row", scatter_dimension=0, tiled=True)
 
 
 def row_sum(blocks, size):
@@ -335,6 +343,13 @@
     keyval_rows = lax.all_gather(keyval_own, "col", axis=0, tiled=True)
     keyval_rows, out_packed = tie(keyval_rows, out_packed)
     out_gathered = lax.all_gather(out_packed, ("row", "col"), axis=0, tiled=True)
+    if by_pairs:
+        keyval_rows, upper_y, lower_x, upper_x, lower_y, cot_mixed = tie(
+            keyval_rows, upper_y, lower_x, upper_x, lower_y, cot_mixed
+        )
+        far_upper = swap(upper_y, "row", 4, 1)
+        far_lower = swap(lower_x, "row", 4, 2)
+        cot_six = swap(cot_mixed, "col", 8, 6)
     key_rows = keyval_rows[:, :HD]
     value_rows = keyval_rows[:, HD:]
     row_index = start_row + jnp.arange(row_total, dtype=jnp.int32) // NH
@@ -347,13 +362,6 @@
     top_value = jnp.max(scores, axis=1)
     total_value = jnp.sum(jnp.exp(scores - top_value[:, None]), axis=1)
     log_norm = top_value + jnp.log(total_value)
-    if by_pairs:
-        log_norm, upper_y, lower_x, upper_x, lower_y, cot_mixed = tie(
-            log_norm, upper_y, lower_x, upper_x, lower_y, cot_mixed
-        )
-        far_upper = swap(upper_y, "row", 4, 1)
-        far_lower = swap(lower_x, "row", 4, 2)
-        cot_six = swap(cot_mixed, "col", 8, 6)
     probs = convert_half(jnp.exp(scores - log_norm[:, None]))
     mixed_rows = matrix_product(probs, value_rows)
     head_context = convert_half(mixed_rows.reshape(tok_dev, NH * HD))
@@ -428,10 +436,6 @@
 
     grad_down = convert_half(product(cot_rows, hidden_activated, contract_first))
     grad_down, gate_grad, up_grad = tie(grad_down, gate_grad, up_grad)
-    down_blocks = [
-        jnp.concatenate([one, two], axis=0)
-        for one, two in zip(blocks_of(grad_down[:width]), blocks_of(grad_down[width:]))
-    ]
     half_width = width // 2
 
     def normed_part(start, left_gate, left_up):
@@ -448,54 +452,60 @@
         return convert_half(product(hidden_activated, down_weight[start:stop], contract_last))
 
     if row_size == 4:
-        own_down, far, free, last = split_blocks(down_blocks)
-        far = send_pair(far)
+        down_total = row_scatter(
+            jnp.concatenate(
+                [
+                    jnp.concatenate([one, two], axis=0)
+                    for one, two in zip(blocks_of(grad_down[:width]), blocks_of(grad_down[width:]))
+                ],
+                axis=0,
+            ),
+            order,
+        )
+        rank_partial = down_product(width, width + rank_width)
+        first_part = jnp.concatenate([normed_part(0, gate_grad, up_grad), rank_partial], axis=1)
+        second_part = normed_part(half_width, gate_grad, up_grad)
+        down_total, first_part, second_part, gate_grad, up_grad, hidden_activated = tie(
+            down_total, first_part, second_part, gate_grad, up_grad, hidden_activated
+        )
+        first_sum = col_sum(first_part)
+        second_sum = col_sum(second_part)
+        first_sum, rank_sums = first_sum[:, :half_width], first_sum[:, half_width:]
         grad_gate = convert_half(product(ffn_in, gate_grad, contract_first))
-        *far, grad_gate, up_grad, free_x, free_y = tie(*far, grad_gate, up_grad, *free)
-        last = add_pair(last, far)
-        down_free = send_pair((free_x, free_y))
+        grad_gate, up_grad = tie(grad_gate, up_grad)
         own_gate, gate_far, gate_free, gate_last = split_blocks(blocks_of(grad_gate))
+        far = send_pair(gate_far)
         grad_up = convert_half(product(ffn_in, up_grad, contract_first))
-        *down_free, grad_up, gate_grad, last_x, last_y, far_x, far_y = tie(
-            *down_free, grad_up, gate_grad, *last, *gate_far
-        )
-        down_last = send_pair((last_x, last_y))
-        far = send_pair((far_x, far_y))
-        own_up, up_far, up_free, up_last = split_blocks(blocks_of(grad_up))
-        first_part = normed_part(0, gate_grad, up_grad)
-        *down_last, far_x, far_y, first_part, gate_grad, free_x, free_y, next_x, next_y = tie(
-            *down_last, *far, first_part, gate_grad, *gate_free, *up_far
-        )
-        first_sum = col_sum(first_part)
-        gate_last = add_pair(gate_last, (far_x, far_y))
+        *far, grad_up, hidden_activated, free_x, free_y = tie(
+            *far, grad_up, hidden_activated, *gate_free
+        )
+        up_total = row_scatter(grad_up, order)
+        gate_last = add_pair(gate_last, far)
         gate_free = send_pair((free_x, free_y))
-        up_far = send_pair((next_x, next_y))
-        second_part = normed_part(half_width, gate_grad, up_grad)
-        *gate_free, far_x, far_y, second_part, last_x, last_y, free_x, free_y, hidden_activated = tie(
-            *gate_free, *up_far, second_part, *gate_last, *up_free, hidden_activated
-        )
-        second_sum = col_sum(second_part)
-        up_last = add_pair(up_last, (far_x, far_y))
+        down_partial = down_product(0, width)
+        *gate_free, second_sum, down_partial, last_x, last_y = tie(
+            *gate_free, second_sum, down_partial, *gate_last
+        )
         gate_last = send_pair((last_x, last_y))
-        up_free = send_pair((free_x, free_y))
-        rank_partial = down_product(width, width + rank_width)
-        down_partial = down_product(0, width)
-        *gate_last, free_x, free_y, second_sum, down_partial, last_x, last_y = tie(
-            *gate_last, *up_free, second_sum, down_partial, *up_last
-        )
-        up_free = (free_x, free_y)
-        up_last = send_pair((last_x, last_y))
     else:
         down_partial = down_product(0, width)
         first_sum = col_sum(normed_part(0, gate_grad, up_grad))
         second_sum = col_sum(normed_part(half_width, gate_grad, up_grad))
-        rank_partial = down_product(width, width + rank_width)
+        rank_sums = col_sum(down_product(width, width + rank_width))
         grad_gate = convert_half(product(ffn_in, gate_grad, contract_first))
         grad_up = convert_half(product(ffn_in, up_grad, contract_first))
-        down_total = row_sum(down_blocks, row_size)
+        down_total = row_scatter(
+            jnp.concatenate(
+                [
+                    jnp.concatenate([one, two], axis=0)
+                    for one, two in zip(blocks_of(grad_down[:width]), blocks_of(grad_down[width:]))
+                ],
+                axis=0,
+            ),
+            order,
+        )
         gate_sum = row_sum(blocks_of(grad_gate), row_size)
-        up_sum = row_sum(blocks_of(grad_up), row_size)
-    rank_sums = col_sum(rank_partial)
+        up_total = row_scatter(grad_up, order)
     normed_grad = jnp.concatenate([first_sum, second_sum], axis=1)
 
     normed_grad = reorder(normed_grad, order).astype(jnp.float32)
@@ -508,7 +518,7 @@
     context_grad = product(out_grad, out_weight, contract_last)
     grad_rows = convert_half(context_grad).reshape(row_total, HD)
     if row_size == 4:
-        *up_last, grad_rows = tie(*up_last, grad_rows)
+        *gate_last, grad_rows = tie(*gate_last, grad_rows)
     delta = jnp.sum(grad_rows.astype(jnp.float32) * mixed_rows, axis=1)
     weight_grad = product(grad_rows, value_rows, contract_last)
     score_grad = convert_half(probs.astype(jnp.float32) * (weight_grad - delta[:, None]))
@@ -522,7 +532,7 @@
     key_acc = product(score_grad, query_rows, contract_first)
     value_acc = product(probs, grad_rows, contract_first)
     keyval_part = jnp.concatenate([convert_half(key_acc), convert_half(value_acc)], axis=1)
-    keyval_part, rank_sums = tie(keyval_part, rank_sums)
+    keyval_part, up_total = tie(keyval_part, up_total)
     keyval_sum = col_sum(keyval_part)
     core = lax.axis_index("col") % 2
     query_right = halves_with_partner(query_grad, col_size)
@@ -544,13 +554,10 @@
     out_parts = row_first(out_group, row_size, col_size)
     keyval_sum, down_partial, *parts = tie(keyval_sum, down_partial, *query_parts, *out_parts)
     query_parts, out_parts = parts[:2], parts[2:]
-    if row_size == 4:
-        down_total = finish_sum(own_down, down_free, down_last)
-        gate_sum = finish_sum(own_gate, gate_free, gate_last)
-        up_sum = finish_sum(own_up, up_free, up_last)
-    down_sum, rank_sum = down_total[:model_rows], down_total[model_rows:]
     query_lines = row_rest(query_parts, row_size)
     out_lines = row_rest(out_parts, row_size)
+    lines = jnp.concatenate([query_lines, out_lines], axis=2)
+    lines, keyval_sum = tie(lines, keyval_sum)
     down_rank_rows = reorder(rank_sums, order)
     summed = col_sum(down_partial)
     layer_out = convert_half(
@@ -587,8 +594,12 @@
         ],
         axis=2,
     )
-    lines = jnp.concatenate([query_lines, out_lines], axis=2)
-    lines, keyval_group = tie(lines, keyval_group)
+    if row_size == 4:
+        lines, *sums = tie(lines, own_gate, *gate_free, *gate_last)
+        gate_sum = finish_sum(sums[0], sums[1:3], sums[3:])
+    down_total = down_total.astype(jnp.float32)
+    down_sum, rank_sum = down_total[:model_rows], down_total[model_rows:]
+    up_sum = up_total.astype(jnp.float32)
     first, second = share_cores(line_stage(lines, col_size), col_size)
     keyval_first, keyval_second = share_cores(
         line_stage(row_rest(row_first(keyval_group, row_size, col_size, parts=1), row_size), col_size), col_size

time: 1230 us -> 1240 us (level)
  waiting for transfers between devices: 464 us -> 493 us
  starting transfers between devices: 70 us -> 51.3 us
    reduce_scatter x0 -> x2, waiting for transfers between devices: none -> 56 us  [row_scatter(): return lax.psum_scatter(natural, 'row', scatter_dimension=0, tiled=True)]
    ppermute x56 -> x44, waiting for transfers between devices: 324 us -> 283 us  [swap(): return lax.ppermute(values, axis, [(i, i ^ bit) for i in range(size)])]
    ppermute x56 -> x44, starting transfers between devices: 69 us -> 50.7 us  [swap(): return lax.ppermute(values, axis, [(i, i ^ bit) for i in range(size)])]
    reduce_scatter x5 -> x4, waiting for transfers between devices: 8.73 us -> 23.1 us  [col_sum(): return lax.psum_scatter(values, 'col', scatter_dimension=0, tiled=True)]
    concatenate x2 -> x4, other arithmetic: 1.22 us -> 15.4 us  [the longest x2 10.7 us: row_scatter(): jnp.concatenate([lax.dynamic_slice_in_dim(values, place * size, size) for...]
    unnamed x260 -> x245, local copies, waits for them, and re-layouts: 30.5 us -> 43.6 us
    convert_element_type x24 -> x21, other arithmetic: 75 us -> 66.7 us  [convert_half(): return values.astype(jnp.bfloat16)]
  transfers between devices with their start and end apart: 65 -> 54, of which waited for: 30 -> 23; matrix products, arithmetic and copies ran while one was open for 40% -> 41% of each run, Pallas kernels for 0% -> 0%
where the time goes in v7:
time: 1240 us; the launch traced here: 1230 us
  waiting for transfers between devices  493 us (40%)
  matrix products  350 us (28%)
  local copies, waits for them, and re-layouts  163 us (13%)
  other arithmetic  155 us (12%)
  starting transfers between devices  51.3 us (4%)
  between operations  16.2 us (1%)
    ppermute x44, waiting for transfers between devices, swap(): return lax.ppermute(values, axis, [(i, i ^ bit) for i in range(size)])  283 us
    dot_general x22, matrix products, product(): lax.dot_general(left_side, right_side, dims, preferred_element_type=jnp.f...  239 us
    dot_general x9, matrix products, matrix_product(): return jnp.dot(left_side, right_side, preferred_element_type=jnp.float32)  111 us
    all_gather x1, waiting for transfers between devices, per_device(): lax.all_gather(jnp.concatenate([convert_half(query_matrix), convert_half(...  106 us
    convert_element_type x21, other arithmetic, convert_half(): return values.astype(jnp.bfloat16)  66.7 us
    reduce_scatter x2, waiting for transfers between devices, row_scatter(): return lax.psum_scatter(natural, 'row', scatter_dimension=0, tiled=True)  56 us
    ppermute x44, starting transfers between devices, swap(): return lax.ppermute(values, axis, [(i, i ^ bit) for i in range(size)])  50.7 us
    unnamed x245, local copies, waits for them, and re-layouts  43.6 us
  transfers between devices with their start and end apart: 54, of which 23 were waited for; matrix products, arithmetic and copies ran while one was open for 41% of the time, Pallas kernels for 0%

profile of v7, /device:TPU:0, one launch (start us, length us, event | category | flops | bytes accessed | tf_op | source)
XLA Modules:
  0.0 1228.5 jit_solution(14566036292463068800)
XLA Ops:
  37.0 106.5 %all-gather.5.cloned.1.call-done = bf16[2048,2688]{1,0:T(8,128)(2,1)} async-done(((bf16[64,2688]{1,0:T(8,128)(2,1)}), bf16[2048,2688]{1,0:T(8,128)(2,1)}) %all-gather.5.cloned.1.call-update) | async-done | bytes 11010064 | tf_op jit(solution)/shard_map/all_gather | solution.py:254
  162.4 24.1 %all-gather.7.cloned.1.call-done = bf16[2304,512]{1,0:T(8,128)(2,1)} async-done(((bf16[288,512]{1,0:T(8,128)(2,1)}), bf16[2304,512]{1,0:T(8,128)(2,1)}) %all-gather.7.cloned.1.call-update) | async-done | bytes 2359312 | tf_op jit(solution)/shard_map/all_gather | solution.py:343
  202.6 88.1 %collective-permute-done.4 = bf16[800,2048]{1,0:T(8,128)(2,1)} collective-permute-done((bf16[800,2048]{1,0:T(8,128)(2,1)}, bf16[800,2048]{1,0:T(8,128)(2,1)}, u32[]{:S(2)}, u32[]{:S(2)}) %collective-permute-start.4) | collective-permute-done | bytes 3276832 | tf_op jit(solution)/shard_map/ppermute | solution.py:61
  296.4 8.6 fusion.161
  314.2 8.8 fusion.162
  363.9 32.8 %collective-permute-done.7 = bf16[800,2048]{1,0:T(8,128)(2,1)} collective-permute-done((bf16[800,2048]{1,0:T(8,128)(2,1)}, bf16[800,2048]{1,0:T(8,128)(2,1)}, u32[]{:S(2)}, u32[]{:S(2)}) %collective-permute-start.7) | collective-permute-done | bytes 3276832 | tf_op jit(solution)/shard_map/ppermute | solution.py:61
  467.1 29.8 %fusion.24 = f32[2304,2048]{1,0:T(8,128)} fusion(bf16[2304,2048]{1,0:T(8,128)(2,1)} %get-tuple-element.206, bf16[2304,256]{1,0:T(8,128)(2,1)S(1)} %copy.40, bf16[2304,2048]{1,0:T(8,128)(2,1)} %slice_dynamic-update-slice_fusion.4), kind=kOutput, calls=%fused_computation.44 | convolution fusion | flops 21764505600 | bytes 38928384 | tf_op jit(solution)/shard_map/dot_general | solution.py:28
  496.9 26.8 %fusion.165 = f32[2304,2048]{1,0:T(8,128)} fusion(bf16[2304,2048]{1,0:T(8,128)(2,1)} %all-gather.11.cloned.1.call-done, bf16[2048,2048]{1,0:T(8,128)(2,1)} %slice_dynamic-update-slice_fusion.11), kind=kOutput, calls=%fused_computation.392 | convolution fusion | flops 19327352832 | bytes 36700160 | tf_op jit(solution)/shard_map/dot_general | solution.py:28
  523.7 24.4 %fusion.164 = f32[2304,2048]{1,0:T(8,128)} fusion(bf16[2304,2048]{1,0:T(8,128)(2,1)S(1)} %copy-done.97, bf16[2048,2048]{1,0:T(8,128)(2,1)} %pad_maximum_fusion.2), kind=kOutput, calls=%fused_computation.391 | convolution fusion | flops 19327352832 | bytes 36700160 | tf_op jit(solution)/shard_map/dot_general | solution.py:28
  548.2 29.8 %multiply_convert_fusion.1 = (bf16[2304,2048]{1,0:T(8,128)(2,1)}, bf16[2304,2048]{1,0:T(8,128)(2,1)}, bf16[2304,2048]{1,0:T(8,128)(2,1)}) fusion(f32[2304,2048]{1,0:T(8,128)S(1)} %bitcast.89, f32[2304,2048]{1,0:T(8,128)} %fusion.164, f32[2304,2048]{1,0:T(8,128)} %fusion.165), kind=kLoop, calls=%fused_computation.15 | loop fusion | flops 122683392 | bytes 84934656 | tf_op jit(solution)/shard_map/convert_element_type | solution.py:20
  578.0 29.9 %convolution_convert_fusion.1 = bf16[2304,2048]{1,0:T(8,128)(2,1)} fusion(bf16[2304,2048]{1,0:T(8,128)(2,1)} %get-tuple-element.127, bf16[2304,256]{1,0:T(8,128)(2,1)} %copy-done.62, bf16[2304,2048]{1,0:T(8,128)(2,1)} %slice_dynamic-update-slice_fusion.4), kind=kOutput, calls=%fused_computation.19 | convolution fusion | flops 21769224192 | bytes 29491200 | tf_op jit(solution)/shard_map/dot_general | solution.py:24
  637.4 16.6 %fusion.29 = f32[2304,1024]{1,0:T(8,128)} fusion(bf16[2304,2048]{1,0:T(8,128)(2,1)} %get-tuple-element.119, bf16[2048,2048]{1,0:T(8,128)(2,1)} %pad_maximum_fusion.2), kind=kOutput, calls=%fused_computation.57 | convolution fusion | flops 9663676416 | bytes 23068672 | tf_op jit(solution)/shard_map/dot_general | solution.py:24
  654.1 14.1 %add_convert_fusion.1 = bf16[2304,1024]{1,0:T(8,128)(2,1)S(1)} fusion(f32[2304,1024]{1,0:T(8,128)} %fusion.29, bf16[2304,2048]{1,0:T(8,128)(2,1)S(1)} %bitcast.95, bf16[2048,2048]{1,0:T(8,128)(2,1)} %slice_dynamic-update-slice_fusion.11), kind=kOutput, calls=%fused_computation.23 | convolution fusion | flops 9668395008 | bytes 27787264 | tf_op jit(solution)/shard_map/dot_general | solution.py:24
  671.2 16.3 %fusion.26 = f32[2304,1024]{1,0:T(8,128)} fusion(bf16[2304,2048]{1,0:T(8,128)(2,1)} %get-tuple-element.119, bf16[2048,2048]{1,0:T(8,128)(2,1)} %pad_maximum_fusion.2), kind=kOutput, calls=%fused_computation.54 | convolution fusion | flops 9663676416 | bytes 23068672 | tf_op jit(solution)/shard_map/dot_general | solution.py:24
  687.6 14.7 %add_convert_fusion = bf16[2304,1024]{1,0:T(8,128)(2,1)} fusion(f32[2304,1024]{1,0:T(8,128)} %fusion.26, bf16[2304,2048]{1,0:T(8,128)(2,1)S(1)} %bitcast.97, bf16[2048,2048]{1,0:T(8,128)(2,1)} %slice_dynamic-update-slice_fusion.11), kind=kOutput, calls=%fused_computation.22 | convolution fusion | flops 9668395008 | bytes 27787264 | tf_op jit(solution)/shard_map/dot_general | solution.py:24
  702.2 19.2 %reduce-scatter.7.cloned.1.call-done = bf16[576,2048]{1,0:T(8,128)(2,1)} async-done(((bf16[2304,2048]{1,0:T(8,128)(2,1)}), bf16[576,2048]{1,0:T(8,128)(2,1)}) %reduce-scatter.7.cloned.1.call-update) | async-done | bytes 2359312 | tf_op jit(solution)/shard_map/reduce_scatter | solution.py:134
  722.3 25.3 %convolution_convert_fusion.4 = bf16[2048,2048]{1,0:T(8,128)(2,1)S(1)} fusion(bf16[2304,2048]{1,0:T(8,128)(2,1)} %all-gather.11.cloned.1.call-done, bf16[2304,2048]{1,0:T(8,128)(2,1)} %get-tuple-element.119), kind=kOutput, calls=%fused_computation.43 | convolution fusion | flops 19331547136 | bytes 27262976 | tf_op jit(solution)/shard_map/dot_general | solution.py:24
  753.6 25.0 %convolution_convert_fusion.3 = bf16[2048,2048]{1,0:T(8,128)(2,1)S(1)} fusion(bf16[2304,2048]{1,0:T(8,128)(2,1)} %all-gather.11.cloned.1.call-done, bf16[2304,2048]{1,0:T(8,128)(2,1)} %get-tuple-element.122), kind=kOutput, calls=%fused_computation.42 | convolution fusion | flops 19331547136 | bytes 27262976 | tf_op jit(solution)/shard_map/dot_general | solution.py:24
  788.0 27.6 %convolution_convert_fusion = bf16[2304,2048]{1,0:T(8,128)(2,1)} fusion(bf16[2304,2048]{1,0:T(8,128)(2,1)} %get-tuple-element.127, bf16[512,2048]{1,0:T(8,128)(2,1)} %get-tuple-element.199, bf16[512,2048]{1,0:T(8,128)(2,1)} %get-tuple-element.197, bf16[512,2048]{1,0:T(8,128)(2,1)} %get-tuple-element.195, bf16[512,2048]{1,0:T(8,128)(2,1)S(1)} %copy-done.18), kind=kOutput, calls=%fused_computation.18 | convolution fusion | flops 19365625856 | bytes 27262976 | tf_op jit(solution)/shard_map/dot_general | solution.py:24
  822.2 23.1 %reduce-scatter.11.cloned.1.call-done = bf16[288,1280]{1,0:T(8,128)(2,1)} async-done(((bf16[2304,1280]{1,0:T(8,128)(2,1)}), bf16[288,1280]{1,0:T(8,128)(2,1)}) %reduce-scatter.11.cloned.1.call-update) | async-done | bytes 737296 | tf_op jit(solution)/shard_map/reduce_scatter | solution.py:449
  853.3 7.7 fusion.35
  870.4 8.6 multiply_convert_fusion
  896.5 36.8 %reduce-scatter.13.cloned.1.call-done = bf16[512,2048]{1,0:T(8,128)(2,1)} async-done(((bf16[2048,2048]{1,0:T(8,128)(2,1)}), bf16[512,2048]{1,0:T(8,128)(2,1)}) %reduce-scatter.13.cloned.1.call-update) | async-done | bytes 2097168 | tf_op jit(solution)/shard_map/reduce_scatter | solution.py:134
  965.5 10.5 collective-permute-done.22
  981.9 21.2 %collective-permute-done.26 = bf16[2,1,4,128,640]{4,3,2,1,0:T(8,128)(2,1)} collective-permute-done((bf16[2,1,4,128,640]{4,3,2,1,0:T(8,128)(2,1)}, bf16[2,1,4,128,640]{4,3,2,1,0:T(8,128)(2,1)}, u32[]{:S(2)}, u32[]{:S(2)}) %collective-permute-start.26) | collective-permute-done | bytes 1310752 | tf_op jit(solution)/shard_map/ppermute | solution.py:61
  1033.6 10.1 collective-permute-done.29
  1070.6 33.1 %collective-permute-done.40 = bf16[128,2304]{1,0:T(8,128)(2,1)} collective-permute-done((bf16[128,2304]{1,0:T(8,128)(2,1)}, bf16[128,2304]{1,0:T(8,128)(2,1)}, u32[]{:S(2)}, u32[]{:S(2)}) %collective-permute-start.40) | collective-permute-done | bytes 589856 | tf_op jit(solution)/shard_map/ppermute | solution.py:61
  1110.1 28.7 %collective-permute-done.42 = bf16[128,2304]{1,0:T(8,128)(2,1)} collective-permute-done((bf16[128,2304]{1,0:T(8,128)(2,1)}, bf16[128,2304]{1,0:T(8,128)(2,1)}, u32[]{:S(2)}, u32[]{:S(2)}) %collective-permute-start.42) | collective-permute-done | bytes 589856 | tf_op jit(solution)/shard_map/ppermute | solution.py:61
  1145.1 23.8 %collective-permute-done.34 = bf16[1,2,4,128,512]{4,3,2,1,0:T(8,128)(2,1)S(1)} collective-permute-done((bf16[1,2,4,128,512]{4,3,2,1,0:T(8,128)(2,1)S(1)}, bf16[1,2,4,128,512]{4,3,2,1,0:T(8,128)(2,1)S(1)}, u32[]{:S(2)}, u32[]{:S(2)}) %collective-permute-start.34) | collective-permute-done | bytes 1048608 | tf_op jit(solution)/shard_map/ppermute | solution.py:61
  1174.3 9.5 collective-permute-done.35
  1185.0 10.2 collective-permute-start.36
  1199.1 7.7 collective-permute-done.37
  (547 shorter events, 413.1 us)
Async XLA Ops:
  7.2 136.3 %all-gather.5.cloned.1.call-start = ((), (), s32[]{:S(2)}) async-start(), calls=%async_computation.6 | async-start | bytes 11354112 | tf_op jit(solution)/shard_map/all_gather | solution.py:254
  10.8 175.7 %all-gather.7.cloned.1.call-start = ((), (), s32[]{:S(2)}) async-start(), calls=%async_computation.7 | async-start | bytes 2654208 | tf_op jit(solution)/shard_map/all_gather | solution.py:343
  22.8 120.7 %collective-permute-start = (bf16[800,2048]{1,0:T(8,128)(2,1)}, bf16[800,2048]{1,0:T(8,128)(2,1)}, u32[]{:S(2)}, u32[]{:S(2)}) collective-permute-start(bf16[800,2048]{1,0:T(8,128)(2,1)} %get-tuple-element.96), channel_id=1, source_target_pairs={{0,16},{8,24},{16,0},{24,8},{1,17},{9,25},{17,1},{25,9},{2,18},{10... | collective-permute-start | bytes 9830408 | tf_op jit(solution)/shard_map/ppermute | solution.py:61
  25.8 117.6 %collective-permute-start.1 = (bf16[800,2048]{1,0:T(8,128)(2,1)}, bf16[800,2048]{1,0:T(8,128)(2,1)}, u32[]{:S(2)}, u32[]{:S(2)}) collective-permute-start(bf16[800,2048]{1,0:T(8,128)(2,1)} %get-tuple-element.97), channel_id=1, source_target_pairs={{0,8},{8,0},{16,24},{24,16},{1,9},{9,1},{17,25},{25,17},{2,10},{10... | collective-permute-start | bytes 9830408 | tf_op jit(solution)/shard_map/ppermute | solution.py:61
  28.6 114.8 %collective-permute-start.2 = (bf16[288,2048]{1,0:T(8,128)(2,1)}, bf16[288,2048]{1,0:T(8,128)(2,1)}, u32[]{:S(2)}, u32[]{:S(2)}) collective-permute-start(bf16[288,2048]{1,0:T(8,128)(2,1)} %pad_maximum_fusion.17), channel_id=1, source_target_pairs={{0,2},{1,3},{2,0},{3,1},{4,6},{5,7},{6,4},{7,5},{8,10},{9,11},{10,... | collective-permute-start | bytes 3538952 | tf_op jit(solution)/shard_map/ppermute | solution.py:61
  30.2 113.3 %collective-permute-start.3 = (bf16[288,2048]{1,0:T(8,128)(2,1)}, bf16[288,2048]{1,0:T(8,128)(2,1)}, u32[]{:S(2)}, u32[]{:S(2)}) collective-permute-start(bf16[288,2048]{1,0:T(8,128)(2,1)} %pad_maximum_fusion.17), channel_id=1, source_target_pairs={{0,4},{1,5},{2,6},{3,7},{4,0},{5,1},{6,2},{7,3},{8,12},{9,13},{10,... | collective-permute-start | bytes 3538952 | tf_op jit(solution)/shard_map/ppermute | solution.py:61
  156.3 186.1 %all-gather.9.cloned.1.call-start = ((), (), s32[]{:S(2)}) async-start(), calls=%async_computation.8 | async-start | bytes 11894784 | tf_op jit(solution)/shard_map/all_gather | solution.py:345
  186.6 310.3 %all-gather.11.cloned.1.call-start = ((), (), s32[]{:S(2)}) async-start(), calls=%async_computation.9 | async-start | bytes 10616832 | tf_op jit(solution)/shard_map/all_gather | solution.py:398
  186.8 103.9 %collective-permute-start.4 = (bf16[800,2048]{1,0:T(8,128)(2,1)}, bf16[800,2048]{1,0:T(8,128)(2,1)}, u32[]{:S(2)}, u32[]{:S(2)}) collective-permute-start(bf16[800,2048]{1,0:T(8,128)(2,1)} %get-tuple-element.96), channel_id=1, source_target_pairs={{0,8},{8,0},{16,24},{24,16},{1,9},{9,1},{17,25},{25,17},{2,10},{10... | collective-permute-start | bytes 9830408 | tf_op jit(solution)/shard_map/ppermute | solution.py:61
  188.3 102.3 %collective-permute-start.5 = (bf16[800,2048]{1,0:T(8,128)(2,1)}, bf16[800,2048]{1,0:T(8,128)(2,1)}, u32[]{:S(2)}, u32[]{:S(2)}) collective-permute-start(bf16[800,2048]{1,0:T(8,128)(2,1)} %get-tuple-element.97), channel_id=1, source_target_pairs={{0,16},{8,24},{16,0},{24,8},{1,17},{9,25},{17,1},{25,9},{2,18},{10... | collective-permute-start | bytes 9830408 | tf_op jit(solution)/shard_map/ppermute | solution.py:61
  290.7 73.2 %collective-permute-start.6 = (bf16[800,2048]{1,0:T(8,128)(2,1)}, bf16[800,2048]{1,0:T(8,128)(2,1)}, u32[]{:S(2)}, u32[]{:S(2)}) collective-permute-start(bf16[800,2048]{1,0:T(8,128)(2,1)} %collective-permute-done), channel_id=1, source_target_pairs={{0,8},{8,0},{16,24},{24,16},{1,9},{9,1},{17,25},{25,17},{2,10},{10... | collective-permute-start | bytes 9830408 | tf_op jit(solution)/shard_map/ppermute | solution.py:61
  325.9 70.7 %collective-permute-start.7 = (bf16[800,2048]{1,0:T(8,128)(2,1)}, bf16[800,2048]{1,0:T(8,128)(2,1)}, u32[]{:S(2)}, u32[]{:S(2)}) collective-permute-start(bf16[800,2048]{1,0:T(8,128)(2,1)} %collective-permute-done.1), channel_id=1, source_target_pairs={{0,16},{8,24},{16,0},{24,8},{1,17},{9,25},{17,1},{25,9},{2,18},{10... | collective-permute-start | bytes 9830408 | tf_op jit(solution)/shard_map/ppermute | solution.py:61
  327.1 31.0 %collective-permute-start.8 = (bf16[288,2048]{1,0:T(8,128)(2,1)}, bf16[288,2048]{1,0:T(8,128)(2,1)S(1)}, u32[]{:S(2)}, u32[]{:S(2)}) collective-permute-start(bf16[288,2048]{1,0:T(8,128)(2,1)} %pad_maximum_fusion.17), channel_id=1, source_target_pairs={{0,6},{1,7},{2,4},{3,5},{4,2},{5,3},{6,0},{7,1},{8,14},{9,15},{10,... | collective-permute-start | bytes 3538952 | tf_op jit(solution)/shard_map/ppermute | solution.py:61
  330.3 84.3 %collective-permute-start.11 = (bf16[288,2048]{1,0:T(8,128)(2,1)}, bf16[288,2048]{1,0:T(8,128)(2,1)}, u32[]{:S(2)}, u32[]{:S(2)}) collective-permute-start(bf16[288,2048]{1,0:T(8,128)(2,1)} %convert_element_type.344), channel_id=1, source_target_pairs={{0,1},{1,0},{2,3},{3,2},{4,5},{5,4},{6,7},{7,6},{8,9},{9,8},{10,11... | collective-permute-start | bytes 3538952 | tf_op jit(solution)/shard_map/ppermute | solution.py:61
  396.7 324.8 %reduce-scatter.7.cloned.1.call-start = ((), (), s32[]{:S(2)}) async-start(), calls=%async_computation.10 | async-start | bytes 11796480 | tf_op jit(solution)/shard_map/reduce_scatter | solution.py:134
  423.1 27.3 %collective-permute-start.9 = (bf16[1152,2048]{1,0:T(8,128)(2,1)}, bf16[1152,2048]{1,0:T(8,128)(2,1)}, u32[]{:S(2)}, u32[]{:S(2)}) collective-permute-start(bf16[1152,2048]{1,0:T(8,128)(2,1)} %pad_maximum_fusion.7), channel_id=1, source_target_pairs={{0,1},{1,0},{2,3},{3,2},{4,5},{5,4},{6,7},{7,6},{8,9},{9,8},{10,11... | collective-permute-start | bytes 14155784 | tf_op jit(solution)/shard_map/ppermute | solution.py:61
  629.0 191.1 %reduce-scatter.9.cloned.1.call-start = ((), (), s32[]{:S(2)}) async-start(), calls=%async_computation.11 | async-start | bytes 5308416 | tf_op jit(solution)/shard_map/reduce_scatter | solution.py:449
  721.5 123.9 %reduce-scatter.11.cloned.1.call-start = ((), (), s32[]{:S(2)}) async-start(), calls=%async_computation.12 | async-start | bytes 6635520 | tf_op jit(solution)/shard_map/reduce_scatter | solution.py:449
  722.2 211.0 %reduce-scatter.13.cloned.1.call-start = ((), (), s32[]{:S(2)}) async-start(), calls=%async_computation.13 | async-start | bytes 10485760 | tf_op jit(solution)/shard_map/reduce_scatter | solution.py:134
  785.8 222.7 %reduce-scatter.15.cloned.1.call-start = ((), (), s32[]{:S(2)}) async-start(), calls=%async_computation.14 | async-start | bytes 2654208 | tf_op jit(solution)/shard_map/reduce_scatter | solution.py:449
  785.9 34.1 %collective-permute-start.16 = (bf16[256,2048]{1,0:T(8,128)(2,1)}, bf16[256,2048]{1,0:T(8,128)(2,1)S(1)}, u32[]{:S(2)}, u32[]{:S(2)}) collective-permute-start(bf16[256,2048]{1,0:T(8,128)(2,1)} %get-tuple-element.124), channel_id=1, source_target_pairs={{0,8},{8,0},{16,24},{24,16},{1,9},{9,1},{17,25},{25,17},{2,10},{10... | collective-permute-start | bytes 3145736 | tf_op jit(solution)/shard_map/ppermute | solution.py:61
  787.4 32.6 %collective-permute-start.17 = (bf16[256,2048]{1,0:T(8,128)(2,1)}, bf16[256,2048]{1,0:T(8,128)(2,1)}, u32[]{:S(2)}, u32[]{:S(2)}) collective-permute-start(bf16[256,2048]{1,0:T(8,128)(2,1)} %get-tuple-element.125), channel_id=1, source_target_pairs={{0,16},{8,24},{16,0},{24,8},{1,17},{9,25},{17,1},{25,9},{2,18},{10... | collective-permute-start | bytes 3145736 | tf_op jit(solution)/shard_map/ppermute | solution.py:61
  820.1 44.2 %collective-permute-start.18 = (bf16[256,2048]{1,0:T(8,128)(2,1)}, bf16[256,2048]{1,0:T(8,128)(2,1)}, u32[]{:S(2)}, u32[]{:S(2)}) collective-permute-start(bf16[256,2048]{1,0:T(8,128)(2,1)} %get-tuple-element.130), channel_id=1, source_target_pairs={{0,8},{8,0},{16,24},{24,16},{1,9},{9,1},{17,25},{25,17},{2,10},{10... | collective-permute-start | bytes 3145736 | tf_op jit(solution)/shard_map/ppermute | solution.py:61
  821.6 42.6 %collective-permute-start.19 = (bf16[256,2048]{1,0:T(8,128)(2,1)}, bf16[256,2048]{1,0:T(8,128)(2,1)}, u32[]{:S(2)}, u32[]{:S(2)}) collective-permute-start(bf16[256,2048]{1,0:T(8,128)(2,1)} %get-tuple-element.131), channel_id=1, source_target_pairs={{0,16},{8,24},{16,0},{24,8},{1,17},{9,25},{17,1},{25,9},{2,18},{10... | collective-permute-start | bytes 3145736 | tf_op jit(solution)/shard_map/ppermute | solution.py:61
  851.6 86.1 %collective-permute-start.23 = (bf16[288,1024]{1,0:T(8,128)(2,1)}, bf16[288,1024]{1,0:T(8,128)(2,1)}, u32[]{:S(2)}, u32[]{:S(2)}) collective-permute-start(bf16[288,1024]{1,0:T(8,128)(2,1)} %get-tuple-element.227), channel_id=1, source_target_pairs={{0,1},{1,0},{2,3},{3,2},{4,5},{5,4},{6,7},{7,6},{8,9},{9,8},{10,11... | collective-permute-start | bytes 1769480 | tf_op jit(solution)/shard_map/ppermute | solution.py:61
  933.2 285.4 %reduce-scatter.17.cloned.1.call-start = ((), (), s32[]{:S(2)}) async-start(), calls=%async_computation.15 | async-start | bytes 10616832 | tf_op jit(solution)/shard_map/reduce_scatter | solution.py:449
  960.0 43.1 %collective-permute-start.26 = (bf16[2,1,4,128,640]{4,3,2,1,0:T(8,128)(2,1)}, bf16[2,1,4,128,640]{4,3,2,1,0:T(8,128)(2,1)}, u32[]{:S(2)}, u32[]{:S(2)}) collective-permute-start(bf16[2,1,4,128,640]{4,3,2,1,0:T(8,128)(2,1)} %fusion.67), channel_id=1, source_target_pairs={{0,8},{8,0},{16,24},{24,16},{1,9},{9,1},{17,25},{25,17},{2,10},{10... | collective-permute-start | bytes 3932168 | tf_op jit(solution)/shard_map/ppermute | solution.py:61
  964.3 41.5 %collective-permute-start.25 = (bf16[1,2,4,128,640]{4,3,2,1,0:T(8,128)(2,1)}, bf16[1,2,4,128,640]{4,3,2,1,0:T(8,128)(2,1)}, u32[]{:S(2)}, u32[]{:S(2)}) collective-permute-start(bf16[1,2,4,128,640]{4,3,2,1,0:T(8,128)(2,1)} %constant_dynamic-slice_fusion.20), channel_id=1, source_target_pairs={{0,16},{8,24},{16,0},{24,8},{1,17},{9,25},{17,1},{25,9},{2,18},{10... | collective-permute-start | bytes 3932168 | tf_op jit(solution)/shard_map/ppermute | solution.py:61
  1047.6 93.2 %collective-permute-start.31 = (bf16[288,256]{1,0:T(8,128)(2,1)}, bf16[288,256]{1,0:T(8,128)(2,1)}, u32[]{:S(2)}, u32[]{:S(2)}) collective-permute-start(bf16[288,256]{1,0:T(8,128)(2,1)} %get-tuple-element.268), channel_id=1, source_target_pairs={{0,1},{1,0},{2,3},{3,2},{4,5},{5,4},{6,7},{7,6},{8,9},{9,8},{10,11... | collective-permute-start | bytes 442376 | tf_op jit(solution)/shard_map/ppermute | solution.py:61
  1057.3 46.4 %collective-permute-start.40 = (bf16[128,2304]{1,0:T(8,128)(2,1)}, bf16[128,2304]{1,0:T(8,128)(2,1)}, u32[]{:S(2)}, u32[]{:S(2)}) collective-permute-start(bf16[128,2304]{1,0:T(8,128)(2,1)} %get-tuple-element.213), channel_id=1, source_target_pairs={{0,2},{1,3},{2,0},{3,1},{4,6},{5,7},{6,4},{7,5},{8,10},{9,11},{10,... | collective-permute-start | bytes 1769480 | tf_op jit(solution)/shard_map/ppermute | solution.py:61
  1058.7 51.3 %collective-permute-start.41 = (bf16[128,2304]{1,0:T(8,128)(2,1)}, bf16[128,2304]{1,0:T(8,128)(2,1)}, u32[]{:S(2)}, u32[]{:S(2)}) collective-permute-start(bf16[128,2304]{1,0:T(8,128)(2,1)} %get-tuple-element.215), channel_id=1, source_target_pairs={{0,4},{1,5},{2,6},{3,7},{4,0},{5,1},{6,2},{7,3},{8,12},{9,13},{10,... | collective-permute-start | bytes 1769480 | tf_op jit(solution)/shard_map/ppermute | solution.py:61
  1061.2 77.6 %collective-permute-start.42 = (bf16[128,2304]{1,0:T(8,128)(2,1)}, bf16[128,2304]{1,0:T(8,128)(2,1)}, u32[]{:S(2)}, u32[]{:S(2)}) collective-permute-start(bf16[128,2304]{1,0:T(8,128)(2,1)} %get-tuple-element.214), channel_id=1, source_target_pairs={{0,6},{1,7},{2,4},{3,5},{4,2},{5,3},{6,0},{7,1},{8,14},{9,15},{10,... | collective-permute-start | bytes 1769480 | tf_op jit(solution)/shard_map/ppermute | solution.py:61
  (140 other events, 2157.5 us)
Sparse Core Ops, SparseCore 0:
  11.6 131.8 all-gather.4
  156.4 30.0 all-gather.6
  190.0 120.2 all-gather.8
  396.8 88.1 all-gather.10
  629.1 92.2 reduce-scatter.6
  723.6 54.8 reduce-scatter.8
  780.8 64.4 reduce-scatter.10
  848.4 84.7 reduce-scatter.12
  936.1 37.0 reduce-scatter.14
  1008.7 137.4 reduce-scatter.16

commit v8 on v4

--- a/solution.py
+++ b/solution.py
@@ -148,7 +148,7 @@
     return add_half(kept, swap(sent, axis, size, bit))
 
 
-def scatter_chips(values, row_size, col_size, parts=2):
+def row_stages(values, row_size, col_size, parts=2):
     chips, rows, width = values.shape
     line = col_size // 2
     bits = [1 << k for k in reversed(range(row_size.bit_length() - 1))]
@@ -160,7 +160,11 @@
         for bit in bits if place % 2 == 0 else bits[::-1]:
             piece = halve(piece, bits.index(bit), "row", row_size, bit)
         pieces.append(piece.reshape(line, rows, part))
-    whole = jnp.concatenate(pieces, axis=-1)
+    return jnp.concatenate(pieces, axis=-1)
+
+
+def line_stage(whole, col_size):
+    line = col_size // 2
     at = lax.axis_index("col") // 2
     total = lax.dynamic_index_in_dim(whole, at, 0, keepdims=False).astype(jnp.float32)
     for step in range(1, line):
@@ -433,7 +437,6 @@
         for one, two in zip(blocks_of(grad_down[:width]), blocks_of(grad_down[width:]))
     ]
     half_width = width // 2
-    down_split = half_width + rank_width
 
     def normed_part(start, left_gate, left_up):
         stop = start + half_width
@@ -445,9 +448,8 @@
     def col_sum(values):
         return lax.psum_scatter(values, "col", scatter_dimension=0, tiled=True)
 
-    def down_product():
-        weight = jnp.concatenate([down_weight[half_width:], down_weight[:half_width]], axis=0)
-        return convert_half(product(hidden_activated, weight, contract_last))
+    def down_product(start, stop):
+        return convert_half(product(hidden_activated, down_weight[start:stop], contract_last))
 
     if row_size == 4:
         own_down, far, free, last = split_blocks(down_blocks)
@@ -458,43 +460,35 @@
         )
         first_sum = col_sum(first_part)
         last = add_pair(last, far)
-        free = send_pair((free_x, free_y))
+        down_free = send_pair((free_x, free_y))
+        down_last = send_pair(last)
         second_part = normed_part(half_width, gate_grad, up_grad)
-        *free, second_part, gate_grad, up_grad, last_x, last_y = tie(
-            *free, second_part, gate_grad, up_grad, *last
+        rank_partial = down_product(width, width + rank_width)
+        *down_free, second_part, gate_grad, up_grad, rank_partial, hidden_activated = tie(
+            *down_free, second_part, gate_grad, up_grad, rank_partial, hidden_activated
         )
         second_sum = col_sum(second_part)
-        last = send_pair((last_x, last_y))
         grad_gate = convert_half(product(ffn_in, gate_grad, contract_first))
-        *down_parts, grad_gate, up_grad = tie(own_down, *free, *last, grad_gate, up_grad)
-        down_total = finish_sum(down_parts[0], down_parts[1:3], down_parts[3:])
-        own_gate, far, free, last = split_blocks(blocks_of(grad_gate))
+        *down_last, grad_gate, up_grad = tie(*down_last, grad_gate, up_grad)
+        own_gate, far, free, gate_last = split_blocks(blocks_of(grad_gate))
         far = send_pair(far)
+        gate_free = send_pair(free)
         grad_up = convert_half(product(ffn_in, up_grad, contract_first))
-        *far, grad_up, hidden_activated, free_x, free_y = tie(
-            *far, grad_up, hidden_activated, *free
-        )
-        gate_last = add_pair(last, far)
-        gate_free = send_pair((free_x, free_y))
-        down_partial = down_product()
-        *gate_free, last_x, last_y, down_partial, grad_up = tie(
-            *gate_free, *gate_last, down_partial, grad_up
-        )
-        own_up, far, up_free, up_last = split_blocks(blocks_of(grad_up))
-        gate_last = send_pair((last_x, last_y))
-        up_far = send_pair(far)
+        *far, grad_up = tie(*far, grad_up)
+        gate_last = add_pair(gate_last, far)
+        own_up, up_far, up_free, up_last = split_blocks(blocks_of(grad_up))
+        gate_last = send_pair(gate_last)
+        up_far = send_pair(up_far)
     else:
         first_sum = col_sum(normed_part(0, gate_grad, up_grad))
         second_sum = col_sum(normed_part(half_width, gate_grad, up_grad))
+        rank_partial = down_product(width, width + rank_width)
         grad_gate = convert_half(product(ffn_in, gate_grad, contract_first))
         grad_up = convert_half(product(ffn_in, up_grad, contract_first))
-        down_partial = down_product()
         down_total = row_sum(down_blocks, row_size)
         gate_sum = row_sum(blocks_of(grad_gate), row_size)
         up_sum = row_sum(blocks_of(grad_up), row_size)
-    down_sum, rank_sum = down_total[:model_rows], down_total[model_rows:]
-    summed = col_sum(down_partial[:, :down_split])
-    down_rest = down_partial[:, down_split:]
+    rank_sums = col_sum(rank_partial)
     normed_grad = jnp.concatenate([first_sum, second_sum], axis=1)
 
     normed_grad = reorder(normed_grad, order).astype(jnp.float32)
@@ -506,16 +500,16 @@
     out_grad = jnp.concatenate([attn_grad, rank_out_grad], axis=1)
     context_grad = product(out_grad, out_weight, contract_last)
     grad_rows = convert_half(context_grad).reshape(row_total, HD)
+    if row_size == 4:
+        *sums, far_x, far_y, grad_rows, free_x, free_y = tie(
+            *gate_free, *gate_last, *up_far, grad_rows, *up_free
+        )
+        gate_free, gate_last = sums[:2], sums[2:]
+        up_last = send_pair(add_pair(up_last, (far_x, far_y)))
+        up_free = send_pair((free_x, free_y))
     delta = jnp.sum(grad_rows.astype(jnp.float32) * mixed_rows, axis=1)
     weight_grad = product(grad_rows, value_rows, contract_last)
     score_grad = convert_half(probs.astype(jnp.float32) * (weight_grad - delta[:, None]))
-    if row_size == 4:
-        *gate_last, far_x, far_y, score_grad, free_x, free_y = tie(
-            *gate_last, *up_far, score_grad, *up_free
-        )
-        gate_sum = finish_sum(own_gate, gate_free, gate_last)
-        up_last = add_pair(up_last, (far_x, far_y))
-        up_free = send_pair((free_x, free_y))
     query_acc = matrix_product(score_grad, key_rows)
     query_grad = convert_half(
         unrotate(
@@ -526,12 +520,7 @@
     key_acc = product(score_grad, query_rows, contract_first)
     value_acc = product(probs, grad_rows, contract_first)
     keyval_part = jnp.concatenate([convert_half(key_acc), convert_half(value_acc)], axis=1)
-    if row_size == 4:
-        *up_free, keyval_part, query_grad, last_x, last_y = tie(
-            *up_free, keyval_part, query_grad, *up_last
-        )
-        up_last = send_pair((last_x, last_y))
-    keyval_part, summed = tie(keyval_part, summed)
+    keyval_part, rank_sums = tie(keyval_part, rank_sums)
     keyval_sum = col_sum(keyval_part)
     core = lax.axis_index("col") % 2
     query_right = halves_with_partner(query_grad, col_size)
@@ -549,16 +538,21 @@
     grad_out_upper = product(rank_both, out_right, contract_first)
     out_group = jnp.concatenate([shared(grad_out), shared(grad_out_upper)], axis=2)
     query_group = shared(grad_query)
+    down_partial = down_product(0, width)
     if row_size == 4:
-        *up_last, out_group, query_group = tie(*up_last, out_group, query_group)
-        up_sum = finish_sum(own_up, up_free, up_last)
-    down_rank_rows = reorder(summed[:, half_width:], order)
-    keyval_sum, down_rest = tie(keyval_sum, down_rest)
-    down_rest = col_sum(down_rest)
-    down_all = jnp.concatenate([down_rest, summed[:, :half_width]], axis=1)
+        *sums, keyval_sum, down_partial, out_group, query_group = tie(
+            *up_free, *up_last, keyval_sum, down_partial, out_group, query_group
+        )
+        up_free, up_last = sums[:2], sums[2:]
+    else:
+        keyval_sum, down_partial = tie(keyval_sum, down_partial)
+    query_lines = row_stages(query_group, row_size, col_size)
+    out_lines = row_stages(out_group, row_size, col_size)
+    down_rank_rows = reorder(rank_sums, order)
+    summed = col_sum(down_partial)
     layer_out = convert_half(
         layer_state
-        + reorder(down_all, order).astype(jnp.float32)
+        + reorder(summed, order).astype(jnp.float32)
         + matrix_product(down_rank_rows, down_upper)
     )
     keyval_sum = keyval_sum.astype(jnp.float32)
@@ -582,28 +576,29 @@
     gain = lax.dynamic_index_in_dim(gains, core, 0, keepdims=False) + swap(
         lax.dynamic_index_in_dim(gains, 1 - core, 0, keepdims=False), "col", col_size, 1
     )
-    out_first, out_second = share_cores(
-        scatter_chips(out_group, row_size, col_size), col_size
-    )
-    query_first, query_second = share_cores(
-        scatter_chips(query_group, row_size, col_size), col_size
-    )
+    keyval_group = jnp.concatenate(
+        [
+            shared(grad_keyval),
+            shared(grad_down_upper),
+            jnp.pad(shared(gain), ((0, 0), (0, 0), (0, 127))),
+        ],
+        axis=2,
+    )
+    lines = jnp.concatenate([query_lines, out_lines], axis=2)
+    lines, keyval_group = tie(lines, keyval_group)
+    if row_size == 4:
+        lines, own_down, own_gate, own_up = tie(lines, own_down, own_gate, own_up)
+        down_total = finish_sum(own_down, down_free, down_last)
+        gate_sum = finish_sum(own_gate, gate_free, gate_last)
+        up_sum = finish_sum(own_up, up_free, up_last)
+    down_sum, rank_sum = down_total[:model_rows], down_total[model_rows:]
+    first, second = share_cores(line_stage(lines, col_size), col_size)
     keyval_first, keyval_second = share_cores(
-        scatter_chips(
-            jnp.concatenate(
-                [
-                    shared(grad_keyval),
-                    shared(grad_down_upper),
-                    jnp.pad(shared(gain), ((0, 0), (0, 0), (0, 127))),
-                ],
-                axis=2,
-            ),
-            row_size,
-            col_size,
-            parts=1,
-        ),
-        col_size,
-    )
+        line_stage(row_stages(keyval_group, row_size, col_size, parts=1), col_size), col_size
+    )
+    half_query = query_width // 2
+    query_first, query_second = first[:, :half_query], second[:, :half_query]
+    out_first, out_second = first[:, half_query:], second[:, half_query:]
 
     def joined(first, second, start, size):
         return jnp.concatenate([first[:, start : start + size], second[:, start : start + size]], axis=1)

time: 1170 us -> 1150 us (0.983)
  waiting for transfers between devices: 372 us -> 399 us
  local copies, waits for them, and re-layouts: 190 us -> 167 us
  other arithmetic: 165 us -> 145 us
    ppermute x62 -> x58, waiting for transfers between devices: 249 us -> 270 us  [swap(): return lax.ppermute(values, axis, [(i, i ^ bit) for i in range(size)])]
    ppermute x62 -> x58, starting transfers between devices: 68.3 us -> 60.9 us  [swap(): return lax.ppermute(values, axis, [(i, i ^ bit) for i in range(size)])]
    unnamed x268 -> x275, local copies, waits for them, and re-layouts: 62.8 us -> 58.4 us
    dot_general x21 -> x22, matrix products: 237 us -> 239 us  [product(): lax.dot_general(left_side, right_side, dims, preferred_element_type=jnp.f...]
  transfers between devices with their start and end apart: 71 -> 67, of which waited for: 27 -> 29; matrix products, arithmetic and copies ran while one was open for 46% -> 43% of each run, Pallas kernels for 0% -> 0%
where the time goes in v8:
time: 1150 us; the launch traced here: 1140 us
  waiting for transfers between devices  399 us (35%)
  matrix products  353 us (31%)
  local copies, waits for them, and re-layouts  167 us (15%)
  other arithmetic  145 us (13%)
  starting transfers between devices  61.8 us (5%)
  between operations  16.1 us (1%)
    ppermute x58, waiting for transfers between devices, swap(): return lax.ppermute(values, axis, [(i, i ^ bit) for i in range(size)])  270 us
    dot_general x22, matrix products, product(): lax.dot_general(left_side, right_side, dims, preferred_element_type=jnp.f...  239 us
    dot_general x9, matrix products, matrix_product(): return jnp.dot(left_side, right_side, preferred_element_type=jnp.float32)  114 us
    all_gather x1, waiting for transfers between devices, per_device(): lax.all_gather(jnp.concatenate([convert_half(query_matrix), convert_half(...  76.3 us
    convert_element_type x23, other arithmetic, convert_half(): return values.astype(jnp.bfloat16)  64.8 us
    ppermute x58, starting transfers between devices, swap(): return lax.ppermute(values, axis, [(i, i ^ bit) for i in range(size)])  60.9 us
    unnamed x275, local copies, waits for them, and re-layouts  58.4 us
    all_gather x1, waiting for transfers between devices, per_device(): lax.all_gather(jnp.concatenate([convert_half(rotate(keyval_pre[:, :HD], c...  52 us
  transfers between devices with their start and end apart: 67, of which 29 were waited for; matrix products, arithmetic and copies ran while one was open for 43% of the time, Pallas kernels for 0%

profile of v8, /device:TPU:0, one launch (start us, length us, event | category | flops | bytes accessed | tf_op | source)
XLA Modules:
  0.0 1141.0 jit_solution(16947952534863415676)
XLA Ops:
  26.4 76.3 %all-gather.5.cloned.1.call-done = bf16[2048,2688]{1,0:T(8,128)(2,1)} async-done(((bf16[64,2688]{1,0:T(8,128)(2,1)}), bf16[2048,2688]{1,0:T(8,128)(2,1)}) %all-gather.5.cloned.1.call-update) | async-done | bytes 11010064 | tf_op jit(solution)/shard_map/all_gather | solution.py:233
  124.0 52.0 %all-gather.7.cloned.1.call-done = bf16[2304,512]{1,0:T(8,128)(2,1)} async-done(((bf16[288,512]{1,0:T(8,128)(2,1)}), bf16[2304,512]{1,0:T(8,128)(2,1)}) %all-gather.7.cloned.1.call-update) | async-done | bytes 2359312 | tf_op jit(solution)/shard_map/all_gather | solution.py:291
  176.0 11.6 %collective-permute-done.2 = bf16[288,2048]{1,0:T(8,128)(2,1)} collective-permute-done((bf16[288,2048]{1,0:T(8,128)(2,1)}, bf16[288,2048]{1,0:T(8,128)(2,1)}, u32[]{:S(2)}, u32[]{:S(2)}) %collective-permute-start.2) | collective-permute-done | bytes 1179680 | tf_op jit(solution)/shard_map/ppermute | solution.py:61
  225.2 8.8 fusion.152
  242.8 18.6 %collective-permute-done.6 = bf16[288,2048]{1,0:T(8,128)(2,1)S(1)} collective-permute-done((bf16[288,2048]{1,0:T(8,128)(2,1)S(1)}, bf16[288,2048]{1,0:T(8,128)(2,1)S(1)}, u32[]{:S(2)}, u32[]{:S(2)}) %collective-permute-start.6) | collective-permute-done | bytes 1179680 | tf_op jit(solution)/shard_map/ppermute | solution.py:61
  261.4 41.6 %collective-permute-done.4 = bf16[800,2048]{1,0:T(8,128)(2,1)} collective-permute-done((bf16[800,2048]{1,0:T(8,128)(2,1)}, bf16[800,2048]{1,0:T(8,128)(2,1)}, u32[]{:S(2)}, u32[]{:S(2)}) %collective-permute-start.4) | collective-permute-done | bytes 3276832 | tf_op jit(solution)/shard_map/ppermute | solution.py:61
  344.5 9.3 collective-permute-done.7
  412.1 12.0 %collective-permute-done.10 = bf16[400,2048]{1,0:T(8,128)(2,1)S(1)} collective-permute-done((bf16[400,2048]{1,0:T(8,128)(2,1)S(1)}, bf16[400,2048]{1,0:T(8,128)(2,1)S(1)}, u32[]{:S(2)}, u32[]{:S(2)}) %collective-permute-start.10) | collective-permute-done | bytes 1638432 | tf_op jit(solution)/shard_map/ppermute | solution.py:61
  437.6 29.4 %fusion.17 = f32[2304,2048]{1,0:T(8,128)} fusion(bf16[2304,2048]{1,0:T(8,128)(2,1)} %get-tuple-element.267, bf16[2304,256]{1,0:T(8,128)(2,1)S(1)} %copy.37, bf16[2304,2048]{1,0:T(8,128)(2,1)} %slice_dynamic-update-slice_fusion.11), kind=kOutput, calls=%fused_computation.34 | convolution fusion | flops 21764505600 | bytes 38928384 | tf_op jit(solution)/shard_map/dot_general | solution.py:28
  467.0 26.9 %fusion.155 = f32[2304,2048]{1,0:T(8,128)} fusion(bf16[2304,2048]{1,0:T(8,128)(2,1)} %all-gather.11.cloned.1.call-done, bf16[2048,2048]{1,0:T(8,128)(2,1)} %slice_dynamic-update-slice_fusion.15), kind=kOutput, calls=%fused_computation.385 | convolution fusion | flops 19327352832 | bytes 36700160 | tf_op jit(solution)/shard_map/dot_general | solution.py:28
  494.0 24.4 %fusion.154 = f32[2304,2048]{1,0:T(8,128)} fusion(bf16[2304,2048]{1,0:T(8,128)(2,1)S(1)} %copy-done.106, bf16[2048,2048]{1,0:T(8,128)(2,1)} %slice_dynamic-update-slice_fusion.20), kind=kOutput, calls=%fused_computation.384 | convolution fusion | flops 19327352832 | bytes 36700160 | tf_op jit(solution)/shard_map/dot_general | solution.py:28
  518.4 29.9 %multiply_convert_fusion.1 = (bf16[2304,2048]{1,0:T(8,128)(2,1)}, bf16[2304,2048]{1,0:T(8,128)(2,1)}, bf16[2304,2048]{1,0:T(8,128)(2,1)}) fusion(f32[2304,2048]{1,0:T(8,128)S(1)} %bitcast.92, f32[2304,2048]{1,0:T(8,128)} %fusion.154, f32[2304,2048]{1,0:T(8,128)} %fusion.155), kind=kLoop, calls=%fused_computation.15 | loop fusion | flops 122683392 | bytes 84934656 | tf_op jit(solution)/shard_map/convert_element_type | solution.py:20
  548.2 28.7 %convolution_convert_fusion.1 = bf16[2304,2048]{1,0:T(8,128)(2,1)S(1)} fusion(bf16[2304,2048]{1,0:T(8,128)(2,1)} %get-tuple-element.163, bf16[2304,256]{1,0:T(8,128)(2,1)} %copy-done.72, bf16[2304,2048]{1,0:T(8,128)(2,1)} %slice_dynamic-update-slice_fusion.11), kind=kOutput, calls=%fused_computation.19 | convolution fusion | flops 21769224192 | bytes 29491200 | tf_op jit(solution)/shard_map/dot_general | solution.py:24
  586.8 14.7 %fusion.22 = f32[2304,1024]{1,0:T(8,128)} fusion(bf16[2304,2048]{1,0:T(8,128)(2,1)S(1)} %copy-done.16, bf16[2048,2048]{1,0:T(8,128)(2,1)} %slice_dynamic-update-slice_fusion.20), kind=kOutput, calls=%fused_computation.50 | convolution fusion | flops 9663676416 | bytes 23068672 | tf_op jit(solution)/shard_map/dot_general | solution.py:24
  605.8 14.9 %add_convert_fusion.1 = bf16[2304,1024]{1,0:T(8,128)(2,1)} fusion(f32[2304,1024]{1,0:T(8,128)} %fusion.22, bf16[2304,2048]{1,0:T(8,128)(2,1)S(1)} %bitcast.98, bf16[2048,2048]{1,0:T(8,128)(2,1)} %slice_dynamic-update-slice_fusion.15), kind=kOutput, calls=%fused_computation.22 | convolution fusion | flops 9668395008 | bytes 27787264 | tf_op jit(solution)/shard_map/dot_general | solution.py:24
  621.8 8.8 collective-permute-done.17
  643.0 16.4 %fusion.18 = f32[2304,1024]{1,0:T(8,128)} fusion(bf16[2304,2048]{1,0:T(8,128)(2,1)} %get-tuple-element.149, bf16[2048,2048]{1,0:T(8,128)(2,1)} %slice_dynamic-update-slice_fusion.15), kind=kOutput, calls=%fused_computation.46 | convolution fusion | flops 9663676416 | bytes 23068672 | tf_op jit(solution)/shard_map/dot_general | solution.py:24
  659.3 14.8 %add_convert_fusion = bf16[2304,1024]{1,0:T(8,128)(2,1)} fusion(f32[2304,1024]{1,0:T(8,128)} %fusion.18, bf16[2304,2048]{1,0:T(8,128)(2,1)S(1)} %bitcast.102, bf16[2048,2048]{1,0:T(8,128)(2,1)} %slice_dynamic-update-slice_fusion.20), kind=kOutput, calls=%fused_computation.21 | convolution fusion | flops 9668395008 | bytes 27787264 | tf_op jit(solution)/shard_map/dot_general | solution.py:24
  681.7 26.0 %convolution_convert_fusion.4 = bf16[2048,2048]{1,0:T(8,128)(2,1)S(1)} fusion(bf16[2304,2048]{1,0:T(8,128)(2,1)} %all-gather.11.cloned.1.call-done, bf16[2304,2048]{1,0:T(8,128)(2,1)} %get-tuple-element.146), kind=kOutput, calls=%fused_computation.33 | convolution fusion | flops 19331547136 | bytes 27262976 | tf_op jit(solution)/shard_map/dot_general | solution.py:24
  714.1 24.5 %convolution_convert_fusion.3 = bf16[2048,2048]{1,0:T(8,128)(2,1)} fusion(bf16[2304,2048]{1,0:T(8,128)(2,1)} %all-gather.11.cloned.1.call-done, bf16[2304,2048]{1,0:T(8,128)(2,1)S(1)} %bitcast.100), kind=kOutput, calls=%fused_computation.32 | convolution fusion | flops 19331547136 | bytes 27262976 | tf_op jit(solution)/shard_map/dot_general | solution.py:24
  776.8 10.6 collective-permute-done.28
  788.4 16.5 %collective-permute-done.26 = bf16[256,2048]{1,0:T(8,128)(2,1)} collective-permute-done((bf16[256,2048]{1,0:T(8,128)(2,1)}, bf16[256,2048]{1,0:T(8,128)(2,1)}, u32[]{:S(2)}, u32[]{:S(2)}) %collective-permute-start.26) | collective-permute-done | bytes 1048608 | tf_op jit(solution)/shard_map/ppermute | solution.py:61
  835.7 26.4 %convolution_convert_fusion = bf16[2304,2048]{1,0:T(8,128)(2,1)} fusion(bf16[2304,2048]{1,0:T(8,128)(2,1)} %get-tuple-element.163, bf16[2048,2048]{1,0:T(8,128)(2,1)} %get-tuple-element.262), kind=kOutput, calls=%fused_computation.18 | convolution fusion | flops 19332071424 | bytes 27262976 | tf_op jit(solution)/shard_map/dot_general | solution.py:24
  897.3 21.0 %collective-permute-done.30 = bf16[256,2048]{1,0:T(8,128)(2,1)} collective-permute-done((bf16[256,2048]{1,0:T(8,128)(2,1)}, bf16[256,2048]{1,0:T(8,128)(2,1)}, u32[]{:S(2)}, u32[]{:S(2)}) %collective-permute-start.30) | collective-permute-done | bytes 1048608 | tf_op jit(solution)/shard_map/ppermute | solution.py:61
  933.7 9.0 fusion.34
  961.4 11.6 %collective-permute-done.37 = bf16[1,2,4,128,512]{4,3,2,1,0:T(8,128)(2,1)} collective-permute-done((bf16[1,2,4,128,512]{4,3,2,1,0:T(8,128)(2,1)}, bf16[1,2,4,128,512]{4,3,2,1,0:T(8,128)(2,1)}, u32[]{:S(2)}, u32[]{:S(2)}) %collective-permute-start.37) | collective-permute-done | bytes 1048608 | tf_op jit(solution)/shard_map/ppermute | solution.py:61
  977.6 23.3 %collective-permute-done.41 = bf16[1,2,4,128,640]{4,3,2,1,0:T(8,128)(2,1)} collective-permute-done((bf16[1,2,4,128,640]{4,3,2,1,0:T(8,128)(2,1)}, bf16[1,2,4,128,640]{4,3,2,1,0:T(8,128)(2,1)}, u32[]{:S(2)}, u32[]{:S(2)}) %collective-permute-start.41) | collective-permute-done | bytes 1310752 | tf_op jit(solution)/shard_map/ppermute | solution.py:61
  1014.0 13.3 %collective-permute-done.42 = bf16[1,1,4,128,640]{4,3,2,1,0:T(8,128)(2,1)S(1)} collective-permute-done((bf16[1,1,4,128,640]{4,3,2,1,0:T(8,128)(2,1)S(1)}, bf16[1,1,4,128,640]{4,3,2,1,0:T(8,128)(2,1)S(1)}, u32[]{:S(2)}, u32[]{:S(2)}) %collective-permute-start.42) | collective-permute-done | bytes 655392 | tf_op jit(solution)/shard_map/ppermute | solution.py:61
  1048.9 10.9 collective-permute-done.54
  1059.8 15.8 %collective-permute-done.55 = bf16[128,2304]{1,0:T(8,128)(2,1)S(1)} collective-permute-done((bf16[128,2304]{1,0:T(8,128)(2,1)S(1)}, bf16[128,2304]{1,0:T(8,128)(2,1)S(1)}, u32[]{:S(2)}, u32[]{:S(2)}) %collective-permute-start.55) | collective-permute-done | bytes 589856 | tf_op jit(solution)/shard_map/ppermute | solution.py:61
  1085.2 9.0 collective-permute-done.49
  1095.4 12.0 %collective-permute-start.50 = (bf16[128,512]{1,0:T(8,128)(2,1)S(1)}, bf16[128,512]{1,0:T(8,128)(2,1)S(1)}, u32[]{:S(2)}, u32[]{:S(2)}) collective-permute-start(bf16[128,512]{1,0:T(8,128)(2,1)S(1)} %get-tuple-element.308), channel_id=1, source_target_pairs={{0,2},{1,3},{2,0},{3,1},{4,6},{5,7},{6,4},{7,5},{8,10},{9,11},{10,... | collective-permute-start | bytes 393224 | tf_op jit(solution)/shard_map/ppermute | solution.py:61
  (608 shorter events, 456.0 us)
Async XLA Ops:
  7.2 95.5 %all-gather.5.cloned.1.call-start = ((), (), s32[]{:S(2)}) async-start(), calls=%async_computation.5 | async-start | bytes 11354112 | tf_op jit(solution)/shard_map/all_gather | solution.py:233
  11.1 165.0 %all-gather.7.cloned.1.call-start = ((), (), s32[]{:S(2)}) async-start(), calls=%async_computation.6 | async-start | bytes 2654208 | tf_op jit(solution)/shard_map/all_gather | solution.py:291
  114.1 211.5 %all-gather.9.cloned.1.call-start = ((), (), s32[]{:S(2)}) async-start(), calls=%async_computation.7 | async-start | bytes 11894784 | tf_op jit(solution)/shard_map/all_gather | solution.py:330
  114.1 76.2 %collective-permute-start = (bf16[800,2048]{1,0:T(8,128)(2,1)}, bf16[800,2048]{1,0:T(8,128)(2,1)}, u32[]{:S(2)}, u32[]{:S(2)}) collective-permute-start(bf16[800,2048]{1,0:T(8,128)(2,1)} %get-tuple-element.113), channel_id=1, source_target_pairs={{0,16},{8,24},{16,0},{24,8},{1,17},{9,25},{17,1},{25,9},{2,18},{10... | collective-permute-start | bytes 9830408 | tf_op jit(solution)/shard_map/ppermute | solution.py:61
  115.6 74.7 %collective-permute-start.1 = (bf16[800,2048]{1,0:T(8,128)(2,1)}, bf16[800,2048]{1,0:T(8,128)(2,1)}, u32[]{:S(2)}, u32[]{:S(2)}) collective-permute-start(bf16[800,2048]{1,0:T(8,128)(2,1)} %get-tuple-element.114), channel_id=1, source_target_pairs={{0,8},{8,0},{16,24},{24,16},{1,9},{9,1},{17,25},{25,17},{2,10},{10... | collective-permute-start | bytes 9830408 | tf_op jit(solution)/shard_map/ppermute | solution.py:61
  116.2 71.5 %collective-permute-start.2 = (bf16[288,2048]{1,0:T(8,128)(2,1)}, bf16[288,2048]{1,0:T(8,128)(2,1)}, u32[]{:S(2)}, u32[]{:S(2)}) collective-permute-start(bf16[288,2048]{1,0:T(8,128)(2,1)} %pad_maximum_fusion.19), channel_id=1, source_target_pairs={{0,2},{1,3},{2,0},{3,1},{4,6},{5,7},{6,4},{7,5},{8,10},{9,11},{10,... | collective-permute-start | bytes 3538952 | tf_op jit(solution)/shard_map/ppermute | solution.py:61
  117.5 72.8 %collective-permute-start.3 = (bf16[288,2048]{1,0:T(8,128)(2,1)}, bf16[288,2048]{1,0:T(8,128)(2,1)}, u32[]{:S(2)}, u32[]{:S(2)}) collective-permute-start(bf16[288,2048]{1,0:T(8,128)(2,1)} %pad_maximum_fusion.19), channel_id=1, source_target_pairs={{0,4},{1,5},{2,6},{3,7},{4,0},{5,1},{6,2},{7,3},{8,12},{9,13},{10,... | collective-permute-start | bytes 3538952 | tf_op jit(solution)/shard_map/ppermute | solution.py:61
  190.3 276.7 %all-gather.11.cloned.1.call-start = ((), (), s32[]{:S(2)}) async-start(), calls=%async_computation.8 | async-start | bytes 10616832 | tf_op jit(solution)/shard_map/all_gather | solution.py:394
  203.7 99.4 %collective-permute-start.4 = (bf16[800,2048]{1,0:T(8,128)(2,1)}, bf16[800,2048]{1,0:T(8,128)(2,1)}, u32[]{:S(2)}, u32[]{:S(2)}) collective-permute-start(bf16[800,2048]{1,0:T(8,128)(2,1)} %get-tuple-element.113), channel_id=1, source_target_pairs={{0,8},{8,0},{16,24},{24,16},{1,9},{9,1},{17,25},{25,17},{2,10},{10... | collective-permute-start | bytes 9830408 | tf_op jit(solution)/shard_map/ppermute | solution.py:61
  205.2 97.9 %collective-permute-start.5 = (bf16[800,2048]{1,0:T(8,128)(2,1)}, bf16[800,2048]{1,0:T(8,128)(2,1)}, u32[]{:S(2)}, u32[]{:S(2)}) collective-permute-start(bf16[800,2048]{1,0:T(8,128)(2,1)} %get-tuple-element.114), channel_id=1, source_target_pairs={{0,16},{8,24},{16,0},{24,8},{1,17},{9,25},{17,1},{25,9},{2,18},{10... | collective-permute-start | bytes 9830408 | tf_op jit(solution)/shard_map/ppermute | solution.py:61
  306.8 51.2 %collective-permute-start.9 = (bf16[1152,2048]{1,0:T(8,128)(2,1)}, bf16[1152,2048]{1,0:T(8,128)(2,1)}, u32[]{:S(2)}, u32[]{:S(2)}) collective-permute-start(bf16[1152,2048]{1,0:T(8,128)(2,1)} %pad_maximum_fusion.4), channel_id=1, source_target_pairs={{0,1},{1,0},{2,3},{3,2},{4,5},{5,4},{6,7},{7,6},{8,9},{9,8},{10,11... | collective-permute-start | bytes 14155784 | tf_op jit(solution)/shard_map/ppermute | solution.py:61
  314.5 39.3 %collective-permute-start.7 = (bf16[400,2048]{1,0:T(8,128)(2,1)}, bf16[400,2048]{1,0:T(8,128)(2,1)}, u32[]{:S(2)}, u32[]{:S(2)}) collective-permute-start(bf16[400,2048]{1,0:T(8,128)(2,1)} %slice.389), channel_id=1, source_target_pairs={{0,8},{8,0},{16,24},{24,16},{1,9},{9,1},{17,25},{25,17},{2,10},{10... | collective-permute-start | bytes 4915208 | tf_op jit(solution)/shard_map/ppermute | solution.py:61
  319.6 38.3 %collective-permute-start.8 = (bf16[400,2048]{1,0:T(8,128)(2,1)}, bf16[400,2048]{1,0:T(8,128)(2,1)}, u32[]{:S(2)}, u32[]{:S(2)}) collective-permute-start(bf16[400,2048]{1,0:T(8,128)(2,1)} %slice.390), channel_id=1, source_target_pairs={{0,16},{8,24},{16,0},{24,8},{1,17},{9,25},{17,1},{25,9},{2,18},{10... | collective-permute-start | bytes 4915208 | tf_op jit(solution)/shard_map/ppermute | solution.py:61
  319.6 39.5 %collective-permute-start.13 = (bf16[288,2048]{1,0:T(8,128)(2,1)S(1)}, bf16[288,2048]{1,0:T(8,128)(2,1)}, u32[]{:S(2)}, u32[]{:S(2)}) collective-permute-start(bf16[288,2048]{1,0:T(8,128)(2,1)S(1)} %copy-done.36), channel_id=1, source_target_pairs={{0,1},{1,0},{2,3},{3,2},{4,5},{5,4},{6,7},{7,6},{8,9},{9,8},{10,11... | collective-permute-start | bytes 3538952 | tf_op jit(solution)/shard_map/ppermute | solution.py:61
  358.0 392.7 %reduce-scatter.6.cloned.1.call-start = ((), (), s32[]{:S(2)}) async-start(), calls=%async_computation.9 | async-start | bytes 5308416 | tf_op jit(solution)/shard_map/reduce_scatter | solution.py:449
  366.1 65.0 %collective-permute-start.11 = (bf16[400,2048]{1,0:T(8,128)(2,1)}, bf16[400,2048]{1,0:T(8,128)(2,1)}, u32[]{:S(2)}, u32[]{:S(2)}) collective-permute-start(bf16[400,2048]{1,0:T(8,128)(2,1)} %slice.406), channel_id=1, source_target_pairs={{0,8},{8,0},{16,24},{24,16},{1,9},{9,1},{17,25},{25,17},{2,10},{10... | collective-permute-start | bytes 4915208 | tf_op jit(solution)/shard_map/ppermute | solution.py:61
  631.7 120.1 %reduce-scatter.8.cloned.1.call-start = ((), (), s32[]{:S(2)}) async-start(), calls=%async_computation.10 | async-start | bytes 5308416 | tf_op jit(solution)/shard_map/reduce_scatter | solution.py:449
  675.2 160.5 %reduce-scatter.10.cloned.1.call-start = ((), (), s32[]{:S(2)}) async-start(), calls=%async_computation.11 | async-start | bytes 1327104 | tf_op jit(solution)/shard_map/reduce_scatter | solution.py:449
  740.6 178.5 %reduce-scatter.12.cloned.1.call-start = ((), (), s32[]{:S(2)}) async-start(), calls=%async_computation.12 | async-start | bytes 2654208 | tf_op jit(solution)/shard_map/reduce_scatter | solution.py:449
  745.4 42.0 %collective-permute-start.28 = (bf16[256,2048]{1,0:T(8,128)(2,1)}, bf16[256,2048]{1,0:T(8,128)(2,1)}, u32[]{:S(2)}, u32[]{:S(2)}) collective-permute-start(bf16[256,2048]{1,0:T(8,128)(2,1)} %get-tuple-element.224), channel_id=1, source_target_pairs={{0,8},{8,0},{16,24},{24,16},{1,9},{9,1},{17,25},{25,17},{2,10},{10... | collective-permute-start | bytes 3145736 | tf_op jit(solution)/shard_map/ppermute | solution.py:61
  746.4 42.0 %collective-permute-start.29 = (bf16[256,2048]{1,0:T(8,128)(2,1)}, bf16[256,2048]{1,0:T(8,128)(2,1)}, u32[]{:S(2)}, u32[]{:S(2)}) collective-permute-start(bf16[256,2048]{1,0:T(8,128)(2,1)} %get-tuple-element.223), channel_id=1, source_target_pairs={{0,16},{8,24},{16,0},{24,8},{1,17},{9,25},{17,1},{25,9},{2,18},{10... | collective-permute-start | bytes 3145736 | tf_op jit(solution)/shard_map/ppermute | solution.py:61
  749.7 55.2 %collective-permute-start.26 = (bf16[256,2048]{1,0:T(8,128)(2,1)}, bf16[256,2048]{1,0:T(8,128)(2,1)}, u32[]{:S(2)}, u32[]{:S(2)}) collective-permute-start(bf16[256,2048]{1,0:T(8,128)(2,1)} %get-tuple-element.226), channel_id=1, source_target_pairs={{0,8},{8,0},{16,24},{24,16},{1,9},{9,1},{17,25},{25,17},{2,10},{10... | collective-permute-start | bytes 3145736 | tf_op jit(solution)/shard_map/ppermute | solution.py:61
  764.9 40.6 %collective-permute-start.27 = (bf16[256,2048]{1,0:T(8,128)(2,1)}, bf16[256,2048]{1,0:T(8,128)(2,1)}, u32[]{:S(2)}, u32[]{:S(2)}) collective-permute-start(bf16[256,2048]{1,0:T(8,128)(2,1)} %get-tuple-element.225), channel_id=1, source_target_pairs={{0,16},{8,24},{16,0},{24,8},{1,17},{9,25},{17,1},{25,9},{2,18},{10... | collective-permute-start | bytes 3145736 | tf_op jit(solution)/shard_map/ppermute | solution.py:61
  835.7 295.7 %reduce-scatter.14.cloned.1.call-start = ((), (), s32[]{:S(2)}) async-start(), calls=%async_computation.13 | async-start | bytes 10616832 | tf_op jit(solution)/shard_map/reduce_scatter | solution.py:449
  871.6 46.8 %collective-permute-start.30 = (bf16[256,2048]{1,0:T(8,128)(2,1)}, bf16[256,2048]{1,0:T(8,128)(2,1)}, u32[]{:S(2)}, u32[]{:S(2)}) collective-permute-start(bf16[256,2048]{1,0:T(8,128)(2,1)} %get-tuple-element.155), channel_id=1, source_target_pairs={{0,8},{8,0},{16,24},{24,16},{1,9},{9,1},{17,25},{25,17},{2,10},{10... | collective-permute-start | bytes 3145736 | tf_op jit(solution)/shard_map/ppermute | solution.py:61
  872.2 46.9 %collective-permute-start.31 = (bf16[256,2048]{1,0:T(8,128)(2,1)}, bf16[256,2048]{1,0:T(8,128)(2,1)}, u32[]{:S(2)}, u32[]{:S(2)}) collective-permute-start(bf16[256,2048]{1,0:T(8,128)(2,1)} %get-tuple-element.156), channel_id=1, source_target_pairs={{0,16},{8,24},{16,0},{24,8},{1,17},{9,25},{17,1},{25,9},{2,18},{10... | collective-permute-start | bytes 3145736 | tf_op jit(solution)/shard_map/ppermute | solution.py:61
  951.0 50.0 %collective-permute-start.41 = (bf16[1,2,4,128,640]{4,3,2,1,0:T(8,128)(2,1)}, bf16[1,2,4,128,640]{4,3,2,1,0:T(8,128)(2,1)}, u32[]{:S(2)}, u32[]{:S(2)}) collective-permute-start(bf16[1,2,4,128,640]{4,3,2,1,0:T(8,128)(2,1)} %constant_dynamic-slice_fusion.13), channel_id=1, source_target_pairs={{0,16},{8,24},{16,0},{24,8},{1,17},{9,25},{17,1},{25,9},{2,18},{10... | collective-permute-start | bytes 3932168 | tf_op jit(solution)/shard_map/ppermute | solution.py:61
  956.4 47.0 %collective-permute-start.43 = (bf16[2,1,4,128,640]{4,3,2,1,0:T(8,128)(2,1)}, bf16[2,1,4,128,640]{4,3,2,1,0:T(8,128)(2,1)}, u32[]{:S(2)}, u32[]{:S(2)}) collective-permute-start(bf16[2,1,4,128,640]{4,3,2,1,0:T(8,128)(2,1)} %constant_dynamic-slice_fusion.11), channel_id=1, source_target_pairs={{0,8},{8,0},{16,24},{24,16},{1,9},{9,1},{17,25},{25,17},{2,10},{10... | collective-permute-start | bytes 3932168 | tf_op jit(solution)/shard_map/ppermute | solution.py:61
  974.5 39.2 %collective-permute-start.38 = (bf16[1,1,4,128,512]{4,3,2,1,0:T(8,128)(2,1)S(1)}, bf16[1,1,4,128,512]{4,3,2,1,0:T(8,128)(2,1)S(1)}, u32[]{:S(2)}, u32[]{:S(2)}) collective-permute-start(bf16[1,1,4,128,512]{4,3,2,1,0:T(8,128)(2,1)S(1)} %constant_dynamic-slice_fusion.16), channel_id=1, source_target_pairs={{0,8},{8,0},{16,24},{24,16},{1,9},{9,1},{17,25},{25,17},{2,10},{10... | collective-permute-start | bytes 1572872 | tf_op jit(solution)/shard_map/ppermute | solution.py:61
  1028.0 50.4 %collective-permute-start.48 = (bf16[1,2,4,128,512]{4,3,2,1,0:T(8,128)(2,1)S(1)}, bf16[1,2,4,128,512]{4,3,2,1,0:T(8,128)(2,1)S(1)}, u32[]{:S(2)}, u32[]{:S(2)}) collective-permute-start(bf16[1,2,4,128,512]{4,3,2,1,0:T(8,128)(2,1)S(1)} %constant_dynamic-slice_fusion.5), channel_id=1, source_target_pairs={{0,16},{8,24},{16,0},{24,8},{1,17},{9,25},{17,1},{25,9},{2,18},{10... | collective-permute-start | bytes 3145736 | tf_op jit(solution)/shard_map/ppermute | solution.py:61
  1033.1 42.4 %collective-permute-start.55 = (bf16[128,2304]{1,0:T(8,128)(2,1)S(1)}, bf16[128,2304]{1,0:T(8,128)(2,1)S(1)}, u32[]{:S(2)}, u32[]{:S(2)}) collective-permute-start(bf16[128,2304]{1,0:T(8,128)(2,1)S(1)} %get-tuple-element.253), channel_id=1, source_target_pairs={{0,4},{1,5},{2,6},{3,7},{4,0},{5,1},{6,2},{7,3},{8,12},{9,13},{10,... | collective-permute-start | bytes 1769480 | tf_op jit(solution)/shard_map/ppermute | solution.py:61
  1033.5 42.0 %collective-permute-start.56 = (bf16[128,2304]{1,0:T(8,128)(2,1)S(1)}, bf16[128,2304]{1,0:T(8,128)(2,1)S(1)}, u32[]{:S(2)}, u32[]{:S(2)}) collective-permute-start(bf16[128,2304]{1,0:T(8,128)(2,1)S(1)} %get-tuple-element.252), channel_id=1, source_target_pairs={{0,6},{1,7},{2,4},{3,5},{4,2},{5,3},{6,0},{7,1},{8,14},{9,15},{10,... | collective-permute-start | bytes 1769480 | tf_op jit(solution)/shard_map/ppermute | solution.py:61
  (167 other events, 2398.9 us)
Sparse Core Ops, SparseCore 0:
  11.6 91.0 all-gather.4
  114.2 61.8 all-gather.6
  190.5 131.6 all-gather.8
  358.1 87.8 all-gather.10
  630.8 52.9 reduce-scatter.5
  686.0 53.3 reduce-scatter.7
  742.3 31.4 reduce-scatter.9
  835.8 34.1 reduce-scatter.11
  919.2 96.2 reduce-scatter.13

commit v9 on v8

--- a/solution.py
+++ b/solution.py
@@ -148,19 +148,32 @@
     return add_half(kept, swap(sent, axis, size, bit))
 
 
-def row_stages(values, row_size, col_size, parts=2):
+def row_bits(row_size, place):
+    bits = [1 << k for k in reversed(range(row_size.bit_length() - 1))]
+    return bits, bits if place % 2 == 0 else bits[::-1]
+
+
+def row_first(values, row_size, col_size, parts=2):
     chips, rows, width = values.shape
-    line = col_size // 2
-    bits = [1 << k for k in reversed(range(row_size.bit_length() - 1))]
-    shaped = values.reshape((2,) * len(bits) + (line, rows, width))
+    bits, order = row_bits(row_size, 0)
+    shaped = values.reshape((2,) * len(bits) + (col_size // 2, rows, width))
     part = width // parts
     pieces = []
     for place in range(parts):
+        bits, order = row_bits(row_size, place)
         piece = shaped[..., part * place : part * (place + 1)]
-        for bit in bits if place % 2 == 0 else bits[::-1]:
+        pieces.append(halve(piece, bits.index(order[0]), "row", row_size, order[0]))
+    return pieces
+
+
+def row_rest(pieces, row_size):
+    done = []
+    for place, piece in enumerate(pieces):
+        bits, order = row_bits(row_size, place)
+        for bit in order[1:]:
             piece = halve(piece, bits.index(bit), "row", row_size, bit)
-        pieces.append(piece.reshape(line, rows, part))
-    return jnp.concatenate(pieces, axis=-1)
+        done.append(piece.reshape(piece.shape[-3:]))
+    return jnp.concatenate(done, axis=-1)
 
 
 def line_stage(whole, col_size):
@@ -505,7 +518,7 @@
             *gate_free, *gate_last, *up_far, grad_rows, *up_free
         )
         gate_free, gate_last = sums[:2], sums[2:]
-        up_last = send_pair(add_pair(up_last, (far_x, far_y)))
+        up_last = add_pair(up_last, (far_x, far_y))
         up_free = send_pair((free_x, free_y))
     delta = jnp.sum(grad_rows.astype(jnp.float32) * mixed_rows, axis=1)
     weight_grad = product(grad_rows, value_rows, contract_last)
@@ -522,6 +535,12 @@
     keyval_part = jnp.concatenate([convert_half(key_acc), convert_half(value_acc)], axis=1)
     keyval_part, rank_sums = tie(keyval_part, rank_sums)
     keyval_sum = col_sum(keyval_part)
+    down_partial = down_product(0, width)
+    if row_size == 4:
+        *up_free, down_partial, normed_both, context_both, last_x, last_y = tie(
+            *up_free, down_partial, normed_both, context_both, *up_last
+        )
+        up_last = send_pair((last_x, last_y))
     core = lax.axis_index("col") % 2
     query_right = halves_with_partner(query_grad, col_size)
     grad_query = convert_half(product(normed_both, query_right, contract_first))
@@ -538,16 +557,11 @@
     grad_out_upper = product(rank_both, out_right, contract_first)
     out_group = jnp.concatenate([shared(grad_out), shared(grad_out_upper)], axis=2)
     query_group = shared(grad_query)
-    down_partial = down_product(0, width)
-    if row_size == 4:
-        *sums, keyval_sum, down_partial, out_group, query_group = tie(
-            *up_free, *up_last, keyval_sum, down_partial, out_group, query_group
-        )
-        up_free, up_last = sums[:2], sums[2:]
-    else:
-        keyval_sum, down_partial = tie(keyval_sum, down_partial)
-    query_lines = row_stages(query_group, row_size, col_size)
-    out_lines = row_stages(out_group, row_size, col_size)
+    *up_last, keyval_sum, down_partial, out_group, query_group = tie(
+        *(up_last if row_size == 4 else ()), keyval_sum, down_partial, out_group, query_group
+    )
+    query_parts = row_first(query_group, row_size, col_size)
+    out_parts = row_first(out_group, row_size, col_size)
     down_rank_rows = reorder(rank_sums, order)
     summed = col_sum(down_partial)
     layer_out = convert_half(
@@ -561,14 +575,16 @@
         axis=1,
     )
     in_grad = jnp.concatenate([query_grad, keyval_grad], axis=1)
+    grad_keyval = product(
+        normed_both, halves_with_partner(keyval_grad, col_size), contract_first
+    )
+    in_grad, grad_keyval, *parts = tie(in_grad, grad_keyval, *query_parts, *out_parts)
+    lines = jnp.concatenate([row_rest(parts[:2], row_size), row_rest(parts[2:], row_size)], axis=2)
     normed_back = product(in_grad, in_weight, contract_last)
     normed_out, first_pull = jax.vjp(rms_scale, inputs, gain_attn)
     input_part, grad_gain_attn = first_pull(normed_back)
     input_grad = convert_half(state_grad + input_part)
 
-    grad_keyval = product(
-        normed_both, halves_with_partner(keyval_grad, col_size), contract_first
-    )
     grad_down_upper = product(
         with_partner(down_rank_rows, col_size), cot_both, contract_first
     )
@@ -584,7 +600,6 @@
         ],
         axis=2,
     )
-    lines = jnp.concatenate([query_lines, out_lines], axis=2)
     lines, keyval_group = tie(lines, keyval_group)
     if row_size == 4:
         lines, own_down, own_gate, own_up = tie(lines, own_down, own_gate, own_up)
@@ -594,7 +609,7 @@
     down_sum, rank_sum = down_total[:model_rows], down_total[model_rows:]
     first, second = share_cores(line_stage(lines, col_size), col_size)
     keyval_first, keyval_second = share_cores(
-        line_stage(row_stages(keyval_group, row_size, col_size, parts=1), col_size), col_size
+        line_stage(row_rest(row_first(keyval_group, row_size, col_size, parts=1), row_size), col_size), col_size
     )
     half_query = query_width // 2
     query_first, query_second = first[:, :half_query], second[:, :half_query]

time: 1150 us -> 1140 us (level)
    unnamed x275 -> x271, local copies, waits for them, and re-layouts: 58.4 us -> 62.5 us
  transfers between devices with their start and end apart: 67 -> 67, of which waited for: 29 -> 32; matrix products, arithmetic and copies ran while one was open for 43% -> 43% of each run, Pallas kernels for 0% -> 0%
where the time goes in v9:
time: 1140 us; the launch traced here: 1130 us
  waiting for transfers between devices  394 us (35%)
  matrix products  350 us (31%)
  local copies, waits for them, and re-layouts  170 us (15%)
  other arithmetic  142 us (12%)
  starting transfers between devices  59.2 us (5%)
  between operations  16.1 us (1%)
    ppermute x58, waiting for transfers between devices, swap(): return lax.ppermute(values, axis, [(i, i ^ bit) for i in range(size)])  265 us
    dot_general x22, matrix products, product(): lax.dot_general(left_side, right_side, dims, preferred_element_type=jnp.f...  236 us
    dot_general x9, matrix products, matrix_product(): return jnp.dot(left_side, right_side, preferred_element_type=jnp.float32)  114 us
    all_gather x1, waiting for transfers between devices, per_device(): lax.all_gather(jnp.concatenate([convert_half(query_matrix), convert_half(...  76.3 us
    unnamed x271, local copies, waits for them, and re-layouts  62.5 us
    convert_element_type x23, other arithmetic, convert_half(): return values.astype(jnp.bfloat16)  59.6 us
    ppermute x58, starting transfers between devices, swap(): return lax.ppermute(values, axis, [(i, i ^ bit) for i in range(size)])  58.2 us
    all_gather x1, waiting for transfers between devices, per_device(): lax.all_gather(jnp.concatenate([convert_half(rotate(keyval_pre[:, :HD], c...  52.1 us
  transfers between devices with their start and end apart: 67, of which 32 were waited for; matrix products, arithmetic and copies ran while one was open for 43% of the time, Pallas kernels for 0%

profile of v9, /device:TPU:0, one launch (start us, length us, event | category | flops | bytes accessed | tf_op | source)
XLA Modules:
  0.0 1130.7 jit_solution(6448993014997760437)
XLA Ops:
  26.4 76.3 %all-gather.5.cloned.1.call-done = bf16[2048,2688]{1,0:T(8,128)(2,1)} async-done(((bf16[64,2688]{1,0:T(8,128)(2,1)}), bf16[2048,2688]{1,0:T(8,128)(2,1)}) %all-gather.5.cloned.1.call-update) | async-done | bytes 11010064 | tf_op jit(solution)/shard_map/all_gather | solution.py:246
  124.0 52.1 %all-gather.7.cloned.1.call-done = bf16[2304,512]{1,0:T(8,128)(2,1)} async-done(((bf16[288,512]{1,0:T(8,128)(2,1)}), bf16[2304,512]{1,0:T(8,128)(2,1)}) %all-gather.7.cloned.1.call-update) | async-done | bytes 2359312 | tf_op jit(solution)/shard_map/all_gather | solution.py:304
  176.1 11.5 %collective-permute-done.2 = bf16[288,2048]{1,0:T(8,128)(2,1)} collective-permute-done((bf16[288,2048]{1,0:T(8,128)(2,1)}, bf16[288,2048]{1,0:T(8,128)(2,1)}, u32[]{:S(2)}, u32[]{:S(2)}) %collective-permute-start.2) | collective-permute-done | bytes 1179680 | tf_op jit(solution)/shard_map/ppermute | solution.py:61
  205.8 8.6 fusion.144
  225.4 8.8 fusion.145
  242.9 18.9 %collective-permute-done.6 = bf16[288,2048]{1,0:T(8,128)(2,1)S(1)} collective-permute-done((bf16[288,2048]{1,0:T(8,128)(2,1)S(1)}, bf16[288,2048]{1,0:T(8,128)(2,1)S(1)}, u32[]{:S(2)}, u32[]{:S(2)}) %collective-permute-start.6) | collective-permute-done | bytes 1179680 | tf_op jit(solution)/shard_map/ppermute | solution.py:61
  261.8 41.4 %collective-permute-done.4 = bf16[800,2048]{1,0:T(8,128)(2,1)} collective-permute-done((bf16[800,2048]{1,0:T(8,128)(2,1)}, bf16[800,2048]{1,0:T(8,128)(2,1)}, u32[]{:S(2)}, u32[]{:S(2)}) %collective-permute-start.4) | collective-permute-done | bytes 3276832 | tf_op jit(solution)/shard_map/ppermute | solution.py:61
  344.6 9.3 collective-permute-done.7
  412.2 12.0 %collective-permute-done.10 = bf16[400,2048]{1,0:T(8,128)(2,1)S(1)} collective-permute-done((bf16[400,2048]{1,0:T(8,128)(2,1)S(1)}, bf16[400,2048]{1,0:T(8,128)(2,1)S(1)}, u32[]{:S(2)}, u32[]{:S(2)}) %collective-permute-start.10) | collective-permute-done | bytes 1638432 | tf_op jit(solution)/shard_map/ppermute | solution.py:61
  437.8 29.4 %fusion.17 = f32[2304,2048]{1,0:T(8,128)} fusion(bf16[2304,2048]{1,0:T(8,128)(2,1)} %get-tuple-element.289, bf16[2304,256]{1,0:T(8,128)(2,1)S(1)} %copy.37, bf16[2304,2048]{1,0:T(8,128)(2,1)} %slice_dynamic-update-slice_fusion.11), kind=kOutput, calls=%fused_computation.34 | convolution fusion | flops 21764505600 | bytes 38928384 | tf_op jit(solution)/shard_map/dot_general | solution.py:28
  467.2 26.9 %fusion.148 = f32[2304,2048]{1,0:T(8,128)} fusion(bf16[2304,2048]{1,0:T(8,128)(2,1)} %all-gather.11.cloned.1.call-done, bf16[2048,2048]{1,0:T(8,128)(2,1)} %slice_dynamic-update-slice_fusion.15), kind=kOutput, calls=%fused_computation.378 | convolution fusion | flops 19327352832 | bytes 36700160 | tf_op jit(solution)/shard_map/dot_general | solution.py:28
  494.2 24.4 %fusion.147 = f32[2304,2048]{1,0:T(8,128)} fusion(bf16[2304,2048]{1,0:T(8,128)(2,1)S(1)} %copy-done.105, bf16[2048,2048]{1,0:T(8,128)(2,1)} %slice_dynamic-update-slice_fusion.20), kind=kOutput, calls=%fused_computation.377 | convolution fusion | flops 19327352832 | bytes 36700160 | tf_op jit(solution)/shard_map/dot_general | solution.py:28
  518.6 29.9 %multiply_convert_fusion.1 = (bf16[2304,2048]{1,0:T(8,128)(2,1)}, bf16[2304,2048]{1,0:T(8,128)(2,1)}, bf16[2304,2048]{1,0:T(8,128)(2,1)}) fusion(f32[2304,2048]{1,0:T(8,128)S(1)} %bitcast.91, f32[2304,2048]{1,0:T(8,128)} %fusion.147, f32[2304,2048]{1,0:T(8,128)} %fusion.148), kind=kLoop, calls=%fused_computation.15 | loop fusion | flops 122683392 | bytes 84934656 | tf_op jit(solution)/shard_map/convert_element_type | solution.py:20
  548.4 28.8 %convolution_convert_fusion.1 = bf16[2304,2048]{1,0:T(8,128)(2,1)S(1)} fusion(bf16[2304,2048]{1,0:T(8,128)(2,1)} %get-tuple-element.168, bf16[2304,256]{1,0:T(8,128)(2,1)} %copy-done.74, bf16[2304,2048]{1,0:T(8,128)(2,1)} %slice_dynamic-update-slice_fusion.11), kind=kOutput, calls=%fused_computation.19 | convolution fusion | flops 21769224192 | bytes 29491200 | tf_op jit(solution)/shard_map/dot_general | solution.py:24
  587.0 14.7 %fusion.22 = f32[2304,1024]{1,0:T(8,128)} fusion(bf16[2304,2048]{1,0:T(8,128)(2,1)S(1)} %copy-done.13, bf16[2048,2048]{1,0:T(8,128)(2,1)} %slice_dynamic-update-slice_fusion.20), kind=kOutput, calls=%fused_computation.50 | convolution fusion | flops 9663676416 | bytes 23068672 | tf_op jit(solution)/shard_map/dot_general | solution.py:24
  606.0 14.9 %add_convert_fusion.1 = bf16[2304,1024]{1,0:T(8,128)(2,1)} fusion(f32[2304,1024]{1,0:T(8,128)} %fusion.22, bf16[2304,2048]{1,0:T(8,128)(2,1)S(1)} %bitcast.99, bf16[2048,2048]{1,0:T(8,128)(2,1)} %slice_dynamic-update-slice_fusion.15), kind=kOutput, calls=%fused_computation.22 | convolution fusion | flops 9668395008 | bytes 27787264 | tf_op jit(solution)/shard_map/dot_general | solution.py:24
  622.1 8.8 collective-permute-done.17
  643.3 16.4 %fusion.18 = f32[2304,1024]{1,0:T(8,128)} fusion(bf16[2304,2048]{1,0:T(8,128)(2,1)} %get-tuple-element.160, bf16[2048,2048]{1,0:T(8,128)(2,1)} %slice_dynamic-update-slice_fusion.15), kind=kOutput, calls=%fused_computation.46 | convolution fusion | flops 9663676416 | bytes 23068672 | tf_op jit(solution)/shard_map/dot_general | solution.py:24
  659.7 14.8 %add_convert_fusion = bf16[2304,1024]{1,0:T(8,128)(2,1)} fusion(f32[2304,1024]{1,0:T(8,128)} %fusion.18, bf16[2304,2048]{1,0:T(8,128)(2,1)S(1)} %bitcast.103, bf16[2048,2048]{1,0:T(8,128)(2,1)} %slice_dynamic-update-slice_fusion.20), kind=kOutput, calls=%fused_computation.21 | convolution fusion | flops 9668395008 | bytes 27787264 | tf_op jit(solution)/shard_map/dot_general | solution.py:24
  681.9 26.0 %convolution_convert_fusion.4 = bf16[2048,2048]{1,0:T(8,128)(2,1)S(1)} fusion(bf16[2304,2048]{1,0:T(8,128)(2,1)} %all-gather.11.cloned.1.call-done, bf16[2304,2048]{1,0:T(8,128)(2,1)} %get-tuple-element.157), kind=kOutput, calls=%fused_computation.33 | convolution fusion | flops 19331547136 | bytes 27262976 | tf_op jit(solution)/shard_map/dot_general | solution.py:24
  714.2 24.5 %convolution_convert_fusion.3 = bf16[2048,2048]{1,0:T(8,128)(2,1)} fusion(bf16[2304,2048]{1,0:T(8,128)(2,1)} %all-gather.11.cloned.1.call-done, bf16[2304,2048]{1,0:T(8,128)(2,1)S(1)} %bitcast.101), kind=kOutput, calls=%fused_computation.32 | convolution fusion | flops 19331547136 | bytes 27262976 | tf_op jit(solution)/shard_map/dot_general | solution.py:24
  756.6 8.5 collective-permute-done.22
  777.1 10.5 collective-permute-done.28
  788.4 16.7 %collective-permute-done.26 = bf16[256,2048]{1,0:T(8,128)(2,1)} collective-permute-done((bf16[256,2048]{1,0:T(8,128)(2,1)}, bf16[256,2048]{1,0:T(8,128)(2,1)}, u32[]{:S(2)}, u32[]{:S(2)}) %collective-permute-start.26) | collective-permute-done | bytes 1048608 | tf_op jit(solution)/shard_map/ppermute | solution.py:61
  836.0 26.5 %convolution_convert_fusion = bf16[2304,2048]{1,0:T(8,128)(2,1)} fusion(bf16[2304,2048]{1,0:T(8,128)(2,1)} %get-tuple-element.168, bf16[2048,2048]{1,0:T(8,128)(2,1)} %get-tuple-element.284), kind=kOutput, calls=%fused_computation.18 | convolution fusion | flops 19332071424 | bytes 27262976 | tf_op jit(solution)/shard_map/dot_general | solution.py:24
  876.5 8.5 collective-permute-done.30
  929.8 44.9 %collective-permute-done.39 = bf16[2,1,4,128,512]{4,3,2,1,0:T(8,128)(2,1)S(1)} collective-permute-done((bf16[2,1,4,128,512]{4,3,2,1,0:T(8,128)(2,1)S(1)}, bf16[2,1,4,128,512]{4,3,2,1,0:T(8,128)(2,1)S(1)}, u32[]{:S(2)}, u32[]{:S(2)}) %collective-permute-start.39) | collective-permute-done | bytes 1048608 | tf_op jit(solution)/shard_map/ppermute | solution.py:61
  1004.2 10.5 collective-permute-done.44
  1038.5 9.8 collective-permute-done.54
  1048.3 17.4 %collective-permute-done.55 = bf16[128,2304]{1,0:T(8,128)(2,1)S(1)} collective-permute-done((bf16[128,2304]{1,0:T(8,128)(2,1)S(1)}, bf16[128,2304]{1,0:T(8,128)(2,1)S(1)}, u32[]{:S(2)}, u32[]{:S(2)}) %collective-permute-start.55) | collective-permute-done | bytes 589856 | tf_op jit(solution)/shard_map/ppermute | solution.py:61
  1075.7 8.7 collective-permute-done.49
  1085.6 11.7 %collective-permute-start.50 = (bf16[128,512]{1,0:T(8,128)(2,1)S(1)}, bf16[128,512]{1,0:T(8,128)(2,1)S(1)}, u32[]{:S(2)}, u32[]{:S(2)}) collective-permute-start(bf16[128,512]{1,0:T(8,128)(2,1)S(1)} %get-tuple-element.330), channel_id=1, source_target_pairs={{0,2},{1,3},{2,0},{3,1},{4,6},{5,7},{6,4},{7,5},{8,10},{9,11},{10,... | collective-permute-start | bytes 393224 | tf_op jit(solution)/shard_map/ppermute | solution.py:61
  (604 shorter events, 442.7 us)
Async XLA Ops:
  7.2 95.5 %all-gather.5.cloned.1.call-start = ((), (), s32[]{:S(2)}) async-start(), calls=%async_computation.5 | async-start | bytes 11354112 | tf_op jit(solution)/shard_map/all_gather | solution.py:246
  11.1 165.1 %all-gather.7.cloned.1.call-start = ((), (), s32[]{:S(2)}) async-start(), calls=%async_computation.6 | async-start | bytes 2654208 | tf_op jit(solution)/shard_map/all_gather | solution.py:304
  114.1 211.6 %all-gather.9.cloned.1.call-start = ((), (), s32[]{:S(2)}) async-start(), calls=%async_computation.7 | async-start | bytes 11894784 | tf_op jit(solution)/shard_map/all_gather | solution.py:343
  114.1 76.2 %collective-permute-start = (bf16[800,2048]{1,0:T(8,128)(2,1)}, bf16[800,2048]{1,0:T(8,128)(2,1)}, u32[]{:S(2)}, u32[]{:S(2)}) collective-permute-start(bf16[800,2048]{1,0:T(8,128)(2,1)} %get-tuple-element.124), channel_id=1, source_target_pairs={{0,16},{8,24},{16,0},{24,8},{1,17},{9,25},{17,1},{25,9},{2,18},{10... | collective-permute-start | bytes 9830408 | tf_op jit(solution)/shard_map/ppermute | solution.py:61
  115.6 74.7 %collective-permute-start.1 = (bf16[800,2048]{1,0:T(8,128)(2,1)}, bf16[800,2048]{1,0:T(8,128)(2,1)}, u32[]{:S(2)}, u32[]{:S(2)}) collective-permute-start(bf16[800,2048]{1,0:T(8,128)(2,1)} %get-tuple-element.125), channel_id=1, source_target_pairs={{0,8},{8,0},{16,24},{24,16},{1,9},{9,1},{17,25},{25,17},{2,10},{10... | collective-permute-start | bytes 9830408 | tf_op jit(solution)/shard_map/ppermute | solution.py:61
  116.2 71.5 %collective-permute-start.2 = (bf16[288,2048]{1,0:T(8,128)(2,1)}, bf16[288,2048]{1,0:T(8,128)(2,1)}, u32[]{:S(2)}, u32[]{:S(2)}) collective-permute-start(bf16[288,2048]{1,0:T(8,128)(2,1)} %pad_maximum_fusion.20), channel_id=1, source_target_pairs={{0,2},{1,3},{2,0},{3,1},{4,6},{5,7},{6,4},{7,5},{8,10},{9,11},{10,... | collective-permute-start | bytes 3538952 | tf_op jit(solution)/shard_map/ppermute | solution.py:61
  117.5 72.8 %collective-permute-start.3 = (bf16[288,2048]{1,0:T(8,128)(2,1)}, bf16[288,2048]{1,0:T(8,128)(2,1)}, u32[]{:S(2)}, u32[]{:S(2)}) collective-permute-start(bf16[288,2048]{1,0:T(8,128)(2,1)} %pad_maximum_fusion.20), channel_id=1, source_target_pairs={{0,4},{1,5},{2,6},{3,7},{4,0},{5,1},{6,2},{7,3},{8,12},{9,13},{10,... | collective-permute-start | bytes 3538952 | tf_op jit(solution)/shard_map/ppermute | solution.py:61
  190.3 276.8 %all-gather.11.cloned.1.call-start = ((), (), s32[]{:S(2)}) async-start(), calls=%async_computation.8 | async-start | bytes 10616832 | tf_op jit(solution)/shard_map/all_gather | solution.py:407
  203.8 99.4 %collective-permute-start.4 = (bf16[800,2048]{1,0:T(8,128)(2,1)}, bf16[800,2048]{1,0:T(8,128)(2,1)}, u32[]{:S(2)}, u32[]{:S(2)}) collective-permute-start(bf16[800,2048]{1,0:T(8,128)(2,1)} %get-tuple-element.124), channel_id=1, source_target_pairs={{0,8},{8,0},{16,24},{24,16},{1,9},{9,1},{17,25},{25,17},{2,10},{10... | collective-permute-start | bytes 9830408 | tf_op jit(solution)/shard_map/ppermute | solution.py:61
  205.2 97.9 %collective-permute-start.5 = (bf16[800,2048]{1,0:T(8,128)(2,1)}, bf16[800,2048]{1,0:T(8,128)(2,1)}, u32[]{:S(2)}, u32[]{:S(2)}) collective-permute-start(bf16[800,2048]{1,0:T(8,128)(2,1)} %get-tuple-element.125), channel_id=1, source_target_pairs={{0,16},{8,24},{16,0},{24,8},{1,17},{9,25},{17,1},{25,9},{2,18},{10... | collective-permute-start | bytes 9830408 | tf_op jit(solution)/shard_map/ppermute | solution.py:61
  223.4 38.4 %collective-permute-start.6 = (bf16[288,2048]{1,0:T(8,128)(2,1)S(1)}, bf16[288,2048]{1,0:T(8,128)(2,1)S(1)}, u32[]{:S(2)}, u32[]{:S(2)}) collective-permute-start(bf16[288,2048]{1,0:T(8,128)(2,1)S(1)} %copy-done.9), channel_id=1, source_target_pairs={{0,6},{1,7},{2,4},{3,5},{4,2},{5,3},{6,0},{7,1},{8,14},{9,15},{10,... | collective-permute-start | bytes 3538952 | tf_op jit(solution)/shard_map/ppermute | solution.py:61
  306.9 51.2 %collective-permute-start.9 = (bf16[1152,2048]{1,0:T(8,128)(2,1)}, bf16[1152,2048]{1,0:T(8,128)(2,1)}, u32[]{:S(2)}, u32[]{:S(2)}) collective-permute-start(bf16[1152,2048]{1,0:T(8,128)(2,1)} %pad_maximum_fusion.4), channel_id=1, source_target_pairs={{0,1},{1,0},{2,3},{3,2},{4,5},{5,4},{6,7},{7,6},{8,9},{9,8},{10,11... | collective-permute-start | bytes 14155784 | tf_op jit(solution)/shard_map/ppermute | solution.py:61
  314.6 39.3 %collective-permute-start.7 = (bf16[400,2048]{1,0:T(8,128)(2,1)}, bf16[400,2048]{1,0:T(8,128)(2,1)}, u32[]{:S(2)}, u32[]{:S(2)}) collective-permute-start(bf16[400,2048]{1,0:T(8,128)(2,1)} %slice.389), channel_id=1, source_target_pairs={{0,8},{8,0},{16,24},{24,16},{1,9},{9,1},{17,25},{25,17},{2,10},{10... | collective-permute-start | bytes 4915208 | tf_op jit(solution)/shard_map/ppermute | solution.py:61
  319.8 38.4 %collective-permute-start.8 = (bf16[400,2048]{1,0:T(8,128)(2,1)}, bf16[400,2048]{1,0:T(8,128)(2,1)}, u32[]{:S(2)}, u32[]{:S(2)}) collective-permute-start(bf16[400,2048]{1,0:T(8,128)(2,1)} %slice.390), channel_id=1, source_target_pairs={{0,16},{8,24},{16,0},{24,8},{1,17},{9,25},{17,1},{25,9},{2,18},{10... | collective-permute-start | bytes 4915208 | tf_op jit(solution)/shard_map/ppermute | solution.py:61
  319.8 39.6 %collective-permute-start.13 = (bf16[288,2048]{1,0:T(8,128)(2,1)S(1)}, bf16[288,2048]{1,0:T(8,128)(2,1)}, u32[]{:S(2)}, u32[]{:S(2)}) collective-permute-start(bf16[288,2048]{1,0:T(8,128)(2,1)S(1)} %copy-done.32), channel_id=1, source_target_pairs={{0,1},{1,0},{2,3},{3,2},{4,5},{5,4},{6,7},{7,6},{8,9},{9,8},{10,11... | collective-permute-start | bytes 3538952 | tf_op jit(solution)/shard_map/ppermute | solution.py:61
  358.2 392.5 %reduce-scatter.6.cloned.1.call-start = ((), (), s32[]{:S(2)}) async-start(), calls=%async_computation.9 | async-start | bytes 5308416 | tf_op jit(solution)/shard_map/reduce_scatter | solution.py:462
  366.3 65.0 %collective-permute-start.11 = (bf16[400,2048]{1,0:T(8,128)(2,1)}, bf16[400,2048]{1,0:T(8,128)(2,1)}, u32[]{:S(2)}, u32[]{:S(2)}) collective-permute-start(bf16[400,2048]{1,0:T(8,128)(2,1)} %slice.406), channel_id=1, source_target_pairs={{0,8},{8,0},{16,24},{24,16},{1,9},{9,1},{17,25},{25,17},{2,10},{10... | collective-permute-start | bytes 4915208 | tf_op jit(solution)/shard_map/ppermute | solution.py:61
  631.9 119.9 %reduce-scatter.8.cloned.1.call-start = ((), (), s32[]{:S(2)}) async-start(), calls=%async_computation.10 | async-start | bytes 5308416 | tf_op jit(solution)/shard_map/reduce_scatter | solution.py:462
  675.5 160.4 %reduce-scatter.10.cloned.1.call-start = ((), (), s32[]{:S(2)}) async-start(), calls=%async_computation.11 | async-start | bytes 1327104 | tf_op jit(solution)/shard_map/reduce_scatter | solution.py:462
  740.7 165.3 %reduce-scatter.12.cloned.1.call-start = ((), (), s32[]{:S(2)}) async-start(), calls=%async_computation.12 | async-start | bytes 2654208 | tf_op jit(solution)/shard_map/reduce_scatter | solution.py:462
  745.5 42.0 %collective-permute-start.28 = (bf16[256,2048]{1,0:T(8,128)(2,1)}, bf16[256,2048]{1,0:T(8,128)(2,1)}, u32[]{:S(2)}, u32[]{:S(2)}) collective-permute-start(bf16[256,2048]{1,0:T(8,128)(2,1)} %get-tuple-element.246), channel_id=1, source_target_pairs={{0,8},{8,0},{16,24},{24,16},{1,9},{9,1},{17,25},{25,17},{2,10},{10... | collective-permute-start | bytes 3145736 | tf_op jit(solution)/shard_map/ppermute | solution.py:61
  746.6 41.8 %collective-permute-start.29 = (bf16[256,2048]{1,0:T(8,128)(2,1)}, bf16[256,2048]{1,0:T(8,128)(2,1)}, u32[]{:S(2)}, u32[]{:S(2)}) collective-permute-start(bf16[256,2048]{1,0:T(8,128)(2,1)} %get-tuple-element.245), channel_id=1, source_target_pairs={{0,16},{8,24},{16,0},{24,8},{1,17},{9,25},{17,1},{25,9},{2,18},{10... | collective-permute-start | bytes 3145736 | tf_op jit(solution)/shard_map/ppermute | solution.py:61
  749.8 55.4 %collective-permute-start.26 = (bf16[256,2048]{1,0:T(8,128)(2,1)}, bf16[256,2048]{1,0:T(8,128)(2,1)}, u32[]{:S(2)}, u32[]{:S(2)}) collective-permute-start(bf16[256,2048]{1,0:T(8,128)(2,1)} %get-tuple-element.248), channel_id=1, source_target_pairs={{0,8},{8,0},{16,24},{24,16},{1,9},{9,1},{17,25},{25,17},{2,10},{10... | collective-permute-start | bytes 3145736 | tf_op jit(solution)/shard_map/ppermute | solution.py:61
  765.0 40.7 %collective-permute-start.27 = (bf16[256,2048]{1,0:T(8,128)(2,1)}, bf16[256,2048]{1,0:T(8,128)(2,1)}, u32[]{:S(2)}, u32[]{:S(2)}) collective-permute-start(bf16[256,2048]{1,0:T(8,128)(2,1)} %get-tuple-element.247), channel_id=1, source_target_pairs={{0,16},{8,24},{16,0},{24,8},{1,17},{9,25},{17,1},{25,9},{2,18},{10... | collective-permute-start | bytes 3145736 | tf_op jit(solution)/shard_map/ppermute | solution.py:61
  836.0 285.1 %reduce-scatter.14.cloned.1.call-start = ((), (), s32[]{:S(2)}) async-start(), calls=%async_computation.13 | async-start | bytes 10616832 | tf_op jit(solution)/shard_map/reduce_scatter | solution.py:462
  921.0 55.0 %collective-permute-start.41 = (bf16[2,1,4,128,640]{4,3,2,1,0:T(8,128)(2,1)S(1)}, bf16[2,1,4,128,640]{4,3,2,1,0:T(8,128)(2,1)S(1)}, u32[]{:S(2)}, u32[]{:S(2)}) collective-permute-start(bf16[2,1,4,128,640]{4,3,2,1,0:T(8,128)(2,1)S(1)} %constant_dynamic-slice_fusion.12), channel_id=1, source_target_pairs={{0,8},{8,0},{16,24},{24,16},{1,9},{9,1},{17,25},{25,17},{2,10},{10... | collective-permute-start | bytes 3932168 | tf_op jit(solution)/shard_map/ppermute | solution.py:61
  922.2 54.2 %collective-permute-start.40 = (bf16[1,2,4,128,640]{4,3,2,1,0:T(8,128)(2,1)S(1)}, bf16[1,2,4,128,640]{4,3,2,1,0:T(8,128)(2,1)S(1)}, u32[]{:S(2)}, u32[]{:S(2)}) collective-permute-start(bf16[1,2,4,128,640]{4,3,2,1,0:T(8,128)(2,1)S(1)} %constant_dynamic-slice_fusion.13), channel_id=1, source_target_pairs={{0,16},{8,24},{16,0},{24,8},{1,17},{9,25},{17,1},{25,9},{2,18},{10... | collective-permute-start | bytes 3932168 | tf_op jit(solution)/shard_map/ppermute | solution.py:61
  923.8 50.9 %collective-permute-start.39 = (bf16[2,1,4,128,512]{4,3,2,1,0:T(8,128)(2,1)S(1)}, bf16[2,1,4,128,512]{4,3,2,1,0:T(8,128)(2,1)S(1)}, u32[]{:S(2)}, u32[]{:S(2)}) collective-permute-start(bf16[2,1,4,128,512]{4,3,2,1,0:T(8,128)(2,1)S(1)} %constant_dynamic-slice_fusion.14), channel_id=1, source_target_pairs={{0,8},{8,0},{16,24},{24,16},{1,9},{9,1},{17,25},{25,17},{2,10},{10... | collective-permute-start | bytes 3145736 | tf_op jit(solution)/shard_map/ppermute | solution.py:61
  925.0 50.6 %collective-permute-start.38 = (bf16[1,2,4,128,512]{4,3,2,1,0:T(8,128)(2,1)S(1)}, bf16[1,2,4,128,512]{4,3,2,1,0:T(8,128)(2,1)S(1)}, u32[]{:S(2)}, u32[]{:S(2)}) collective-permute-start(bf16[1,2,4,128,512]{4,3,2,1,0:T(8,128)(2,1)S(1)} %constant_dynamic-slice_fusion.15), channel_id=1, source_target_pairs={{0,16},{8,24},{16,0},{24,8},{1,17},{9,25},{17,1},{25,9},{2,18},{10... | collective-permute-start | bytes 3145736 | tf_op jit(solution)/shard_map/ppermute | solution.py:61
  1017.9 50.7 %collective-permute-start.48 = (bf16[1,2,4,128,512]{4,3,2,1,0:T(8,128)(2,1)S(1)}, bf16[1,2,4,128,512]{4,3,2,1,0:T(8,128)(2,1)S(1)}, u32[]{:S(2)}, u32[]{:S(2)}) collective-permute-start(bf16[1,2,4,128,512]{4,3,2,1,0:T(8,128)(2,1)S(1)} %constant_dynamic-slice_fusion.5), channel_id=1, source_target_pairs={{0,16},{8,24},{16,0},{24,8},{1,17},{9,25},{17,1},{25,9},{2,18},{10... | collective-permute-start | bytes 3145736 | tf_op jit(solution)/shard_map/ppermute | solution.py:61
  1023.4 42.4 %collective-permute-start.55 = (bf16[128,2304]{1,0:T(8,128)(2,1)S(1)}, bf16[128,2304]{1,0:T(8,128)(2,1)S(1)}, u32[]{:S(2)}, u32[]{:S(2)}) collective-permute-start(bf16[128,2304]{1,0:T(8,128)(2,1)S(1)} %get-tuple-element.275), channel_id=1, source_target_pairs={{0,4},{1,5},{2,6},{3,7},{4,0},{5,1},{6,2},{7,3},{8,12},{9,13},{10,... | collective-permute-start | bytes 1769480 | tf_op jit(solution)/shard_map/ppermute | solution.py:61
  1024.6 41.1 %collective-permute-start.56 = (bf16[128,2304]{1,0:T(8,128)(2,1)S(1)}, bf16[128,2304]{1,0:T(8,128)(2,1)S(1)}, u32[]{:S(2)}, u32[]{:S(2)}) collective-permute-start(bf16[128,2304]{1,0:T(8,128)(2,1)S(1)} %get-tuple-element.274), channel_id=1, source_target_pairs={{0,6},{1,7},{2,4},{3,5},{4,2},{5,3},{6,0},{7,1},{8,14},{9,15},{10,... | collective-permute-start | bytes 1769480 | tf_op jit(solution)/shard_map/ppermute | solution.py:61
  (165 other events, 2307.9 us)
Sparse Core Ops, SparseCore 0:
  11.6 91.0 all-gather.4
  114.2 61.9 all-gather.6
  190.5 131.6 all-gather.8
  358.3 87.6 all-gather.10
  631.1 53.0 reduce-scatter.5
  686.3 53.3 reduce-scatter.7
  742.6 31.4 reduce-scatter.9
  836.1 34.6 reduce-scatter.11
  906.2 97.4 reduce-scatter.13

commit v10 on v9

--- a/solution.py
+++ b/solution.py
@@ -513,9 +513,10 @@
     out_grad = jnp.concatenate([attn_grad, rank_out_grad], axis=1)
     context_grad = product(out_grad, out_weight, contract_last)
     grad_rows = convert_half(context_grad).reshape(row_total, HD)
+    down_partial = down_product(0, width)
     if row_size == 4:
-        *sums, far_x, far_y, grad_rows, free_x, free_y = tie(
-            *gate_free, *gate_last, *up_far, grad_rows, *up_free
+        *sums, far_x, far_y, grad_rows, free_x, free_y, down_partial = tie(
+            *gate_free, *gate_last, *up_far, grad_rows, *up_free, down_partial
         )
         gate_free, gate_last = sums[:2], sums[2:]
         up_last = add_pair(up_last, (far_x, far_y))
@@ -535,7 +536,6 @@
     keyval_part = jnp.concatenate([convert_half(key_acc), convert_half(value_acc)], axis=1)
     keyval_part, rank_sums = tie(keyval_part, rank_sums)
     keyval_sum = col_sum(keyval_part)
-    down_partial = down_product(0, width)
     if row_size == 4:
         *up_free, down_partial, normed_both, context_both, last_x, last_y = tie(
             *up_free, down_partial, normed_both, context_both, *up_last

time: 1140 us -> 1130 us (level)
  waiting for transfers between devices: 394 us -> 369 us
    ppermute x58, waiting for transfers between devices: 265 us -> 240 us  [swap(): return lax.ppermute(values, axis, [(i, i ^ bit) for i in range(size)])]
    unnamed x271 -> x255, local copies, waits for them, and re-layouts: 62.5 us -> 58.9 us
  transfers between devices with their start and end apart: 67 -> 67, of which waited for: 32 -> 29; matrix products, arithmetic and copies ran while one was open for 43% -> 44% of each run, Pallas kernels for 0% -> 0%
where the time goes in v10:
time: 1130 us; the launch traced here: 1120 us
  waiting for transfers between devices  369 us (33%)
  matrix products  352 us (31%)
  local copies, waits for them, and re-layouts  167 us (15%)
  other arithmetic  147 us (13%)
  starting transfers between devices  66.4 us (6%)
  between operations  16.1 us (1%)
    ppermute x58, waiting for transfers between devices, swap(): return lax.ppermute(values, axis, [(i, i ^ bit) for i in range(size)])  240 us
    dot_general x22, matrix products, product(): lax.dot_general(left_side, right_side, dims, preferred_element_type=jnp.f...  237 us
    dot_general x9, matrix products, matrix_product(): return jnp.dot(left_side, right_side, preferred_element_type=jnp.float32)  114 us
    all_gather x1, waiting for transfers between devices, per_device(): lax.all_gather(jnp.concatenate([convert_half(query_matrix), convert_half(...  76.4 us
    ppermute x58, starting transfers between devices, swap(): return lax.ppermute(values, axis, [(i, i ^ bit) for i in range(size)])  65.1 us
    convert_element_type x23, other arithmetic, convert_half(): return values.astype(jnp.bfloat16)  62.8 us
    unnamed x255, local copies, waits for them, and re-layouts  58.9 us
    all_gather x1, waiting for transfers between devices, per_device(): lax.all_gather(jnp.concatenate([convert_half(rotate(keyval_pre[:, :HD], c...  52.2 us
  transfers between devices with their start and end apart: 67, of which 29 were waited for; matrix products, arithmetic and copies ran while one was open for 44% of the time, Pallas kernels for 0%

profile of v10, /device:TPU:0, one launch (start us, length us, event | category | flops | bytes accessed | tf_op | source)
XLA Modules:
  0.0 1117.0 jit_solution(8248665936681402283)
XLA Ops:
  26.3 76.4 %all-gather.5.cloned.1.call-done = bf16[2048,2688]{1,0:T(8,128)(2,1)} async-done(((bf16[64,2688]{1,0:T(8,128)(2,1)}), bf16[2048,2688]{1,0:T(8,128)(2,1)}) %all-gather.5.cloned.1.call-update) | async-done | bytes 11010064 | tf_op jit(solution)/shard_map/all_gather | solution.py:246
  124.0 52.2 %all-gather.7.cloned.1.call-done = bf16[2304,512]{1,0:T(8,128)(2,1)} async-done(((bf16[288,512]{1,0:T(8,128)(2,1)}), bf16[2304,512]{1,0:T(8,128)(2,1)}) %all-gather.7.cloned.1.call-update) | async-done | bytes 2359312 | tf_op jit(solution)/shard_map/all_gather | solution.py:304
  176.1 11.5 %collective-permute-done.2 = bf16[288,2048]{1,0:T(8,128)(2,1)} collective-permute-done((bf16[288,2048]{1,0:T(8,128)(2,1)}, bf16[288,2048]{1,0:T(8,128)(2,1)}, u32[]{:S(2)}, u32[]{:S(2)}) %collective-permute-start.2) | collective-permute-done | bytes 1179680 | tf_op jit(solution)/shard_map/ppermute | solution.py:61
  205.7 8.6 fusion.144
  225.3 8.8 fusion.145
  242.8 18.6 %collective-permute-done.6 = bf16[288,2048]{1,0:T(8,128)(2,1)S(1)} collective-permute-done((bf16[288,2048]{1,0:T(8,128)(2,1)S(1)}, bf16[288,2048]{1,0:T(8,128)(2,1)S(1)}, u32[]{:S(2)}, u32[]{:S(2)}) %collective-permute-start.6) | collective-permute-done | bytes 1179680 | tf_op jit(solution)/shard_map/ppermute | solution.py:61
  261.4 41.7 %collective-permute-done.4 = bf16[800,2048]{1,0:T(8,128)(2,1)} collective-permute-done((bf16[800,2048]{1,0:T(8,128)(2,1)}, bf16[800,2048]{1,0:T(8,128)(2,1)}, u32[]{:S(2)}, u32[]{:S(2)}) %collective-permute-start.4) | collective-permute-done | bytes 3276832 | tf_op jit(solution)/shard_map/ppermute | solution.py:61
  325.6 8.1 fusion.15
  344.5 9.3 collective-permute-done.7
  412.1 12.1 %collective-permute-done.10 = bf16[400,2048]{1,0:T(8,128)(2,1)S(1)} collective-permute-done((bf16[400,2048]{1,0:T(8,128)(2,1)S(1)}, bf16[400,2048]{1,0:T(8,128)(2,1)S(1)}, u32[]{:S(2)}, u32[]{:S(2)}) %collective-permute-start.10) | collective-permute-done | bytes 1638432 | tf_op jit(solution)/shard_map/ppermute | solution.py:61
  437.7 29.5 %fusion.17 = f32[2304,2048]{1,0:T(8,128)} fusion(bf16[2304,2048]{1,0:T(8,128)(2,1)} %get-tuple-element.291, bf16[2304,256]{1,0:T(8,128)(2,1)S(1)} %copy.37, bf16[2304,2048]{1,0:T(8,128)(2,1)} %slice_dynamic-update-slice_fusion.11), kind=kOutput, calls=%fused_computation.34 | convolution fusion | flops 21764505600 | bytes 38928384 | tf_op jit(solution)/shard_map/dot_general | solution.py:28
  467.2 27.0 %fusion.148 = f32[2304,2048]{1,0:T(8,128)} fusion(bf16[2304,2048]{1,0:T(8,128)(2,1)} %all-gather.11.cloned.1.call-done, bf16[2048,2048]{1,0:T(8,128)(2,1)} %slice_dynamic-update-slice_fusion.15), kind=kOutput, calls=%fused_computation.378 | convolution fusion | flops 19327352832 | bytes 36700160 | tf_op jit(solution)/shard_map/dot_general | solution.py:28
  494.2 24.4 %fusion.147 = f32[2304,2048]{1,0:T(8,128)} fusion(bf16[2304,2048]{1,0:T(8,128)(2,1)S(1)} %copy-done.100, bf16[2048,2048]{1,0:T(8,128)(2,1)} %slice_dynamic-update-slice_fusion.20), kind=kOutput, calls=%fused_computation.377 | convolution fusion | flops 19327352832 | bytes 36700160 | tf_op jit(solution)/shard_map/dot_general | solution.py:28
  518.7 29.9 %multiply_convert_fusion.1 = (bf16[2304,2048]{1,0:T(8,128)(2,1)}, bf16[2304,2048]{1,0:T(8,128)(2,1)}, bf16[2304,2048]{1,0:T(8,128)(2,1)}) fusion(f32[2304,2048]{1,0:T(8,128)S(1)} %bitcast.91, f32[2304,2048]{1,0:T(8,128)} %fusion.147, f32[2304,2048]{1,0:T(8,128)} %fusion.148), kind=kLoop, calls=%fused_computation.15 | loop fusion | flops 122683392 | bytes 84934656 | tf_op jit(solution)/shard_map/convert_element_type | solution.py:20
  548.5 28.7 %convolution_convert_fusion.1 = bf16[2304,2048]{1,0:T(8,128)(2,1)S(1)} fusion(bf16[2304,2048]{1,0:T(8,128)(2,1)} %get-tuple-element.167, bf16[2304,256]{1,0:T(8,128)(2,1)} %copy-done.69, bf16[2304,2048]{1,0:T(8,128)(2,1)} %slice_dynamic-update-slice_fusion.11), kind=kOutput, calls=%fused_computation.19 | convolution fusion | flops 21769224192 | bytes 29491200 | tf_op jit(solution)/shard_map/dot_general | solution.py:24
  587.1 14.8 %fusion.22 = f32[2304,1024]{1,0:T(8,128)} fusion(bf16[2304,2048]{1,0:T(8,128)(2,1)S(1)} %copy-done.13, bf16[2048,2048]{1,0:T(8,128)(2,1)} %slice_dynamic-update-slice_fusion.20), kind=kOutput, calls=%fused_computation.50 | convolution fusion | flops 9663676416 | bytes 23068672 | tf_op jit(solution)/shard_map/dot_general | solution.py:24
  606.2 14.9 %add_convert_fusion.1 = bf16[2304,1024]{1,0:T(8,128)(2,1)} fusion(f32[2304,1024]{1,0:T(8,128)} %fusion.22, bf16[2304,2048]{1,0:T(8,128)(2,1)S(1)} %bitcast.99, bf16[2048,2048]{1,0:T(8,128)(2,1)} %slice_dynamic-update-slice_fusion.15), kind=kOutput, calls=%fused_computation.22 | convolution fusion | flops 9668395008 | bytes 27787264 | tf_op jit(solution)/shard_map/dot_general | solution.py:24
  623.1 7.9 collective-permute-done.17
  650.5 16.7 %fusion.18 = f32[2304,1024]{1,0:T(8,128)} fusion(bf16[2304,2048]{1,0:T(8,128)(2,1)} %get-tuple-element.161, bf16[2048,2048]{1,0:T(8,128)(2,1)} %slice_dynamic-update-slice_fusion.15), kind=kOutput, calls=%fused_computation.46 | convolution fusion | flops 9663676416 | bytes 23068672 | tf_op jit(solution)/shard_map/dot_general | solution.py:24
  667.2 15.0 %add_convert_fusion = bf16[2304,1024]{1,0:T(8,128)(2,1)} fusion(f32[2304,1024]{1,0:T(8,128)} %fusion.18, bf16[2304,2048]{1,0:T(8,128)(2,1)S(1)} %bitcast.101, bf16[2048,2048]{1,0:T(8,128)(2,1)} %slice_dynamic-update-slice_fusion.20), kind=kOutput, calls=%fused_computation.21 | convolution fusion | flops 9668395008 | bytes 27787264 | tf_op jit(solution)/shard_map/dot_general | solution.py:24
  682.3 25.4 %convolution_convert_fusion.4 = bf16[2048,2048]{1,0:T(8,128)(2,1)S(1)} fusion(bf16[2304,2048]{1,0:T(8,128)(2,1)} %all-gather.11.cloned.1.call-done, bf16[2304,2048]{1,0:T(8,128)(2,1)} %get-tuple-element.158), kind=kOutput, calls=%fused_computation.33 | convolution fusion | flops 19331547136 | bytes 27262976 | tf_op jit(solution)/shard_map/dot_general | solution.py:24
  716.4 26.0 %convolution_convert_fusion = bf16[2304,2048]{1,0:T(8,128)(2,1)} fusion(bf16[2304,2048]{1,0:T(8,128)(2,1)} %get-tuple-element.167, bf16[2048,2048]{1,0:T(8,128)(2,1)} %get-tuple-element.286), kind=kOutput, calls=%fused_computation.18 | convolution fusion | flops 19332071424 | bytes 27262976 | tf_op jit(solution)/shard_map/dot_general | solution.py:24
  742.4 26.4 %convolution_convert_fusion.3 = bf16[2048,2048]{1,0:T(8,128)(2,1)} fusion(bf16[2304,2048]{1,0:T(8,128)(2,1)} %all-gather.11.cloned.1.call-done, bf16[2304,2048]{1,0:T(8,128)(2,1)} %get-tuple-element.161), kind=kOutput, calls=%fused_computation.32 | convolution fusion | flops 19331547136 | bytes 27262976 | tf_op jit(solution)/shard_map/dot_general | solution.py:24
  801.1 15.4 %collective-permute-done.26 = bf16[256,2048]{1,0:T(8,128)(2,1)} collective-permute-done((bf16[256,2048]{1,0:T(8,128)(2,1)}, bf16[256,2048]{1,0:T(8,128)(2,1)}, u32[]{:S(2)}, u32[]{:S(2)}) %collective-permute-start.26) | collective-permute-done | bytes 1048608 | tf_op jit(solution)/shard_map/ppermute | solution.py:61
  823.1 8.1 multiply_convert_fusion
  915.1 44.1 %collective-permute-done.39 = bf16[2,1,4,128,512]{4,3,2,1,0:T(8,128)(2,1)S(1)} collective-permute-done((bf16[2,1,4,128,512]{4,3,2,1,0:T(8,128)(2,1)S(1)}, bf16[2,1,4,128,512]{4,3,2,1,0:T(8,128)(2,1)S(1)}, u32[]{:S(2)}, u32[]{:S(2)}) %collective-permute-start.39) | collective-permute-done | bytes 1048608 | tf_op jit(solution)/shard_map/ppermute | solution.py:61
  988.7 10.9 collective-permute-done.44
  1024.2 10.4 collective-permute-done.54
  1034.7 17.1 %collective-permute-done.55 = bf16[128,2304]{1,0:T(8,128)(2,1)S(1)} collective-permute-done((bf16[128,2304]{1,0:T(8,128)(2,1)S(1)}, bf16[128,2304]{1,0:T(8,128)(2,1)S(1)}, u32[]{:S(2)}, u32[]{:S(2)}) %collective-permute-start.55) | collective-permute-done | bytes 589856 | tf_op jit(solution)/shard_map/ppermute | solution.py:61
  1061.6 8.7 collective-permute-done.49
  1071.6 11.6 %collective-permute-start.50 = (bf16[128,512]{1,0:T(8,128)(2,1)S(1)}, bf16[128,512]{1,0:T(8,128)(2,1)S(1)}, u32[]{:S(2)}, u32[]{:S(2)}) collective-permute-start(bf16[128,512]{1,0:T(8,128)(2,1)S(1)} %get-tuple-element.332), channel_id=1, source_target_pairs={{0,2},{1,3},{2,0},{3,1},{4,6},{5,7},{6,4},{7,5},{8,10},{9,11},{10,... | collective-permute-start | bytes 393224 | tf_op jit(solution)/shard_map/ppermute | solution.py:61
  1087.5 8.1 collective-permute-done.51
  (587 shorter events, 432.8 us)
Async XLA Ops:
  7.2 95.5 %all-gather.5.cloned.1.call-start = ((), (), s32[]{:S(2)}) async-start(), calls=%async_computation.5 | async-start | bytes 11354112 | tf_op jit(solution)/shard_map/all_gather | solution.py:246
  11.1 165.1 %all-gather.7.cloned.1.call-start = ((), (), s32[]{:S(2)}) async-start(), calls=%async_computation.6 | async-start | bytes 2654208 | tf_op jit(solution)/shard_map/all_gather | solution.py:304
  114.1 211.5 %all-gather.9.cloned.1.call-start = ((), (), s32[]{:S(2)}) async-start(), calls=%async_computation.7 | async-start | bytes 11894784 | tf_op jit(solution)/shard_map/all_gather | solution.py:343
  114.1 76.2 %collective-permute-start = (bf16[800,2048]{1,0:T(8,128)(2,1)}, bf16[800,2048]{1,0:T(8,128)(2,1)}, u32[]{:S(2)}, u32[]{:S(2)}) collective-permute-start(bf16[800,2048]{1,0:T(8,128)(2,1)} %get-tuple-element.125), channel_id=1, source_target_pairs={{0,16},{8,24},{16,0},{24,8},{1,17},{9,25},{17,1},{25,9},{2,18},{10... | collective-permute-start | bytes 9830408 | tf_op jit(solution)/shard_map/ppermute | solution.py:61
  115.6 74.7 %collective-permute-start.1 = (bf16[800,2048]{1,0:T(8,128)(2,1)}, bf16[800,2048]{1,0:T(8,128)(2,1)}, u32[]{:S(2)}, u32[]{:S(2)}) collective-permute-start(bf16[800,2048]{1,0:T(8,128)(2,1)} %get-tuple-element.126), channel_id=1, source_target_pairs={{0,8},{8,0},{16,24},{24,16},{1,9},{9,1},{17,25},{25,17},{2,10},{10... | collective-permute-start | bytes 9830408 | tf_op jit(solution)/shard_map/ppermute | solution.py:61
  116.2 71.5 %collective-permute-start.2 = (bf16[288,2048]{1,0:T(8,128)(2,1)}, bf16[288,2048]{1,0:T(8,128)(2,1)}, u32[]{:S(2)}, u32[]{:S(2)}) collective-permute-start(bf16[288,2048]{1,0:T(8,128)(2,1)} %pad_maximum_fusion.20), channel_id=1, source_target_pairs={{0,2},{1,3},{2,0},{3,1},{4,6},{5,7},{6,4},{7,5},{8,10},{9,11},{10,... | collective-permute-start | bytes 3538952 | tf_op jit(solution)/shard_map/ppermute | solution.py:61
  117.5 72.8 %collective-permute-start.3 = (bf16[288,2048]{1,0:T(8,128)(2,1)}, bf16[288,2048]{1,0:T(8,128)(2,1)}, u32[]{:S(2)}, u32[]{:S(2)}) collective-permute-start(bf16[288,2048]{1,0:T(8,128)(2,1)} %pad_maximum_fusion.20), channel_id=1, source_target_pairs={{0,4},{1,5},{2,6},{3,7},{4,0},{5,1},{6,2},{7,3},{8,12},{9,13},{10,... | collective-permute-start | bytes 3538952 | tf_op jit(solution)/shard_map/ppermute | solution.py:61
  190.3 276.9 %all-gather.11.cloned.1.call-start = ((), (), s32[]{:S(2)}) async-start(), calls=%async_computation.8 | async-start | bytes 10616832 | tf_op jit(solution)/shard_map/all_gather | solution.py:407
  203.7 99.4 %collective-permute-start.4 = (bf16[800,2048]{1,0:T(8,128)(2,1)}, bf16[800,2048]{1,0:T(8,128)(2,1)}, u32[]{:S(2)}, u32[]{:S(2)}) collective-permute-start(bf16[800,2048]{1,0:T(8,128)(2,1)} %get-tuple-element.125), channel_id=1, source_target_pairs={{0,8},{8,0},{16,24},{24,16},{1,9},{9,1},{17,25},{25,17},{2,10},{10... | collective-permute-start | bytes 9830408 | tf_op jit(solution)/shard_map/ppermute | solution.py:61
  205.2 97.9 %collective-permute-start.5 = (bf16[800,2048]{1,0:T(8,128)(2,1)}, bf16[800,2048]{1,0:T(8,128)(2,1)}, u32[]{:S(2)}, u32[]{:S(2)}) collective-permute-start(bf16[800,2048]{1,0:T(8,128)(2,1)} %get-tuple-element.126), channel_id=1, source_target_pairs={{0,16},{8,24},{16,0},{24,8},{1,17},{9,25},{17,1},{25,9},{2,18},{10... | collective-permute-start | bytes 9830408 | tf_op jit(solution)/shard_map/ppermute | solution.py:61
  306.8 51.2 %collective-permute-start.9 = (bf16[1152,2048]{1,0:T(8,128)(2,1)}, bf16[1152,2048]{1,0:T(8,128)(2,1)}, u32[]{:S(2)}, u32[]{:S(2)}) collective-permute-start(bf16[1152,2048]{1,0:T(8,128)(2,1)} %pad_maximum_fusion.4), channel_id=1, source_target_pairs={{0,1},{1,0},{2,3},{3,2},{4,5},{5,4},{6,7},{7,6},{8,9},{9,8},{10,11... | collective-permute-start | bytes 14155784 | tf_op jit(solution)/shard_map/ppermute | solution.py:61
  358.1 423.0 %reduce-scatter.6.cloned.1.call-start = ((), (), s32[]{:S(2)}) async-start(), calls=%async_computation.9 | async-start | bytes 5308416 | tf_op jit(solution)/shard_map/reduce_scatter | solution.py:462
  366.2 65.0 %collective-permute-start.11 = (bf16[400,2048]{1,0:T(8,128)(2,1)}, bf16[400,2048]{1,0:T(8,128)(2,1)}, u32[]{:S(2)}, u32[]{:S(2)}) collective-permute-start(bf16[400,2048]{1,0:T(8,128)(2,1)} %slice.406), channel_id=1, source_target_pairs={{0,8},{8,0},{16,24},{24,16},{1,9},{9,1},{17,25},{25,17},{2,10},{10... | collective-permute-start | bytes 4915208 | tf_op jit(solution)/shard_map/ppermute | solution.py:61
  632.0 150.2 %reduce-scatter.8.cloned.1.call-start = ((), (), s32[]{:S(2)}) async-start(), calls=%async_computation.10 | async-start | bytes 5308416 | tf_op jit(solution)/shard_map/reduce_scatter | solution.py:462
  640.4 41.8 %collective-permute-start.20 = (bf16[288,2048]{1,0:T(8,128)(2,1)}, bf16[288,2048]{1,0:T(8,128)(2,1)S(1)}, u32[]{:S(2)}, u32[]{:S(2)}) collective-permute-start(bf16[288,2048]{1,0:T(8,128)(2,1)} %get-tuple-element.154), channel_id=1, source_target_pairs={{0,8},{8,0},{16,24},{24,16},{1,9},{9,1},{17,25},{25,17},{2,10},{10... | collective-permute-start | bytes 3538952 | tf_op jit(solution)/shard_map/ppermute | solution.py:61
  642.0 40.3 %collective-permute-start.21 = (bf16[288,2048]{1,0:T(8,128)(2,1)}, bf16[288,2048]{1,0:T(8,128)(2,1)}, u32[]{:S(2)}, u32[]{:S(2)}) collective-permute-start(bf16[288,2048]{1,0:T(8,128)(2,1)} %pad_maximum_fusion.17), channel_id=1, source_target_pairs={{0,16},{8,24},{16,0},{24,8},{1,17},{9,25},{17,1},{25,9},{2,18},{10... | collective-permute-start | bytes 3538952 | tf_op jit(solution)/shard_map/ppermute | solution.py:61
  646.5 61.4 %collective-permute-start.19 = (bf16[288,2048]{1,0:T(8,128)(2,1)}, bf16[288,2048]{1,0:T(8,128)(2,1)}, u32[]{:S(2)}, u32[]{:S(2)}) collective-permute-start(bf16[288,2048]{1,0:T(8,128)(2,1)} %add_convert_fusion.4), channel_id=1, source_target_pairs={{0,16},{8,24},{16,0},{24,8},{1,17},{9,25},{17,1},{25,9},{2,18},{10... | collective-permute-start | bytes 3538952 | tf_op jit(solution)/shard_map/ppermute | solution.py:61
  650.1 57.7 %collective-permute-start.18 = (bf16[288,2048]{1,0:T(8,128)(2,1)}, bf16[288,2048]{1,0:T(8,128)(2,1)S(1)}, u32[]{:S(2)}, u32[]{:S(2)}) collective-permute-start(bf16[288,2048]{1,0:T(8,128)(2,1)} %add_convert_fusion.5), channel_id=1, source_target_pairs={{0,8},{8,0},{16,24},{24,16},{1,9},{9,1},{17,25},{25,17},{2,10},{10... | collective-permute-start | bytes 3538952 | tf_op jit(solution)/shard_map/ppermute | solution.py:61
  682.3 165.1 %reduce-scatter.10.cloned.1.call-start = ((), (), s32[]{:S(2)}) async-start(), calls=%async_computation.11 | async-start | bytes 1327104 | tf_op jit(solution)/shard_map/reduce_scatter | solution.py:462
  712.4 56.6 %collective-permute-start.24 = (bf16[256,2048]{1,0:T(8,128)(2,1)}, bf16[256,2048]{1,0:T(8,128)(2,1)S(1)}, u32[]{:S(2)}, u32[]{:S(2)}) collective-permute-start(bf16[256,2048]{1,0:T(8,128)(2,1)} %get-tuple-element.252), channel_id=1, source_target_pairs={{0,8},{8,0},{16,24},{24,16},{1,9},{9,1},{17,25},{25,17},{2,10},{10... | collective-permute-start | bytes 3145736 | tf_op jit(solution)/shard_map/ppermute | solution.py:61
  713.6 55.3 %collective-permute-start.25 = (bf16[256,2048]{1,0:T(8,128)(2,1)}, bf16[256,2048]{1,0:T(8,128)(2,1)S(1)}, u32[]{:S(2)}, u32[]{:S(2)}) collective-permute-start(bf16[256,2048]{1,0:T(8,128)(2,1)} %get-tuple-element.251), channel_id=1, source_target_pairs={{0,16},{8,24},{16,0},{24,8},{1,17},{9,25},{17,1},{25,9},{2,18},{10... | collective-permute-start | bytes 3145736 | tf_op jit(solution)/shard_map/ppermute | solution.py:61
  715.0 71.9 %collective-permute-start.22 = (bf16[256,2048]{1,0:T(8,128)(2,1)}, bf16[256,2048]{1,0:T(8,128)(2,1)}, u32[]{:S(2)}, u32[]{:S(2)}) collective-permute-start(bf16[256,2048]{1,0:T(8,128)(2,1)} %get-tuple-element.254), channel_id=1, source_target_pairs={{0,8},{8,0},{16,24},{24,16},{1,9},{9,1},{17,25},{25,17},{2,10},{10... | collective-permute-start | bytes 3145736 | tf_op jit(solution)/shard_map/ppermute | solution.py:61
  716.2 82.3 %collective-permute-start.23 = (bf16[256,2048]{1,0:T(8,128)(2,1)}, bf16[256,2048]{1,0:T(8,128)(2,1)}, u32[]{:S(2)}, u32[]{:S(2)}) collective-permute-start(bf16[256,2048]{1,0:T(8,128)(2,1)} %get-tuple-element.253), channel_id=1, source_target_pairs={{0,16},{8,24},{16,0},{24,8},{1,17},{9,25},{17,1},{25,9},{2,18},{10... | collective-permute-start | bytes 3145736 | tf_op jit(solution)/shard_map/ppermute | solution.py:61
  768.9 121.4 %reduce-scatter.12.cloned.1.call-start = ((), (), s32[]{:S(2)}) async-start(), calls=%async_computation.12 | async-start | bytes 2654208 | tf_op jit(solution)/shard_map/reduce_scatter | solution.py:462
  847.4 260.0 %reduce-scatter.14.cloned.1.call-start = ((), (), s32[]{:S(2)}) async-start(), calls=%async_computation.13 | async-start | bytes 10616832 | tf_op jit(solution)/shard_map/reduce_scatter | solution.py:462
  905.4 55.4 %collective-permute-start.41 = (bf16[2,1,4,128,640]{4,3,2,1,0:T(8,128)(2,1)S(1)}, bf16[2,1,4,128,640]{4,3,2,1,0:T(8,128)(2,1)S(1)}, u32[]{:S(2)}, u32[]{:S(2)}) collective-permute-start(bf16[2,1,4,128,640]{4,3,2,1,0:T(8,128)(2,1)S(1)} %constant_dynamic-slice_fusion.12), channel_id=1, source_target_pairs={{0,8},{8,0},{16,24},{24,16},{1,9},{9,1},{17,25},{25,17},{2,10},{10... | collective-permute-start | bytes 3932168 | tf_op jit(solution)/shard_map/ppermute | solution.py:61
  907.0 54.2 %collective-permute-start.40 = (bf16[1,2,4,128,640]{4,3,2,1,0:T(8,128)(2,1)S(1)}, bf16[1,2,4,128,640]{4,3,2,1,0:T(8,128)(2,1)S(1)}, u32[]{:S(2)}, u32[]{:S(2)}) collective-permute-start(bf16[1,2,4,128,640]{4,3,2,1,0:T(8,128)(2,1)S(1)} %constant_dynamic-slice_fusion.13), channel_id=1, source_target_pairs={{0,16},{8,24},{16,0},{24,8},{1,17},{9,25},{17,1},{25,9},{2,18},{10... | collective-permute-start | bytes 3932168 | tf_op jit(solution)/shard_map/ppermute | solution.py:61
  909.3 49.8 %collective-permute-start.39 = (bf16[2,1,4,128,512]{4,3,2,1,0:T(8,128)(2,1)S(1)}, bf16[2,1,4,128,512]{4,3,2,1,0:T(8,128)(2,1)S(1)}, u32[]{:S(2)}, u32[]{:S(2)}) collective-permute-start(bf16[2,1,4,128,512]{4,3,2,1,0:T(8,128)(2,1)S(1)} %constant_dynamic-slice_fusion.14), channel_id=1, source_target_pairs={{0,8},{8,0},{16,24},{24,16},{1,9},{9,1},{17,25},{25,17},{2,10},{10... | collective-permute-start | bytes 3145736 | tf_op jit(solution)/shard_map/ppermute | solution.py:61
  910.0 50.5 %collective-permute-start.38 = (bf16[1,2,4,128,512]{4,3,2,1,0:T(8,128)(2,1)S(1)}, bf16[1,2,4,128,512]{4,3,2,1,0:T(8,128)(2,1)S(1)}, u32[]{:S(2)}, u32[]{:S(2)}) collective-permute-start(bf16[1,2,4,128,512]{4,3,2,1,0:T(8,128)(2,1)S(1)} %constant_dynamic-slice_fusion.15), channel_id=1, source_target_pairs={{0,16},{8,24},{16,0},{24,8},{1,17},{9,25},{17,1},{25,9},{2,18},{10... | collective-permute-start | bytes 3145736 | tf_op jit(solution)/shard_map/ppermute | solution.py:61
  1002.4 52.2 %collective-permute-start.48 = (bf16[1,2,4,128,512]{4,3,2,1,0:T(8,128)(2,1)S(1)}, bf16[1,2,4,128,512]{4,3,2,1,0:T(8,128)(2,1)S(1)}, u32[]{:S(2)}, u32[]{:S(2)}) collective-permute-start(bf16[1,2,4,128,512]{4,3,2,1,0:T(8,128)(2,1)S(1)} %constant_dynamic-slice_fusion.5), channel_id=1, source_target_pairs={{0,16},{8,24},{16,0},{24,8},{1,17},{9,25},{17,1},{25,9},{2,18},{10... | collective-permute-start | bytes 3145736 | tf_op jit(solution)/shard_map/ppermute | solution.py:61
  1009.3 42.4 %collective-permute-start.55 = (bf16[128,2304]{1,0:T(8,128)(2,1)S(1)}, bf16[128,2304]{1,0:T(8,128)(2,1)S(1)}, u32[]{:S(2)}, u32[]{:S(2)}) collective-permute-start(bf16[128,2304]{1,0:T(8,128)(2,1)S(1)} %get-tuple-element.277), channel_id=1, source_target_pairs={{0,4},{1,5},{2,6},{3,7},{4,0},{5,1},{6,2},{7,3},{8,12},{9,13},{10,... | collective-permute-start | bytes 1769480 | tf_op jit(solution)/shard_map/ppermute | solution.py:61
  1010.3 41.4 %collective-permute-start.56 = (bf16[128,2304]{1,0:T(8,128)(2,1)S(1)}, bf16[128,2304]{1,0:T(8,128)(2,1)S(1)}, u32[]{:S(2)}, u32[]{:S(2)}) collective-permute-start(bf16[128,2304]{1,0:T(8,128)(2,1)S(1)} %get-tuple-element.276), channel_id=1, source_target_pairs={{0,6},{1,7},{2,4},{3,5},{4,2},{5,3},{6,0},{7,1},{8,14},{9,15},{10,... | collective-permute-start | bytes 1769480 | tf_op jit(solution)/shard_map/ppermute | solution.py:61
  (157 other events, 2203.1 us)
Sparse Core Ops, SparseCore 0:
  11.6 91.0 all-gather.4
  114.2 61.9 all-gather.6
  190.5 131.6 all-gather.8
  358.2 87.8 all-gather.10
  631.2 53.1 reduce-scatter.5
  686.5 53.3 reduce-scatter.7
  769.0 30.8 reduce-scatter.9
  847.6 34.8 reduce-scatter.11
  890.4 97.8 reduce-scatter.13
